TPU v7x, 256 devices: a whole 4x4x8 slice. The times are simulated.
256 devices in a mesh: seq: 32 (over z, x), head: 8 (over y, core).
Axes of the slice: x: 4, y: 4, z: 8, core: 2. Of those that a mesh axis runs over, the one named last changes fastest.
Arguments:
- corpus: bfloat16 [128, 128, 4096], P('seq'), may hold values from -8 to 8
- enc_qkv: bfloat16 [4096, 16, 3, 128], P(None, 'head'), may hold values from -0.1015625 to 0.1015625
- enc_out: bfloat16 [16, 128, 4096], P('head'), may hold values from -0.375 to 0.375
- cca_kv: bfloat16 [4096, 16, 2, 128], P('seq', 'head'), may hold values from -0.09375 to 0.09375
- gain_in: float32 [4096], replicated, may hold values from 0.5 to 2
- gain_out: float32 [4096], replicated, may hold values from 0.5 to 2
- queries: bfloat16 [16384, 16, 128], P('seq', 'head'), may hold values from -100 to 100
- nbr_ids: int32 [256, 2], P('seq'), may hold values from 0 to 127, as said below
Outputs:
- cca_out: bfloat16 [16384, 16, 128], P('seq', 'head')
Inputs may be any that keep to these rules, and one draw needn't show every extreme that they name: `nbr_ids`: entry [u, n] is the corpus row of group u's n-th neighbour; row r is held by index r // 4 of seq. The neighbours of one group differ. Among the requests of the 8 groups of one index of seq no owner is named more than 2 times, and in every draw some owner is named exactly 2 times by every index of seq.
All inputs are finite; a program needn't handle non-finite values.
Results may differ from a plain program's by a relative error of at most 0.03.
Values may be sent and summed in bfloat16 or wider, within the bound.
No kernel may reach another device: no remote copies, remote signals or barrier semaphores. Data moves between devices by JAX's collectives and lax.ppermute only.
A program may use at most 128 MiB of HBM per device.

v0:
```python
import jax
import jax.numpy as jnp
from jax import lax
from jax.sharding import PartitionSpec as P

GROUP = 64
NBRS = 2
CAP = 2


EPS = 1e-06


def passed_along(value, axis, steps):
    count = lax.axis_size(axis)
    first, last = (max(0, -steps), min(count, count - steps))
    return lax.ppermute(value, axis, [(source, source + steps) for source in range(first, last)])


def rms_scale(values, gain):
    mean_square = jnp.mean(values * values, axis=-1, keepdims=True)
    return values * lax.rsqrt(mean_square + EPS) * gain


def attend(query_blocks, key_blocks, value_blocks):
    scale = query_blocks.shape[-1] ** (-0.5)
    scores = (
        jnp.einsum("bqhs,bkhs->bhqk", query_blocks, key_blocks, preferred_element_type=jnp.float32)
        * scale
    )
    probs = jax.nn.softmax(scores, axis=-1).astype(jnp.bfloat16)
    return jnp.einsum("bhqk,bkhs->bqhs", probs, value_blocks, preferred_element_type=jnp.float32)


def on_device(corpus, enc_qkv, enc_out, cca_kv, gain_in, gain_out, queries, nbr_ids):
    corp_rows, row_tokens, model_width = corpus.shape
    heads_here = enc_qkv.shape[1]
    head_size = enc_qkv.shape[3]
    row_total = corp_rows * row_tokens
    corpus_flat = corpus.reshape(row_total, model_width)
    normed_in = rms_scale(corpus_flat.astype(jnp.float32), gain_in).astype(jnp.bfloat16)
    projected = jnp.dot(
        normed_in,
        enc_qkv.reshape(model_width, heads_here * 3 * head_size),
        preferred_element_type=jnp.float32,
    )
    projected = projected.astype(jnp.bfloat16).reshape(
        corp_rows, row_tokens, heads_here, 3, head_size
    )
    attended = attend(projected[:, :, :, 0], projected[:, :, :, 1], projected[:, :, :, 2]).astype(
        jnp.bfloat16
    )
    attended = attended.reshape(row_total, heads_here * head_size)
    out_weight = enc_out.reshape(heads_here * head_size, model_width)
    partial_terms = jnp.dot(attended, out_weight, preferred_element_type=jnp.float32)
    enc_sum = lax.psum(partial_terms, "head")
    normed = rms_scale(corpus_flat.astype(jnp.float32) + enc_sum, gain_out).astype(jnp.bfloat16)
    memory_cols = heads_here * 2 * head_size
    shard_piece = lax.all_gather(cca_kv, "seq", axis=0, tiled=True)
    memory = jnp.dot(
        normed,
        shard_piece.reshape(shard_piece.shape[0], memory_cols),
        preferred_element_type=jnp.float32,
    )
    memory = memory.astype(jnp.bfloat16).reshape(corp_rows, row_tokens, heads_here, 2, head_size)
    request_ids = nbr_ids.reshape(-1)
    demand = request_ids.shape[0]
    owners = request_ids // corp_rows
    local_row = request_ids % corp_rows
    request_order = jnp.arange(demand)
    earlier = request_order[None, :] < request_order[:, None]
    same_owner = owners[:, None] == owners[None, :]
    slot_rank = jnp.sum(jnp.logical_and(same_owner, earlier), axis=1)
    slot_index = owners * CAP + slot_rank
    devices = lax.axis_size("seq")
    positions = jnp.arange(devices * CAP)
    matched = positions[:, None] == slot_index[None, :]
    wanted = jnp.sum(jnp.where(matched, local_row[None, :], 0), axis=1).reshape(devices, CAP)
    picked = jnp.take(
        memory, lax.all_to_all(wanted, "seq", split_axis=0, concat_axis=0, tiled=True), axis=0
    )
    fetched = lax.all_to_all(picked, "seq", split_axis=0, concat_axis=0, tiled=True)
    fetched = fetched.reshape(devices * CAP, row_tokens, heads_here, 2, head_size)
    group_memory = jnp.take(fetched, slot_index, axis=0)
    groups_here = nbr_ids.shape[0]
    group_memory = group_memory.reshape(groups_here, NBRS * row_tokens, heads_here, 2, head_size)
    token_count = queries.shape[0]
    lead = GROUP - 1
    before = passed_along(group_memory[groups_here - 1 :], "seq", 1)
    window_memory = jnp.concatenate([before, group_memory], axis=0)
    padded_queries = jnp.concatenate(
        [
            jnp.zeros((1, heads_here, head_size), jnp.bfloat16),
            queries,
            jnp.zeros((lead, heads_here, head_size), jnp.bfloat16),
        ],
        axis=0,
    ).reshape(groups_here + 1, GROUP, heads_here, head_size)
    extended = attend(padded_queries, window_memory[:, :, :, 0], window_memory[:, :, :, 1])
    extended = extended.reshape((groups_here + 1) * GROUP, heads_here, head_size)
    result = extended[1 : 1 + token_count].astype(jnp.bfloat16)
    return result


def solution(mesh):
    placed = (
        P("seq", None, None),
        P(None, "head", None, None),
        P("head", None, None),
        P("seq", "head", None, None),
        P(),
        P(),
        P("seq", "head", None),
        P("seq", None),
    )
    return jax.shard_map(
        on_device, mesh=mesh, in_specs=placed, out_specs=P("seq", "head", None), check_vma=False
    )
```

profile of v0, /device:TPU:104, one launch (start us, length us, event | category | flops | bytes accessed | tf_op | source)
XLA Modules:
  0.0 442.5 jit_solution(8818635364731222058)
XLA Ops:
  7.4 16.4 %copy.108 = bf16[4096,2,3,128]{0,3,2,1:T(8,128)(2,1)} copy(bf16[4096,2,3,128]{3,1,2,0:T(2,128)(2,1)} %param.9) | data formatting | bytes 12582912 | tf_op args[1]
  23.8 3.2 multiply_reduce_fusion.1
  27.2 1.7 multiply_convert_fusion.1
  28.9 1.1 copy-done.3
  30.0 3.5 convolution_convert_fusion
  33.5 1.2 copy.109
  34.6 1.7 reshape.286
  36.4 1.0 fusion.50
  37.4 0.2 copy.129
  37.6 0.2 copy.130
  37.8 0.3 convolution_multiply_fusion.1
  38.1 0.4 fusion.51
  38.5 1.3 fusion.19
  39.9 4.5 %fusion.22 = f32[512,4096]{1,0:T(8,128)} fusion(bf16[256,4096]{1,0:T(8,128)(2,1)S(1)} %bitcast.79, bf16[64,8,2,128]{3,2,1,0:T(2,128)(2,1)S(1)} %bitcast.85), kind=kOutput, calls=%fused_computation.38 | convolution fusion | flops 1073741824 | bytes 10747904 | tf_op jit(solution)/shard_map/dot_general | solution.py:55
  44.5 0.5 all-gather.2.cloned.1.call-update
  45.7 16.9 %all_to_all.20 = s32[32,1,2]{2,1,0:T(1,128)S(1)} all-to-all(s32[32,1,2]{2,1,0:T(1,128)S(1)} %bitcast.88), channel_id=1, replica_groups=mesh['seq'=32,'head'=8] {'seq'}, dimensions={0} | all-to-all | bytes 512 | tf_op jit(solution)/shard_map/all_to_all | solution.py:80
  63.0 90.3 %all-reduce.2.cloned.1.call-done = f32[512,4096]{1,0:T(8,128)} async-done(((f32[512,4096]{1,0:T(8,128)}), f32[512,4096]{1,0:T(8,128)}) %all-reduce.2.cloned.1.call-update) | async-done | bytes 8388624 | tf_op jit(solution)/shard_map/psum | solution.py:56
  153.3 8.9 %multiply_reduce_fusion = (f32[512]{0:T(512)S(1)}, f32[512,4096]{1,0:T(8,128)}) fusion(f32[512,4096]{1,0:T(8,128)} %all-reduce.2.cloned.1.call-done, bf16[4,128,4096]{2,1,0:T(8,128)(2,1)} %param.8), kind=kLoop, calls=%fused_computation.7 | loop fusion | flops 8388096 | bytes 20973568 | tf_op jit(solution)/shard_map/reduce_sum | solution.py:21
  162.2 7.2 %reshape.289 = bf16[4096,512]{1,0:T(8,128)(2,1)} reshape(bf16[4096,2,2,128]{3,2,1,0:T(2,128)(2,1)} %all-gather.2.cloned.1.call-done) | data formatting | bytes 8388608 | tf_op jit(solution)/shard_map/reshape | solution.py:62
  169.4 6.9 %fusion.7 = bf16[512,512]{1,0:T(8,128)(2,1)S(1)} fusion(bf16[4096,512]{1,0:T(8,128)(2,1)} %reshape.289, f32[512,4096]{1,0:T(8,128)} %get-tuple-element.8, f32[4096]{0:T(1024)S(1)} %copy-done.7, f32[512]{0:T(512)S(1)} %add_rsqrt_fusion), kind=kOutput, calls=%fused_computation.20 | convolution fusion | flops 2154037248 | bytes 13125632 | tf_op jit(solution)/shard_map/dot_general | solution.py:60
  176.5 18.3 %gather_fusion = bf16[64,128,2,2,128]{4,3,2,1,0:T(2,128)(2,1)} fusion(bf16[4,128,2,2,128]{4,3,2,1,0:T(2,128)(2,1)S(1)} %reshape.290, s32[1024]{0:T(1024)S(1)} %pad_clamp_fusion.1), kind=kCustom, calls=%fused_computation | custom fusion | bytes 16777472 | tf_op jit(solution)/shard_map/jit(_take)/gather | solution.py:79
  194.8 7.7 %copy_select_fusion = bf16[32,2,128,2,2,128]{5,2,4,3,1,0:T(8,128)(2,1)} fusion(bf16[32,2,128,2,2,128]{5,4,3,2,1,0:T(2,128)(2,1)} %bitcast.80, pred[32,2]{1,0:T(8,128)(4,1)S(1)} %copy.107), kind=kLoop, calls=%fused_computation.5 | loop fusion | flops 4194304 | bytes 16777280 | tf_op jit(solution)/shard_map/jit(_take)/select_n | solution.py:79
  202.6 10.1 %all-to-all-start.1 = ((bf16[32,2,128,2,2,128]{5,2,4,3,1,0:T(8,128)(2,1)}), bf16[32,2,128,2,2,128]{5,2,4,3,1,0:T(8,128)(2,1)}, u32[]{:S(2)}, u32[]{:S(2)}) async-start(bf16[32,2,128,2,2,128]{5,2,4,3,1,0:T(8,128)(2,1)} %copy_select_fusion), calls=%async_computation.1 | async-start | bytes 16777216 | tf_op jit(solution)/shard_map/all_to_all | solution.py:82
  213.2 0.2 maximum_maximum_fusion
  213.4 198.6 %all-to-all-done.1 = bf16[32,2,128,2,2,128]{5,2,4,3,1,0:T(8,128)(2,1)} async-done(((bf16[32,2,128,2,2,128]{5,2,4,3,1,0:T(8,128)(2,1)}), bf16[32,2,128,2,2,128]{5,2,4,3,1,0:T(8,128)(2,1)}, u32[]{:S(2)}, u32[]{:S(2)}) %all-to-all-start.1) | async-done | bytes 8388640 | tf_op jit(solution)/shard_map/all_to_all | solution.py:82
  412.0 4.3 gather_fusion.1
  416.6 1.9 collective-permute-start
  418.6 1.6 copy_select_fusion.1
  420.1 8.8 %collective-permute-done = bf16[1,256,2,2,128]{4,1,2,0,3:T(8,128)(2,1)S(1)} collective-permute-done((bf16[1,256,2,2,128]{4,1,2,0,3:T(8,128)(2,1)S(1)}, bf16[1,256,2,2,128]{4,1,2,0,3:T(8,128)(2,1)S(1)}, u32[]{:S(2)}, u32[]{:S(2)}) %collective-permute-start) | collective-permute-done | bytes 262176 | tf_op jit(solution)/shard_map/ppermute | solution.py:17
  428.9 3.1 fusion.56
  432.0 2.0 fusion.16
  434.0 1.0 copy.126
  (54 shorter events, 2.5 us)
Async XLA Ops:
  7.4 32.6 %copy-start = (bf16[2,128,4096]{2,1,0:T(8,128)(2,1)S(1)}, bf16[2,128,4096]{2,1,0:T(8,128)(2,1)}, u32[]{:S(2)}) copy-start(bf16[2,128,4096]{2,1,0:T(8,128)(2,1)} %param.10) | copy-start | bytes 6291460
  7.4 145.9 %all-reduce.2.cloned.1.call-start = ((), (), s32[]{:S(2)}) async-start(), calls=%async_computation.2 | async-start | bytes 16777216 | tf_op jit(solution)/shard_map/psum | solution.py:56
  7.4 19.6 %copy-start.5 = (f32[4096]{0:T(1024)S(1)}, f32[4096]{0:T(1024)}, u32[]{:S(2)}) copy-start(f32[4096]{0:T(1024)} %param.12) | copy-start | bytes 49156
  23.8 3.4 copy-start.2
  27.2 2.8 copy-start.3
  44.4 0.7 copy-start.6
  44.4 117.7 %all-gather.2.cloned.1.call-start = ((), (), s32[]{:S(2)}) async-start(), calls=%async_computation.3 | async-start | bytes 4325376 | tf_op jit(solution)/shard_map/all_gather | solution.py:59
  162.1 7.3 %copy-start.7 = (f32[4096]{0:T(1024)S(1)}, f32[4096]{0:T(1024)}, u32[]{:S(2)}) copy-start(f32[4096]{0:T(1024)} %param.13) | copy-start | bytes 49156
  202.6 10.4 %copy-start.4 = (bf16[512,2,128]{2,1,0:T(2,128)(2,1)S(1)}, bf16[512,2,128]{2,1,0:T(2,128)(2,1)}, u32[]{:S(2)}) copy-start(bf16[512,2,128]{2,1,0:T(2,128)(2,1)} %param.14) | copy-start | bytes 786436
  202.6 209.5 %all-to-all-start.1 = ((bf16[32,2,128,2,2,128]{5,2,4,3,1,0:T(8,128)(2,1)}), bf16[32,2,128,2,2,128]{5,2,4,3,1,0:T(8,128)(2,1)}, u32[]{:S(2)}, u32[]{:S(2)}) async-start(bf16[32,2,128,2,2,128]{5,2,4,3,1,0:T(8,128)(2,1)} %copy_select_fusion), calls=%async_computation.1 | async-start | bytes 16777216 | tf_op jit(solution)/shard_map/all_to_all | solution.py:82
  416.6 12.3 %collective-permute-start = (bf16[1,256,2,2,128]{4,1,2,0,3:T(8,128)(2,1)S(1)}, bf16[1,256,2,2,128]{4,1,2,0,3:T(8,128)(2,1)S(1)}, u32[]{:S(2)}, u32[]{:S(2)}) collective-permute-start(bf16[1,256,2,2,128]{4,1,2,0,3:T(8,128)(2,1)S(1)} %bitcast.87), channel_id=1, source_target_pairs={{0,8},{8,16},{16,24},{24,32},{32,40},{40,48},{48,56},{56,64},{64,7... | collective-permute-start | bytes 786440 | tf_op jit(solution)/shard_map/ppermute | solution.py:17
  428.9 6.1 %copy-start.1 = (bf16[2,128,4096]{2,1,0:T(8,128)(2,1)S(1)}, bf16[2,128,4096]{2,1,0:T(8,128)(2,1)}, u32[]{:S(2)}) copy-start(bf16[2,128,4096]{2,1,0:T(8,128)(2,1)} %param.10) | copy-start | bytes 6291460
Sparse Core Ops, SparseCore 0:
  44.6 108.6 all-reduce.1
Sparse Core Ops, SparseCore 1:
  47.5 83.2 all-gather.1
where the time goes:
time: 443 us; the launch traced here: 442 us
  waiting for transfers between devices  298 us (67%)
  local copies, waits for them, and re-layouts  54.7 us (12%)
  other arithmetic  23.7 us (5%)
  matrix products  21.9 us (5%)
  blocking collectives  16.9 us (4%)
  between operations  15.1 us (3%)
  starting transfers between devices  12 us (3%)
    all_to_all x1, waiting for transfers between devices, on_device(): lax.all_to_all(picked, 'seq', split_axis=0, concat_axis=0, tiled=True)  199 us
    psum x1, waiting for transfers between devices, on_device(): enc_sum = lax.psum(partial_terms, 'head')  90.3 us
    gather x1, local copies, waits for them, and re-layouts, on_device(): jnp.take(memory, lax.all_to_all(wanted, 'seq', split_axis=0, concat_axis=...  18.3 us
    unnamed x21, local copies, waits for them, and re-layouts  18.3 us
    all_to_all x1, blocking collectives, on_device(): lax.all_to_all(wanted, 'seq', split_axis=0, concat_axis=0, tiled=True)  16.9 us
    reduce_sum x2, other arithmetic, rms_scale(): mean_square = jnp.mean(values * values, axis=-1, keepdims=True)  12.1 us
    all_to_all x1, starting transfers between devices, on_device(): lax.all_to_all(picked, 'seq', split_axis=0, concat_axis=0, tiled=True)  10.1 us
  transfers between devices with their start and end apart: 4, of which 3 were waited for; matrix products, arithmetic and copies ran while one was open for 3% of the time, Pallas kernels for 0%

commit v1 on v0

v1 whole, which is shorter than its diff:
```python
import functools

import jax
import jax.numpy as jnp
from jax import lax
from jax.experimental import pallas as pl
from jax.experimental.pallas import tpu as pltpu
from jax.sharding import Mesh, PartitionSpec as P

GROUP = 64
EPS = 1e-06
NZ, NX, NY, NC = 8, 4, 4, 2
ROW = 128
HS = 128
CHUNKS = 2
MASKED = -1e30
BF = jnp.bfloat16
F32 = jnp.float32
ANY = pl.BlockSpec(memory_space=pl.ANY)
VMEM_ALL = pl.BlockSpec(memory_space=pltpu.VMEM)


def shifted(value, axis, steps):
    n = lax.axis_size(axis)
    return lax.ppermute(value, axis, [(i, (i + steps) % n) for i in range(n)])


def spread(value, axis):
    n = lax.axis_size(axis)
    copies = jnp.broadcast_to(value[None], (n,) + value.shape)
    return lax.all_to_all(copies, axis, split_axis=0, concat_axis=0, tiled=True)


def encoder_kernel(core_ref, x_ref, w_ref, g_ref, out_ref, wide, wmat, acc, ssq):
    step = pl.program_id(0)
    depth = x_ref.shape[1]

    @pl.when(step == 0)
    def _():
        acc[...] = jnp.zeros_like(acc)
        ssq[...] = jnp.zeros_like(ssq)

    wide[...] = w_ref[...].astype(F32)
    for col in range(6):
        wmat[:, col * HS:(col + 1) * HS] = wide[pl.ds(col, depth, stride=6), :].astype(BF)
    x = x_ref[...].astype(F32)
    ssq[...] += jnp.sum(x * x, axis=1, keepdims=True)
    xg = (x * g_ref[...]).astype(BF)
    acc[...] += jnp.dot(xg, wmat[...], preferred_element_type=F32)

    @pl.when(step == pl.num_programs(0) - 1)
    def _():
        core = core_ref[0]
        total = depth * pl.num_programs(0)
        rinv = lax.rsqrt(ssq[...] / total + EPS)
        rows = x_ref.shape[0] // ROW
        for r in range(rows):
            sl = slice(r * ROW, (r + 1) * ROW)
            scale = rinv[sl]
            parts = []
            for h in range(2):
                q = (acc[sl, h * HS:(h + 1) * HS] * scale).astype(BF)
                k = (acc[sl, (2 + h) * HS:(3 + h) * HS] * scale).astype(BF)
                v = (acc[sl, (4 + h) * HS:(5 + h) * HS] * scale).astype(BF)
                s = lax.dot_general(q, k, (((1,), (1,)), ((), ())), preferred_element_type=F32)
                s = s * (HS ** -0.5)
                m = jnp.max(s, axis=1, keepdims=True)
                p = jnp.exp(s - m)
                p = (p / jnp.sum(p, axis=1, keepdims=True)).astype(BF)
                parts.append(jnp.dot(p, v, preferred_element_type=F32).astype(BF))
            place = (r // 2 + core) % 2
            att = jnp.concatenate(parts, axis=1)
            out_ref[place, r % 2] = att


def encode(corpus_flat, w_rows, gain, core):
    tokens, width = corpus_flat.shape
    steps = 8
    depth = width // steps
    return pl.pallas_call(
        encoder_kernel,
        grid_spec=pltpu.PrefetchScalarGridSpec(
            num_scalar_prefetch=1,
            grid=(steps,),
            in_specs=[
                pl.BlockSpec((tokens, depth), lambda i, c: (0, i)),
                pl.BlockSpec((depth * 6, HS), lambda i, c: (i, 0)),
                pl.BlockSpec((1, depth), lambda i, c: (0, i)),
            ],
            out_specs=pl.BlockSpec((2, 2, ROW, 2 * HS), lambda i, c: (0, 0, 0, 0)),
            scratch_shapes=[
                pltpu.VMEM((depth * 6, HS), F32),
                pltpu.VMEM((depth, 6 * HS), BF),
                pltpu.VMEM((tokens, 6 * HS), F32),
                pltpu.VMEM((tokens, 1), F32),
            ],
        ),
        out_shape=jax.ShapeDtypeStruct((2, 2, ROW, 2 * HS), BF),
        cost_estimate=pl.CostEstimate(
            flops=2 * tokens * width * 6 * HS, bytes_accessed=(tokens + 768) * width * 2, transcendentals=0
        ),
        name="encoder",
    )(core, corpus_flat, w_rows, gain)


def project_kernel(a_ref, b_ref, ea_ref, eb_ref, out_ref):
    total = jnp.dot(a_ref[...], ea_ref[...], preferred_element_type=F32)
    total += jnp.dot(b_ref[...], eb_ref[...], preferred_element_type=F32)
    out_ref[...] = total.astype(BF)


def project(att_own, att_other, e_own, e_other):
    tokens, depth = att_own.shape
    width = e_own.shape[1]
    cols = 1024
    return pl.pallas_call(
        project_kernel,
        grid=(width // cols,),
        in_specs=[
            pl.BlockSpec((tokens, depth), lambda i: (0, 0)),
            pl.BlockSpec((tokens, depth), lambda i: (0, 0)),
            pl.BlockSpec((depth, cols), lambda i: (0, i)),
            pl.BlockSpec((depth, cols), lambda i: (0, i)),
        ],
        out_specs=pl.BlockSpec((tokens, cols), lambda i: (0, i)),
        out_shape=jax.ShapeDtypeStruct((tokens, width), BF),
        cost_estimate=pl.CostEstimate(
            flops=4 * tokens * depth * width, bytes_accessed=4 * depth * width, transcendentals=0
        ),
        name="project",
    )(att_own, att_other, e_own, e_other)


def norm_kernel(block_ref, terms_ref, x_ref, g_ref, out_ref):
    total = x_ref[...].astype(F32)
    for i in range(NY):
        total += terms_ref[i].astype(F32)
    rinv = lax.rsqrt(jnp.mean(total * total, axis=1, keepdims=True) + EPS)
    u = (total * rinv * g_ref[...]).astype(BF)
    for z in range(NZ):
        for x in range(NX):
            src, dst = (z * NX + x) * HS, (x * NZ + z) * HS
            piece = u[:, src:src + HS]
            for i in range(NY):
                out_ref[i, :, dst:dst + HS] = piece


def normalise(terms, corpus_flat, gain, block):
    _, rows, width = terms.shape
    return pl.pallas_call(
        norm_kernel,
        grid_spec=pltpu.PrefetchScalarGridSpec(
            num_scalar_prefetch=1,
            grid=(1,),
            in_specs=[
                pl.BlockSpec((NY, rows, width), lambda i, b: (0, 0, 0)),
                pl.BlockSpec((rows, width), lambda i, b: (b[0], 0)),
                pl.BlockSpec((1, width), lambda i, b: (0, 0)),
            ],
            out_specs=pl.BlockSpec((NY, rows, width), lambda i, b: (0, 0, 0)),
        ),
        out_shape=jax.ShapeDtypeStruct((NY, rows, width), BF),
        cost_estimate=pl.CostEstimate(flops=8 * rows * width, bytes_accessed=18 * rows * width, transcendentals=0),
        name="normalise",
    )(block, terms, corpus_flat, gain)


def memory_kernel(a_ref, b_ref, k_ref, out_ref, acc):
    step = pl.program_id(0)
    half = a_ref.shape[0]

    @pl.when(step == 0)
    def _():
        acc[...] = jnp.zeros_like(acc)

    u = jnp.concatenate([a_ref[...], b_ref[...]], axis=0)
    acc[...] += jnp.dot(u, k_ref[...], preferred_element_type=F32)

    @pl.when(step == pl.num_programs(0) - 1)
    def _():
        out_ref[...] = acc[...].astype(BF)


def memorise(u_own, u_other, weight):
    half, width = u_own.shape
    cols = weight.shape[1]
    steps = 4
    depth = width // steps
    return pl.pallas_call(
        memory_kernel,
        grid=(steps,),
        in_specs=[
            pl.BlockSpec((half, depth), lambda i: (0, i)),
            pl.BlockSpec((half, depth), lambda i: (0, i)),
            pl.BlockSpec((depth, cols), lambda i: (i, 0)),
        ],
        out_specs=pl.BlockSpec((2 * half, cols), lambda i: (0, 0)),
        scratch_shapes=[pltpu.VMEM((2 * half, cols), F32)],
        out_shape=jax.ShapeDtypeStruct((2 * half, cols), BF),
        cost_estimate=pl.CostEstimate(
            flops=4 * half * width * cols, bytes_accessed=2 * width * cols, transcendentals=0
        ),
        name="memorise",
    )(u_own, u_other, weight)


def ring_pieces(block):
    rows = block.shape[0]
    half = rows // 2
    pieces = [(0, 0, rows, block)]
    up = down = block
    for s in range(1, NZ // 2):
        up = shifted(up, "z", 1)
        down = shifted(down, "z", -1)
        pieces += [(s, 0, rows, up), (NZ - s, 0, rows, down)]
    pieces += [
        (NZ // 2, 0, half, shifted(up[:half], "z", 1)),
        (NZ // 2, half, half, shifted(down[half:], "z", -1)),
    ]
    return pieces


PAD = 8


def window_kernel(layout, ids_ref, at_ref, q_ref, *refs):
    pieces = refs[:len(layout)]
    out_ref = refs[len(layout)]
    table, qs, outs, stats, sem = refs[len(layout) + 1:]
    copies = []
    for i, (chunk, distance, first, rows) in enumerate(layout):
        copies.append(
            pltpu.make_async_copy(pieces[i], table.at[distance, chunk, pl.ds(first, rows)], sem.at[i])
        )
    for copy in copies:
        copy.start()
    my_z, my_x, core = at_ref[0], at_ref[1], at_ref[2]
    plane_rows = NX * 1024
    qs[0:PAD, :] = jnp.zeros((PAD, HS), F32)
    qs[PAD + plane_rows:, :] = jnp.zeros((qs.shape[0] - PAD - plane_rows, HS), F32)
    for x in range(NX):
        qs[PAD + x * 1024:PAD + (x + 1) * 1024, :] = q_ref[x, 0:1024].astype(F32)
    for copy in copies:
        copy.wait()

    def place(row):
        row = jnp.maximum(row, 0)
        distance = lax.rem(my_z - row // 16 + NZ, NZ)
        local = lax.rem(row, 4)
        chunk = lax.rem(local, 2)
        half = lax.rem(local // 2 + core, 2)
        return distance, chunk, pl.multiple_of(half * ROW, ROW)

    def held(row):
        return jnp.logical_and(row >= 0, lax.rem(jnp.maximum(row, 0) // 4, NX) == my_x)

    def body(w, carry):
        start = PAD + 2 * (GROUP * w - 1)
        rows = [ids_ref[w, n] for n in range(2)]
        ok = [held(row) for row in rows]
        any_ok = jnp.logical_or(ok[0], ok[1])

        @pl.when(any_ok)
        def _():
            spots = [place(row) for row in rows]
            for h in range(2):
                q = qs[pl.ds(start + h, GROUP, stride=2), :].astype(BF)
                scores = []
                for n in range(2):
                    d, c, first = spots[n]
                    k = table[d, c, pl.ds(first, ROW), h * 256:h * 256 + HS]
                    s = lax.dot_general(q, k, (((1,), (1,)), ((), ())), preferred_element_type=F32)
                    s = s * (HS ** -0.5)
                    scores.append(jnp.where(ok[n], s, MASKED))
                m = jnp.maximum(
                    jnp.max(scores[0], axis=1, keepdims=True), jnp.max(scores[1], axis=1, keepdims=True)
                )
                probs = [jnp.exp(s - m) for s in scores]
                total = jnp.sum(probs[0], axis=1, keepdims=True) + jnp.sum(probs[1], axis=1, keepdims=True)
                inv = 1.0 / total
                out = jnp.zeros((GROUP, HS), F32)
                for n in range(2):
                    d, c, first = spots[n]
                    v = table[d, c, pl.ds(first, ROW), h * 256 + HS:h * 256 + 2 * HS]
                    out += jnp.dot((probs[n] * inv).astype(BF), v, preferred_element_type=F32)
                outs[pl.ds(start + h, GROUP, stride=2), :] = out
                lse = m + jnp.log(total)
                stats[pl.ds(start + h, GROUP, stride=2), :] = jnp.broadcast_to(lse, (GROUP, HS))

        @pl.when(jnp.logical_not(any_ok))
        def _():
            for h in range(2):
                outs[pl.ds(start + h, GROUP, stride=2), :] = jnp.zeros((GROUP, HS), F32)
                stats[pl.ds(start + h, GROUP, stride=2), :] = jnp.full((GROUP, HS), MASKED, F32)

        return carry

    lax.fori_loop(0, ids_ref.shape[0], body, 0)
    eye = lax.broadcasted_iota(jnp.int32, (HS, HS), 0) == lax.broadcasted_iota(jnp.int32, (HS, HS), 1)
    for x in range(NX):
        base = PAD + x * 1024
        out_ref[x, 0:1024] = outs[base:base + 1024, :].astype(BF)
        lines = []
        for b in range(8):
            block = stats[base + b * HS:base + (b + 1) * HS, :]
            lines.append(jnp.sum(jnp.where(eye, block, 0.0), axis=0, keepdims=True))
        lse = jnp.concatenate(lines, axis=0)
        high = lse.astype(BF)
        rest = lse - high.astype(F32)
        middle = rest.astype(BF)
        low = (rest - middle.astype(F32)).astype(BF)
        tail = jnp.concatenate([high.astype(F32), middle.astype(F32), low.astype(F32), jnp.zeros((8, HS), F32)], axis=0)
        out_ref[x, 1024:1056] = tail.astype(BF)


def windows(ids, at, q_plane, pieces):
    layout = tuple((chunk, d, first, rows) for chunk, d, first, rows, _ in pieces)
    total = PAD + NX * 1024 + 2 * GROUP
    return pl.pallas_call(
        functools.partial(window_kernel, layout),
        grid_spec=pltpu.PrefetchScalarGridSpec(
            num_scalar_prefetch=2,
            grid=(1,),
            in_specs=[pl.BlockSpec(q_plane.shape, lambda i, a, b: (0, 0, 0))] + [ANY] * len(pieces),
            out_specs=pl.BlockSpec((NX, 1056, HS), lambda i, a, b: (0, 0, 0)),
            scratch_shapes=[
                pltpu.VMEM((NZ, CHUNKS, 4 * ROW // CHUNKS, 512), BF),
                pltpu.VMEM((total, HS), F32),
                pltpu.VMEM((total, HS), F32),
                pltpu.VMEM((total, HS), F32),
                pltpu.SemaphoreType.DMA((len(pieces),)),
            ],
        ),
        out_shape=jax.ShapeDtypeStruct((NX, 1056, HS), BF),
        cost_estimate=pl.CostEstimate(flops=10**9, bytes_accessed=8 * 2**20, transcendentals=10**6),
        name="windows",
    )(ids, at, q_plane, *[piece[-1] for piece in pieces])


def combine_kernel(parts_ref, out_ref):
    logs = []
    for x in range(NX):
        tail = parts_ref[x, 1024:1056].astype(F32)
        logs.append(tail[0:8] + tail[8:16] + tail[16:24])
    m = functools.reduce(jnp.maximum, logs)
    weights = [jnp.exp(v - m) for v in logs]
    inv = 1.0 / functools.reduce(jnp.add, weights)
    weights = [w * inv for w in weights]
    eye = lax.broadcasted_iota(jnp.int32, (HS, HS), 0) == lax.broadcasted_iota(jnp.int32, (HS, HS), 1)
    for b in range(8):
        total = jnp.zeros((HS, HS), F32)
        for x in range(NX):
            line = jnp.broadcast_to(weights[x][b:b + 1, :], (HS, HS))
            column = jnp.sum(jnp.where(eye, line, 0.0), axis=1, keepdims=True)
            total += column * parts_ref[x, b * HS:(b + 1) * HS].astype(F32)
        out_ref[b * HS:(b + 1) * HS, :] = total.astype(BF)


def combine(parts):
    return pl.pallas_call(
        combine_kernel,
        in_specs=[VMEM_ALL],
        out_specs=VMEM_ALL,
        out_shape=jax.ShapeDtypeStruct((1024, HS), BF),
        cost_estimate=pl.CostEstimate(flops=10**7, bytes_accessed=2 * 2**20, transcendentals=0),
        name="combine",
    )(parts)


def on_device(corpus, enc_qkv, enc_out, cca_kv, gain_in, gain_out, queries, nbr_ids):
    width = corpus.shape[2]
    my_z, my_x, my_y, core = (lax.axis_index(a) for a in ("z", "x", "y", "c"))
    corpus_flat = corpus.reshape(-1, width)
    e_own = enc_out.reshape(2 * HS, width)
    e_other = shifted(e_own, "c", 1)

    kv = lax.optimization_barrier(cca_kv.reshape(cca_kv.shape[0], 512))
    kv = spread(kv, "z").reshape(-1, 512)
    kv = spread(kv, "x").reshape(-1, 512)

    last = lax.ppermute(
        nbr_ids[7:], ("z", "x"), [(i, i + 1) for i in range(NZ * NX - 1)]
    )
    last = jnp.where(jnp.logical_and(my_z == 0, my_x == 0), -1, last)
    ids = jnp.concatenate([last, nbr_ids], axis=0).astype(BF)
    ids = jnp.pad(ids, ((0, 7), (0, HS - 2)))
    q_rows = jnp.concatenate([queries.reshape(1024, HS), ids], axis=0)
    q_plane = spread(q_rows, "x").reshape(NX, 1040, HS)
    got = q_plane[:, 1024:1033, 0:2].astype(jnp.int32)
    plane_ids = jnp.concatenate([got[0], got[1, 1:], got[2, 1:], got[3, 1:]], axis=0)

    w_rows = enc_qkv.transpose(0, 2, 1, 3).reshape(width * 6, HS)
    att = encode(corpus_flat, w_rows, gain_in.reshape(1, width), core.reshape(1).astype(jnp.int32))
    att_own, att_send = att[0], att[1]
    att_other = shifted(att_send, "c", 1)

    pieces = []
    for j in range(CHUNKS):
        own = att_own[j]
        other = att_other[j]
        partial = project(own, other, e_own, e_other).reshape(NY, ROW // NY, width)
        terms = lax.all_to_all(partial, "y", split_axis=0, concat_axis=0, tiled=True)
        block = ((2 * core + j) * NY + my_y).reshape(1).astype(jnp.int32)
        copies = normalise(terms, corpus_flat, gain_out.reshape(1, width), block)
        u = lax.all_to_all(copies, "y", split_axis=0, concat_axis=0, tiled=True)
        u_own = u.reshape(ROW, width)
        u_other = shifted(u_own, "c", 1)
        memory = memorise(u_own, u_other, kv)
        pieces += [(j,) + piece for piece in ring_pieces(memory)]

    at = jnp.stack([my_z, my_x, core]).astype(jnp.int32)
    parts = windows(plane_ids, at, q_plane, pieces)
    parts = lax.all_to_all(parts, "x", split_axis=0, concat_axis=0, tiled=True)
    return combine(parts).reshape(512, 2, HS)


def solution(mesh):
    inner = Mesh(mesh.devices.reshape(NZ, NX, NY, NC), ("z", "x", "y", "c"))
    seq, head = ("z", "x"), ("y", "c")
    placed = (
        P(seq, None, None),
        P(None, head, None, None),
        P(head, None, None),
        P(seq, head, None, None),
        P(),
        P(),
        P(seq, head, None),
        P(seq, None),
    )
    return jax.shard_map(
        on_device, mesh=inner, in_specs=placed, out_specs=P(seq, head, None), check_vma=False
    )
```

time: 443 us -> 271 us (0.61)
  the two profiles are of different devices: /device:TPU:104 before, /device:TPU:2 now
where the time goes in v1:
time: 271 us; the launch traced here: 269 us
  waiting for transfers between devices  89 us (33%)
  starting transfers between devices  61.3 us (23%)
  Pallas kernels  56 us (21%)
  blocking collectives  37.1 us (14%)
  local copies, waits for them, and re-layouts  23.5 us (9%)
    ppermute x1, waiting for transfers between devices, on_device(): lax.ppermute(nbr_ids[7:], ('z', 'x'), [(i, i + 1) for i in range(NZ * NX...  37.9 us
    ppermute x20, starting transfers between devices, shifted(): return lax.ppermute(value, axis, [(i, (i + steps) % n) for i in range(n)])  26.8 us
    all_to_all x2, waiting for transfers between devices, on_device(): lax.all_to_all(partial, 'y', split_axis=0, concat_axis=0, tiled=True)  22.3 us
    all_to_all x1, blocking collectives, on_device(): parts = lax.all_to_all(parts, 'x', split_axis=0, concat_axis=0, tiled=True)  20.5 us
    all_to_all x3, starting transfers between devices, spread(): return lax.all_to_all(copies, axis, split_axis=0, concat_axis=0, tiled=True)  18.9 us
    all_to_all x1, blocking collectives, on_device(): u = lax.all_to_all(copies, 'y', split_axis=0, concat_axis=0, tiled=True)  16.6 us
    pallas_call x1, Pallas kernels, windows(): pl.pallas_call(functools.partial(window_kernel, layout), grid_spec=pltpu....  15.7 us
    pallas_call x1, Pallas kernels, encode(): pl.pallas_call(encoder_kernel, grid_spec=pltpu.PrefetchScalarGridSpec(num...  13 us
  transfers between devices with their start and end apart: 27, of which 11 were waited for; matrix products, arithmetic and copies ran while one was open for 7% of the time, Pallas kernels for 14%

profile of v1, /device:TPU:2, one launch (start us, length us, event | category | flops | bytes accessed | tf_op | source)
XLA Modules:
  0.0 269.3 jit_solution(17604892559293194092)
XLA Ops:
  2.0 8.5 %all-to-all-start.3 = ((bf16[8,128,512]{2,1,0:T(8,128)(2,1)}), bf16[8,128,512]{2,1,0:T(8,128)(2,1)S(1)}, u32[]{:S(2)}, u32[]{:S(2)}) async-start(bf16[8,128,512]{2,1,0:T(8,128)(2,1)} %broadcast_in_dim.25), calls=%async_computation.3 | async-start | bytes 2097152 | tf_op jit(solution)/shard_map/all_to_all | solution.py:31
  10.5 13.0 %encoder.1 = bf16[2,2,128,256]{3,2,1,0:T(8,128)(2,1)} custom-call(s32[1]{0:T(128)} %bitcast.7.core_ref, bf16[512,4096]{1,0:T(8,128)(2,1)} %bitcast.34, bf16[24576,128]{1,0:T(8,128)(2,1)} %bitcast.50, f32[1,4096]{1,0:T(1,128)} %bitcast.51), custom_call_target="tpu_custom_call" | custom-call | flops 3221225472 | bytes 10485760 | tf_op jit(solution)/shard_map/encoder/pallas_call | solution.py:80
  28.3 4.6 %project.3 = bf16[128,4096]{1,0:T(8,128)(2,1)} custom-call(bf16[128,256]{1,0:T(8,128)(2,1)} %get-tuple-element.5.a_ref, bf16[128,256]{1,0:T(8,128)(2,1)} %get-tuple-element.7.b_ref, bf16[256,4096]{1,0:T(8,128)(2,1)} %bitcast.38, bf16[256,4096]{1,0:T(8,128)(2,1)} %copy-done), custom_call_target="tpu_custom_call" | custom-call | flops 536870912 | bytes 4194304 | tf_op jit(solution)/shard_map/project/pallas_call | solution.py:116
  32.8 7.1 %all-to-all-done.3 = bf16[8,128,512]{2,1,0:T(8,128)(2,1)S(1)} async-done(((bf16[8,128,512]{2,1,0:T(8,128)(2,1)}), bf16[8,128,512]{2,1,0:T(8,128)(2,1)S(1)}, u32[]{:S(2)}, u32[]{:S(2)}) %all-to-all-start.3) | async-done | bytes 1048608 | tf_op jit(solution)/shard_map/all_to_all | solution.py:31
  39.9 4.5 %all-to-all-start.5 = ((bf16[4,32,4096]{2,1,0:T(8,128)(2,1)}), bf16[4,32,4096]{2,1,0:T(8,128)(2,1)S(1)}, u32[]{:S(2)}, u32[]{:S(2)}) async-start(bf16[4,32,4096]{2,1,0:T(8,128)(2,1)} %bitcast.42), calls=%async_computation.5 | async-start | bytes 2097152 | tf_op jit(solution)/shard_map/all_to_all | solution.py:402
  44.4 4.6 %project.2 = bf16[128,4096]{1,0:T(8,128)(2,1)} custom-call(bf16[128,256]{1,0:T(8,128)(2,1)} %get-tuple-element.6.a_ref, bf16[128,256]{1,0:T(8,128)(2,1)} %get-tuple-element.8.b_ref, bf16[256,4096]{1,0:T(8,128)(2,1)} %bitcast.39, bf16[256,4096]{1,0:T(8,128)(2,1)} %copy-done), custom_call_target="tpu_custom_call" | custom-call | flops 536870912 | bytes 4194304 | tf_op jit(solution)/shard_map/project/pallas_call | solution.py:116
  49.0 10.7 %all-to-all-done.5.terms_ref = bf16[4,32,4096]{2,1,0:T(8,128)(2,1)S(1)} async-done(((bf16[4,32,4096]{2,1,0:T(8,128)(2,1)}), bf16[4,32,4096]{2,1,0:T(8,128)(2,1)S(1)}, u32[]{:S(2)}, u32[]{:S(2)}) %all-to-all-start.5) | async-done | bytes 1048608 | tf_op jit(solution)/shard_map/all_to_all | solution.py:402
  59.7 3.5 %all-to-all-start.1 = ((bf16[4,32,4096]{2,1,0:T(8,128)(2,1)}), bf16[4,32,4096]{2,1,0:T(8,128)(2,1)S(1)}, u32[]{:S(2)}, u32[]{:S(2)}) async-start(bf16[4,32,4096]{2,1,0:T(8,128)(2,1)} %bitcast.41), calls=%async_computation.1 | async-start | bytes 2097152 | tf_op jit(solution)/shard_map/all_to_all | solution.py:402
  63.3 2.8 %normalise.3 = bf16[4,32,4096]{2,1,0:T(8,128)(2,1)} custom-call(s32[1]{0:T(128)} %bitcast.22.block_ref, bf16[4,32,4096]{2,1,0:T(8,128)(2,1)} %copy-done.3, bf16[512,4096]{1,0:T(8,128)(2,1)} %bitcast.35, f32[1,4096]{1,0:T(1,128)} %bitcast.44), custom_call_target="tpu_custom_call" | custom-call | flops 1048576 | bytes 2359296 | tf_op jit(solution)/shard_map/normalise/pallas_call | solution.py:150
  66.0 11.6 %all-to-all-done.1.terms_ref = bf16[4,32,4096]{2,1,0:T(8,128)(2,1)S(1)} async-done(((bf16[4,32,4096]{2,1,0:T(8,128)(2,1)}), bf16[4,32,4096]{2,1,0:T(8,128)(2,1)S(1)}, u32[]{:S(2)}, u32[]{:S(2)}) %all-to-all-start.1) | async-done | bytes 1048608 | tf_op jit(solution)/shard_map/all_to_all | solution.py:402
  77.6 4.3 %all-to-all-start.6 = ((bf16[4,32,4096]{2,1,0:T(8,128)(2,1)}), bf16[4,32,4096]{2,1,0:T(8,128)(2,1)}, u32[]{:S(2)}, u32[]{:S(2)}) async-start(bf16[4,32,4096]{2,1,0:T(8,128)(2,1)} %normalise.3), calls=%async_computation.6 | async-start | bytes 2097152 | tf_op jit(solution)/shard_map/all_to_all | solution.py:405
  81.9 2.8 %normalise.2 = bf16[4,32,4096]{2,1,0:T(8,128)(2,1)} custom-call(s32[1]{0:T(128)} %bitcast.8.block_ref, bf16[4,32,4096]{2,1,0:T(8,128)(2,1)} %copy-done.2, bf16[512,4096]{1,0:T(8,128)(2,1)} %bitcast.36, f32[1,4096]{1,0:T(1,128)} %bitcast.45), custom_call_target="tpu_custom_call" | custom-call | flops 1048576 | bytes 2359296 | tf_op jit(solution)/shard_map/normalise/pallas_call | solution.py:150
  84.7 10.8 %all-to-all-done.6 = bf16[4,32,4096]{2,1,0:T(8,128)(2,1)} async-done(((bf16[4,32,4096]{2,1,0:T(8,128)(2,1)}), bf16[4,32,4096]{2,1,0:T(8,128)(2,1)}, u32[]{:S(2)}, u32[]{:S(2)}) %all-to-all-start.6) | async-done | bytes 1048608 | tf_op jit(solution)/shard_map/all_to_all | solution.py:405
  95.5 16.6 %all_to_all.40 = bf16[4,32,4096]{2,1,0:T(8,128)(2,1)} all-to-all(bf16[4,32,4096]{2,1,0:T(8,128)(2,1)} %normalise.2), channel_id=1, replica_groups=mesh['z'=8,'x'=4,'y'=4,'c'=2] {'y'}, dimensions={0} | all-to-all | bytes 2097152 | tf_op jit(solution)/shard_map/all_to_all | solution.py:405
  114.4 5.5 %all-to-all-start.4 = ((bf16[4,1024,512]{2,1,0:T(8,128)(2,1)}), bf16[4,1024,512]{2,1,0:T(8,128)(2,1)}, u32[]{:S(2)}, u32[]{:S(2)}) async-start(bf16[4,1024,512]{2,1,0:T(8,128)(2,1)} %broadcast_in_dim.27), calls=%async_computation.4 | async-start | bytes 8388608 | tf_op jit(solution)/shard_map/all_to_all | solution.py:31
  120.5 3.4 %collective-permute-start = (s32[1,2]{0,1:T(2,128)S(1)}, s32[1,2]{0,1:T(2,128)S(1)}, u32[]{:S(2)}, u32[]{:S(2)}) collective-permute-start(s32[1,2]{0,1:T(2,128)S(1)} %slice.50), channel_id=1, source_target_pairs={{0,8},{8,16},{16,24},{24,32},{32,40},{40,48},{48,56},{56,64},{64,7... | collective-permute-start | bytes 32 | tf_op jit(solution)/shard_map/ppermute | solution.py:381
  123.9 37.9 %collective-permute-done = s32[1,2]{0,1:T(2,128)S(1)} collective-permute-done((s32[1,2]{0,1:T(2,128)S(1)}, s32[1,2]{0,1:T(2,128)S(1)}, u32[]{:S(2)}, u32[]{:S(2)}) %collective-permute-start) | collective-permute-done | bytes 40 | tf_op jit(solution)/shard_map/ppermute | solution.py:381
  164.7 5.0 %all-to-all-start = ((bf16[4,1040,128]{2,1,0:T(8,128)(2,1)}), bf16[4,1040,128]{2,1,0:T(8,128)(2,1)S(1)}, u32[]{:S(2)}, u32[]{:S(2)}) async-start(bf16[4,1040,128]{2,1,0:T(8,128)(2,1)} %broadcast_in_dim.24), calls=%async_computation | async-start | bytes 2129920 | tf_op jit(solution)/shard_map/all_to_all | solution.py:31
  170.7 5.0 %memorise.3.refs_9_ = bf16[256,512]{1,0:T(8,128)(2,1)} custom-call(bf16[128,4096]{1,0:T(8,128)(2,1)} %bitcast.26.a_ref, bf16[128,4096]{1,0:T(8,128)(2,1)} %copy-done.5, bf16[4096,512]{1,0:T(8,128)(2,1)} %bitcast.21.k_ref), custom_call_target="tpu_custom_call" | custom-call | flops 1073741824 | bytes 4194304 | tf_op jit(solution)/shard_map/memorise/pallas_call | solution.py:189
  175.7 3.2 %collective-permute-start.14 = (bf16[256,512]{1,0:T(8,128)(2,1)}, bf16[256,512]{1,0:T(8,128)(2,1)S(1)}, u32[]{:S(2)}, u32[]{:S(2)}) collective-permute-start(bf16[256,512]{1,0:T(8,128)(2,1)} %memorise.3.refs_9_), channel_id=1, source_target_pairs={{0,224},{32,0},{64,32},{96,64},{128,96},{160,128},{192,160},{224,1... | collective-permute-start | bytes 786440 | tf_op jit(solution)/shard_map/ppermute | solution.py:25
  180.0 5.0 %memorise.2.refs_0_ = bf16[256,512]{1,0:T(8,128)(2,1)} custom-call(bf16[128,4096]{1,0:T(8,128)(2,1)} %bitcast.19.a_ref, bf16[128,4096]{1,0:T(8,128)(2,1)} %copy-done.4, bf16[4096,512]{1,0:T(8,128)(2,1)} %bitcast.21.k_ref), custom_call_target="tpu_custom_call" | custom-call | flops 1073741824 | bytes 4194304 | tf_op jit(solution)/shard_map/memorise/pallas_call | solution.py:189
  185.0 3.2 %collective-permute-start.5 = (bf16[256,512]{1,0:T(8,128)(2,1)}, bf16[256,512]{1,0:T(8,128)(2,1)S(1)}, u32[]{:S(2)}, u32[]{:S(2)}) collective-permute-start(bf16[256,512]{1,0:T(8,128)(2,1)} %memorise.2.refs_0_), channel_id=1, source_target_pairs={{0,224},{32,0},{64,32},{96,64},{128,96},{160,128},{192,160},{224,1... | collective-permute-start | bytes 786440 | tf_op jit(solution)/shard_map/ppermute | solution.py:25
  188.2 3.2 %collective-permute-start.16 = (bf16[256,512]{1,0:T(8,128)(2,1)S(1)}, bf16[256,512]{1,0:T(8,128)(2,1)}, u32[]{:S(2)}, u32[]{:S(2)}) collective-permute-start(bf16[256,512]{1,0:T(8,128)(2,1)S(1)} %collective-permute-done.14.refs_11_), channel_id=1, source_target_pairs={{0,224},{32,0},{64,32},{96,64},{128,96},{160,128},{192,160},{224,1... | collective-permute-start | bytes 786440 | tf_op jit(solution)/shard_map/ppermute | solution.py:25
  191.5 4.1 %collective-permute-done.4.refs_1_ = bf16[256,512]{1,0:T(8,128)(2,1)S(1)} collective-permute-done((bf16[256,512]{1,0:T(8,128)(2,1)}, bf16[256,512]{1,0:T(8,128)(2,1)S(1)}, u32[]{:S(2)}, u32[]{:S(2)}) %collective-permute-start.4) | collective-permute-done | bytes 262176 | tf_op jit(solution)/shard_map/ppermute | solution.py:25
  195.6 3.2 %collective-permute-start.7 = (bf16[256,512]{1,0:T(8,128)(2,1)S(1)}, bf16[256,512]{1,0:T(8,128)(2,1)}, u32[]{:S(2)}, u32[]{:S(2)}) collective-permute-start(bf16[256,512]{1,0:T(8,128)(2,1)S(1)} %collective-permute-done.5.refs_2_), channel_id=1, source_target_pairs={{0,224},{32,0},{64,32},{96,64},{128,96},{160,128},{192,160},{224,1... | collective-permute-start | bytes 786440 | tf_op jit(solution)/shard_map/ppermute | solution.py:25
  201.2 3.3 %collective-permute-start.18 = (bf16[256,512]{1,0:T(8,128)(2,1)}, bf16[256,512]{1,0:T(8,128)(2,1)S(1)}, u32[]{:S(2)}, u32[]{:S(2)}) collective-permute-start(bf16[256,512]{1,0:T(8,128)(2,1)} %collective-permute-done.16.refs_13_), channel_id=1, source_target_pairs={{0,224},{32,0},{64,32},{96,64},{128,96},{160,128},{192,160},{224,1... | collective-permute-start | bytes 786440 | tf_op jit(solution)/shard_map/ppermute | solution.py:25
  206.9 3.2 %collective-permute-start.9 = (bf16[256,512]{1,0:T(8,128)(2,1)}, bf16[256,512]{1,0:T(8,128)(2,1)S(1)}, u32[]{:S(2)}, u32[]{:S(2)}) collective-permute-start(bf16[256,512]{1,0:T(8,128)(2,1)} %collective-permute-done.7.refs_4_), channel_id=1, source_target_pairs={{0,224},{32,0},{64,32},{96,64},{128,96},{160,128},{192,160},{224,1... | collective-permute-start | bytes 786440 | tf_op jit(solution)/shard_map/ppermute | solution.py:25
  212.5 3.2 %collective-permute-start.20 = (bf16[128,512]{1,0:T(8,128)(2,1)}, bf16[128,512]{1,0:T(8,128)(2,1)}, u32[]{:S(2)}, u32[]{:S(2)}) collective-permute-start(bf16[128,512]{1,0:T(8,128)(2,1)} %slice.78), channel_id=1, source_target_pairs={{0,224},{32,0},{64,32},{96,64},{128,96},{160,128},{192,160},{224,1... | collective-permute-start | bytes 393224 | tf_op jit(solution)/shard_map/ppermute | solution.py:25
  217.4 3.2 %collective-permute-start.11 = (bf16[128,512]{1,0:T(8,128)(2,1)}, bf16[128,512]{1,0:T(8,128)(2,1)}, u32[]{:S(2)}, u32[]{:S(2)}) collective-permute-start(bf16[128,512]{1,0:T(8,128)(2,1)} %slice.74), channel_id=1, source_target_pairs={{0,224},{32,0},{64,32},{96,64},{128,96},{160,128},{192,160},{224,1... | collective-permute-start | bytes 393224 | tf_op jit(solution)/shard_map/ppermute | solution.py:25
  230.5 15.7 %windows.1 = bf16[4,1056,128]{2,1,0:T(8,128)(2,1)} custom-call(s32[33,2]{1,0:T(8,128)} %copy.23.ids_ref, s32[3]{0:T(128)} %pad_add_fusion.1.at_ref, bf16[4,1040,128]{2,1,0:T(8,128)(2,1)} %copy-done.1, bf16[256,512]{1,0:T(8,128)(2,1)} %memorise.2.refs_0_, bf16[256,512]{1,0:T(8,128)(2,1)} %copy-done.12, bf16[256,512]{1,0:T(8,128)(2,1)} %copy-done.13, ...), custom_call_target="tpu_custom_call" | custom-call | flops 1000000000 | bytes 8388608 | tf_op jit(solution)/shard_map/windows/pallas_call | solution.py:319
  246.2 20.5 %all_to_all.41.parts_ref = bf16[4,1056,128]{2,1,0:T(8,128)(2,1)} all-to-all(bf16[4,1056,128]{2,1,0:T(8,128)(2,1)} %windows.1), channel_id=1, replica_groups=mesh['z'=8,'x'=4,'y'=4,'c'=2] {'x'}, dimensions={0} | all-to-all | bytes 2162688 | tf_op jit(solution)/shard_map/all_to_all | solution.py:413
  266.7 2.6 combine.1
  (96 shorter events, 33.2 us)
Async XLA Ops:
  0.0 26.9 %collective-permute-start.2 = (bf16[256,4096]{1,0:T(8,128)(2,1)}, bf16[256,4096]{1,0:T(8,128)(2,1)S(1)}, u32[]{:S(2)}, u32[]{:S(2)}) collective-permute-start(bf16[256,4096]{1,0:T(8,128)(2,1)} %bitcast.37), channel_id=1, source_target_pairs={{0,1},{1,0},{2,3},{3,2},{4,5},{5,4},{6,7},{7,6},{8,9},{9,8},{10,11... | collective-permute-start | bytes 6291464 | tf_op jit(solution)/shard_map/ppermute | solution.py:25
  2.0 37.9 %all-to-all-start.3 = ((bf16[8,128,512]{2,1,0:T(8,128)(2,1)}), bf16[8,128,512]{2,1,0:T(8,128)(2,1)S(1)}, u32[]{:S(2)}, u32[]{:S(2)}) async-start(bf16[8,128,512]{2,1,0:T(8,128)(2,1)} %broadcast_in_dim.25), calls=%async_computation.3 | async-start | bytes 2097152 | tf_op jit(solution)/shard_map/all_to_all | solution.py:31
  24.5 1.8 collective-permute-start.1
  39.9 19.8 %all-to-all-start.5 = ((bf16[4,32,4096]{2,1,0:T(8,128)(2,1)}), bf16[4,32,4096]{2,1,0:T(8,128)(2,1)S(1)}, u32[]{:S(2)}, u32[]{:S(2)}) async-start(bf16[4,32,4096]{2,1,0:T(8,128)(2,1)} %bitcast.42), calls=%async_computation.5 | async-start | bytes 2097152 | tf_op jit(solution)/shard_map/all_to_all | solution.py:402
  59.7 17.9 %all-to-all-start.1 = ((bf16[4,32,4096]{2,1,0:T(8,128)(2,1)}), bf16[4,32,4096]{2,1,0:T(8,128)(2,1)S(1)}, u32[]{:S(2)}, u32[]{:S(2)}) async-start(bf16[4,32,4096]{2,1,0:T(8,128)(2,1)} %bitcast.41), calls=%async_computation.1 | async-start | bytes 2097152 | tf_op jit(solution)/shard_map/all_to_all | solution.py:402
  77.6 17.8 %all-to-all-start.6 = ((bf16[4,32,4096]{2,1,0:T(8,128)(2,1)}), bf16[4,32,4096]{2,1,0:T(8,128)(2,1)}, u32[]{:S(2)}, u32[]{:S(2)}) async-start(bf16[4,32,4096]{2,1,0:T(8,128)(2,1)} %normalise.3), calls=%async_computation.6 | async-start | bytes 2097152 | tf_op jit(solution)/shard_map/all_to_all | solution.py:405
  114.4 47.6 %copy-start.15 = (bf16[512,2,128]{2,1,0:T(2,128)(2,1)S(1)}, bf16[512,2,128]{2,1,0:T(2,128)(2,1)}, u32[]{:S(2)}) copy-start(bf16[512,2,128]{2,1,0:T(2,128)(2,1)} %param.14) | copy-start | bytes 786436
  114.4 49.2 %all-to-all-start.4 = ((bf16[4,1024,512]{2,1,0:T(8,128)(2,1)}), bf16[4,1024,512]{2,1,0:T(8,128)(2,1)}, u32[]{:S(2)}, u32[]{:S(2)}) async-start(bf16[4,1024,512]{2,1,0:T(8,128)(2,1)} %broadcast_in_dim.27), calls=%async_computation.4 | async-start | bytes 8388608 | tf_op jit(solution)/shard_map/all_to_all | solution.py:31
  119.9 49.8 %collective-permute-start.12 = (bf16[128,4096]{1,0:T(8,128)(2,1)}, bf16[128,4096]{1,0:T(8,128)(2,1)S(1)}, u32[]{:S(2)}, u32[]{:S(2)}) collective-permute-start(bf16[128,4096]{1,0:T(8,128)(2,1)} %bitcast.26.a_ref), channel_id=1, source_target_pairs={{0,1},{1,0},{2,3},{3,2},{4,5},{5,4},{6,7},{7,6},{8,9},{9,8},{10,11... | collective-permute-start | bytes 3145736 | tf_op jit(solution)/shard_map/ppermute | solution.py:25
  119.9 59.1 %collective-permute-start.3 = (bf16[128,4096]{1,0:T(8,128)(2,1)}, bf16[128,4096]{1,0:T(8,128)(2,1)S(1)}, u32[]{:S(2)}, u32[]{:S(2)}) collective-permute-start(bf16[128,4096]{1,0:T(8,128)(2,1)} %bitcast.19.a_ref), channel_id=1, source_target_pairs={{0,1},{1,0},{2,3},{3,2},{4,5},{5,4},{6,7},{7,6},{8,9},{9,8},{10,11... | collective-permute-start | bytes 3145736 | tf_op jit(solution)/shard_map/ppermute | solution.py:25
  120.5 41.3 %collective-permute-start = (s32[1,2]{0,1:T(2,128)S(1)}, s32[1,2]{0,1:T(2,128)S(1)}, u32[]{:S(2)}, u32[]{:S(2)}) collective-permute-start(s32[1,2]{0,1:T(2,128)S(1)} %slice.50), channel_id=1, source_target_pairs={{0,8},{8,16},{16,24},{24,32},{32,40},{40,48},{48,56},{56,64},{64,7... | collective-permute-start | bytes 32 | tf_op jit(solution)/shard_map/ppermute | solution.py:381
  164.7 46.1 %all-to-all-start = ((bf16[4,1040,128]{2,1,0:T(8,128)(2,1)}), bf16[4,1040,128]{2,1,0:T(8,128)(2,1)S(1)}, u32[]{:S(2)}, u32[]{:S(2)}) async-start(bf16[4,1040,128]{2,1,0:T(8,128)(2,1)} %broadcast_in_dim.24), calls=%async_computation | async-start | bytes 2129920 | tf_op jit(solution)/shard_map/all_to_all | solution.py:31
  175.7 12.5 %collective-permute-start.13 = (bf16[256,512]{1,0:T(8,128)(2,1)}, bf16[256,512]{1,0:T(8,128)(2,1)S(1)}, u32[]{:S(2)}, u32[]{:S(2)}) collective-permute-start(bf16[256,512]{1,0:T(8,128)(2,1)} %memorise.3.refs_9_), channel_id=1, source_target_pairs={{0,32},{32,64},{64,96},{96,128},{128,160},{160,192},{192,224},{224... | collective-permute-start | bytes 786440 | tf_op jit(solution)/shard_map/ppermute | solution.py:25
  175.7 12.5 %collective-permute-start.14 = (bf16[256,512]{1,0:T(8,128)(2,1)}, bf16[256,512]{1,0:T(8,128)(2,1)S(1)}, u32[]{:S(2)}, u32[]{:S(2)}) collective-permute-start(bf16[256,512]{1,0:T(8,128)(2,1)} %memorise.3.refs_9_), channel_id=1, source_target_pairs={{0,224},{32,0},{64,32},{96,64},{128,96},{160,128},{192,160},{224,1... | collective-permute-start | bytes 786440 | tf_op jit(solution)/shard_map/ppermute | solution.py:25
  185.0 10.6 %collective-permute-start.4 = (bf16[256,512]{1,0:T(8,128)(2,1)}, bf16[256,512]{1,0:T(8,128)(2,1)S(1)}, u32[]{:S(2)}, u32[]{:S(2)}) collective-permute-start(bf16[256,512]{1,0:T(8,128)(2,1)} %memorise.2.refs_0_), channel_id=1, source_target_pairs={{0,32},{32,64},{64,96},{96,128},{128,160},{160,192},{192,224},{224... | collective-permute-start | bytes 786440 | tf_op jit(solution)/shard_map/ppermute | solution.py:25
  185.0 10.6 %collective-permute-start.5 = (bf16[256,512]{1,0:T(8,128)(2,1)}, bf16[256,512]{1,0:T(8,128)(2,1)S(1)}, u32[]{:S(2)}, u32[]{:S(2)}) collective-permute-start(bf16[256,512]{1,0:T(8,128)(2,1)} %memorise.2.refs_0_), channel_id=1, source_target_pairs={{0,224},{32,0},{64,32},{96,64},{128,96},{160,128},{192,160},{224,1... | collective-permute-start | bytes 786440 | tf_op jit(solution)/shard_map/ppermute | solution.py:25
  188.2 41.7 %copy-start.10 = (bf16[256,512]{1,0:T(8,128)(2,1)}, bf16[256,512]{1,0:T(8,128)(2,1)S(1)}, u32[]{:S(2)}) copy-start(bf16[256,512]{1,0:T(8,128)(2,1)S(1)} %collective-permute-done.13.refs_10_) | copy-start | bytes 786436
  188.2 13.0 %collective-permute-start.15 = (bf16[256,512]{1,0:T(8,128)(2,1)S(1)}, bf16[256,512]{1,0:T(8,128)(2,1)S(1)}, u32[]{:S(2)}, u32[]{:S(2)}) collective-permute-start(bf16[256,512]{1,0:T(8,128)(2,1)S(1)} %collective-permute-done.13.refs_10_), channel_id=1, source_target_pairs={{0,32},{32,64},{64,96},{96,128},{128,160},{160,192},{192,224},{224... | collective-permute-start | bytes 786440 | tf_op jit(solution)/shard_map/ppermute | solution.py:25
  188.2 41.7 %copy-start.11 = (bf16[256,512]{1,0:T(8,128)(2,1)}, bf16[256,512]{1,0:T(8,128)(2,1)S(1)}, u32[]{:S(2)}) copy-start(bf16[256,512]{1,0:T(8,128)(2,1)S(1)} %collective-permute-done.14.refs_11_) | copy-start | bytes 786436
  188.2 13.0 %collective-permute-start.16 = (bf16[256,512]{1,0:T(8,128)(2,1)S(1)}, bf16[256,512]{1,0:T(8,128)(2,1)}, u32[]{:S(2)}, u32[]{:S(2)}) collective-permute-start(bf16[256,512]{1,0:T(8,128)(2,1)S(1)} %collective-permute-done.14.refs_11_), channel_id=1, source_target_pairs={{0,224},{32,0},{64,32},{96,64},{128,96},{160,128},{192,160},{224,1... | collective-permute-start | bytes 786440 | tf_op jit(solution)/shard_map/ppermute | solution.py:25
  195.6 34.3 %copy-start.12 = (bf16[256,512]{1,0:T(8,128)(2,1)}, bf16[256,512]{1,0:T(8,128)(2,1)S(1)}, u32[]{:S(2)}) copy-start(bf16[256,512]{1,0:T(8,128)(2,1)S(1)} %collective-permute-done.4.refs_1_) | copy-start | bytes 786436
  195.6 11.3 %collective-permute-start.6 = (bf16[256,512]{1,0:T(8,128)(2,1)S(1)}, bf16[256,512]{1,0:T(8,128)(2,1)}, u32[]{:S(2)}, u32[]{:S(2)}) collective-permute-start(bf16[256,512]{1,0:T(8,128)(2,1)S(1)} %collective-permute-done.4.refs_1_), channel_id=1, source_target_pairs={{0,32},{32,64},{64,96},{96,128},{128,160},{160,192},{192,224},{224... | collective-permute-start | bytes 786440 | tf_op jit(solution)/shard_map/ppermute | solution.py:25
  195.6 34.3 %copy-start.13 = (bf16[256,512]{1,0:T(8,128)(2,1)}, bf16[256,512]{1,0:T(8,128)(2,1)S(1)}, u32[]{:S(2)}) copy-start(bf16[256,512]{1,0:T(8,128)(2,1)S(1)} %collective-permute-done.5.refs_2_) | copy-start | bytes 786436
  195.6 11.3 %collective-permute-start.7 = (bf16[256,512]{1,0:T(8,128)(2,1)S(1)}, bf16[256,512]{1,0:T(8,128)(2,1)}, u32[]{:S(2)}, u32[]{:S(2)}) collective-permute-start(bf16[256,512]{1,0:T(8,128)(2,1)S(1)} %collective-permute-done.5.refs_2_), channel_id=1, source_target_pairs={{0,224},{32,0},{64,32},{96,64},{128,96},{160,128},{192,160},{224,1... | collective-permute-start | bytes 786440 | tf_op jit(solution)/shard_map/ppermute | solution.py:25
  201.2 9.8 %collective-permute-start.17 = (bf16[256,512]{1,0:T(8,128)(2,1)S(1)}, bf16[256,512]{1,0:T(8,128)(2,1)S(1)}, u32[]{:S(2)}, u32[]{:S(2)}) collective-permute-start(bf16[256,512]{1,0:T(8,128)(2,1)S(1)} %collective-permute-done.15.refs_12_), channel_id=1, source_target_pairs={{0,32},{32,64},{64,96},{96,128},{128,160},{160,192},{192,224},{224... | collective-permute-start | bytes 786440 | tf_op jit(solution)/shard_map/ppermute | solution.py:25
  201.2 10.7 %collective-permute-start.18 = (bf16[256,512]{1,0:T(8,128)(2,1)}, bf16[256,512]{1,0:T(8,128)(2,1)S(1)}, u32[]{:S(2)}, u32[]{:S(2)}) collective-permute-start(bf16[256,512]{1,0:T(8,128)(2,1)} %collective-permute-done.16.refs_13_), channel_id=1, source_target_pairs={{0,224},{32,0},{64,32},{96,64},{128,96},{160,128},{192,160},{224,1... | collective-permute-start | bytes 786440 | tf_op jit(solution)/shard_map/ppermute | solution.py:25
  206.9 9.0 %collective-permute-start.8 = (bf16[256,512]{1,0:T(8,128)(2,1)}, bf16[256,512]{1,0:T(8,128)(2,1)S(1)}, u32[]{:S(2)}, u32[]{:S(2)}) collective-permute-start(bf16[256,512]{1,0:T(8,128)(2,1)} %collective-permute-done.6.refs_3_), channel_id=1, source_target_pairs={{0,32},{32,64},{64,96},{96,128},{128,160},{160,192},{192,224},{224... | collective-permute-start | bytes 786440 | tf_op jit(solution)/shard_map/ppermute | solution.py:25
  206.9 9.8 %collective-permute-start.9 = (bf16[256,512]{1,0:T(8,128)(2,1)}, bf16[256,512]{1,0:T(8,128)(2,1)S(1)}, u32[]{:S(2)}, u32[]{:S(2)}) collective-permute-start(bf16[256,512]{1,0:T(8,128)(2,1)} %collective-permute-done.7.refs_4_), channel_id=1, source_target_pairs={{0,224},{32,0},{64,32},{96,64},{128,96},{160,128},{192,160},{224,1... | collective-permute-start | bytes 786440 | tf_op jit(solution)/shard_map/ppermute | solution.py:25
  211.8 18.0 %collective-permute-start.19 = (bf16[128,512]{1,0:T(8,128)(2,1)}, bf16[128,512]{1,0:T(8,128)(2,1)S(1)}, u32[]{:S(2)}, u32[]{:S(2)}) collective-permute-start(bf16[128,512]{1,0:T(8,128)(2,1)} %slice.77), channel_id=1, source_target_pairs={{0,32},{32,64},{64,96},{96,128},{128,160},{160,192},{192,224},{224... | collective-permute-start | bytes 393224 | tf_op jit(solution)/shard_map/ppermute | solution.py:25
  212.5 17.3 %collective-permute-start.20 = (bf16[128,512]{1,0:T(8,128)(2,1)}, bf16[128,512]{1,0:T(8,128)(2,1)}, u32[]{:S(2)}, u32[]{:S(2)}) collective-permute-start(bf16[128,512]{1,0:T(8,128)(2,1)} %slice.78), channel_id=1, source_target_pairs={{0,224},{32,0},{64,32},{96,64},{128,96},{160,128},{192,160},{224,1... | collective-permute-start | bytes 393224 | tf_op jit(solution)/shard_map/ppermute | solution.py:25
  216.7 13.2 %collective-permute-start.10 = (bf16[128,512]{1,0:T(8,128)(2,1)}, bf16[128,512]{1,0:T(8,128)(2,1)}, u32[]{:S(2)}, u32[]{:S(2)}) collective-permute-start(bf16[128,512]{1,0:T(8,128)(2,1)} %slice.73), channel_id=1, source_target_pairs={{0,32},{32,64},{64,96},{96,128},{128,160},{160,192},{192,224},{224... | collective-permute-start | bytes 393224 | tf_op jit(solution)/shard_map/ppermute | solution.py:25
  217.4 12.5 %collective-permute-start.11 = (bf16[128,512]{1,0:T(8,128)(2,1)}, bf16[128,512]{1,0:T(8,128)(2,1)}, u32[]{:S(2)}, u32[]{:S(2)}) collective-permute-start(bf16[128,512]{1,0:T(8,128)(2,1)} %slice.74), channel_id=1, source_target_pairs={{0,224},{32,0},{64,32},{96,64},{128,96},{160,128},{192,160},{224,1... | collective-permute-start | bytes 393224 | tf_op jit(solution)/shard_map/ppermute | solution.py:25
  (13 other events, 130.0 us)

commit v2 on v1

--- a/solution.py
+++ b/solution.py
@@ -12,7 +12,6 @@
 NZ, NX, NY, NC = 8, 4, 4, 2
 ROW = 128
 HS = 128
-CHUNKS = 2
 MASKED = -1e30
 BF = jnp.bfloat16
 F32 = jnp.float32
@@ -31,7 +30,7 @@
     return lax.all_to_all(copies, axis, split_axis=0, concat_axis=0, tiled=True)
 
 
-def encoder_kernel(core_ref, x_ref, w_ref, g_ref, out_ref, wide, wmat, acc, ssq):
+def encoder_kernel(core_ref, x_ref, w_ref, g_ref, own_ref, send_ref, wide, wmat, acc, ssq):
     step = pl.program_id(0)
     depth = x_ref.shape[1]
 
@@ -68,9 +67,16 @@
                 p = jnp.exp(s - m)
                 p = (p / jnp.sum(p, axis=1, keepdims=True)).astype(BF)
                 parts.append(jnp.dot(p, v, preferred_element_type=F32).astype(BF))
-            place = (r // 2 + core) % 2
             att = jnp.concatenate(parts, axis=1)
-            out_ref[place, r % 2] = att
+            spot = slice((r % 2) * ROW, (r % 2 + 1) * ROW)
+
+            @pl.when(core == r // 2)
+            def _():
+                own_ref[spot, :] = att
+
+            @pl.when(core != r // 2)
+            def _():
+                send_ref[spot, :] = att
 
 
 def encode(corpus_flat, w_rows, gain, core):
@@ -87,7 +93,7 @@
                 pl.BlockSpec((depth * 6, HS), lambda i, c: (i, 0)),
                 pl.BlockSpec((1, depth), lambda i, c: (0, i)),
             ],
-            out_specs=pl.BlockSpec((2, 2, ROW, 2 * HS), lambda i, c: (0, 0, 0, 0)),
+            out_specs=[pl.BlockSpec((2 * ROW, 2 * HS), lambda i, c: (0, 0))] * 2,
             scratch_shapes=[
                 pltpu.VMEM((depth * 6, HS), F32),
                 pltpu.VMEM((depth, 6 * HS), BF),
@@ -95,7 +101,7 @@
                 pltpu.VMEM((tokens, 1), F32),
             ],
         ),
-        out_shape=jax.ShapeDtypeStruct((2, 2, ROW, 2 * HS), BF),
+        out_shape=[jax.ShapeDtypeStruct((2 * ROW, 2 * HS), BF)] * 2,
         cost_estimate=pl.CostEstimate(
             flops=2 * tokens * width * 6 * HS, bytes_accessed=(tokens + 768) * width * 2, transcendentals=0
         ),
@@ -153,7 +159,7 @@
             num_scalar_prefetch=1,
             grid=(1,),
             in_specs=[
-                pl.BlockSpec((NY, rows, width), lambda i, b: (0, 0, 0)),
+                VMEM_ALL,
                 pl.BlockSpec((rows, width), lambda i, b: (b[0], 0)),
                 pl.BlockSpec((1, width), lambda i, b: (0, 0)),
             ],
@@ -165,43 +171,53 @@
     )(block, terms, corpus_flat, gain)
 
 
-def memory_kernel(a_ref, b_ref, k_ref, out_ref, acc):
-    step = pl.program_id(0)
-    half = a_ref.shape[0]
-
-    @pl.when(step == 0)
-    def _():
-        acc[...] = jnp.zeros_like(acc)
-
-    u = jnp.concatenate([a_ref[...], b_ref[...]], axis=0)
-    acc[...] += jnp.dot(u, k_ref[...], preferred_element_type=F32)
-
-    @pl.when(step == pl.num_programs(0) - 1)
-    def _():
-        out_ref[...] = acc[...].astype(BF)
-
-
-def memorise(u_own, u_other, weight):
+ORDER = (0, NX - 1, 1, 2)
+
+
+def memory_kernel(x_ref, a_ref, b_ref, k0, k1, k2, k3, out_ref, ua, ub, kv, sem):
+    depth = NZ * HS
+    half = ua.shape[1]
+    copies = []
+    for i, k_ref in enumerate((k0, k1, k2, k3)):
+        first = pl.multiple_of(lax.rem(x_ref[0] + ORDER[i], NX) * depth, depth)
+        copies.append((
+            pltpu.make_async_copy(k_ref.at[pl.ds(0, depth)], kv.at[i], sem.at[0, i]),
+            pltpu.make_async_copy(a_ref.at[:, pl.ds(first, depth)], ua.at[i], sem.at[1, i]),
+            pltpu.make_async_copy(b_ref.at[:, pl.ds(first, depth)], ub.at[i], sem.at[2, i]),
+        ))
+    for group in copies:
+        for copy in group:
+            copy.start()
+    totals = [jnp.zeros((half, out_ref.shape[1]), F32) for _ in range(2)]
+    for i, group in enumerate(copies):
+        for copy in group:
+            copy.wait()
+        for part, u in enumerate((ua, ub)):
+            totals[part] += jnp.dot(u[i], kv[i], preferred_element_type=F32)
+    for part in range(2):
+        out_ref[part * half:(part + 1) * half, :] = totals[part].astype(BF)
+
+
+def memorise(my_x, u_own, u_other, payloads):
     half, width = u_own.shape
-    cols = weight.shape[1]
-    steps = 4
-    depth = width // steps
+    cols = payloads[0].shape[1]
+    depth = width // NX
     return pl.pallas_call(
         memory_kernel,
-        grid=(steps,),
-        in_specs=[
-            pl.BlockSpec((half, depth), lambda i: (0, i)),
-            pl.BlockSpec((half, depth), lambda i: (0, i)),
-            pl.BlockSpec((depth, cols), lambda i: (i, 0)),
+        in_specs=[pl.BlockSpec(memory_space=pltpu.SMEM)] + [ANY] * 6,
+        out_specs=VMEM_ALL,
+        scratch_shapes=[
+            pltpu.VMEM((NX, half, depth), BF),
+            pltpu.VMEM((NX, half, depth), BF),
+            pltpu.VMEM((NX, depth, cols), BF),
+            pltpu.SemaphoreType.DMA((3, NX)),
         ],
-        out_specs=pl.BlockSpec((2 * half, cols), lambda i: (0, 0)),
-        scratch_shapes=[pltpu.VMEM((2 * half, cols), F32)],
         out_shape=jax.ShapeDtypeStruct((2 * half, cols), BF),
         cost_estimate=pl.CostEstimate(
             flops=4 * half * width * cols, bytes_accessed=2 * width * cols, transcendentals=0
         ),
         name="memorise",
-    )(u_own, u_other, weight)
+    )(my_x, u_own, u_other, *payloads)
 
 
 def ring_pieces(block):
@@ -221,81 +237,102 @@
 
 
 PAD = 8
-
-
-def window_kernel(layout, ids_ref, at_ref, q_ref, *refs):
-    pieces = refs[:len(layout)]
-    out_ref = refs[len(layout)]
-    table, qs, outs, stats, sem = refs[len(layout) + 1:]
-    copies = []
-    for i, (chunk, distance, first, rows) in enumerate(layout):
-        copies.append(
-            pltpu.make_async_copy(pieces[i], table.at[distance, chunk, pl.ds(first, rows)], sem.at[i])
-        )
-    for copy in copies:
+Q_FIRST = NZ * HS
+
+
+def window_kernel(layout, ids_ref, at_ref, *refs):
+    payloads = refs[:NX]
+    pieces = refs[NX:NX + len(layout)]
+    out_ref = refs[NX + len(layout)]
+    table, q_in, qs, outs, stats, active, sem, q_sem = refs[NX + len(layout) + 1:]
+    my_z, my_x, core = at_ref[0], at_ref[1], at_ref[2]
+    count_all = NX * 8 + 1
+    plane_rows = NX * 1024
+    total_rows = qs.shape[0]
+    q_copies = [
+        pltpu.make_async_copy(payloads[i].at[pl.ds(Q_FIRST, 256)], q_in.at[i], q_sem.at[i]) for i in range(NX)
+    ]
+    copies = [
+        pltpu.make_async_copy(pieces[i], table.at[distance, pl.ds(first, rows)], sem.at[i])
+        for i, (distance, first, rows) in enumerate(layout)
+    ]
+    for copy in q_copies + copies:
         copy.start()
-    my_z, my_x, core = at_ref[0], at_ref[1], at_ref[2]
-    plane_rows = NX * 1024
+    outs[...] = jnp.zeros_like(outs)
+    stats[...] = jnp.full_like(stats, MASKED)
     qs[0:PAD, :] = jnp.zeros((PAD, HS), F32)
-    qs[PAD + plane_rows:, :] = jnp.zeros((qs.shape[0] - PAD - plane_rows, HS), F32)
-    for x in range(NX):
-        qs[PAD + x * 1024:PAD + (x + 1) * 1024, :] = q_ref[x, 0:1024].astype(F32)
+    qs[PAD + plane_rows:, :] = jnp.zeros((total_rows - PAD - plane_rows, HS), F32)
+    for i in range(NX):
+        base = PAD + lax.rem(my_x + ORDER[i], NX) * 1024
+        q_copies[i].wait()
+        for b in range(4):
+            first = pl.multiple_of(base + b * 256, 8)
+            qs[pl.ds(first, 256), :] = q_in[i, :, b * HS:(b + 1) * HS].astype(F32)
     for copy in copies:
         copy.wait()
+
+    def held(row):
+        return jnp.logical_and(row >= 0, lax.rem(jnp.maximum(row, 0) // 4, NX) == my_x)
+
+    def wanted(w, n):
+        group = jnp.maximum(w - 1, 0)
+        step = lax.rem(group // 8 - my_x + NX, NX)
+        return ids_ref[step * 18 + jnp.where(w == 0, 0, lax.rem(group, 8) + 1) * 2 + n]
+
+    def note(w, count):
+        use = jnp.logical_or(held(wanted(w, 0)), held(wanted(w, 1)))
+        active[count] = w
+        return count + use.astype(jnp.int32)
+
+    count = lax.fori_loop(0, count_all, note, 0)
 
     def place(row):
         row = jnp.maximum(row, 0)
         distance = lax.rem(my_z - row // 16 + NZ, NZ)
         local = lax.rem(row, 4)
-        chunk = lax.rem(local, 2)
         half = lax.rem(local // 2 + core, 2)
-        return distance, chunk, pl.multiple_of(half * ROW, ROW)
-
-    def held(row):
-        return jnp.logical_and(row >= 0, lax.rem(jnp.maximum(row, 0) // 4, NX) == my_x)
-
-    def body(w, carry):
+        return distance, pl.multiple_of(half * 2 * ROW + lax.rem(local, 2) * ROW, ROW)
+
+    def window(w):
         start = PAD + 2 * (GROUP * w - 1)
-        rows = [ids_ref[w, n] for n in range(2)]
+        rows = [wanted(w, n) for n in range(2)]
         ok = [held(row) for row in rows]
-        any_ok = jnp.logical_or(ok[0], ok[1])
-
-        @pl.when(any_ok)
-        def _():
-            spots = [place(row) for row in rows]
-            for h in range(2):
-                q = qs[pl.ds(start + h, GROUP, stride=2), :].astype(BF)
-                scores = []
-                for n in range(2):
-                    d, c, first = spots[n]
-                    k = table[d, c, pl.ds(first, ROW), h * 256:h * 256 + HS]
-                    s = lax.dot_general(q, k, (((1,), (1,)), ((), ())), preferred_element_type=F32)
-                    s = s * (HS ** -0.5)
-                    scores.append(jnp.where(ok[n], s, MASKED))
-                m = jnp.maximum(
-                    jnp.max(scores[0], axis=1, keepdims=True), jnp.max(scores[1], axis=1, keepdims=True)
-                )
-                probs = [jnp.exp(s - m) for s in scores]
-                total = jnp.sum(probs[0], axis=1, keepdims=True) + jnp.sum(probs[1], axis=1, keepdims=True)
-                inv = 1.0 / total
-                out = jnp.zeros((GROUP, HS), F32)
-                for n in range(2):
-                    d, c, first = spots[n]
-                    v = table[d, c, pl.ds(first, ROW), h * 256 + HS:h * 256 + 2 * HS]
-                    out += jnp.dot((probs[n] * inv).astype(BF), v, preferred_element_type=F32)
-                outs[pl.ds(start + h, GROUP, stride=2), :] = out
-                lse = m + jnp.log(total)
-                stats[pl.ds(start + h, GROUP, stride=2), :] = jnp.broadcast_to(lse, (GROUP, HS))
-
-        @pl.when(jnp.logical_not(any_ok))
-        def _():
-            for h in range(2):
-                outs[pl.ds(start + h, GROUP, stride=2), :] = jnp.zeros((GROUP, HS), F32)
-                stats[pl.ds(start + h, GROUP, stride=2), :] = jnp.full((GROUP, HS), MASKED, F32)
-
+        spots = [place(row) for row in rows]
+        results = []
+        for h in range(2):
+            q = qs[pl.ds(start + h, GROUP, stride=2), :].astype(BF)
+            scores = []
+            for n in range(2):
+                d, first = spots[n]
+                k = table[d, pl.ds(first, ROW), h * 256:h * 256 + HS]
+                s = lax.dot_general(q, k, (((1,), (1,)), ((), ())), preferred_element_type=F32)
+                s = s * (HS ** -0.5)
+                scores.append(jnp.where(ok[n], s, MASKED))
+            m = jnp.max(jnp.maximum(scores[0], scores[1]), axis=1, keepdims=True)
+            probs = [jnp.exp(s - m) for s in scores]
+            total = jnp.sum(probs[0] + probs[1], axis=1, keepdims=True)
+            inv = 1.0 / total
+            out = jnp.zeros((GROUP, HS), F32)
+            for n in range(2):
+                d, first = spots[n]
+                v = table[d, pl.ds(first, ROW), h * 256 + HS:h * 256 + 2 * HS]
+                out += jnp.dot((probs[n] * inv).astype(BF), v, preferred_element_type=F32)
+            lse = jnp.broadcast_to(m + jnp.log(total), (GROUP, HS))
+            results.append((start + h, out, lse))
+        return results
+
+    side = 2
+
+    def body(i, carry):
+        results = []
+        for lane in range(side):
+            results += window(active[jnp.minimum(i * side + lane, count - 1)])
+        for first, out, lse in results:
+            outs[pl.ds(first, GROUP, stride=2), :] = out
+            stats[pl.ds(first, GROUP, stride=2), :] = lse
         return carry
 
-    lax.fori_loop(0, ids_ref.shape[0], body, 0)
+    lax.fori_loop(0, (count + side - 1) // side, body, 0)
     eye = lax.broadcasted_iota(jnp.int32, (HS, HS), 0) == lax.broadcasted_iota(jnp.int32, (HS, HS), 1)
     for x in range(NX):
         base = PAD + x * 1024
@@ -313,28 +350,28 @@
         out_ref[x, 1024:1056] = tail.astype(BF)
 
 
-def windows(ids, at, q_plane, pieces):
-    layout = tuple((chunk, d, first, rows) for chunk, d, first, rows, _ in pieces)
+def windows(ids, at, payloads, pieces):
+    layout = tuple((d, first, rows) for d, first, rows, _ in pieces)
     total = PAD + NX * 1024 + 2 * GROUP
+    smem = pl.BlockSpec(memory_space=pltpu.SMEM)
     return pl.pallas_call(
         functools.partial(window_kernel, layout),
-        grid_spec=pltpu.PrefetchScalarGridSpec(
-            num_scalar_prefetch=2,
-            grid=(1,),
-            in_specs=[pl.BlockSpec(q_plane.shape, lambda i, a, b: (0, 0, 0))] + [ANY] * len(pieces),
-            out_specs=pl.BlockSpec((NX, 1056, HS), lambda i, a, b: (0, 0, 0)),
-            scratch_shapes=[
-                pltpu.VMEM((NZ, CHUNKS, 4 * ROW // CHUNKS, 512), BF),
-                pltpu.VMEM((total, HS), F32),
-                pltpu.VMEM((total, HS), F32),
-                pltpu.VMEM((total, HS), F32),
-                pltpu.SemaphoreType.DMA((len(pieces),)),
-            ],
-        ),
+        in_specs=[smem, smem] + [ANY] * (NX + len(pieces)),
+        out_specs=VMEM_ALL,
+        scratch_shapes=[
+            pltpu.VMEM((NZ, 4 * ROW, 512), BF),
+            pltpu.VMEM((NX, 256, 512), BF),
+            pltpu.VMEM((total, HS), F32),
+            pltpu.VMEM((total, HS), F32),
+            pltpu.VMEM((total, HS), F32),
+            pltpu.SMEM((NX * 8 + 2,), jnp.int32),
+            pltpu.SemaphoreType.DMA((len(pieces),)),
+            pltpu.SemaphoreType.DMA((NX,)),
+        ],
         out_shape=jax.ShapeDtypeStruct((NX, 1056, HS), BF),
         cost_estimate=pl.CostEstimate(flops=10**9, bytes_accessed=8 * 2**20, transcendentals=10**6),
         name="windows",
-    )(ids, at, q_plane, *[piece[-1] for piece in pieces])
+    )(ids, at, *payloads, *[piece[-1] for piece in pieces])
 
 
 def combine_kernel(parts_ref, out_ref):
@@ -374,42 +411,41 @@
     e_own = enc_out.reshape(2 * HS, width)
     e_other = shifted(e_own, "c", 1)
 
+    last = lax.ppermute(nbr_ids[7:], ("z", "x"), [(i, i + 1) for i in range(NZ * NX - 1)])
+    last = jnp.where(jnp.logical_and(my_z == 0, my_x == 0), -1, last)
+    ids = jnp.concatenate([last, nbr_ids], axis=0).astype(BF)
+
     kv = lax.optimization_barrier(cca_kv.reshape(cca_kv.shape[0], 512))
     kv = spread(kv, "z").reshape(-1, 512)
-    kv = spread(kv, "x").reshape(-1, 512)
-
-    last = lax.ppermute(
-        nbr_ids[7:], ("z", "x"), [(i, i + 1) for i in range(NZ * NX - 1)]
+    q_rows = queries.reshape(4, 256, HS)
+    q_wide = jnp.concatenate([q_rows[b] for b in range(4)], axis=1)
+    payload = jnp.concatenate([kv, q_wide, jnp.pad(ids, ((0, 7), (0, 510)))], axis=0)
+    from_left = shifted(payload, "x", 1)
+    from_right = shifted(payload, "x", -1)
+    from_far = shifted(payload, "x", 2)
+
+    w_rows = enc_qkv.transpose(0, 2, 1, 3).reshape(width * 6, HS)
+    att_own, att_send = encode(
+        corpus_flat, w_rows, gain_in.reshape(1, width), core.reshape(1).astype(jnp.int32)
     )
-    last = jnp.where(jnp.logical_and(my_z == 0, my_x == 0), -1, last)
-    ids = jnp.concatenate([last, nbr_ids], axis=0).astype(BF)
-    ids = jnp.pad(ids, ((0, 7), (0, HS - 2)))
-    q_rows = jnp.concatenate([queries.reshape(1024, HS), ids], axis=0)
-    q_plane = spread(q_rows, "x").reshape(NX, 1040, HS)
-    got = q_plane[:, 1024:1033, 0:2].astype(jnp.int32)
-    plane_ids = jnp.concatenate([got[0], got[1, 1:], got[2, 1:], got[3, 1:]], axis=0)
-
-    w_rows = enc_qkv.transpose(0, 2, 1, 3).reshape(width * 6, HS)
-    att = encode(corpus_flat, w_rows, gain_in.reshape(1, width), core.reshape(1).astype(jnp.int32))
-    att_own, att_send = att[0], att[1]
     att_other = shifted(att_send, "c", 1)
-
-    pieces = []
-    for j in range(CHUNKS):
-        own = att_own[j]
-        other = att_other[j]
-        partial = project(own, other, e_own, e_other).reshape(NY, ROW // NY, width)
-        terms = lax.all_to_all(partial, "y", split_axis=0, concat_axis=0, tiled=True)
-        block = ((2 * core + j) * NY + my_y).reshape(1).astype(jnp.int32)
-        copies = normalise(terms, corpus_flat, gain_out.reshape(1, width), block)
-        u = lax.all_to_all(copies, "y", split_axis=0, concat_axis=0, tiled=True)
-        u_own = u.reshape(ROW, width)
-        u_other = shifted(u_own, "c", 1)
-        memory = memorise(u_own, u_other, kv)
-        pieces += [(j,) + piece for piece in ring_pieces(memory)]
-
+    partial = project(att_own, att_other, e_own, e_other).reshape(NY, 2 * ROW // NY, width)
+    terms = lax.all_to_all(partial, "y", split_axis=0, concat_axis=0, tiled=True)
+    block = (core * NY + my_y).reshape(1).astype(jnp.int32)
+    copies = normalise(terms, corpus_flat, gain_out.reshape(1, width), block)
+    copies, from_left, from_right = lax.optimization_barrier((copies, from_left, from_right))
+    u_own = lax.all_to_all(copies, "y", split_axis=0, concat_axis=0, tiled=True).reshape(2 * ROW, width)
+    u_own, from_far = lax.optimization_barrier((u_own, from_far))
+    u_other = shifted(u_own, "c", 1)
+    payloads = [payload, from_left, from_right, from_far]
+    memory = memorise(my_x.reshape(1).astype(jnp.int32), u_own, u_other, payloads)
+    pieces = ring_pieces(memory)
+
+    by_step = [payloads[ORDER.index(d)] for d in range(NX)]
+    got = jnp.stack([p[Q_FIRST + 256:Q_FIRST + 265, 0:2] for p in by_step]).astype(jnp.int32)
     at = jnp.stack([my_z, my_x, core]).astype(jnp.int32)
-    parts = windows(plane_ids, at, q_plane, pieces)
+    got, at = lax.optimization_barrier((got.reshape(-1), at))
+    parts = windows(got, at, payloads, pieces)
     parts = lax.all_to_all(parts, "x", split_axis=0, concat_axis=0, tiled=True)
     return combine(parts).reshape(512, 2, HS)
 

time: 271 us -> 223 us (0.82)
  blocking collectives: 37.1 us -> 15.2 us
  starting transfers between devices: 61.3 us -> 41.7 us
  local copies, waits for them, and re-layouts: 23.5 us -> 12.8 us
  waiting for transfers between devices: 89 us -> 96.8 us
  Pallas kernels: 56 us -> 48.4 us
    ppermute x20 -> x14, waiting for transfers between devices: 9.28 us -> 71.4 us  [shifted(): return lax.ppermute(value, axis, [(i, (i + steps) % n) for i in range(n)])]
    ppermute x1, waiting for transfers between devices: 37.9 us -> 0.01 us  [on_device(): lax.ppermute(nbr_ids[7:], ('z', 'x'), [(i, i + 1) for i in range(NZ * NX...]
    all_to_all x1 -> x0, blocking collectives: 16.6 us -> none  [on_device(): u = lax.all_to_all(copies, 'y', split_axis=0, concat_axis=0, tiled=True)]
    all_to_all x1, waiting for transfers between devices: 10.8 us -> 0.01 us  [on_device(): lax.all_to_all(copies, 'y', split_axis=0, concat_axis=0, tiled=True)]
    all_to_all x3 -> x1, starting transfers between devices: 18.9 us -> 8.47 us  [spread(): return lax.all_to_all(copies, axis, split_axis=0, concat_axis=0, tiled=True)]
    all_to_all x3 -> x1, waiting for transfers between devices: 8.7 us -> 2.41 us  [spread(): return lax.all_to_all(copies, axis, split_axis=0, concat_axis=0, tiled=True)]
    ppermute x20 -> x14, starting transfers between devices: 26.8 us -> 20.9 us  [shifted(): return lax.ppermute(value, axis, [(i, (i + steps) % n) for i in range(n)])]
    slice x6 -> x1, local copies, waits for them, and re-layouts: 6.49 us -> 0.83 us  [on_device(): q_wide = jnp.concatenate([q_rows[b] for b in range(4)], axis=1)]
  transfers between devices with their start and end apart: 27 -> 18, of which waited for: 11 -> 11; matrix products, arithmetic and copies ran while one was open for 7% -> 5% of each run, Pallas kernels for 14% -> 10%
where the time goes in v2:
time: 223 us; the launch traced here: 219 us
  waiting for transfers between devices  96.8 us (43%)
  Pallas kernels  48.4 us (22%)
  starting transfers between devices  41.7 us (19%)
  blocking collectives  15.2 us (7%)
  local copies, waits for them, and re-layouts  12.8 us (6%)
  other arithmetic  4.09 us (2%)
    ppermute x14, waiting for transfers between devices, shifted(): return lax.ppermute(value, axis, [(i, (i + steps) % n) for i in range(n)])  71.4 us
    all_to_all x1, waiting for transfers between devices, on_device(): lax.all_to_all(partial, 'y', split_axis=0, concat_axis=0, tiled=True)  23 us
    ppermute x14, starting transfers between devices, shifted(): return lax.ppermute(value, axis, [(i, (i + steps) % n) for i in range(n)])  20.9 us
    pallas_call x1, Pallas kernels, windows(): pl.pallas_call(functools.partial(window_kernel, layout), in_specs=[smem,...  17.4 us
    all_to_all x1, blocking collectives, on_device(): parts = lax.all_to_all(parts, 'x', split_axis=0, concat_axis=0, tiled=True)  15.2 us
    pallas_call x1, Pallas kernels, encode(): pl.pallas_call(encoder_kernel, grid_spec=pltpu.PrefetchScalarGridSpec(num...  13.7 us
    all_to_all x1, starting transfers between devices, spread(): return lax.all_to_all(copies, axis, split_axis=0, concat_axis=0, tiled=True)  8.47 us
    pallas_call x1, Pallas kernels, memorise(): pl.pallas_call(memory_kernel, in_specs=[pl.BlockSpec(memory_space=pltpu.S...  5.51 us
  transfers between devices with their start and end apart: 18, of which 11 were waited for; matrix products, arithmetic and copies ran while one was open for 5% of the time, Pallas kernels for 10%

profile of v2, /device:TPU:2, one launch (start us, length us, event | category | flops | bytes accessed | tf_op | source)
XLA Modules:
  0.0 219.2 jit_solution(983624040063471914)
XLA Ops:
  1.0 1.1 broadcast_in_dim.11
  2.1 8.5 %all-to-all-start.1 = ((bf16[8,128,512]{2,1,0:T(8,128)(2,1)}), bf16[8,128,512]{2,1,0:T(8,128)(2,1)S(1)}, u32[]{:S(2)}, u32[]{:S(2)}) async-start(bf16[8,128,512]{2,1,0:T(8,128)(2,1)} %broadcast_in_dim.11), calls=%async_computation.1 | async-start | bytes 2097152 | tf_op jit(solution)/shard_map/all_to_all | solution.py:30
  10.6 3.4 %collective-permute-start = (s32[1,2]{0,1:T(2,128)S(1)}, s32[1,2]{0,1:T(2,128)S(1)}, u32[]{:S(2)}, u32[]{:S(2)}) collective-permute-start(s32[1,2]{0,1:T(2,128)S(1)} %slice.35), channel_id=1, source_target_pairs={{0,8},{8,16},{16,24},{24,32},{32,40},{40,48},{48,56},{56,64},{64,7... | collective-permute-start | bytes 32 | tf_op jit(solution)/shard_map/ppermute | solution.py:414
  14.0 13.7 %encoder.1 = (bf16[256,256]{1,0:T(8,128)(2,1)}, bf16[256,256]{1,0:T(8,128)(2,1)}) custom-call(s32[1]{0:T(128)} %bitcast.2.core_ref, bf16[512,4096]{1,0:T(8,128)(2,1)} %bitcast.31, bf16[24576,128]{1,0:T(8,128)(2,1)} %bitcast.40, f32[1,4096]{1,0:T(1,128)} %bitcast.41), custom_call_target="tpu_custom_call" | custom-call | flops 3221225472 | bytes 10485760 | tf_op jit(solution)/shard_map/encoder/pallas_call | solution.py:86
  31.2 1.3 copy-done.4
  32.5 5.1 %project.1 = bf16[256,4096]{1,0:T(8,128)(2,1)} custom-call(bf16[256,256]{1,0:T(8,128)(2,1)} %get-tuple-element.14.a_ref, bf16[256,256]{1,0:T(8,128)(2,1)} %collective-permute-done.1.b_ref, bf16[256,4096]{1,0:T(8,128)(2,1)} %bitcast.34, bf16[256,4096]{1,0:T(8,128)(2,1)} %copy-done.4), custom_call_target="tpu_custom_call" | custom-call | flops 1073741824 | bytes 4194304 | tf_op jit(solution)/shard_map/project/pallas_call | solution.py:122
  37.6 2.4 %all-to-all-done.1 = bf16[8,128,512]{2,1,0:T(8,128)(2,1)S(1)} async-done(((bf16[8,128,512]{2,1,0:T(8,128)(2,1)}), bf16[8,128,512]{2,1,0:T(8,128)(2,1)S(1)}, u32[]{:S(2)}, u32[]{:S(2)}) %all-to-all-start.1) | async-done | bytes 1048608 | tf_op jit(solution)/shard_map/all_to_all | solution.py:30
  41.0 4.5 %all-to-all-start = ((bf16[4,64,4096]{2,1,0:T(8,128)(2,1)}), bf16[4,64,4096]{2,1,0:T(8,128)(2,1)S(1)}, u32[]{:S(2)}, u32[]{:S(2)}) async-start(bf16[4,64,4096]{2,1,0:T(8,128)(2,1)} %bitcast.27), calls=%async_computation | async-start | bytes 4194304 | tf_op jit(solution)/shard_map/all_to_all | solution.py:433
  45.5 1.4 fusion.1.k0.refs_0_
  47.5 1.5 collective-permute-start.3
  49.0 23.0 %all-to-all-done.terms_ref = bf16[4,64,4096]{2,1,0:T(8,128)(2,1)S(1)} async-done(((bf16[4,64,4096]{2,1,0:T(8,128)(2,1)}), bf16[4,64,4096]{2,1,0:T(8,128)(2,1)S(1)}, u32[]{:S(2)}, u32[]{:S(2)}) %all-to-all-start) | async-done | bytes 2097184 | tf_op jit(solution)/shard_map/all_to_all | solution.py:433
  72.0 1.4 copy-done.2
  73.4 4.1 %normalise.1 = bf16[4,64,4096]{2,1,0:T(8,128)(2,1)} custom-call(s32[1]{0:T(128)} %bitcast.1.block_ref, bf16[4,64,4096]{2,1,0:T(8,128)(2,1)} %copy-done.2, bf16[512,4096]{1,0:T(8,128)(2,1)} %bitcast.32, f32[1,4096]{1,0:T(1,128)} %bitcast.39), custom_call_target="tpu_custom_call" | custom-call | flops 2097152 | bytes 4718592 | tf_op jit(solution)/shard_map/normalise/pallas_call | solution.py:156
  77.9 1.3 collective-permute-done.3.k1.refs_1_
  79.1 4.5 %all-to-all-start.2 = ((bf16[4,64,4096]{2,1,0:T(8,128)(2,1)}), bf16[4,64,4096]{2,1,0:T(8,128)(2,1)S(1)}, u32[]{:S(2)}, u32[]{:S(2)}) async-start(bf16[4,64,4096]{2,1,0:T(8,128)(2,1)} %normalise.1), calls=%async_computation.2 | async-start | bytes 4194304 | tf_op jit(solution)/shard_map/all_to_all | solution.py:437
  83.7 2.1 collective-permute-start.5
  85.7 28.8 %collective-permute-done.5.k3.refs_3_ = bf16[1296,512]{1,0:T(8,128)(2,1)} collective-permute-done((bf16[1296,512]{1,0:T(8,128)(2,1)S(1)}, bf16[1296,512]{1,0:T(8,128)(2,1)}, u32[]{:S(2)}, u32[]{:S(2)}) %collective-permute-start.5) | collective-permute-done | bytes 1327136 | tf_op jit(solution)/shard_map/ppermute | solution.py:24
  114.6 4.2 %collective-permute-done.6.b_ref = bf16[256,4096]{1,0:T(8,128)(2,1)S(1)} collective-permute-done((bf16[256,4096]{1,0:T(8,128)(2,1)S(1)}, bf16[256,4096]{1,0:T(8,128)(2,1)S(1)}, u32[]{:S(2)}, u32[]{:S(2)}) %collective-permute-start.6) | collective-permute-done | bytes 2097184 | tf_op jit(solution)/shard_map/ppermute | solution.py:24
  118.7 1.4 copy-done.5
  120.1 5.5 %memorise.1.refs_4_ = bf16[512,512]{1,0:T(8,128)(2,1)} custom-call(s32[1]{0:T(128)} %bitcast.20.x_ref, bf16[256,4096]{1,0:T(8,128)(2,1)} %bitcast.29, bf16[256,4096]{1,0:T(8,128)(2,1)} %copy-done.5, bf16[1296,512]{1,0:T(8,128)(2,1)} %copy-done, bf16[1296,512]{1,0:T(8,128)(2,1)} %collective-permute-done.3.k1.refs_1_, ...), custom_call_target="tpu_custom_call" | custom-call | flops 2147483648 | bytes 4194304 | tf_op jit(solution)/shard_map/memorise/pallas_call | solution.py:205
  125.6 5.7 %collective-permute-start.8 = (bf16[512,512]{1,0:T(8,128)(2,1)}, bf16[512,512]{1,0:T(8,128)(2,1)S(1)}, u32[]{:S(2)}, u32[]{:S(2)}) collective-permute-start(bf16[512,512]{1,0:T(8,128)(2,1)} %memorise.1.refs_4_), channel_id=1, source_target_pairs={{0,224},{32,0},{64,32},{96,64},{128,96},{160,128},{192,160},{224,1... | collective-permute-start | bytes 1572872 | tf_op jit(solution)/shard_map/ppermute | solution.py:24
  131.4 11.8 %collective-permute-done.8.refs_6_ = bf16[512,512]{1,0:T(8,128)(2,1)S(1)} collective-permute-done((bf16[512,512]{1,0:T(8,128)(2,1)}, bf16[512,512]{1,0:T(8,128)(2,1)S(1)}, u32[]{:S(2)}, u32[]{:S(2)}) %collective-permute-start.8) | collective-permute-done | bytes 524320 | tf_op jit(solution)/shard_map/ppermute | solution.py:24
  143.2 3.6 %collective-permute-start.10 = (bf16[512,512]{1,0:T(8,128)(2,1)S(1)}, bf16[512,512]{1,0:T(8,128)(2,1)S(1)}, u32[]{:S(2)}, u32[]{:S(2)}) collective-permute-start(bf16[512,512]{1,0:T(8,128)(2,1)S(1)} %collective-permute-done.8.refs_6_), channel_id=1, source_target_pairs={{0,224},{32,0},{64,32},{96,64},{128,96},{160,128},{192,160},{224,1... | collective-permute-start | bytes 1572872 | tf_op jit(solution)/shard_map/ppermute | solution.py:24
  146.8 10.6 %collective-permute-done.10.refs_8_ = bf16[512,512]{1,0:T(8,128)(2,1)S(1)} collective-permute-done((bf16[512,512]{1,0:T(8,128)(2,1)S(1)}, bf16[512,512]{1,0:T(8,128)(2,1)S(1)}, u32[]{:S(2)}, u32[]{:S(2)}) %collective-permute-start.10) | collective-permute-done | bytes 524320 | tf_op jit(solution)/shard_map/ppermute | solution.py:24
  157.4 3.7 %collective-permute-start.12 = (bf16[512,512]{1,0:T(8,128)(2,1)S(1)}, bf16[512,512]{1,0:T(8,128)(2,1)S(1)}, u32[]{:S(2)}, u32[]{:S(2)}) collective-permute-start(bf16[512,512]{1,0:T(8,128)(2,1)S(1)} %collective-permute-done.10.refs_8_), channel_id=1, source_target_pairs={{0,224},{32,0},{64,32},{96,64},{128,96},{160,128},{192,160},{224,1... | collective-permute-start | bytes 1572872 | tf_op jit(solution)/shard_map/ppermute | solution.py:24
  162.8 8.0 %collective-permute-done.12.refs_10_ = bf16[512,512]{1,0:T(8,128)(2,1)S(1)} collective-permute-done((bf16[512,512]{1,0:T(8,128)(2,1)S(1)}, bf16[512,512]{1,0:T(8,128)(2,1)S(1)}, u32[]{:S(2)}, u32[]{:S(2)}) %collective-permute-start.12) | collective-permute-done | bytes 524320 | tf_op jit(solution)/shard_map/ppermute | solution.py:24
  171.6 3.7 %collective-permute-start.14 = (bf16[256,512]{1,0:T(8,128)(2,1)}, bf16[256,512]{1,0:T(8,128)(2,1)S(1)}, u32[]{:S(2)}, u32[]{:S(2)}) collective-permute-start(bf16[256,512]{1,0:T(8,128)(2,1)} %slice.46), channel_id=1, source_target_pairs={{0,224},{32,0},{64,32},{96,64},{128,96},{160,128},{192,160},{224,1... | collective-permute-start | bytes 786440 | tf_op jit(solution)/shard_map/ppermute | solution.py:24
  177.7 1.8 collective-permute-done.14.refs_12_
  179.5 4.5 %collective-permute-done.13.refs_11_ = bf16[256,512]{1,0:T(8,128)(2,1)} collective-permute-done((bf16[256,512]{1,0:T(8,128)(2,1)}, bf16[256,512]{1,0:T(8,128)(2,1)}, u32[]{:S(2)}, u32[]{:S(2)}) %collective-permute-start.13) | collective-permute-done | bytes 262176 | tf_op jit(solution)/shard_map/ppermute | solution.py:24
  184.1 17.4 %windows.1 = bf16[4,1056,128]{2,1,0:T(8,128)(2,1)} custom-call(s32[72]{0:T(128)} %reshape.94.ids_ref, s32[3]{0:T(128)} %pad_add_fusion.at_ref, bf16[1296,512]{1,0:T(8,128)(2,1)} %copy-done, bf16[1296,512]{1,0:T(8,128)(2,1)} %collective-permute-done.3.k1.refs_1_, bf16[1296,512]{1,0:T(8,128)(2,1)} %collective-permute-done.4.k2.refs_2_, ...), custom_call_target="tpu_custom_call" | custom-call | flops 1000000000 | bytes 8388608 | tf_op jit(solution)/shard_map/windows/pallas_call | solution.py:357
  201.5 15.2 %all_to_all.20.parts_ref = bf16[4,1056,128]{2,1,0:T(8,128)(2,1)} all-to-all(bf16[4,1056,128]{2,1,0:T(8,128)(2,1)} %windows.1), channel_id=1, replica_groups=mesh['z'=8,'x'=4,'y'=4,'c'=2] {'x'}, dimensions={0} | all-to-all | bytes 2162688 | tf_op jit(solution)/shard_map/all_to_all | solution.py:449
  216.6 2.6 %combine.1 = bf16[1024,128]{1,0:T(8,128)(2,1)} custom-call(bf16[4,1056,128]{2,1,0:T(8,128)(2,1)} %all_to_all.20.parts_ref), custom_call_target="tpu_custom_call" | custom-call | flops 10000000 | bytes 2097152 | tf_op jit(solution)/shard_map/combine/pallas_call | solution.py:397
  (68 shorter events, 11.4 us)
Async XLA Ops:
  0.0 10.5 %copy-start.14 = (s32[8,2]{0,1:T(2,128)S(1)}, s32[8,2]{0,1:T(2,128)}, u32[]{:S(2)}) copy-start(s32[8,2]{0,1:T(2,128)} %param.15) | copy-start | bytes 196
  0.0 31.2 %collective-permute-start.2 = (bf16[256,4096]{1,0:T(8,128)(2,1)}, bf16[256,4096]{1,0:T(8,128)(2,1)S(1)}, u32[]{:S(2)}, u32[]{:S(2)}) collective-permute-start(bf16[256,4096]{1,0:T(8,128)(2,1)} %bitcast.33), channel_id=1, source_target_pairs={{0,1},{1,0},{2,3},{3,2},{4,5},{5,4},{6,7},{7,6},{8,9},{9,8},{10,11... | collective-permute-start | bytes 6291464 | tf_op jit(solution)/shard_map/ppermute | solution.py:24
  2.1 37.9 %all-to-all-start.1 = ((bf16[8,128,512]{2,1,0:T(8,128)(2,1)}), bf16[8,128,512]{2,1,0:T(8,128)(2,1)S(1)}, u32[]{:S(2)}, u32[]{:S(2)}) async-start(bf16[8,128,512]{2,1,0:T(8,128)(2,1)} %broadcast_in_dim.11), calls=%async_computation.1 | async-start | bytes 2097152 | tf_op jit(solution)/shard_map/all_to_all | solution.py:30
  10.6 18.5 %collective-permute-start = (s32[1,2]{0,1:T(2,128)S(1)}, s32[1,2]{0,1:T(2,128)S(1)}, u32[]{:S(2)}, u32[]{:S(2)}) collective-permute-start(s32[1,2]{0,1:T(2,128)S(1)} %slice.35), channel_id=1, source_target_pairs={{0,8},{8,16},{16,24},{24,32},{32,40},{40,48},{48,56},{56,64},{64,7... | collective-permute-start | bytes 32 | tf_op jit(solution)/shard_map/ppermute | solution.py:414
  14.0 14.2 %copy-start.13 = (bf16[512,2,128]{2,1,0:T(2,128)(2,1)S(1)}, bf16[512,2,128]{2,1,0:T(2,128)(2,1)}, u32[]{:S(2)}) copy-start(bf16[512,2,128]{2,1,0:T(2,128)(2,1)} %param.14) | copy-start | bytes 786436
  27.7 3.5 %collective-permute-start.1 = (bf16[256,256]{1,0:T(8,128)(2,1)}, bf16[256,256]{1,0:T(8,128)(2,1)}, u32[]{:S(2)}, u32[]{:S(2)}) collective-permute-start(bf16[256,256]{1,0:T(8,128)(2,1)} %get-tuple-element.15), channel_id=1, source_target_pairs={{0,1},{1,0},{2,3},{3,2},{4,5},{5,4},{6,7},{7,6},{8,9},{9,8},{10,11... | collective-permute-start | bytes 393224 | tf_op jit(solution)/shard_map/ppermute | solution.py:24
  41.0 31.0 %all-to-all-start = ((bf16[4,64,4096]{2,1,0:T(8,128)(2,1)}), bf16[4,64,4096]{2,1,0:T(8,128)(2,1)S(1)}, u32[]{:S(2)}, u32[]{:S(2)}) async-start(bf16[4,64,4096]{2,1,0:T(8,128)(2,1)} %bitcast.27), calls=%async_computation | async-start | bytes 4194304 | tf_op jit(solution)/shard_map/all_to_all | solution.py:433
  46.9 36.8 %copy-start = (bf16[1296,512]{1,0:T(8,128)(2,1)}, bf16[1296,512]{1,0:T(8,128)(2,1)S(1)}, u32[]{:S(2)}) copy-start(bf16[1296,512]{1,0:T(8,128)(2,1)S(1)} %fusion.1.k0.refs_0_) | copy-start | bytes 3981316
  46.9 31.0 %collective-permute-start.4 = (bf16[1296,512]{1,0:T(8,128)(2,1)S(1)}, bf16[1296,512]{1,0:T(8,128)(2,1)}, u32[]{:S(2)}, u32[]{:S(2)}) collective-permute-start(bf16[1296,512]{1,0:T(8,128)(2,1)S(1)} %fusion.1.k0.refs_0_), channel_id=1, source_target_pairs={{0,24},{8,0},{16,8},{24,16},{1,25},{9,1},{17,9},{25,17},{2,26},{10... | collective-permute-start | bytes 3981320 | tf_op jit(solution)/shard_map/ppermute | solution.py:24
  47.5 31.6 %collective-permute-start.3 = (bf16[1296,512]{1,0:T(8,128)(2,1)S(1)}, bf16[1296,512]{1,0:T(8,128)(2,1)}, u32[]{:S(2)}, u32[]{:S(2)}) collective-permute-start(bf16[1296,512]{1,0:T(8,128)(2,1)S(1)} %fusion.1.k0.refs_0_), channel_id=1, source_target_pairs={{0,8},{8,16},{16,24},{24,0},{1,9},{9,17},{17,25},{25,1},{2,10},{10... | collective-permute-start | bytes 3981320 | tf_op jit(solution)/shard_map/ppermute | solution.py:24
  72.0 1.4 copy-start.2
  79.1 35.4 %all-to-all-start.2 = ((bf16[4,64,4096]{2,1,0:T(8,128)(2,1)}), bf16[4,64,4096]{2,1,0:T(8,128)(2,1)S(1)}, u32[]{:S(2)}, u32[]{:S(2)}) async-start(bf16[4,64,4096]{2,1,0:T(8,128)(2,1)} %normalise.1), calls=%async_computation.2 | async-start | bytes 4194304 | tf_op jit(solution)/shard_map/all_to_all | solution.py:437
  83.7 30.9 %collective-permute-start.5 = (bf16[1296,512]{1,0:T(8,128)(2,1)S(1)}, bf16[1296,512]{1,0:T(8,128)(2,1)}, u32[]{:S(2)}, u32[]{:S(2)}) collective-permute-start(bf16[1296,512]{1,0:T(8,128)(2,1)S(1)} %fusion.1.k0.refs_0_), channel_id=1, source_target_pairs={{0,16},{8,24},{16,0},{24,8},{1,17},{9,25},{17,1},{25,9},{2,18},{10... | collective-permute-start | bytes 3981320 | tf_op jit(solution)/shard_map/ppermute | solution.py:24
  114.6 5.5 %copy-start.1 = (bf16[4,64,4096]{2,1,0:T(8,128)(2,1)}, bf16[4,64,4096]{2,1,0:T(8,128)(2,1)S(1)}, u32[]{:S(2)}) copy-start(bf16[4,64,4096]{2,1,0:T(8,128)(2,1)S(1)} %all-to-all-done.2) | copy-start | bytes 6291460
  114.6 4.2 %collective-permute-start.6 = (bf16[256,4096]{1,0:T(8,128)(2,1)S(1)}, bf16[256,4096]{1,0:T(8,128)(2,1)S(1)}, u32[]{:S(2)}, u32[]{:S(2)}) collective-permute-start(bf16[256,4096]{1,0:T(8,128)(2,1)S(1)} %bitcast.28), channel_id=1, source_target_pairs={{0,1},{1,0},{2,3},{3,2},{4,5},{5,4},{6,7},{7,6},{8,9},{9,8},{10,11... | collective-permute-start | bytes 6291464 | tf_op jit(solution)/shard_map/ppermute | solution.py:24
  120.1 41.0 %copy-start.15 = (s32[8,2]{0,1:T(2,128)S(1)}, s32[8,2]{0,1:T(2,128)}, u32[]{:S(2)}) copy-start(s32[8,2]{0,1:T(2,128)} %param.15) | copy-start | bytes 196
  120.1 41.7 %copy-start.16 = (bf16[2]{0:T(256)(128)(2,1)S(1)}, bf16[2]{0:T(256)(128)(2,1)}, u32[]{:S(2)}) copy-start(bf16[2]{0:T(256)(128)(2,1)} %get-tuple-element.23) | copy-start | bytes 16
  125.6 17.5 %collective-permute-start.8 = (bf16[512,512]{1,0:T(8,128)(2,1)}, bf16[512,512]{1,0:T(8,128)(2,1)S(1)}, u32[]{:S(2)}, u32[]{:S(2)}) collective-permute-start(bf16[512,512]{1,0:T(8,128)(2,1)} %memorise.1.refs_4_), channel_id=1, source_target_pairs={{0,224},{32,0},{64,32},{96,64},{128,96},{160,128},{192,160},{224,1... | collective-permute-start | bytes 1572872 | tf_op jit(solution)/shard_map/ppermute | solution.py:24
  131.4 15.4 %collective-permute-start.7 = (bf16[512,512]{1,0:T(8,128)(2,1)}, bf16[512,512]{1,0:T(8,128)(2,1)S(1)}, u32[]{:S(2)}, u32[]{:S(2)}) collective-permute-start(bf16[512,512]{1,0:T(8,128)(2,1)} %memorise.1.refs_4_), channel_id=1, source_target_pairs={{0,32},{32,64},{64,96},{96,128},{128,160},{160,192},{192,224},{224... | collective-permute-start | bytes 1572872 | tf_op jit(solution)/shard_map/ppermute | solution.py:24
  143.2 40.8 %copy-start.8 = (bf16[512,512]{1,0:T(8,128)(2,1)}, bf16[512,512]{1,0:T(8,128)(2,1)S(1)}, u32[]{:S(2)}) copy-start(bf16[512,512]{1,0:T(8,128)(2,1)S(1)} %collective-permute-done.8.refs_6_) | copy-start | bytes 1572868
  143.2 14.2 %collective-permute-start.10 = (bf16[512,512]{1,0:T(8,128)(2,1)S(1)}, bf16[512,512]{1,0:T(8,128)(2,1)S(1)}, u32[]{:S(2)}, u32[]{:S(2)}) collective-permute-start(bf16[512,512]{1,0:T(8,128)(2,1)S(1)} %collective-permute-done.8.refs_6_), channel_id=1, source_target_pairs={{0,224},{32,0},{64,32},{96,64},{128,96},{160,128},{192,160},{224,1... | collective-permute-start | bytes 1572872 | tf_op jit(solution)/shard_map/ppermute | solution.py:24
  146.8 37.2 %copy-start.9 = (bf16[512,512]{1,0:T(8,128)(2,1)}, bf16[512,512]{1,0:T(8,128)(2,1)S(1)}, u32[]{:S(2)}) copy-start(bf16[512,512]{1,0:T(8,128)(2,1)S(1)} %collective-permute-done.7.refs_5_) | copy-start | bytes 1572868
  146.8 14.3 %collective-permute-start.9 = (bf16[512,512]{1,0:T(8,128)(2,1)S(1)}, bf16[512,512]{1,0:T(8,128)(2,1)S(1)}, u32[]{:S(2)}, u32[]{:S(2)}) collective-permute-start(bf16[512,512]{1,0:T(8,128)(2,1)S(1)} %collective-permute-done.7.refs_5_), channel_id=1, source_target_pairs={{0,32},{32,64},{64,96},{96,128},{128,160},{160,192},{192,224},{224... | collective-permute-start | bytes 1572872 | tf_op jit(solution)/shard_map/ppermute | solution.py:24
  157.4 26.6 %copy-start.10 = (bf16[512,512]{1,0:T(8,128)(2,1)}, bf16[512,512]{1,0:T(8,128)(2,1)S(1)}, u32[]{:S(2)}) copy-start(bf16[512,512]{1,0:T(8,128)(2,1)S(1)} %collective-permute-done.10.refs_8_) | copy-start | bytes 1572868
  157.4 13.4 %collective-permute-start.12 = (bf16[512,512]{1,0:T(8,128)(2,1)S(1)}, bf16[512,512]{1,0:T(8,128)(2,1)S(1)}, u32[]{:S(2)}, u32[]{:S(2)}) collective-permute-start(bf16[512,512]{1,0:T(8,128)(2,1)S(1)} %collective-permute-done.10.refs_8_), channel_id=1, source_target_pairs={{0,224},{32,0},{64,32},{96,64},{128,96},{160,128},{192,160},{224,1... | collective-permute-start | bytes 1572872 | tf_op jit(solution)/shard_map/ppermute | solution.py:24
  161.1 22.9 %copy-start.11 = (bf16[512,512]{1,0:T(8,128)(2,1)}, bf16[512,512]{1,0:T(8,128)(2,1)S(1)}, u32[]{:S(2)}) copy-start(bf16[512,512]{1,0:T(8,128)(2,1)S(1)} %collective-permute-done.9.refs_7_) | copy-start | bytes 1572868
  161.1 14.2 %collective-permute-start.11 = (bf16[512,512]{1,0:T(8,128)(2,1)S(1)}, bf16[512,512]{1,0:T(8,128)(2,1)S(1)}, u32[]{:S(2)}, u32[]{:S(2)}) collective-permute-start(bf16[512,512]{1,0:T(8,128)(2,1)S(1)} %collective-permute-done.9.refs_7_), channel_id=1, source_target_pairs={{0,32},{32,64},{64,96},{96,128},{128,160},{160,192},{192,224},{224... | collective-permute-start | bytes 1572872 | tf_op jit(solution)/shard_map/ppermute | solution.py:24
  170.8 13.2 %copy-start.6 = (bf16[512,512]{1,0:T(8,128)(2,1)}, bf16[512,512]{1,0:T(8,128)(2,1)S(1)}, u32[]{:S(2)}) copy-start(bf16[512,512]{1,0:T(8,128)(2,1)S(1)} %collective-permute-done.12.refs_10_) | copy-start | bytes 1572868
  171.6 7.9 %collective-permute-start.14 = (bf16[256,512]{1,0:T(8,128)(2,1)}, bf16[256,512]{1,0:T(8,128)(2,1)S(1)}, u32[]{:S(2)}, u32[]{:S(2)}) collective-permute-start(bf16[256,512]{1,0:T(8,128)(2,1)} %slice.46), channel_id=1, source_target_pairs={{0,224},{32,0},{64,32},{96,64},{128,96},{160,128},{192,160},{224,1... | collective-permute-start | bytes 786440 | tf_op jit(solution)/shard_map/ppermute | solution.py:24
  175.3 8.7 %copy-start.7 = (bf16[512,512]{1,0:T(8,128)(2,1)}, bf16[512,512]{1,0:T(8,128)(2,1)S(1)}, u32[]{:S(2)}) copy-start(bf16[512,512]{1,0:T(8,128)(2,1)S(1)} %collective-permute-done.11.refs_9_) | copy-start | bytes 1572868
  176.1 7.9 %collective-permute-start.13 = (bf16[256,512]{1,0:T(8,128)(2,1)}, bf16[256,512]{1,0:T(8,128)(2,1)}, u32[]{:S(2)}, u32[]{:S(2)}) collective-permute-start(bf16[256,512]{1,0:T(8,128)(2,1)} %slice.45), channel_id=1, source_target_pairs={{0,32},{32,64},{64,96},{96,128},{128,160},{160,192},{192,224},{224... | collective-permute-start | bytes 786440 | tf_op jit(solution)/shard_map/ppermute | solution.py:24
  179.5 4.5 %copy-start.12 = (bf16[256,512]{1,0:T(8,128)(2,1)}, bf16[256,512]{1,0:T(8,128)(2,1)S(1)}, u32[]{:S(2)}) copy-start(bf16[256,512]{1,0:T(8,128)(2,1)S(1)} %collective-permute-done.14.refs_12_) | copy-start | bytes 786436
  (3 other events, 3.7 us)

commit v3 on v2

--- a/solution.py
+++ b/solution.py
@@ -9,6 +9,7 @@
 
 GROUP = 64
 EPS = 1e-06
+MIB = 2**20
 NZ, NX, NY, NC = 8, 4, 4, 2
 ROW = 128
 HS = 128
@@ -105,139 +106,173 @@
         cost_estimate=pl.CostEstimate(
             flops=2 * tokens * width * 6 * HS, bytes_accessed=(tokens + 768) * width * 2, transcendentals=0
         ),
+        compiler_params=pltpu.CompilerParams(vmem_limit_bytes=60 * MIB),
         name="encoder",
     )(core, corpus_flat, w_rows, gain)
 
 
-def project_kernel(a_ref, b_ref, ea_ref, eb_ref, out_ref):
-    total = jnp.dot(a_ref[...], ea_ref[...], preferred_element_type=F32)
-    total += jnp.dot(b_ref[...], eb_ref[...], preferred_element_type=F32)
-    out_ref[...] = total.astype(BF)
-
-
-def project(att_own, att_other, e_own, e_other):
+def project_kernel(y_ref, a_ref, b_ref, ea_ref, eb_ref, *refs):
+    outs, total = refs[:NY], refs[NY]
+    rows = total.shape[0] // NY
+    value = jnp.dot(a_ref[...], ea_ref[...], preferred_element_type=F32)
+    value += jnp.dot(b_ref[...], eb_ref[...], preferred_element_type=F32)
+    total[...] = value.astype(BF)
+    for k in range(NY):
+        first = pl.multiple_of(lax.rem(y_ref[0] + k, NY) * rows, rows)
+        outs[k][...] = total[pl.ds(first, rows), :]
+
+
+def project(my_y, att_own, att_other, e_own, e_other):
     tokens, depth = att_own.shape
     width = e_own.shape[1]
     cols = 1024
+    rows = tokens // NY
     return pl.pallas_call(
         project_kernel,
-        grid=(width // cols,),
-        in_specs=[
-            pl.BlockSpec((tokens, depth), lambda i: (0, 0)),
-            pl.BlockSpec((tokens, depth), lambda i: (0, 0)),
-            pl.BlockSpec((depth, cols), lambda i: (0, i)),
-            pl.BlockSpec((depth, cols), lambda i: (0, i)),
-        ],
-        out_specs=pl.BlockSpec((tokens, cols), lambda i: (0, i)),
-        out_shape=jax.ShapeDtypeStruct((tokens, width), BF),
+        grid_spec=pltpu.PrefetchScalarGridSpec(
+            num_scalar_prefetch=1,
+            grid=(width // cols,),
+            in_specs=[
+                pl.BlockSpec((tokens, depth), lambda i, y: (0, 0)),
+                pl.BlockSpec((tokens, depth), lambda i, y: (0, 0)),
+                pl.BlockSpec((depth, cols), lambda i, y: (0, i)),
+                pl.BlockSpec((depth, cols), lambda i, y: (0, i)),
+            ],
+            out_specs=[pl.BlockSpec((rows, cols), lambda i, y: (0, i))] * NY,
+            scratch_shapes=[pltpu.VMEM((tokens, cols), BF)],
+        ),
+        out_shape=[jax.ShapeDtypeStruct((rows, width), BF)] * NY,
         cost_estimate=pl.CostEstimate(
             flops=4 * tokens * depth * width, bytes_accessed=4 * depth * width, transcendentals=0
         ),
+        compiler_params=pltpu.CompilerParams(vmem_limit_bytes=12 * MIB),
         name="project",
-    )(att_own, att_other, e_own, e_other)
-
-
-def norm_kernel(block_ref, terms_ref, x_ref, g_ref, out_ref):
+    )(my_y, att_own, att_other, e_own, e_other)
+
+
+def norm_kernel(block_ref, t0, t1, t2, t3, x_ref, g_ref, out_ref):
     total = x_ref[...].astype(F32)
-    for i in range(NY):
-        total += terms_ref[i].astype(F32)
+    for term in (t0, t1, t2, t3):
+        total += term[...].astype(F32)
     rinv = lax.rsqrt(jnp.mean(total * total, axis=1, keepdims=True) + EPS)
     u = (total * rinv * g_ref[...]).astype(BF)
     for z in range(NZ):
         for x in range(NX):
             src, dst = (z * NX + x) * HS, (x * NZ + z) * HS
-            piece = u[:, src:src + HS]
-            for i in range(NY):
-                out_ref[i, :, dst:dst + HS] = piece
+            out_ref[:, dst:dst + HS] = u[:, src:src + HS]
 
 
 def normalise(terms, corpus_flat, gain, block):
-    _, rows, width = terms.shape
+    rows, width = terms[0].shape
+    whole = pl.BlockSpec((rows, width), lambda i, b: (0, 0))
     return pl.pallas_call(
         norm_kernel,
         grid_spec=pltpu.PrefetchScalarGridSpec(
             num_scalar_prefetch=1,
             grid=(1,),
-            in_specs=[
-                VMEM_ALL,
+            in_specs=[whole] * NY
+            + [
                 pl.BlockSpec((rows, width), lambda i, b: (b[0], 0)),
                 pl.BlockSpec((1, width), lambda i, b: (0, 0)),
             ],
-            out_specs=pl.BlockSpec((NY, rows, width), lambda i, b: (0, 0, 0)),
+            out_specs=whole,
         ),
-        out_shape=jax.ShapeDtypeStruct((NY, rows, width), BF),
-        cost_estimate=pl.CostEstimate(flops=8 * rows * width, bytes_accessed=18 * rows * width, transcendentals=0),
+        out_shape=jax.ShapeDtypeStruct((rows, width), BF),
+        cost_estimate=pl.CostEstimate(flops=8 * rows * width, bytes_accessed=12 * rows * width, transcendentals=0),
+        compiler_params=pltpu.CompilerParams(vmem_limit_bytes=60 * MIB),
         name="normalise",
-    )(block, terms, corpus_flat, gain)
+    )(block, *terms, corpus_flat, gain)
 
 
 ORDER = (0, NX - 1, 1, 2)
 
 
-def memory_kernel(x_ref, a_ref, b_ref, k0, k1, k2, k3, out_ref, ua, ub, kv, sem):
+def memory_kernel(parts, at_ref, *refs):
+    us = refs[:parts]
+    k0, k1, k2, k3, k4 = refs[parts:parts + 5]
+    out_ref = refs[parts + 5]
+    rest = refs[parts + 6:]
+    if parts > 1:
+        whole, rest = rest[0], rest[1:]
+    ua, kv, sem, out_sem = rest
     depth = NZ * HS
-    half = ua.shape[1]
-    copies = []
-    for i, k_ref in enumerate((k0, k1, k2, k3)):
-        first = pl.multiple_of(lax.rem(x_ref[0] + ORDER[i], NX) * depth, depth)
-        copies.append((
-            pltpu.make_async_copy(k_ref.at[pl.ds(0, depth)], kv.at[i], sem.at[0, i]),
-            pltpu.make_async_copy(a_ref.at[:, pl.ds(first, depth)], ua.at[i], sem.at[1, i]),
-            pltpu.make_async_copy(b_ref.at[:, pl.ds(first, depth)], ub.at[i], sem.at[2, i]),
-        ))
-    for group in copies:
-        for copy in group:
-            copy.start()
-    totals = [jnp.zeros((half, out_ref.shape[1]), F32) for _ in range(2)]
-    for i, group in enumerate(copies):
-        for copy in group:
+    rows = ua.shape[0] // parts
+    u_copies = []
+    for k in range(parts):
+        first = pl.multiple_of(lax.rem(at_ref[1] - k + parts, parts) * rows, rows)
+        u_copies.append(pltpu.make_async_copy(us[k], ua.at[pl.ds(first, rows)], sem.at[k]))
+    near = [
+        pltpu.make_async_copy(k_ref.at[pl.ds(0, depth)], kv.at[i], sem.at[NY + i])
+        for i, k_ref in enumerate((k0, k1, k2))
+    ]
+    top, bottom = k3.shape[0], depth - k3.shape[0]
+    far = [
+        pltpu.make_async_copy(k3, kv.at[3, pl.ds(0, top)], sem.at[NY + 3]),
+        pltpu.make_async_copy(k4.at[pl.ds(0, bottom)], kv.at[3, pl.ds(top, bottom)], sem.at[NY + 4]),
+    ]
+    for copy in u_copies + near + far:
+        copy.start()
+    for copy in u_copies:
+        copy.wait()
+    if parts > 1:
+        back = pltpu.make_async_copy(ua, whole, out_sem)
+        back.start()
+    total = jnp.zeros(out_ref.shape, F32)
+    for i in range(NX):
+        for copy in (near[i:i + 1] if i < 3 else far):
             copy.wait()
-        for part, u in enumerate((ua, ub)):
-            totals[part] += jnp.dot(u[i], kv[i], preferred_element_type=F32)
-    for part in range(2):
-        out_ref[part * half:(part + 1) * half, :] = totals[part].astype(BF)
-
-
-def memorise(my_x, u_own, u_other, payloads):
-    half, width = u_own.shape
+        first = pl.multiple_of(lax.rem(at_ref[0] + ORDER[i], NX) * depth, depth)
+        total += jnp.dot(ua[:, pl.ds(first, depth)], kv[i], preferred_element_type=F32)
+    out_ref[...] = total.astype(BF)
+    if parts > 1:
+        back.wait()
+
+
+def memorise(at, us, payloads):
+    width = us[0].shape[1]
+    tokens = us[0].shape[0] * len(us)
     cols = payloads[0].shape[1]
     depth = width // NX
+    memory = jax.ShapeDtypeStruct((tokens, cols), BF)
+    assembled = [jax.ShapeDtypeStruct((tokens, width), BF)] if len(us) > 1 else []
     return pl.pallas_call(
-        memory_kernel,
-        in_specs=[pl.BlockSpec(memory_space=pltpu.SMEM)] + [ANY] * 6,
-        out_specs=VMEM_ALL,
+        functools.partial(memory_kernel, len(us)),
+        in_specs=[pl.BlockSpec(memory_space=pltpu.SMEM)] + [ANY] * (len(us) + 5),
+        out_specs=[VMEM_ALL] + [ANY] * len(assembled),
         scratch_shapes=[
-            pltpu.VMEM((NX, half, depth), BF),
-            pltpu.VMEM((NX, half, depth), BF),
+            pltpu.VMEM((tokens, width), BF),
             pltpu.VMEM((NX, depth, cols), BF),
-            pltpu.SemaphoreType.DMA((3, NX)),
+            pltpu.SemaphoreType.DMA((NY + 5,)),
+            pltpu.SemaphoreType.DMA,
         ],
-        out_shape=jax.ShapeDtypeStruct((2 * half, cols), BF),
+        out_shape=[memory] + assembled,
         cost_estimate=pl.CostEstimate(
-            flops=4 * half * width * cols, bytes_accessed=2 * width * cols, transcendentals=0
+            flops=2 * tokens * width * cols, bytes_accessed=2 * width * cols, transcendentals=0
         ),
+        compiler_params=pltpu.CompilerParams(vmem_limit_bytes=12 * MIB),
         name="memorise",
-    )(my_x, u_own, u_other, *payloads)
-
-
-def ring_pieces(block):
+    )(at, *us, *payloads)
+
+
+def ring_pieces(block, base):
     rows = block.shape[0]
     half = rows // 2
-    pieces = [(0, 0, rows, block)]
+    pieces = [(0, base, rows, block)]
     up = down = block
     for s in range(1, NZ // 2):
         up = shifted(up, "z", 1)
         down = shifted(down, "z", -1)
-        pieces += [(s, 0, rows, up), (NZ - s, 0, rows, down)]
+        pieces += [(s, base, rows, up), (NZ - s, base, rows, down)]
     pieces += [
-        (NZ // 2, 0, half, shifted(up[:half], "z", 1)),
-        (NZ // 2, half, half, shifted(down[half:], "z", -1)),
+        (NZ // 2, base, half, shifted(up[:half], "z", 1)),
+        (NZ // 2, base + half, half, shifted(down[half:], "z", -1)),
     ]
     return pieces
 
 
 PAD = 8
 Q_FIRST = NZ * HS
+PAYLOAD_TOP = 640
 
 
 def window_kernel(layout, ids_ref, at_ref, *refs):
@@ -245,12 +280,13 @@
     pieces = refs[NX:NX + len(layout)]
     out_ref = refs[NX + len(layout)]
     table, q_in, qs, outs, stats, active, sem, q_sem = refs[NX + len(layout) + 1:]
+    q_first = (Q_FIRST, Q_FIRST, Q_FIRST, Q_FIRST - PAYLOAD_TOP)
     my_z, my_x, core = at_ref[0], at_ref[1], at_ref[2]
     count_all = NX * 8 + 1
     plane_rows = NX * 1024
     total_rows = qs.shape[0]
     q_copies = [
-        pltpu.make_async_copy(payloads[i].at[pl.ds(Q_FIRST, 256)], q_in.at[i], q_sem.at[i]) for i in range(NX)
+        pltpu.make_async_copy(payloads[i].at[pl.ds(q_first[i], 256)], q_in.at[i], q_sem.at[i]) for i in range(NX)
     ]
     copies = [
         pltpu.make_async_copy(pieces[i], table.at[distance, pl.ds(first, rows)], sem.at[i])
@@ -370,6 +406,7 @@
         ],
         out_shape=jax.ShapeDtypeStruct((NX, 1056, HS), BF),
         cost_estimate=pl.CostEstimate(flops=10**9, bytes_accessed=8 * 2**20, transcendentals=10**6),
+        compiler_params=pltpu.CompilerParams(vmem_limit_bytes=58 * MIB),
         name="windows",
     )(ids, at, *payloads, *[piece[-1] for piece in pieces])
 
@@ -400,8 +437,13 @@
         out_specs=VMEM_ALL,
         out_shape=jax.ShapeDtypeStruct((1024, HS), BF),
         cost_estimate=pl.CostEstimate(flops=10**7, bytes_accessed=2 * 2**20, transcendentals=0),
+        compiler_params=pltpu.CompilerParams(vmem_limit_bytes=8 * MIB),
         name="combine",
     )(parts)
+
+
+def as_index(*values):
+    return jnp.stack(values).astype(jnp.int32)
 
 
 def on_device(corpus, enc_qkv, enc_out, cca_kv, gain_in, gain_out, queries, nbr_ids):
@@ -411,40 +453,46 @@
     e_own = enc_out.reshape(2 * HS, width)
     e_other = shifted(e_own, "c", 1)
 
+    kv = lax.optimization_barrier(cca_kv.reshape(cca_kv.shape[0], 512))
+    kv = spread(kv, "z").reshape(-1, 512)
+
+    w_rows = enc_qkv.transpose(0, 2, 1, 3).reshape(width * 6, HS)
+    att_own, att_send = encode(corpus_flat, w_rows, gain_in.reshape(1, width), as_index(core))
+    nbr_ids, queries, att_send = lax.optimization_barrier((nbr_ids, queries, att_send))
+    att_other = shifted(att_send, "c", 1)
+
     last = lax.ppermute(nbr_ids[7:], ("z", "x"), [(i, i + 1) for i in range(NZ * NX - 1)])
     last = jnp.where(jnp.logical_and(my_z == 0, my_x == 0), -1, last)
     ids = jnp.concatenate([last, nbr_ids], axis=0).astype(BF)
-
-    kv = lax.optimization_barrier(cca_kv.reshape(cca_kv.shape[0], 512))
-    kv = spread(kv, "z").reshape(-1, 512)
+    terms = project(as_index(my_y), att_own, att_other, e_own, e_other)
+
+    kv, terms = lax.optimization_barrier((kv, terms))
     q_rows = queries.reshape(4, 256, HS)
     q_wide = jnp.concatenate([q_rows[b] for b in range(4)], axis=1)
     payload = jnp.concatenate([kv, q_wide, jnp.pad(ids, ((0, 7), (0, 510)))], axis=0)
     from_left = shifted(payload, "x", 1)
     from_right = shifted(payload, "x", -1)
-    from_far = shifted(payload, "x", 2)
-
-    w_rows = enc_qkv.transpose(0, 2, 1, 3).reshape(width * 6, HS)
-    att_own, att_send = encode(
-        corpus_flat, w_rows, gain_in.reshape(1, width), core.reshape(1).astype(jnp.int32)
-    )
-    att_other = shifted(att_send, "c", 1)
-    partial = project(att_own, att_other, e_own, e_other).reshape(NY, 2 * ROW // NY, width)
-    terms = lax.all_to_all(partial, "y", split_axis=0, concat_axis=0, tiled=True)
-    block = (core * NY + my_y).reshape(1).astype(jnp.int32)
-    copies = normalise(terms, corpus_flat, gain_out.reshape(1, width), block)
-    copies, from_left, from_right = lax.optimization_barrier((copies, from_left, from_right))
-    u_own = lax.all_to_all(copies, "y", split_axis=0, concat_axis=0, tiled=True).reshape(2 * ROW, width)
-    u_own, from_far = lax.optimization_barrier((u_own, from_far))
+
+    terms = [terms[0]] + [shifted(terms[k], "y", k) for k in range(1, NY)]
+    u = normalise(terms, corpus_flat, gain_out.reshape(1, width), as_index(core * NY + my_y))
+    u, from_left, from_right = lax.optimization_barrier((u, from_left, from_right))
+    far_top = shifted(from_left[:PAYLOAD_TOP], "x", 1)
+    far_bottom = shifted(from_right[PAYLOAD_TOP:], "x", -1)
+    payloads = [payload, from_left, from_right, far_top, far_bottom]
+    us = [u] + [shifted(u, "y", k) for k in range(1, NY)]
+    at = as_index(my_x, my_y)
+    memory_own, u_own = memorise(at, us, payloads)
     u_other = shifted(u_own, "c", 1)
-    payloads = [payload, from_left, from_right, from_far]
-    memory = memorise(my_x.reshape(1).astype(jnp.int32), u_own, u_other, payloads)
-    pieces = ring_pieces(memory)
-
-    by_step = [payloads[ORDER.index(d)] for d in range(NX)]
-    got = jnp.stack([p[Q_FIRST + 256:Q_FIRST + 265, 0:2] for p in by_step]).astype(jnp.int32)
-    at = jnp.stack([my_z, my_x, core]).astype(jnp.int32)
-    got, at = lax.optimization_barrier((got.reshape(-1), at))
+    pieces = ring_pieces(memory_own, 0)
+    (memory_other,) = memorise(at, [u_other], payloads)
+    pieces += ring_pieces(memory_other, 2 * ROW)
+
+    ids_first = Q_FIRST + 256
+    near = [p[ids_first:ids_first + 9, 0:2] for p in payloads[:3]]
+    far = far_bottom[ids_first - PAYLOAD_TOP:ids_first - PAYLOAD_TOP + 9, 0:2]
+    got = jnp.stack([near[0], near[2], far, near[1]]).astype(jnp.int32)
+    got, at = lax.optimization_barrier((got.reshape(-1), as_index(my_z, my_x, core)))
+    payloads = payloads[:3] + [far_bottom]
     parts = windows(got, at, payloads, pieces)
     parts = lax.all_to_all(parts, "x", split_axis=0, concat_axis=0, tiled=True)
     return combine(parts).reshape(512, 2, HS)

time: 223 us -> 199 us (0.89)
  the two profiles are of different devices: /device:TPU:2 before, /device:TPU:96 now
where the time goes in v3:
time: 199 us; the launch traced here: 196 us
  waiting for transfers between devices  65.8 us (33%)
  starting transfers between devices  55.4 us (28%)
  Pallas kernels  45.9 us (23%)
  blocking collectives  18.8 us (9%)
  local copies, waits for them, and re-layouts  7.83 us (4%)
  other arithmetic  2.28 us (1%)
    ppermute x29, waiting for transfers between devices, shifted(): return lax.ppermute(value, axis, [(i, (i + steps) % n) for i in range(n)])  57.3 us
    ppermute x29, starting transfers between devices, shifted(): return lax.ppermute(value, axis, [(i, (i + steps) % n) for i in range(n)])  44.4 us
    all_to_all x1, blocking collectives, on_device(): parts = lax.all_to_all(parts, 'x', split_axis=0, concat_axis=0, tiled=True)  18.8 us
    pallas_call x1, Pallas kernels, windows(): pl.pallas_call(functools.partial(window_kernel, layout), in_specs=[smem,...  16.1 us
    pallas_call x1, Pallas kernels, encode(): pl.pallas_call(encoder_kernel, grid_spec=pltpu.PrefetchScalarGridSpec(num...  13.8 us
    ppermute x1, waiting for transfers between devices, on_device(): lax.ppermute(nbr_ids[7:], ('z', 'x'), [(i, i + 1) for i in range(NZ * NX...  8.52 us
    all_to_all x1, starting transfers between devices, spread(): return lax.all_to_all(copies, axis, split_axis=0, concat_axis=0, tiled=True)  7.66 us
    pallas_call x2, Pallas kernels, memorise(): pl.pallas_call(functools.partial(memory_kernel, len(us)), in_specs=[pl.Bl...  6.86 us
  transfers between devices with their start and end apart: 31, of which 14 were waited for; matrix products, arithmetic and copies ran while one was open for 3% of the time, Pallas kernels for 13%

profile of v3, /device:TPU:96, one launch (start us, length us, event | category | flops | bytes accessed | tf_op | source)
XLA Modules:
  0.0 196.4 jit_solution(12911630797203763638)
XLA Ops:
  2.0 7.7 %all-to-all-start = ((bf16[8,128,512]{2,1,0:T(8,128)(2,1)}), bf16[8,128,512]{2,1,0:T(8,128)(2,1)}, u32[]{:S(2)}, u32[]{:S(2)}) async-start(bf16[8,128,512]{2,1,0:T(8,128)(2,1)} %broadcast_in_dim.11), calls=%async_computation | async-start | bytes 2097152 | tf_op jit(solution)/shard_map/all_to_all | solution.py:31
  9.7 13.8 %encoder.1 = (bf16[256,256]{1,0:T(8,128)(2,1)}, bf16[256,256]{1,0:T(8,128)(2,1)}) custom-call(s32[1]{0:T(128)} %bitcast.core_ref, bf16[512,4096]{1,0:T(8,128)(2,1)} %bitcast.28, bf16[24576,128]{1,0:T(8,128)(2,1)} %bitcast.35, f32[1,4096]{1,0:T(1,128)} %bitcast.36), custom_call_target="tpu_custom_call" | custom-call | flops 3221225472 | bytes 10485760 | tf_op jit(solution)/shard_map/encoder/pallas_call | solution.py:87
  23.6 3.4 %collective-permute-start = (s32[1,2]{0,1:T(2,128)S(1)}, s32[1,2]{0,1:T(2,128)S(1)}, u32[]{:S(2)}, u32[]{:S(2)}) collective-permute-start(s32[1,2]{0,1:T(2,128)S(1)} %slice.47), channel_id=1, source_target_pairs={{0,8},{8,16},{16,24},{24,32},{32,40},{40,48},{48,56},{56,64},{64,7... | collective-permute-start | bytes 32 | tf_op jit(solution)/shard_map/ppermute | solution.py:464
  27.2 8.5 %collective-permute-done = s32[1,2]{0,1:T(2,128)S(1)} collective-permute-done((s32[1,2]{0,1:T(2,128)S(1)}, s32[1,2]{0,1:T(2,128)S(1)}, u32[]{:S(2)}, u32[]{:S(2)}) %collective-permute-start) | collective-permute-done | bytes 40 | tf_op jit(solution)/shard_map/ppermute | solution.py:464
  36.9 4.7 %project.1 = (bf16[64,4096]{1,0:T(8,128)(2,1)S(1)}, bf16[64,4096]{1,0:T(8,128)(2,1)}, bf16[64,4096]{1,0:T(8,128)(2,1)}, bf16[64,4096]{1,0:T(8,128)(2,1)S(1)}) custom-call(s32[1]{0:T(128)} %bitcast.8.y_ref, bf16[256,256]{1,0:T(8,128)(2,1)S(1)} %copy-done.8, bf16[256,256]{1,0:T(8,128)(2,1)S(1)} %collective-permute-done.1.b_ref, ...), custom_call_target="tpu_custom_call" | custom-call | flops 1073741824 | bytes 4194304 | tf_op jit(solution)/shard_map/project/pallas_call | solution.py:130
  43.8 3.2 %collective-permute-start.7 = (bf16[1296,512]{1,0:T(8,128)(2,1)S(1)}, bf16[1296,512]{1,0:T(8,128)(2,1)S(1)}, u32[]{:S(2)}, u32[]{:S(2)}) collective-permute-start(bf16[1296,512]{1,0:T(8,128)(2,1)S(1)} %fusion.1.refs_4_.refs_1_.refs_0_), channel_id=1, source_target_pairs={{0,24},{8,0},{16,8},{24,16},{1,25},{9,1},{17,9},{25,17},{2,26},{10... | collective-permute-start | bytes 3981320 | tf_op jit(solution)/shard_map/ppermute | solution.py:25
  47.1 1.6 collective-permute-start.3
  48.6 2.9 %collective-permute-start.4 = (bf16[64,4096]{1,0:T(8,128)(2,1)}, bf16[64,4096]{1,0:T(8,128)(2,1)}, u32[]{:S(2)}, u32[]{:S(2)}) collective-permute-start(bf16[64,4096]{1,0:T(8,128)(2,1)} %get-tuple-element.36), channel_id=1, source_target_pairs={{0,4},{2,6},{4,0},{6,2},{1,5},{3,7},{5,1},{7,3},{8,12},{10,14},{12... | collective-permute-start | bytes 1572872 | tf_op jit(solution)/shard_map/ppermute | solution.py:25
  52.9 9.4 %collective-permute-done.3.t1 = bf16[64,4096]{1,0:T(8,128)(2,1)} collective-permute-done((bf16[64,4096]{1,0:T(8,128)(2,1)}, bf16[64,4096]{1,0:T(8,128)(2,1)}, u32[]{:S(2)}, u32[]{:S(2)}) %collective-permute-start.3) | collective-permute-done | bytes 524320 | tf_op jit(solution)/shard_map/ppermute | solution.py:25
  62.3 11.8 %collective-permute-done.4.t2 = bf16[64,4096]{1,0:T(8,128)(2,1)} collective-permute-done((bf16[64,4096]{1,0:T(8,128)(2,1)}, bf16[64,4096]{1,0:T(8,128)(2,1)}, u32[]{:S(2)}, u32[]{:S(2)}) %collective-permute-start.4) | collective-permute-done | bytes 524320 | tf_op jit(solution)/shard_map/ppermute | solution.py:25
  74.1 3.1 %normalise.1.refs_0_ = bf16[64,4096]{1,0:T(8,128)(2,1)} custom-call(s32[1]{0:T(128)} %bitcast.6.block_ref, bf16[64,4096]{1,0:T(8,128)(2,1)} %copy-done.6, bf16[64,4096]{1,0:T(8,128)(2,1)} %collective-permute-done.3.t1, bf16[64,4096]{1,0:T(8,128)(2,1)} %collective-permute-done.4.t2, bf16[64,4096]{1,0:T(8,128)(2,1)} %collective-permute-done.5.t3, ...), custom_call_target="tpu_custom_call" | custom-call | flops 2097152 | bytes 3145728 | tf_op jit(solution)/shard_map/normalise/pallas_call | solution.py:168
  77.3 1.6 collective-permute-start.8
  80.6 2.8 %collective-permute-start.10 = (bf16[64,4096]{1,0:T(8,128)(2,1)S(1)}, bf16[64,4096]{1,0:T(8,128)(2,1)S(1)}, u32[]{:S(2)}, u32[]{:S(2)}) collective-permute-start(bf16[64,4096]{1,0:T(8,128)(2,1)S(1)} %copy-done.4), channel_id=1, source_target_pairs={{0,4},{2,6},{4,0},{6,2},{1,5},{3,7},{5,1},{7,3},{8,12},{10,14},{12... | collective-permute-start | bytes 1572872 | tf_op jit(solution)/shard_map/ppermute | solution.py:25
  85.5 11.5 %collective-permute-done.10.refs_2_ = bf16[64,4096]{1,0:T(8,128)(2,1)S(1)} collective-permute-done((bf16[64,4096]{1,0:T(8,128)(2,1)S(1)}, bf16[64,4096]{1,0:T(8,128)(2,1)S(1)}, u32[]{:S(2)}, u32[]{:S(2)}) %collective-permute-start.10) | collective-permute-done | bytes 524320 | tf_op jit(solution)/shard_map/ppermute | solution.py:25
  97.0 9.0 %collective-permute-done.11.refs_3_ = bf16[64,4096]{1,0:T(8,128)(2,1)S(1)} collective-permute-done((bf16[64,4096]{1,0:T(8,128)(2,1)S(1)}, bf16[64,4096]{1,0:T(8,128)(2,1)S(1)}, u32[]{:S(2)}, u32[]{:S(2)}) %collective-permute-start.11) | collective-permute-done | bytes 524320 | tf_op jit(solution)/shard_map/ppermute | solution.py:25
  106.1 3.4 %memorise.2 = (bf16[256,512]{1,0:T(8,128)(2,1)S(1)}, bf16[256,4096]{1,0:T(8,128)(2,1)S(1)}) custom-call(s32[2]{0:T(128)S(1)} %pad_add_fusion.1.at_ref, bf16[64,4096]{1,0:T(8,128)(2,1)S(1)} %copy-done.4, bf16[64,4096]{1,0:T(8,128)(2,1)S(1)} %collective-permute-done.9.refs_1_, bf16[64,4096]{1,0:T(8,128)(2,1)S(1)} %collective-permute-done.10.refs_2_, ...), custom_call_target="tpu_custom_call" | custom-call | flops 1073741824 | bytes 4194304 | tf_op jit(solution)/shard_map/memorise/pallas_call | solution.py:238
  109.6 2.9 %collective-permute-start.13 = (bf16[256,512]{1,0:T(8,128)(2,1)S(1)}, bf16[256,512]{1,0:T(8,128)(2,1)S(1)}, u32[]{:S(2)}, u32[]{:S(2)}) collective-permute-start(bf16[256,512]{1,0:T(8,128)(2,1)S(1)} %get-tuple-element.45.refs_4_), channel_id=1, source_target_pairs={{0,32},{32,64},{64,96},{96,128},{128,160},{160,192},{192,224},{224... | collective-permute-start | bytes 786440 | tf_op jit(solution)/shard_map/ppermute | solution.py:25
  113.8 3.4 %memorise.3.refs_13_ = bf16[256,512]{1,0:T(8,128)(2,1)S(1)} custom-call(s32[2]{0:T(128)S(1)} %pad_add_fusion.1.at_ref, bf16[256,4096]{1,0:T(8,128)(2,1)S(1)} %collective-permute-done.21.refs_0_, bf16[1296,512]{1,0:T(8,128)(2,1)S(1)} %fusion.1.refs_4_.refs_1_.refs_0_, bf16[1296,512]{1,0:T(8,128)(2,1)} %collective-permute-done.6.refs_5_.refs_2_.refs_1_, ...), custom_call_target="tpu_custom_call" | custom-call | flops 1073741824 | bytes 4194304 | tf_op jit(solution)/shard_map/memorise/pallas_call | solution.py:238
  117.2 2.9 %collective-permute-start.22 = (bf16[256,512]{1,0:T(8,128)(2,1)S(1)}, bf16[256,512]{1,0:T(8,128)(2,1)S(1)}, u32[]{:S(2)}, u32[]{:S(2)}) collective-permute-start(bf16[256,512]{1,0:T(8,128)(2,1)S(1)} %memorise.3.refs_13_), channel_id=1, source_target_pairs={{0,32},{32,64},{64,96},{96,128},{128,160},{160,192},{192,224},{224... | collective-permute-start | bytes 786440 | tf_op jit(solution)/shard_map/ppermute | solution.py:25
  120.2 3.2 %collective-permute-start.15 = (bf16[256,512]{1,0:T(8,128)(2,1)S(1)}, bf16[256,512]{1,0:T(8,128)(2,1)}, u32[]{:S(2)}, u32[]{:S(2)}) collective-permute-start(bf16[256,512]{1,0:T(8,128)(2,1)S(1)} %collective-permute-done.13.refs_5_), channel_id=1, source_target_pairs={{0,32},{32,64},{64,96},{96,128},{128,160},{160,192},{192,224},{224... | collective-permute-start | bytes 786440 | tf_op jit(solution)/shard_map/ppermute | solution.py:25
  123.4 3.4 %collective-permute-done.22.refs_14_ = bf16[256,512]{1,0:T(8,128)(2,1)S(1)} collective-permute-done((bf16[256,512]{1,0:T(8,128)(2,1)S(1)}, bf16[256,512]{1,0:T(8,128)(2,1)S(1)}, u32[]{:S(2)}, u32[]{:S(2)}) %collective-permute-start.22) | collective-permute-done | bytes 262176 | tf_op jit(solution)/shard_map/ppermute | solution.py:25
  126.8 3.7 %collective-permute-start.24 = (bf16[256,512]{1,0:T(8,128)(2,1)S(1)}, bf16[256,512]{1,0:T(8,128)(2,1)}, u32[]{:S(2)}, u32[]{:S(2)}) collective-permute-start(bf16[256,512]{1,0:T(8,128)(2,1)S(1)} %collective-permute-done.22.refs_14_), channel_id=1, source_target_pairs={{0,32},{32,64},{64,96},{96,128},{128,160},{160,192},{192,224},{224... | collective-permute-start | bytes 786440 | tf_op jit(solution)/shard_map/ppermute | solution.py:25
  130.6 1.9 collective-permute-done.15.refs_7_
  132.4 3.8 %collective-permute-start.17 = (bf16[256,512]{1,0:T(8,128)(2,1)}, bf16[256,512]{1,0:T(8,128)(2,1)S(1)}, u32[]{:S(2)}, u32[]{:S(2)}) collective-permute-start(bf16[256,512]{1,0:T(8,128)(2,1)} %collective-permute-done.15.refs_7_), channel_id=1, source_target_pairs={{0,32},{32,64},{64,96},{96,128},{128,160},{160,192},{192,224},{224... | collective-permute-start | bytes 786440 | tf_op jit(solution)/shard_map/ppermute | solution.py:25
  136.3 1.8 collective-permute-done.24.refs_16_
  138.1 3.8 %collective-permute-start.26 = (bf16[256,512]{1,0:T(8,128)(2,1)}, bf16[256,512]{1,0:T(8,128)(2,1)S(1)}, u32[]{:S(2)}, u32[]{:S(2)}) collective-permute-start(bf16[256,512]{1,0:T(8,128)(2,1)} %collective-permute-done.24.refs_16_), channel_id=1, source_target_pairs={{0,32},{32,64},{64,96},{96,128},{128,160},{160,192},{192,224},{224... | collective-permute-start | bytes 786440 | tf_op jit(solution)/shard_map/ppermute | solution.py:25
  143.8 3.9 %collective-permute-start.19 = (bf16[128,512]{1,0:T(8,128)(2,1)S(1)}, bf16[128,512]{1,0:T(8,128)(2,1)S(1)}, u32[]{:S(2)}, u32[]{:S(2)}) collective-permute-start(bf16[128,512]{1,0:T(8,128)(2,1)S(1)} %slice.62), channel_id=1, source_target_pairs={{0,32},{32,64},{64,96},{96,128},{128,160},{160,192},{192,224},{224... | collective-permute-start | bytes 393224 | tf_op jit(solution)/shard_map/ppermute | solution.py:25
  147.8 1.6 collective-permute-done.26.refs_18_
  149.4 3.7 %collective-permute-start.28 = (bf16[128,512]{1,0:T(8,128)(2,1)S(1)}, bf16[128,512]{1,0:T(8,128)(2,1)S(1)}, u32[]{:S(2)}, u32[]{:S(2)}) collective-permute-start(bf16[128,512]{1,0:T(8,128)(2,1)S(1)} %slice.64), channel_id=1, source_target_pairs={{0,32},{32,64},{64,96},{96,128},{128,160},{160,192},{192,224},{224... | collective-permute-start | bytes 393224 | tf_op jit(solution)/shard_map/ppermute | solution.py:25
  155.6 3.8 %collective-permute-done.29.refs_21_ = bf16[128,512]{1,0:T(8,128)(2,1)S(1)} collective-permute-done((bf16[128,512]{1,0:T(8,128)(2,1)S(1)}, bf16[128,512]{1,0:T(8,128)(2,1)S(1)}, u32[]{:S(2)}, u32[]{:S(2)}) %collective-permute-start.29) | collective-permute-done | bytes 131104 | tf_op jit(solution)/shard_map/ppermute | solution.py:25
  160.1 16.1 %windows.1 = bf16[4,1056,128]{2,1,0:T(8,128)(2,1)} custom-call(s32[72]{0:T(128)} %reshape.77.ids_ref, s32[3]{0:T(128)} %pad_add_fusion.at_ref, bf16[1296,512]{1,0:T(8,128)(2,1)} %copy-done, bf16[1296,512]{1,0:T(8,128)(2,1)} %collective-permute-done.6.refs_5_.refs_2_.refs_1_, bf16[1296,512]{1,0:T(8,128)(2,1)} %copy-done.1, bf16[656,512]{1,0:T(8,128)(2,1)} %copy-done.2, ...), custom_call_target="tpu_custom_call" | custom-call | flops 1000000000 | bytes 8388608 | tf_op jit(solution)/shard_map/windows/pallas_call | solution.py:393
  176.1 18.8 %all_to_all.10.parts_ref = bf16[4,1056,128]{2,1,0:T(8,128)(2,1)S(1)} all-to-all(bf16[4,1056,128]{2,1,0:T(8,128)(2,1)} %windows.1), channel_id=1, replica_groups=mesh['z'=8,'x'=4,'y'=4,'c'=2] {'x'}, dimensions={0} | all-to-all | bytes 2162688 | tf_op jit(solution)/shard_map/all_to_all | solution.py:497
  (112 shorter events, 18.9 us)
Async XLA Ops:
  0.0 36.0 %collective-permute-start.2 = (bf16[256,4096]{1,0:T(8,128)(2,1)}, bf16[256,4096]{1,0:T(8,128)(2,1)}, u32[]{:S(2)}, u32[]{:S(2)}) collective-permute-start(bf16[256,4096]{1,0:T(8,128)(2,1)} %bitcast.26), channel_id=1, source_target_pairs={{0,1},{1,0},{2,3},{3,2},{4,5},{5,4},{6,7},{7,6},{8,9},{9,8},{10,11... | collective-permute-start | bytes 6291464 | tf_op jit(solution)/shard_map/ppermute | solution.py:25
  2.0 40.4 %all-to-all-start = ((bf16[8,128,512]{2,1,0:T(8,128)(2,1)}), bf16[8,128,512]{2,1,0:T(8,128)(2,1)}, u32[]{:S(2)}, u32[]{:S(2)}) async-start(bf16[8,128,512]{2,1,0:T(8,128)(2,1)} %broadcast_in_dim.11), calls=%async_computation | async-start | bytes 2097152 | tf_op jit(solution)/shard_map/all_to_all | solution.py:31
  23.5 12.5 %collective-permute-start.1 = (bf16[256,256]{1,0:T(8,128)(2,1)}, bf16[256,256]{1,0:T(8,128)(2,1)S(1)}, u32[]{:S(2)}, u32[]{:S(2)}) collective-permute-start(bf16[256,256]{1,0:T(8,128)(2,1)} %get-tuple-element.29), channel_id=1, source_target_pairs={{0,1},{1,0},{2,3},{3,2},{4,5},{5,4},{6,7},{7,6},{8,9},{9,8},{10,11... | collective-permute-start | bytes 393224 | tf_op jit(solution)/shard_map/ppermute | solution.py:25
  23.6 12.1 %collective-permute-start = (s32[1,2]{0,1:T(2,128)S(1)}, s32[1,2]{0,1:T(2,128)S(1)}, u32[]{:S(2)}, u32[]{:S(2)}) collective-permute-start(s32[1,2]{0,1:T(2,128)S(1)} %slice.47), channel_id=1, source_target_pairs={{0,8},{8,16},{16,24},{24,32},{32,40},{40,48},{48,56},{56,64},{64,7... | collective-permute-start | bytes 32 | tf_op jit(solution)/shard_map/ppermute | solution.py:464
  43.7 70.0 %copy-start = (bf16[1296,512]{1,0:T(8,128)(2,1)}, bf16[1296,512]{1,0:T(8,128)(2,1)S(1)}, u32[]{:S(2)}) copy-start(bf16[1296,512]{1,0:T(8,128)(2,1)S(1)} %fusion.1.refs_4_.refs_1_.refs_0_) | copy-start | bytes 3981316
  43.7 33.4 %collective-permute-start.6 = (bf16[1296,512]{1,0:T(8,128)(2,1)S(1)}, bf16[1296,512]{1,0:T(8,128)(2,1)}, u32[]{:S(2)}, u32[]{:S(2)}) collective-permute-start(bf16[1296,512]{1,0:T(8,128)(2,1)S(1)} %fusion.1.refs_4_.refs_1_.refs_0_), channel_id=1, source_target_pairs={{0,8},{8,16},{16,24},{24,0},{1,9},{9,17},{17,25},{25,1},{2,10},{10... | collective-permute-start | bytes 3981320 | tf_op jit(solution)/shard_map/ppermute | solution.py:25
  43.8 33.4 %collective-permute-start.7 = (bf16[1296,512]{1,0:T(8,128)(2,1)S(1)}, bf16[1296,512]{1,0:T(8,128)(2,1)S(1)}, u32[]{:S(2)}, u32[]{:S(2)}) collective-permute-start(bf16[1296,512]{1,0:T(8,128)(2,1)S(1)} %fusion.1.refs_4_.refs_1_.refs_0_), channel_id=1, source_target_pairs={{0,24},{8,0},{16,8},{24,16},{1,25},{9,1},{17,9},{25,17},{2,26},{10... | collective-permute-start | bytes 3981320 | tf_op jit(solution)/shard_map/ppermute | solution.py:25
  47.1 15.3 %collective-permute-start.3 = (bf16[64,4096]{1,0:T(8,128)(2,1)}, bf16[64,4096]{1,0:T(8,128)(2,1)}, u32[]{:S(2)}, u32[]{:S(2)}) collective-permute-start(bf16[64,4096]{1,0:T(8,128)(2,1)} %get-tuple-element.35), channel_id=1, source_target_pairs={{0,2},{2,4},{4,6},{6,0},{1,3},{3,5},{5,7},{7,1},{8,10},{10,12},{12... | collective-permute-start | bytes 1572872 | tf_op jit(solution)/shard_map/ppermute | solution.py:25
  48.6 25.4 %collective-permute-start.4 = (bf16[64,4096]{1,0:T(8,128)(2,1)}, bf16[64,4096]{1,0:T(8,128)(2,1)}, u32[]{:S(2)}, u32[]{:S(2)}) collective-permute-start(bf16[64,4096]{1,0:T(8,128)(2,1)} %get-tuple-element.36), channel_id=1, source_target_pairs={{0,4},{2,6},{4,0},{6,2},{1,5},{3,7},{5,1},{7,3},{8,12},{10,14},{12... | collective-permute-start | bytes 1572872 | tf_op jit(solution)/shard_map/ppermute | solution.py:25
  51.5 22.5 %collective-permute-start.5 = (bf16[64,4096]{1,0:T(8,128)(2,1)S(1)}, bf16[64,4096]{1,0:T(8,128)(2,1)}, u32[]{:S(2)}, u32[]{:S(2)}) collective-permute-start(bf16[64,4096]{1,0:T(8,128)(2,1)S(1)} %get-tuple-element.37), channel_id=1, source_target_pairs={{0,6},{2,0},{4,2},{6,4},{1,7},{3,1},{5,3},{7,5},{8,14},{10,8},{12,... | collective-permute-start | bytes 1572872 | tf_op jit(solution)/shard_map/ppermute | solution.py:25
  77.3 28.8 %collective-permute-start.8 = (bf16[656,512]{1,0:T(8,128)(2,1)S(1)}, bf16[656,512]{1,0:T(8,128)(2,1)S(1)}, u32[]{:S(2)}, u32[]{:S(2)}) collective-permute-start(bf16[656,512]{1,0:T(8,128)(2,1)S(1)} %slice.53), channel_id=1, source_target_pairs={{0,24},{8,0},{16,8},{24,16},{1,25},{9,1},{17,9},{25,17},{2,26},{10... | collective-permute-start | bytes 2015240 | tf_op jit(solution)/shard_map/ppermute | solution.py:25
  80.0 26.0 %collective-permute-start.12 = (bf16[640,512]{1,0:T(8,128)(2,1)S(1)}, bf16[640,512]{1,0:T(8,128)(2,1)S(1)}, u32[]{:S(2)}, u32[]{:S(2)}) collective-permute-start(bf16[640,512]{1,0:T(8,128)(2,1)S(1)} %slice.56), channel_id=1, source_target_pairs={{0,8},{8,16},{16,24},{24,0},{1,9},{9,17},{17,25},{25,1},{2,10},{10... | collective-permute-start | bytes 1966088 | tf_op jit(solution)/shard_map/ppermute | solution.py:25
  80.6 16.4 %collective-permute-start.10 = (bf16[64,4096]{1,0:T(8,128)(2,1)S(1)}, bf16[64,4096]{1,0:T(8,128)(2,1)S(1)}, u32[]{:S(2)}, u32[]{:S(2)}) collective-permute-start(bf16[64,4096]{1,0:T(8,128)(2,1)S(1)} %copy-done.4), channel_id=1, source_target_pairs={{0,4},{2,6},{4,0},{6,2},{1,5},{3,7},{5,1},{7,3},{8,12},{10,14},{12... | collective-permute-start | bytes 1572872 | tf_op jit(solution)/shard_map/ppermute | solution.py:25
  83.4 22.6 %collective-permute-start.11 = (bf16[64,4096]{1,0:T(8,128)(2,1)S(1)}, bf16[64,4096]{1,0:T(8,128)(2,1)S(1)}, u32[]{:S(2)}, u32[]{:S(2)}) collective-permute-start(bf16[64,4096]{1,0:T(8,128)(2,1)S(1)} %copy-done.4), channel_id=1, source_target_pairs={{0,6},{2,0},{4,2},{6,4},{1,7},{3,1},{5,3},{7,5},{8,14},{10,8},{12,... | collective-permute-start | bytes 1572872 | tf_op jit(solution)/shard_map/ppermute | solution.py:25
  84.5 21.6 %collective-permute-start.9 = (bf16[64,4096]{1,0:T(8,128)(2,1)S(1)}, bf16[64,4096]{1,0:T(8,128)(2,1)S(1)}, u32[]{:S(2)}, u32[]{:S(2)}) collective-permute-start(bf16[64,4096]{1,0:T(8,128)(2,1)S(1)} %copy-done.4), channel_id=1, source_target_pairs={{0,2},{2,4},{4,6},{6,0},{1,3},{3,5},{5,7},{7,1},{8,10},{10,12},{12... | collective-permute-start | bytes 1572872 | tf_op jit(solution)/shard_map/ppermute | solution.py:25
  109.5 4.2 %collective-permute-start.21 = (bf16[256,4096]{1,0:T(8,128)(2,1)S(1)}, bf16[256,4096]{1,0:T(8,128)(2,1)S(1)}, u32[]{:S(2)}, u32[]{:S(2)}) collective-permute-start(bf16[256,4096]{1,0:T(8,128)(2,1)S(1)} %get-tuple-element.46), channel_id=1, source_target_pairs={{0,1},{1,0},{2,3},{3,2},{4,5},{5,4},{6,7},{7,6},{8,9},{9,8},{10,11... | collective-permute-start | bytes 6291464 | tf_op jit(solution)/shard_map/ppermute | solution.py:25
  109.6 10.5 %collective-permute-start.13 = (bf16[256,512]{1,0:T(8,128)(2,1)S(1)}, bf16[256,512]{1,0:T(8,128)(2,1)S(1)}, u32[]{:S(2)}, u32[]{:S(2)}) collective-permute-start(bf16[256,512]{1,0:T(8,128)(2,1)S(1)} %get-tuple-element.45.refs_4_), channel_id=1, source_target_pairs={{0,32},{32,64},{64,96},{96,128},{128,160},{160,192},{192,224},{224... | collective-permute-start | bytes 786440 | tf_op jit(solution)/shard_map/ppermute | solution.py:25
  112.6 10.8 %collective-permute-start.14 = (bf16[256,512]{1,0:T(8,128)(2,1)S(1)}, bf16[256,512]{1,0:T(8,128)(2,1)S(1)}, u32[]{:S(2)}, u32[]{:S(2)}) collective-permute-start(bf16[256,512]{1,0:T(8,128)(2,1)S(1)} %get-tuple-element.45.refs_4_), channel_id=1, source_target_pairs={{0,224},{32,0},{64,32},{96,64},{128,96},{160,128},{192,160},{224,1... | collective-permute-start | bytes 786440 | tf_op jit(solution)/shard_map/ppermute | solution.py:25
  117.2 9.6 %collective-permute-start.22 = (bf16[256,512]{1,0:T(8,128)(2,1)S(1)}, bf16[256,512]{1,0:T(8,128)(2,1)S(1)}, u32[]{:S(2)}, u32[]{:S(2)}) collective-permute-start(bf16[256,512]{1,0:T(8,128)(2,1)S(1)} %memorise.3.refs_13_), channel_id=1, source_target_pairs={{0,32},{32,64},{64,96},{96,128},{128,160},{160,192},{192,224},{224... | collective-permute-start | bytes 786440 | tf_op jit(solution)/shard_map/ppermute | solution.py:25
  120.2 10.4 %collective-permute-start.23 = (bf16[256,512]{1,0:T(8,128)(2,1)S(1)}, bf16[256,512]{1,0:T(8,128)(2,1)S(1)}, u32[]{:S(2)}, u32[]{:S(2)}) collective-permute-start(bf16[256,512]{1,0:T(8,128)(2,1)S(1)} %memorise.3.refs_13_), channel_id=1, source_target_pairs={{0,224},{32,0},{64,32},{96,64},{128,96},{160,128},{192,160},{224,1... | collective-permute-start | bytes 786440 | tf_op jit(solution)/shard_map/ppermute | solution.py:25
  120.2 12.3 %collective-permute-start.15 = (bf16[256,512]{1,0:T(8,128)(2,1)S(1)}, bf16[256,512]{1,0:T(8,128)(2,1)}, u32[]{:S(2)}, u32[]{:S(2)}) collective-permute-start(bf16[256,512]{1,0:T(8,128)(2,1)S(1)} %collective-permute-done.13.refs_5_), channel_id=1, source_target_pairs={{0,32},{32,64},{64,96},{96,128},{128,160},{160,192},{192,224},{224... | collective-permute-start | bytes 786440 | tf_op jit(solution)/shard_map/ppermute | solution.py:25
  123.4 12.9 %collective-permute-start.16 = (bf16[256,512]{1,0:T(8,128)(2,1)S(1)}, bf16[256,512]{1,0:T(8,128)(2,1)}, u32[]{:S(2)}, u32[]{:S(2)}) collective-permute-start(bf16[256,512]{1,0:T(8,128)(2,1)S(1)} %collective-permute-done.14.refs_6_), channel_id=1, source_target_pairs={{0,224},{32,0},{64,32},{96,64},{128,96},{160,128},{192,160},{224,1... | collective-permute-start | bytes 786440 | tf_op jit(solution)/shard_map/ppermute | solution.py:25
  126.8 11.2 %collective-permute-start.24 = (bf16[256,512]{1,0:T(8,128)(2,1)S(1)}, bf16[256,512]{1,0:T(8,128)(2,1)}, u32[]{:S(2)}, u32[]{:S(2)}) collective-permute-start(bf16[256,512]{1,0:T(8,128)(2,1)S(1)} %collective-permute-done.22.refs_14_), channel_id=1, source_target_pairs={{0,32},{32,64},{64,96},{96,128},{128,160},{160,192},{192,224},{224... | collective-permute-start | bytes 786440 | tf_op jit(solution)/shard_map/ppermute | solution.py:25
  130.6 11.3 %collective-permute-start.25 = (bf16[256,512]{1,0:T(8,128)(2,1)S(1)}, bf16[256,512]{1,0:T(8,128)(2,1)}, u32[]{:S(2)}, u32[]{:S(2)}) collective-permute-start(bf16[256,512]{1,0:T(8,128)(2,1)S(1)} %collective-permute-done.23.refs_15_), channel_id=1, source_target_pairs={{0,224},{32,0},{64,32},{96,64},{128,96},{160,128},{192,160},{224,1... | collective-permute-start | bytes 786440 | tf_op jit(solution)/shard_map/ppermute | solution.py:25
  132.4 11.3 %collective-permute-start.17 = (bf16[256,512]{1,0:T(8,128)(2,1)}, bf16[256,512]{1,0:T(8,128)(2,1)S(1)}, u32[]{:S(2)}, u32[]{:S(2)}) collective-permute-start(bf16[256,512]{1,0:T(8,128)(2,1)} %collective-permute-done.15.refs_7_), channel_id=1, source_target_pairs={{0,32},{32,64},{64,96},{96,128},{128,160},{160,192},{192,224},{224... | collective-permute-start | bytes 786440 | tf_op jit(solution)/shard_map/ppermute | solution.py:25
  136.3 11.4 %collective-permute-start.18 = (bf16[256,512]{1,0:T(8,128)(2,1)}, bf16[256,512]{1,0:T(8,128)(2,1)S(1)}, u32[]{:S(2)}, u32[]{:S(2)}) collective-permute-start(bf16[256,512]{1,0:T(8,128)(2,1)} %collective-permute-done.16.refs_8_), channel_id=1, source_target_pairs={{0,224},{32,0},{64,32},{96,64},{128,96},{160,128},{192,160},{224,1... | collective-permute-start | bytes 786440 | tf_op jit(solution)/shard_map/ppermute | solution.py:25
  138.1 11.3 %collective-permute-start.26 = (bf16[256,512]{1,0:T(8,128)(2,1)}, bf16[256,512]{1,0:T(8,128)(2,1)S(1)}, u32[]{:S(2)}, u32[]{:S(2)}) collective-permute-start(bf16[256,512]{1,0:T(8,128)(2,1)} %collective-permute-done.24.refs_16_), channel_id=1, source_target_pairs={{0,32},{32,64},{64,96},{96,128},{128,160},{160,192},{192,224},{224... | collective-permute-start | bytes 786440 | tf_op jit(solution)/shard_map/ppermute | solution.py:25
  141.9 11.2 %collective-permute-start.27 = (bf16[256,512]{1,0:T(8,128)(2,1)}, bf16[256,512]{1,0:T(8,128)(2,1)S(1)}, u32[]{:S(2)}, u32[]{:S(2)}) collective-permute-start(bf16[256,512]{1,0:T(8,128)(2,1)} %collective-permute-done.25.refs_17_), channel_id=1, source_target_pairs={{0,224},{32,0},{64,32},{96,64},{128,96},{160,128},{192,160},{224,1... | collective-permute-start | bytes 786440 | tf_op jit(solution)/shard_map/ppermute | solution.py:25
  143.8 10.3 %collective-permute-start.19 = (bf16[128,512]{1,0:T(8,128)(2,1)S(1)}, bf16[128,512]{1,0:T(8,128)(2,1)S(1)}, u32[]{:S(2)}, u32[]{:S(2)}) collective-permute-start(bf16[128,512]{1,0:T(8,128)(2,1)S(1)} %slice.62), channel_id=1, source_target_pairs={{0,32},{32,64},{64,96},{96,128},{128,160},{160,192},{192,224},{224... | collective-permute-start | bytes 393224 | tf_op jit(solution)/shard_map/ppermute | solution.py:25
  147.7 7.0 %collective-permute-start.20 = (bf16[128,512]{1,0:T(8,128)(2,1)S(1)}, bf16[128,512]{1,0:T(8,128)(2,1)S(1)}, u32[]{:S(2)}, u32[]{:S(2)}) collective-permute-start(bf16[128,512]{1,0:T(8,128)(2,1)S(1)} %slice.63), channel_id=1, source_target_pairs={{0,224},{32,0},{64,32},{96,64},{128,96},{160,128},{192,160},{224,1... | collective-permute-start | bytes 393224 | tf_op jit(solution)/shard_map/ppermute | solution.py:25
  149.4 6.2 %collective-permute-start.28 = (bf16[128,512]{1,0:T(8,128)(2,1)S(1)}, bf16[128,512]{1,0:T(8,128)(2,1)S(1)}, u32[]{:S(2)}, u32[]{:S(2)}) collective-permute-start(bf16[128,512]{1,0:T(8,128)(2,1)S(1)} %slice.64), channel_id=1, source_target_pairs={{0,32},{32,64},{64,96},{96,128},{128,160},{160,192},{192,224},{224... | collective-permute-start | bytes 393224 | tf_op jit(solution)/shard_map/ppermute | solution.py:25
  153.1 6.3 %collective-permute-start.29 = (bf16[128,512]{1,0:T(8,128)(2,1)S(1)}, bf16[128,512]{1,0:T(8,128)(2,1)S(1)}, u32[]{:S(2)}, u32[]{:S(2)}) collective-permute-start(bf16[128,512]{1,0:T(8,128)(2,1)S(1)} %slice.65), channel_id=1, source_target_pairs={{0,224},{32,0},{64,32},{96,64},{128,96},{160,128},{192,160},{224,1... | collective-permute-start | bytes 393224 | tf_op jit(solution)/shard_map/ppermute | solution.py:25
  (22 other events, 354.9 us)

commit v4 on v3

--- a/solution.py
+++ b/solution.py
@@ -14,6 +14,7 @@
 ROW = 128
 HS = 128
 MASKED = -1e30
+LOG_SCALE = HS ** -0.5 * 1.4426950408889634
 BF = jnp.bfloat16
 F32 = jnp.float32
 ANY = pl.BlockSpec(memory_space=pl.ANY)
@@ -31,7 +32,7 @@
     return lax.all_to_all(copies, axis, split_axis=0, concat_axis=0, tiled=True)
 
 
-def encoder_kernel(core_ref, x_ref, w_ref, g_ref, own_ref, send_ref, wide, wmat, acc, ssq):
+def encoder_kernel(at_ref, x_ref, w_ref, g_ref, out_ref, wide, wmat, acc, ssq):
     step = pl.program_id(0)
     depth = x_ref.shape[1]
 
@@ -50,39 +51,41 @@
 
     @pl.when(step == pl.num_programs(0) - 1)
     def _():
-        core = core_ref[0]
+        core, my_y = at_ref[0], at_ref[1]
         total = depth * pl.num_programs(0)
-        rinv = lax.rsqrt(ssq[...] / total + EPS)
+        scale = lax.rsqrt(ssq[...] / total + EPS)
         rows = x_ref.shape[0] // ROW
-        for r in range(rows):
-            sl = slice(r * ROW, (r + 1) * ROW)
-            scale = rinv[sl]
-            parts = []
-            for h in range(2):
-                q = (acc[sl, h * HS:(h + 1) * HS] * scale).astype(BF)
-                k = (acc[sl, (2 + h) * HS:(3 + h) * HS] * scale).astype(BF)
-                v = (acc[sl, (4 + h) * HS:(5 + h) * HS] * scale).astype(BF)
-                s = lax.dot_general(q, k, (((1,), (1,)), ((), ())), preferred_element_type=F32)
-                s = s * (HS ** -0.5)
-                m = jnp.max(s, axis=1, keepdims=True)
-                p = jnp.exp(s - m)
-                p = (p / jnp.sum(p, axis=1, keepdims=True)).astype(BF)
-                parts.append(jnp.dot(p, v, preferred_element_type=F32).astype(BF))
-            att = jnp.concatenate(parts, axis=1)
-            spot = slice((r % 2) * ROW, (r % 2 + 1) * ROW)
-
-            @pl.when(core == r // 2)
-            def _():
-                own_ref[spot, :] = att
-
-            @pl.when(core != r // 2)
-            def _():
-                send_ref[spot, :] = att
-
-
-def encode(corpus_flat, w_rows, gain, core):
+        for pair in range(rows // 2):
+            spots = [(r, h) for r in (2 * pair, 2 * pair + 1) for h in range(2)]
+
+            def part(r, col):
+                sl = slice(r * ROW, (r + 1) * ROW)
+                return (acc[sl, col * HS:(col + 1) * HS] * scale[sl]).astype(BF)
+
+            scores = [
+                lax.dot_general(
+                    part(r, h), part(r, 2 + h), (((1,), (1,)), ((), ())), preferred_element_type=F32
+                ) * LOG_SCALE
+                for r, h in spots
+            ]
+            tops = [jnp.max(s, axis=1, keepdims=True) for s in scores]
+            probs = [jnp.exp2(s - m) for s, m in zip(scores, tops)]
+            sums = [jnp.sum(p, axis=1, keepdims=True) for p in probs]
+            atts = [
+                (jnp.dot(p.astype(BF), part(r, 4 + h), preferred_element_type=F32) * (1.0 / total_p)).astype(BF)
+                for (r, h), p, total_p in zip(spots, probs, sums)
+            ]
+            side = lax.rem(pair + core, 2)
+            for i in range(2):
+                att = jnp.concatenate(atts[2 * i:2 * i + 2], axis=1)
+                for half in range(2):
+                    k = lax.rem(2 * i + half - my_y + NY, NY)
+                    out_ref[side, pl.ds(pl.multiple_of(k * 64, 64), 64), :] = att[half * 64:(half + 1) * 64]
+
+
+def encode(corpus_flat, w_rows, gain, at):
     tokens, width = corpus_flat.shape
-    steps = 8
+    steps = 4
     depth = width // steps
     return pl.pallas_call(
         encoder_kernel,
@@ -94,7 +97,7 @@
                 pl.BlockSpec((depth * 6, HS), lambda i, c: (i, 0)),
                 pl.BlockSpec((1, depth), lambda i, c: (0, i)),
             ],
-            out_specs=[pl.BlockSpec((2 * ROW, 2 * HS), lambda i, c: (0, 0))] * 2,
+            out_specs=pl.BlockSpec((2, 2 * ROW, 2 * HS), lambda i, c: (0, 0, 0)),
             scratch_shapes=[
                 pltpu.VMEM((depth * 6, HS), F32),
                 pltpu.VMEM((depth, 6 * HS), BF),
@@ -102,52 +105,45 @@
                 pltpu.VMEM((tokens, 1), F32),
             ],
         ),
-        out_shape=[jax.ShapeDtypeStruct((2 * ROW, 2 * HS), BF)] * 2,
+        out_shape=jax.ShapeDtypeStruct((2, 2 * ROW, 2 * HS), BF),
         cost_estimate=pl.CostEstimate(
             flops=2 * tokens * width * 6 * HS, bytes_accessed=(tokens + 768) * width * 2, transcendentals=0
         ),
         compiler_params=pltpu.CompilerParams(vmem_limit_bytes=60 * MIB),
         name="encoder",
-    )(core, corpus_flat, w_rows, gain)
-
-
-def project_kernel(y_ref, a_ref, b_ref, ea_ref, eb_ref, *refs):
-    outs, total = refs[:NY], refs[NY]
-    rows = total.shape[0] // NY
-    value = jnp.dot(a_ref[...], ea_ref[...], preferred_element_type=F32)
+    )(at, corpus_flat, w_rows, gain)
+
+
+def project_kernel(a_ref, b_ref, ea_ref, eb_ref, *outs):
+    rows = a_ref.shape[1] // NY
+    value = jnp.dot(a_ref[0], ea_ref[...], preferred_element_type=F32)
     value += jnp.dot(b_ref[...], eb_ref[...], preferred_element_type=F32)
-    total[...] = value.astype(BF)
     for k in range(NY):
-        first = pl.multiple_of(lax.rem(y_ref[0] + k, NY) * rows, rows)
-        outs[k][...] = total[pl.ds(first, rows), :]
-
-
-def project(my_y, att_own, att_other, e_own, e_other):
-    tokens, depth = att_own.shape
+        outs[k][...] = value[k * rows:(k + 1) * rows].astype(BF)
+
+
+def project(att, att_other, e_own, e_other):
+    tokens, depth = att_other.shape
     width = e_own.shape[1]
     cols = 1024
     rows = tokens // NY
     return pl.pallas_call(
         project_kernel,
-        grid_spec=pltpu.PrefetchScalarGridSpec(
-            num_scalar_prefetch=1,
-            grid=(width // cols,),
-            in_specs=[
-                pl.BlockSpec((tokens, depth), lambda i, y: (0, 0)),
-                pl.BlockSpec((tokens, depth), lambda i, y: (0, 0)),
-                pl.BlockSpec((depth, cols), lambda i, y: (0, i)),
-                pl.BlockSpec((depth, cols), lambda i, y: (0, i)),
-            ],
-            out_specs=[pl.BlockSpec((rows, cols), lambda i, y: (0, i))] * NY,
-            scratch_shapes=[pltpu.VMEM((tokens, cols), BF)],
-        ),
+        grid=(width // cols,),
+        in_specs=[
+            pl.BlockSpec((1, tokens, depth), lambda i: (0, 0, 0)),
+            pl.BlockSpec((tokens, depth), lambda i: (0, 0)),
+            pl.BlockSpec((depth, cols), lambda i: (0, i)),
+            pl.BlockSpec((depth, cols), lambda i: (0, i)),
+        ],
+        out_specs=[pl.BlockSpec((rows, cols), lambda i: (0, i))] * NY,
         out_shape=[jax.ShapeDtypeStruct((rows, width), BF)] * NY,
         cost_estimate=pl.CostEstimate(
             flops=4 * tokens * depth * width, bytes_accessed=4 * depth * width, transcendentals=0
         ),
         compiler_params=pltpu.CompilerParams(vmem_limit_bytes=12 * MIB),
         name="project",
-    )(my_y, att_own, att_other, e_own, e_other)
+    )(att, att_other, e_own, e_other)
 
 
 def norm_kernel(block_ref, t0, t1, t2, t3, x_ref, g_ref, out_ref):
@@ -279,7 +275,7 @@
     payloads = refs[:NX]
     pieces = refs[NX:NX + len(layout)]
     out_ref = refs[NX + len(layout)]
-    table, q_in, qs, outs, stats, active, sem, q_sem = refs[NX + len(layout) + 1:]
+    table, q_in, qs, outs, stats, one_list, two_list, sem, q_sem = refs[NX + len(layout) + 1:]
     q_first = (Q_FIRST, Q_FIRST, Q_FIRST, Q_FIRST - PAYLOAD_TOP)
     my_z, my_x, core = at_ref[0], at_ref[1], at_ref[2]
     count_all = NX * 8 + 1
@@ -289,7 +285,7 @@
         pltpu.make_async_copy(payloads[i].at[pl.ds(q_first[i], 256)], q_in.at[i], q_sem.at[i]) for i in range(NX)
     ]
     copies = [
-        pltpu.make_async_copy(pieces[i], table.at[distance, pl.ds(first, rows)], sem.at[i])
+        pltpu.make_async_copy(pieces[i], table.at[pl.ds(distance * 512 + first, rows)], sem.at[i])
         for i, (distance, first, rows) in enumerate(layout)
     ]
     for copy in q_copies + copies:
@@ -304,71 +300,76 @@
         for b in range(4):
             first = pl.multiple_of(base + b * 256, 8)
             qs[pl.ds(first, 256), :] = q_in[i, :, b * HS:(b + 1) * HS].astype(F32)
+    def held(row):
+        return jnp.logical_and(row >= 0, jnp.bitwise_and(jnp.right_shift(row, 2), NX - 1) == my_x)
+
+    def wanted(w, n):
+        group = jnp.maximum(w - 1, 0)
+        step = jnp.bitwise_and(jnp.right_shift(group, 3) - my_x, NX - 1)
+        return ids_ref[step * 18 + jnp.where(w == 0, 0, jnp.bitwise_and(group, 7) + 1) * 2 + n]
+
+    def place(row):
+        distance = jnp.bitwise_and(my_z - jnp.right_shift(row, 4), NZ - 1)
+        local = jnp.bitwise_and(row, 3)
+        half = jnp.bitwise_and(jnp.right_shift(local, 1) + core, 1)
+        return distance * 512 + half * 256 + jnp.bitwise_and(local, 1) * 128
+
+    def note(w, counts):
+        ones, twos = counts
+        rows = [wanted(w, n) for n in range(2)]
+        ok = [held(row).astype(jnp.int32) for row in rows]
+        single, both = ok[0] + ok[1] == 1, ok[0] + ok[1] == 2
+        spot = place(jnp.where(ok[0] == 1, rows[0], rows[1]))
+        one_list[2 * ones] = w
+        one_list[2 * ones + 1] = spot
+        two_list[3 * twos] = w
+        two_list[3 * twos + 1] = spot
+        two_list[3 * twos + 2] = place(jnp.maximum(rows[1], 0))
+        return ones + single.astype(jnp.int32), twos + both.astype(jnp.int32)
+
+    ones, twos = lax.fori_loop(0, count_all, note, (0, 0))
     for copy in copies:
         copy.wait()
 
-    def held(row):
-        return jnp.logical_and(row >= 0, lax.rem(jnp.maximum(row, 0) // 4, NX) == my_x)
-
-    def wanted(w, n):
-        group = jnp.maximum(w - 1, 0)
-        step = lax.rem(group // 8 - my_x + NX, NX)
-        return ids_ref[step * 18 + jnp.where(w == 0, 0, lax.rem(group, 8) + 1) * 2 + n]
-
-    def note(w, count):
-        use = jnp.logical_or(held(wanted(w, 0)), held(wanted(w, 1)))
-        active[count] = w
-        return count + use.astype(jnp.int32)
-
-    count = lax.fori_loop(0, count_all, note, 0)
-
-    def place(row):
-        row = jnp.maximum(row, 0)
-        distance = lax.rem(my_z - row // 16 + NZ, NZ)
-        local = lax.rem(row, 4)
-        half = lax.rem(local // 2 + core, 2)
-        return distance, pl.multiple_of(half * 2 * ROW + lax.rem(local, 2) * ROW, ROW)
-
-    def window(w):
-        start = PAD + 2 * (GROUP * w - 1)
-        rows = [wanted(w, n) for n in range(2)]
-        ok = [held(row) for row in rows]
-        spots = [place(row) for row in rows]
-        results = []
-        for h in range(2):
-            q = qs[pl.ds(start + h, GROUP, stride=2), :].astype(BF)
-            scores = []
-            for n in range(2):
-                d, first = spots[n]
-                k = table[d, pl.ds(first, ROW), h * 256:h * 256 + HS]
+    def attend(items):
+        jobs = []
+        for start, spots in items:
+            for h in range(2):
+                q = qs[pl.ds(start + h, GROUP, stride=2), :].astype(BF)
+                k = [table[pl.ds(pl.multiple_of(f, ROW), ROW), h * 256:h * 256 + HS] for f in spots]
+                k = k[0] if len(k) == 1 else jnp.concatenate(k, axis=0)
                 s = lax.dot_general(q, k, (((1,), (1,)), ((), ())), preferred_element_type=F32)
-                s = s * (HS ** -0.5)
-                scores.append(jnp.where(ok[n], s, MASKED))
-            m = jnp.max(jnp.maximum(scores[0], scores[1]), axis=1, keepdims=True)
-            probs = [jnp.exp(s - m) for s in scores]
-            total = jnp.sum(probs[0] + probs[1], axis=1, keepdims=True)
-            inv = 1.0 / total
-            out = jnp.zeros((GROUP, HS), F32)
-            for n in range(2):
-                d, first = spots[n]
-                v = table[d, pl.ds(first, ROW), h * 256 + HS:h * 256 + 2 * HS]
-                out += jnp.dot((probs[n] * inv).astype(BF), v, preferred_element_type=F32)
-            lse = jnp.broadcast_to(m + jnp.log(total), (GROUP, HS))
-            results.append((start + h, out, lse))
-        return results
-
-    side = 2
-
-    def body(i, carry):
-        results = []
-        for lane in range(side):
-            results += window(active[jnp.minimum(i * side + lane, count - 1)])
-        for first, out, lse in results:
+                jobs.append([start + h, h, spots, s])
+        for job in jobs:
+            job[3] = job[3] * LOG_SCALE
+            job.append(jnp.max(job[3], axis=1, keepdims=True))
+        for job in jobs:
+            job[3] = jnp.exp2(job[3] - job[4])
+            job.append(jnp.sum(job[3], axis=1, keepdims=True))
+        for first, h, spots, p, m, total in jobs:
+            v = [table[pl.ds(pl.multiple_of(f, ROW), ROW), h * 256 + HS:h * 256 + 2 * HS] for f in spots]
+            v = v[0] if len(v) == 1 else jnp.concatenate(v, axis=0)
+            out = jnp.dot(p.astype(BF), v, preferred_element_type=F32) * (1.0 / total)
             outs[pl.ds(first, GROUP, stride=2), :] = out
-            stats[pl.ds(first, GROUP, stride=2), :] = lse
+            stats[pl.ds(first, GROUP, stride=2), :] = jnp.broadcast_to(m + jnp.log2(total), (GROUP, HS))
+
+    def query_row(w):
+        return PAD + 2 * (GROUP * w - 1)
+
+    def one_pair(i, carry):
+        items = []
+        for lane in range(2):
+            at = jnp.minimum(2 * i + lane, ones - 1)
+            items.append((query_row(one_list[2 * at]), [one_list[2 * at + 1]]))
+        attend(items)
         return carry
 
-    lax.fori_loop(0, (count + side - 1) // side, body, 0)
+    def two(i, carry):
+        attend([(query_row(two_list[3 * i]), [two_list[3 * i + 1], two_list[3 * i + 2]])])
+        return carry
+
+    lax.fori_loop(0, (ones + 1) // 2, one_pair, 0)
+    lax.fori_loop(0, twos, two, 0)
     eye = lax.broadcasted_iota(jnp.int32, (HS, HS), 0) == lax.broadcasted_iota(jnp.int32, (HS, HS), 1)
     for x in range(NX):
         base = PAD + x * 1024
@@ -395,12 +396,13 @@
         in_specs=[smem, smem] + [ANY] * (NX + len(pieces)),
         out_specs=VMEM_ALL,
         scratch_shapes=[
-            pltpu.VMEM((NZ, 4 * ROW, 512), BF),
+            pltpu.VMEM((NZ * 4 * ROW, 512), BF),
             pltpu.VMEM((NX, 256, 512), BF),
             pltpu.VMEM((total, HS), F32),
             pltpu.VMEM((total, HS), F32),
             pltpu.VMEM((total, HS), F32),
-            pltpu.SMEM((NX * 8 + 2,), jnp.int32),
+            pltpu.SMEM((128,), jnp.int32),
+            pltpu.SMEM((128,), jnp.int32),
             pltpu.SemaphoreType.DMA((len(pieces),)),
             pltpu.SemaphoreType.DMA((NX,)),
         ],
@@ -417,7 +419,7 @@
         tail = parts_ref[x, 1024:1056].astype(F32)
         logs.append(tail[0:8] + tail[8:16] + tail[16:24])
     m = functools.reduce(jnp.maximum, logs)
-    weights = [jnp.exp(v - m) for v in logs]
+    weights = [jnp.exp2(v - m) for v in logs]
     inv = 1.0 / functools.reduce(jnp.add, weights)
     weights = [w * inv for w in weights]
     eye = lax.broadcasted_iota(jnp.int32, (HS, HS), 0) == lax.broadcasted_iota(jnp.int32, (HS, HS), 1)
@@ -457,29 +459,29 @@
     kv = spread(kv, "z").reshape(-1, 512)
 
     w_rows = enc_qkv.transpose(0, 2, 1, 3).reshape(width * 6, HS)
-    att_own, att_send = encode(corpus_flat, w_rows, gain_in.reshape(1, width), as_index(core))
-    nbr_ids, queries, att_send = lax.optimization_barrier((nbr_ids, queries, att_send))
-    att_other = shifted(att_send, "c", 1)
+    att = encode(corpus_flat, w_rows, gain_in.reshape(1, width), as_index(core, my_y))
+    nbr_ids, queries, att = lax.optimization_barrier((nbr_ids, queries, att))
+    att_other = shifted(att[1], "c", 1)
 
     last = lax.ppermute(nbr_ids[7:], ("z", "x"), [(i, i + 1) for i in range(NZ * NX - 1)])
     last = jnp.where(jnp.logical_and(my_z == 0, my_x == 0), -1, last)
     ids = jnp.concatenate([last, nbr_ids], axis=0).astype(BF)
-    terms = project(as_index(my_y), att_own, att_other, e_own, e_other)
-
-    kv, terms = lax.optimization_barrier((kv, terms))
+    terms = project(att, att_other, e_own, e_other)
+
+    terms = [terms[0]] + [shifted(terms[k], "y", k) for k in range(1, NY)]
+    kv, terms[1], terms[3] = lax.optimization_barrier((kv, terms[1], terms[3]))
     q_rows = queries.reshape(4, 256, HS)
     q_wide = jnp.concatenate([q_rows[b] for b in range(4)], axis=1)
     payload = jnp.concatenate([kv, q_wide, jnp.pad(ids, ((0, 7), (0, 510)))], axis=0)
     from_left = shifted(payload, "x", 1)
     from_right = shifted(payload, "x", -1)
 
-    terms = [terms[0]] + [shifted(terms[k], "y", k) for k in range(1, NY)]
     u = normalise(terms, corpus_flat, gain_out.reshape(1, width), as_index(core * NY + my_y))
-    u, from_left, from_right = lax.optimization_barrier((u, from_left, from_right))
+    us = [u] + [shifted(u, "y", k) for k in range(1, NY)]
+    us[1], us[3], from_left, from_right = lax.optimization_barrier((us[1], us[3], from_left, from_right))
     far_top = shifted(from_left[:PAYLOAD_TOP], "x", 1)
     far_bottom = shifted(from_right[PAYLOAD_TOP:], "x", -1)
     payloads = [payload, from_left, from_right, far_top, far_bottom]
-    us = [u] + [shifted(u, "y", k) for k in range(1, NY)]
     at = as_index(my_x, my_y)
     memory_own, u_own = memorise(at, us, payloads)
     u_other = shifted(u_own, "c", 1)

time: 199 us -> 181 us (0.910)
  the two profiles are of different devices: /device:TPU:96 before, /device:TPU:2 now
where the time goes in v4:
time: 181 us; the launch traced here: 179 us
  waiting for transfers between devices  57.9 us (32%)
  starting transfers between devices  55.5 us (31%)
  Pallas kernels  33.6 us (19%)
  blocking collectives  18.5 us (10%)
  local copies, waits for them, and re-layouts  10.2 us (6%)
  other arithmetic  3.25 us (2%)
    ppermute x29, waiting for transfers between devices, shifted(): return lax.ppermute(value, axis, [(i, (i + steps) % n) for i in range(n)])  54 us
    ppermute x29, starting transfers between devices, shifted(): return lax.ppermute(value, axis, [(i, (i + steps) % n) for i in range(n)])  43.6 us
    all_to_all x1, blocking collectives, on_device(): parts = lax.all_to_all(parts, 'x', split_axis=0, concat_axis=0, tiled=True)  18.5 us
    pallas_call x1, Pallas kernels, encode(): pl.pallas_call(encoder_kernel, grid_spec=pltpu.PrefetchScalarGridSpec(num...  10.3 us
    all_to_all x1, starting transfers between devices, spread(): return lax.all_to_all(copies, axis, split_axis=0, concat_axis=0, tiled=True)  8.47 us
    pallas_call x1, Pallas kernels, windows(): pl.pallas_call(functools.partial(window_kernel, layout), in_specs=[smem,...  8.27 us
    pallas_call x2, Pallas kernels, memorise(): pl.pallas_call(functools.partial(memory_kernel, len(us)), in_specs=[pl.Bl...  6.85 us
    all_to_all x1, waiting for transfers between devices, spread(): return lax.all_to_all(copies, axis, split_axis=0, concat_axis=0, tiled=True)  3.88 us
  transfers between devices with their start and end apart: 31, of which 13 were waited for; matrix products, arithmetic and copies ran while one was open for 4% of the time, Pallas kernels for 11%

profile of v4, /device:TPU:2, one launch (start us, length us, event | category | flops | bytes accessed | tf_op | source)
XLA Modules:
  0.0 179.3 jit_solution(14686334560919387435)
XLA Ops:
  2.0 8.5 %all-to-all-start = ((bf16[8,128,512]{2,1,0:T(8,128)(2,1)}), bf16[8,128,512]{2,1,0:T(8,128)(2,1)}, u32[]{:S(2)}, u32[]{:S(2)}) async-start(bf16[8,128,512]{2,1,0:T(8,128)(2,1)} %broadcast_in_dim.11), calls=%async_computation | async-start | bytes 2097152 | tf_op jit(solution)/shard_map/all_to_all | solution.py:32
  11.1 10.3 %encoder.1.a_ref = bf16[2,256,256]{2,1,0:T(8,128)(2,1)} custom-call(s32[2]{0:T(128)} %pad_add_fusion.at_ref, bf16[512,4096]{1,0:T(8,128)(2,1)} %bitcast.30, bf16[24576,128]{1,0:T(8,128)(2,1)} %bitcast.37, f32[1,4096]{1,0:T(1,128)} %bitcast.38), custom_call_target="tpu_custom_call" | custom-call | flops 3221225472 | bytes 10485760 | tf_op jit(solution)/shard_map/encoder/pallas_call | solution.py:90
  22.7 3.4 %collective-permute-start = (s32[1,2]{0,1:T(2,128)S(1)}, s32[1,2]{0,1:T(2,128)S(1)}, u32[]{:S(2)}, u32[]{:S(2)}) collective-permute-start(s32[1,2]{0,1:T(2,128)S(1)} %slice.50), channel_id=1, source_target_pairs={{0,8},{8,16},{16,24},{24,32},{32,40},{40,48},{48,56},{56,64},{64,7... | collective-permute-start | bytes 32 | tf_op jit(solution)/shard_map/ppermute | solution.py:466
  27.1 3.7 %project.1 = (bf16[64,4096]{1,0:T(8,128)(2,1)S(1)}, bf16[64,4096]{1,0:T(8,128)(2,1)S(1)}, bf16[64,4096]{1,0:T(8,128)(2,1)S(1)}, bf16[64,4096]{1,0:T(8,128)(2,1)S(1)}) custom-call(bf16[2,256,256]{2,1,0:T(8,128)(2,1)S(1)} %copy-done.6, bf16[256,256]{1,0:T(8,128)(2,1)S(1)} %collective-permute-done.1.b_ref, bf16[256,4096]{1,0:T(8,128)(2,1)S(1)} %bitcast.29, ...), custom_call_target="tpu_custom_call" | custom-call | flops 1073741824 | bytes 4194304 | tf_op jit(solution)/shard_map/project/pallas_call | solution.py:130
  36.2 3.9 %all-to-all-done = bf16[8,128,512]{2,1,0:T(8,128)(2,1)} async-done(((bf16[8,128,512]{2,1,0:T(8,128)(2,1)}), bf16[8,128,512]{2,1,0:T(8,128)(2,1)}, u32[]{:S(2)}, u32[]{:S(2)}) %all-to-all-start) | async-done | bytes 1048608 | tf_op jit(solution)/shard_map/all_to_all | solution.py:32
  40.0 7.5 %collective-permute-done.3.t1 = bf16[64,4096]{1,0:T(8,128)(2,1)S(1)} collective-permute-done((bf16[64,4096]{1,0:T(8,128)(2,1)S(1)}, bf16[64,4096]{1,0:T(8,128)(2,1)S(1)}, u32[]{:S(2)}, u32[]{:S(2)}) %collective-permute-start.3) | collective-permute-done | bytes 524320 | tf_op jit(solution)/shard_map/ppermute | solution.py:26
  47.6 1.7 fusion.1.refs_4_.refs_1_.refs_0_
  51.4 2.7 %collective-permute-start.5 = (bf16[64,4096]{1,0:T(8,128)(2,1)S(1)}, bf16[64,4096]{1,0:T(8,128)(2,1)}, u32[]{:S(2)}, u32[]{:S(2)}) collective-permute-start(bf16[64,4096]{1,0:T(8,128)(2,1)S(1)} %copy-done.10), channel_id=1, source_target_pairs={{0,4},{2,6},{4,0},{6,2},{1,5},{3,7},{5,1},{7,3},{8,12},{10,14},{12... | collective-permute-start | bytes 1572872 | tf_op jit(solution)/shard_map/ppermute | solution.py:26
  54.1 11.4 %collective-permute-done.5.t2 = bf16[64,4096]{1,0:T(8,128)(2,1)} collective-permute-done((bf16[64,4096]{1,0:T(8,128)(2,1)S(1)}, bf16[64,4096]{1,0:T(8,128)(2,1)}, u32[]{:S(2)}, u32[]{:S(2)}) %collective-permute-start.5) | collective-permute-done | bytes 524320 | tf_op jit(solution)/shard_map/ppermute | solution.py:26
  65.5 3.1 %normalise.1.refs_0_ = bf16[64,4096]{1,0:T(8,128)(2,1)} custom-call(s32[1]{0:T(128)} %bitcast.7.block_ref, bf16[64,4096]{1,0:T(8,128)(2,1)} %copy-done.7, bf16[64,4096]{1,0:T(8,128)(2,1)} %copy-done.15, bf16[64,4096]{1,0:T(8,128)(2,1)} %collective-permute-done.5.t2, bf16[64,4096]{1,0:T(8,128)(2,1)} %copy-done.16, bf16[512,4096]{1,0:T(8,128)(2,1)} %bitcast.31, ...), custom_call_target="tpu_custom_call" | custom-call | flops 2097152 | bytes 3145728 | tf_op jit(solution)/shard_map/normalise/pallas_call | solution.py:164
  69.6 2.2 %collective-permute-start.7 = (bf16[64,4096]{1,0:T(8,128)(2,1)}, bf16[64,4096]{1,0:T(8,128)(2,1)S(1)}, u32[]{:S(2)}, u32[]{:S(2)}) collective-permute-start(bf16[64,4096]{1,0:T(8,128)(2,1)} %normalise.1.refs_0_), channel_id=1, source_target_pairs={{0,6},{2,0},{4,2},{6,4},{1,7},{3,1},{5,3},{7,5},{8,14},{10,8},{12,... | collective-permute-start | bytes 1572872 | tf_op jit(solution)/shard_map/ppermute | solution.py:26
  71.8 9.7 %collective-permute-done.6.refs_1_ = bf16[64,4096]{1,0:T(8,128)(2,1)S(1)} collective-permute-done((bf16[64,4096]{1,0:T(8,128)(2,1)}, bf16[64,4096]{1,0:T(8,128)(2,1)S(1)}, u32[]{:S(2)}, u32[]{:S(2)}) %collective-permute-start.6) | collective-permute-done | bytes 524320 | tf_op jit(solution)/shard_map/ppermute | solution.py:26
  81.7 2.9 %collective-permute-start.10 = (bf16[656,512]{1,0:T(8,128)(2,1)S(1)}, bf16[656,512]{1,0:T(8,128)(2,1)S(1)}, u32[]{:S(2)}, u32[]{:S(2)}) collective-permute-start(bf16[656,512]{1,0:T(8,128)(2,1)S(1)} %slice.57), channel_id=1, source_target_pairs={{0,24},{8,0},{16,8},{24,16},{1,25},{9,1},{17,9},{25,17},{2,26},{10... | collective-permute-start | bytes 2015240 | tf_op jit(solution)/shard_map/ppermute | solution.py:26
  85.8 2.4 %collective-permute-start.11 = (bf16[64,4096]{1,0:T(8,128)(2,1)S(1)}, bf16[64,4096]{1,0:T(8,128)(2,1)S(1)}, u32[]{:S(2)}, u32[]{:S(2)}) collective-permute-start(bf16[64,4096]{1,0:T(8,128)(2,1)S(1)} %copy-done.4), channel_id=1, source_target_pairs={{0,4},{2,6},{4,0},{6,2},{1,5},{3,7},{5,1},{7,3},{8,12},{10,14},{12... | collective-permute-start | bytes 1572872 | tf_op jit(solution)/shard_map/ppermute | solution.py:26
  88.2 10.3 %collective-permute-done.11.refs_2_ = bf16[64,4096]{1,0:T(8,128)(2,1)S(1)} collective-permute-done((bf16[64,4096]{1,0:T(8,128)(2,1)S(1)}, bf16[64,4096]{1,0:T(8,128)(2,1)S(1)}, u32[]{:S(2)}, u32[]{:S(2)}) %collective-permute-start.11) | collective-permute-done | bytes 524320 | tf_op jit(solution)/shard_map/ppermute | solution.py:26
  99.6 3.4 %memorise.2 = (bf16[256,512]{1,0:T(8,128)(2,1)S(1)}, bf16[256,4096]{1,0:T(8,128)(2,1)S(1)}) custom-call(s32[2]{0:T(128)S(1)} %pad_add_fusion.2.at_ref, bf16[64,4096]{1,0:T(8,128)(2,1)S(1)} %copy-done.4, bf16[64,4096]{1,0:T(8,128)(2,1)S(1)} %collective-permute-done.6.refs_1_, bf16[64,4096]{1,0:T(8,128)(2,1)S(1)} %collective-permute-done.11.refs_2_, ...), custom_call_target="tpu_custom_call" | custom-call | flops 1073741824 | bytes 4194304 | tf_op jit(solution)/shard_map/memorise/pallas_call | solution.py:234
  104.4 2.0 %collective-permute-start.14 = (bf16[256,512]{1,0:T(8,128)(2,1)S(1)}, bf16[256,512]{1,0:T(8,128)(2,1)S(1)}, u32[]{:S(2)}, u32[]{:S(2)}) collective-permute-start(bf16[256,512]{1,0:T(8,128)(2,1)S(1)} %get-tuple-element.39.refs_4_), channel_id=1, source_target_pairs={{0,224},{32,0},{64,32},{96,64},{128,96},{160,128},{192,160},{224,1... | collective-permute-start | bytes 786440 | tf_op jit(solution)/shard_map/ppermute | solution.py:26
  107.3 3.4 %memorise.3.refs_13_ = bf16[256,512]{1,0:T(8,128)(2,1)S(1)} custom-call(s32[2]{0:T(128)S(1)} %pad_add_fusion.2.at_ref, bf16[256,4096]{1,0:T(8,128)(2,1)S(1)} %collective-permute-done.21.refs_0_, bf16[1296,512]{1,0:T(8,128)(2,1)S(1)} %fusion.1.refs_4_.refs_1_.refs_0_, bf16[1296,512]{1,0:T(8,128)(2,1)} %collective-permute-done.8.refs_5_.refs_2_.refs_1_, ...), custom_call_target="tpu_custom_call" | custom-call | flops 1073741824 | bytes 4194304 | tf_op jit(solution)/shard_map/memorise/pallas_call | solution.py:234
  112.0 2.0 %collective-permute-start.23 = (bf16[256,512]{1,0:T(8,128)(2,1)S(1)}, bf16[256,512]{1,0:T(8,128)(2,1)S(1)}, u32[]{:S(2)}, u32[]{:S(2)}) collective-permute-start(bf16[256,512]{1,0:T(8,128)(2,1)S(1)} %memorise.3.refs_13_), channel_id=1, source_target_pairs={{0,224},{32,0},{64,32},{96,64},{128,96},{160,128},{192,160},{224,1... | collective-permute-start | bytes 786440 | tf_op jit(solution)/shard_map/ppermute | solution.py:26
  114.1 3.2 %collective-permute-start.16 = (bf16[256,512]{1,0:T(8,128)(2,1)S(1)}, bf16[256,512]{1,0:T(8,128)(2,1)}, u32[]{:S(2)}, u32[]{:S(2)}) collective-permute-start(bf16[256,512]{1,0:T(8,128)(2,1)S(1)} %collective-permute-done.14.refs_6_), channel_id=1, source_target_pairs={{0,224},{32,0},{64,32},{96,64},{128,96},{160,128},{192,160},{224,1... | collective-permute-start | bytes 786440 | tf_op jit(solution)/shard_map/ppermute | solution.py:26
  117.3 3.9 %collective-permute-done.22.refs_14_ = bf16[256,512]{1,0:T(8,128)(2,1)S(1)} collective-permute-done((bf16[256,512]{1,0:T(8,128)(2,1)S(1)}, bf16[256,512]{1,0:T(8,128)(2,1)S(1)}, u32[]{:S(2)}, u32[]{:S(2)}) %collective-permute-start.22) | collective-permute-done | bytes 262176 | tf_op jit(solution)/shard_map/ppermute | solution.py:26
  121.2 3.3 %collective-permute-start.25 = (bf16[256,512]{1,0:T(8,128)(2,1)S(1)}, bf16[256,512]{1,0:T(8,128)(2,1)}, u32[]{:S(2)}, u32[]{:S(2)}) collective-permute-start(bf16[256,512]{1,0:T(8,128)(2,1)S(1)} %collective-permute-done.23.refs_15_), channel_id=1, source_target_pairs={{0,224},{32,0},{64,32},{96,64},{128,96},{160,128},{192,160},{224,1... | collective-permute-start | bytes 786440 | tf_op jit(solution)/shard_map/ppermute | solution.py:26
  124.4 2.4 %collective-permute-done.15.refs_7_ = bf16[256,512]{1,0:T(8,128)(2,1)} collective-permute-done((bf16[256,512]{1,0:T(8,128)(2,1)S(1)}, bf16[256,512]{1,0:T(8,128)(2,1)}, u32[]{:S(2)}, u32[]{:S(2)}) %collective-permute-start.15) | collective-permute-done | bytes 262176 | tf_op jit(solution)/shard_map/ppermute | solution.py:26
  126.9 3.3 %collective-permute-start.18 = (bf16[256,512]{1,0:T(8,128)(2,1)}, bf16[256,512]{1,0:T(8,128)(2,1)S(1)}, u32[]{:S(2)}, u32[]{:S(2)}) collective-permute-start(bf16[256,512]{1,0:T(8,128)(2,1)} %collective-permute-done.16.refs_8_), channel_id=1, source_target_pairs={{0,224},{32,0},{64,32},{96,64},{128,96},{160,128},{192,160},{224,1... | collective-permute-start | bytes 786440 | tf_op jit(solution)/shard_map/ppermute | solution.py:26
  130.2 2.3 %collective-permute-done.24.refs_16_ = bf16[256,512]{1,0:T(8,128)(2,1)} collective-permute-done((bf16[256,512]{1,0:T(8,128)(2,1)S(1)}, bf16[256,512]{1,0:T(8,128)(2,1)}, u32[]{:S(2)}, u32[]{:S(2)}) %collective-permute-start.24) | collective-permute-done | bytes 262176 | tf_op jit(solution)/shard_map/ppermute | solution.py:26
  132.5 3.3 %collective-permute-start.27 = (bf16[256,512]{1,0:T(8,128)(2,1)}, bf16[256,512]{1,0:T(8,128)(2,1)S(1)}, u32[]{:S(2)}, u32[]{:S(2)}) collective-permute-start(bf16[256,512]{1,0:T(8,128)(2,1)} %collective-permute-done.25.refs_17_), channel_id=1, source_target_pairs={{0,224},{32,0},{64,32},{96,64},{128,96},{160,128},{192,160},{224,1... | collective-permute-start | bytes 786440 | tf_op jit(solution)/shard_map/ppermute | solution.py:26
  138.4 3.3 %collective-permute-start.20 = (bf16[128,512]{1,0:T(8,128)(2,1)S(1)}, bf16[128,512]{1,0:T(8,128)(2,1)S(1)}, u32[]{:S(2)}, u32[]{:S(2)}) collective-permute-start(bf16[128,512]{1,0:T(8,128)(2,1)S(1)} %slice.67), channel_id=1, source_target_pairs={{0,224},{32,0},{64,32},{96,64},{128,96},{160,128},{192,160},{224,1... | collective-permute-start | bytes 393224 | tf_op jit(solution)/shard_map/ppermute | solution.py:26
  141.7 2.0 %collective-permute-done.26.refs_18_ = bf16[256,512]{1,0:T(8,128)(2,1)S(1)} collective-permute-done((bf16[256,512]{1,0:T(8,128)(2,1)}, bf16[256,512]{1,0:T(8,128)(2,1)S(1)}, u32[]{:S(2)}, u32[]{:S(2)}) %collective-permute-start.26) | collective-permute-done | bytes 262176 | tf_op jit(solution)/shard_map/ppermute | solution.py:26
  143.8 3.3 %collective-permute-start.29 = (bf16[128,512]{1,0:T(8,128)(2,1)S(1)}, bf16[128,512]{1,0:T(8,128)(2,1)S(1)}, u32[]{:S(2)}, u32[]{:S(2)}) collective-permute-start(bf16[128,512]{1,0:T(8,128)(2,1)S(1)} %slice.69), channel_id=1, source_target_pairs={{0,224},{32,0},{64,32},{96,64},{128,96},{160,128},{192,160},{224,1... | collective-permute-start | bytes 393224 | tf_op jit(solution)/shard_map/ppermute | solution.py:26
  148.0 1.9 %collective-permute-done.28.refs_20_ = bf16[128,512]{1,0:T(8,128)(2,1)S(1)} collective-permute-done((bf16[128,512]{1,0:T(8,128)(2,1)S(1)}, bf16[128,512]{1,0:T(8,128)(2,1)S(1)}, u32[]{:S(2)}, u32[]{:S(2)}) %collective-permute-start.28) | collective-permute-done | bytes 131104 | tf_op jit(solution)/shard_map/ppermute | solution.py:26
  151.2 8.3 %windows.1 = bf16[4,1056,128]{2,1,0:T(8,128)(2,1)} custom-call(s32[72]{0:T(128)} %reshape.77.ids_ref, s32[3]{0:T(128)} %pad_add_fusion.1.at_ref, bf16[1296,512]{1,0:T(8,128)(2,1)} %copy-done, bf16[1296,512]{1,0:T(8,128)(2,1)} %collective-permute-done.8.refs_5_.refs_2_.refs_1_, bf16[1296,512]{1,0:T(8,128)(2,1)} %copy-done.1, bf16[656,512]{1,0:T(8,128)(2,1)} %copy-done.2, ...), custom_call_target="tpu_custom_call" | custom-call | flops 1000000000 | bytes 8388608 | tf_op jit(solution)/shard_map/windows/pallas_call | solution.py:394
  159.5 18.5 %all_to_all.10.parts_ref = bf16[4,1056,128]{2,1,0:T(8,128)(2,1)S(1)} all-to-all(bf16[4,1056,128]{2,1,0:T(8,128)(2,1)} %windows.1), channel_id=1, replica_groups=mesh['z'=8,'x'=4,'y'=4,'c'=2] {'x'}, dimensions={0} | all-to-all | bytes 2162688 | tf_op jit(solution)/shard_map/all_to_all | solution.py:499
  (122 shorter events, 25.6 us)
Async XLA Ops:
  0.0 26.1 %collective-permute-start.2 = (bf16[256,4096]{1,0:T(8,128)(2,1)}, bf16[256,4096]{1,0:T(8,128)(2,1)}, u32[]{:S(2)}, u32[]{:S(2)}) collective-permute-start(bf16[256,4096]{1,0:T(8,128)(2,1)} %bitcast.28), channel_id=1, source_target_pairs={{0,1},{1,0},{2,3},{3,2},{4,5},{5,4},{6,7},{7,6},{8,9},{9,8},{10,11... | collective-permute-start | bytes 6291464 | tf_op jit(solution)/shard_map/ppermute | solution.py:26
  2.0 38.0 %all-to-all-start = ((bf16[8,128,512]{2,1,0:T(8,128)(2,1)}), bf16[8,128,512]{2,1,0:T(8,128)(2,1)}, u32[]{:S(2)}, u32[]{:S(2)}) async-start(bf16[8,128,512]{2,1,0:T(8,128)(2,1)} %broadcast_in_dim.11), calls=%async_computation | async-start | bytes 2097152 | tf_op jit(solution)/shard_map/all_to_all | solution.py:32
  22.3 3.8 %collective-permute-start.1 = (bf16[256,256]{1,0:T(8,128)(2,1)S(1)}, bf16[256,256]{1,0:T(8,128)(2,1)S(1)}, u32[]{:S(2)}, u32[]{:S(2)}) collective-permute-start(bf16[256,256]{1,0:T(8,128)(2,1)S(1)} %slice_bitcast_fusion), channel_id=1, source_target_pairs={{0,1},{1,0},{2,3},{3,2},{4,5},{5,4},{6,7},{7,6},{8,9},{9,8},{10,11... | collective-permute-start | bytes 393224 | tf_op jit(solution)/shard_map/ppermute | solution.py:26
  22.7 13.2 %collective-permute-start = (s32[1,2]{0,1:T(2,128)S(1)}, s32[1,2]{0,1:T(2,128)S(1)}, u32[]{:S(2)}, u32[]{:S(2)}) collective-permute-start(s32[1,2]{0,1:T(2,128)S(1)} %slice.50), channel_id=1, source_target_pairs={{0,8},{8,16},{16,24},{24,32},{32,40},{40,48},{48,56},{56,64},{64,7... | collective-permute-start | bytes 32 | tf_op jit(solution)/shard_map/ppermute | solution.py:466
  32.4 15.1 %collective-permute-start.3 = (bf16[64,4096]{1,0:T(8,128)(2,1)S(1)}, bf16[64,4096]{1,0:T(8,128)(2,1)S(1)}, u32[]{:S(2)}, u32[]{:S(2)}) collective-permute-start(bf16[64,4096]{1,0:T(8,128)(2,1)S(1)} %get-tuple-element.26), channel_id=1, source_target_pairs={{0,2},{2,4},{4,6},{6,0},{1,3},{3,5},{5,7},{7,1},{8,10},{10,12},{12... | collective-permute-start | bytes 1572872 | tf_op jit(solution)/shard_map/ppermute | solution.py:26
  34.0 13.6 %collective-permute-start.4 = (bf16[64,4096]{1,0:T(8,128)(2,1)S(1)}, bf16[64,4096]{1,0:T(8,128)(2,1)S(1)}, u32[]{:S(2)}, u32[]{:S(2)}) collective-permute-start(bf16[64,4096]{1,0:T(8,128)(2,1)S(1)} %get-tuple-element.27), channel_id=1, source_target_pairs={{0,6},{2,0},{4,2},{6,4},{1,7},{3,1},{5,3},{7,5},{8,14},{10,8},{12,... | collective-permute-start | bytes 1572872 | tf_op jit(solution)/shard_map/ppermute | solution.py:26
  49.3 58.0 %copy-start = (bf16[1296,512]{1,0:T(8,128)(2,1)}, bf16[1296,512]{1,0:T(8,128)(2,1)S(1)}, u32[]{:S(2)}) copy-start(bf16[1296,512]{1,0:T(8,128)(2,1)S(1)} %fusion.1.refs_4_.refs_1_.refs_0_) | copy-start | bytes 3981316
  49.3 32.3 %collective-permute-start.8 = (bf16[1296,512]{1,0:T(8,128)(2,1)S(1)}, bf16[1296,512]{1,0:T(8,128)(2,1)}, u32[]{:S(2)}, u32[]{:S(2)}) collective-permute-start(bf16[1296,512]{1,0:T(8,128)(2,1)S(1)} %fusion.1.refs_4_.refs_1_.refs_0_), channel_id=1, source_target_pairs={{0,8},{8,16},{16,24},{24,0},{1,9},{9,17},{17,25},{25,1},{2,10},{10... | collective-permute-start | bytes 3981320 | tf_op jit(solution)/shard_map/ppermute | solution.py:26
  50.6 31.0 %collective-permute-start.9 = (bf16[1296,512]{1,0:T(8,128)(2,1)S(1)}, bf16[1296,512]{1,0:T(8,128)(2,1)S(1)}, u32[]{:S(2)}, u32[]{:S(2)}) collective-permute-start(bf16[1296,512]{1,0:T(8,128)(2,1)S(1)} %fusion.1.refs_4_.refs_1_.refs_0_), channel_id=1, source_target_pairs={{0,24},{8,0},{16,8},{24,16},{1,25},{9,1},{17,9},{25,17},{2,26},{10... | collective-permute-start | bytes 3981320 | tf_op jit(solution)/shard_map/ppermute | solution.py:26
  51.4 14.1 %collective-permute-start.5 = (bf16[64,4096]{1,0:T(8,128)(2,1)S(1)}, bf16[64,4096]{1,0:T(8,128)(2,1)}, u32[]{:S(2)}, u32[]{:S(2)}) collective-permute-start(bf16[64,4096]{1,0:T(8,128)(2,1)S(1)} %copy-done.10), channel_id=1, source_target_pairs={{0,4},{2,6},{4,0},{6,2},{1,5},{3,7},{5,1},{7,3},{8,12},{10,14},{12... | collective-permute-start | bytes 1572872 | tf_op jit(solution)/shard_map/ppermute | solution.py:26
  68.6 13.0 %collective-permute-start.6 = (bf16[64,4096]{1,0:T(8,128)(2,1)}, bf16[64,4096]{1,0:T(8,128)(2,1)S(1)}, u32[]{:S(2)}, u32[]{:S(2)}) collective-permute-start(bf16[64,4096]{1,0:T(8,128)(2,1)} %normalise.1.refs_0_), channel_id=1, source_target_pairs={{0,2},{2,4},{4,6},{6,0},{1,3},{3,5},{5,7},{7,1},{8,10},{10,12},{12... | collective-permute-start | bytes 1572872 | tf_op jit(solution)/shard_map/ppermute | solution.py:26
  69.6 12.0 %collective-permute-start.7 = (bf16[64,4096]{1,0:T(8,128)(2,1)}, bf16[64,4096]{1,0:T(8,128)(2,1)S(1)}, u32[]{:S(2)}, u32[]{:S(2)}) collective-permute-start(bf16[64,4096]{1,0:T(8,128)(2,1)} %normalise.1.refs_0_), channel_id=1, source_target_pairs={{0,6},{2,0},{4,2},{6,4},{1,7},{3,1},{5,3},{7,5},{8,14},{10,8},{12,... | collective-permute-start | bytes 1572872 | tf_op jit(solution)/shard_map/ppermute | solution.py:26
  81.7 17.9 %collective-permute-start.10 = (bf16[656,512]{1,0:T(8,128)(2,1)S(1)}, bf16[656,512]{1,0:T(8,128)(2,1)S(1)}, u32[]{:S(2)}, u32[]{:S(2)}) collective-permute-start(bf16[656,512]{1,0:T(8,128)(2,1)S(1)} %slice.57), channel_id=1, source_target_pairs={{0,24},{8,0},{16,8},{24,16},{1,25},{9,1},{17,9},{25,17},{2,26},{10... | collective-permute-start | bytes 2015240 | tf_op jit(solution)/shard_map/ppermute | solution.py:26
  85.7 13.9 %collective-permute-start.12 = (bf16[640,512]{1,0:T(8,128)(2,1)S(1)}, bf16[640,512]{1,0:T(8,128)(2,1)S(1)}, u32[]{:S(2)}, u32[]{:S(2)}) collective-permute-start(bf16[640,512]{1,0:T(8,128)(2,1)S(1)} %slice.60), channel_id=1, source_target_pairs={{0,8},{8,16},{16,24},{24,0},{1,9},{9,17},{17,25},{25,1},{2,10},{10... | collective-permute-start | bytes 1966088 | tf_op jit(solution)/shard_map/ppermute | solution.py:26
  85.8 12.7 %collective-permute-start.11 = (bf16[64,4096]{1,0:T(8,128)(2,1)S(1)}, bf16[64,4096]{1,0:T(8,128)(2,1)S(1)}, u32[]{:S(2)}, u32[]{:S(2)}) collective-permute-start(bf16[64,4096]{1,0:T(8,128)(2,1)S(1)} %copy-done.4), channel_id=1, source_target_pairs={{0,4},{2,6},{4,0},{6,2},{1,5},{3,7},{5,1},{7,3},{8,12},{10,14},{12... | collective-permute-start | bytes 1572872 | tf_op jit(solution)/shard_map/ppermute | solution.py:26
  103.0 4.2 %collective-permute-start.21 = (bf16[256,4096]{1,0:T(8,128)(2,1)S(1)}, bf16[256,4096]{1,0:T(8,128)(2,1)S(1)}, u32[]{:S(2)}, u32[]{:S(2)}) collective-permute-start(bf16[256,4096]{1,0:T(8,128)(2,1)S(1)} %get-tuple-element.40), channel_id=1, source_target_pairs={{0,1},{1,0},{2,3},{3,2},{4,5},{5,4},{6,7},{7,6},{8,9},{9,8},{10,11... | collective-permute-start | bytes 6291464 | tf_op jit(solution)/shard_map/ppermute | solution.py:26
  103.1 10.9 %collective-permute-start.13 = (bf16[256,512]{1,0:T(8,128)(2,1)S(1)}, bf16[256,512]{1,0:T(8,128)(2,1)S(1)}, u32[]{:S(2)}, u32[]{:S(2)}) collective-permute-start(bf16[256,512]{1,0:T(8,128)(2,1)S(1)} %get-tuple-element.39.refs_4_), channel_id=1, source_target_pairs={{0,32},{32,64},{64,96},{96,128},{128,160},{160,192},{192,224},{224... | collective-permute-start | bytes 786440 | tf_op jit(solution)/shard_map/ppermute | solution.py:26
  104.4 9.6 %collective-permute-start.14 = (bf16[256,512]{1,0:T(8,128)(2,1)S(1)}, bf16[256,512]{1,0:T(8,128)(2,1)S(1)}, u32[]{:S(2)}, u32[]{:S(2)}) collective-permute-start(bf16[256,512]{1,0:T(8,128)(2,1)S(1)} %get-tuple-element.39.refs_4_), channel_id=1, source_target_pairs={{0,224},{32,0},{64,32},{96,64},{128,96},{160,128},{192,160},{224,1... | collective-permute-start | bytes 786440 | tf_op jit(solution)/shard_map/ppermute | solution.py:26
  110.7 10.4 %collective-permute-start.22 = (bf16[256,512]{1,0:T(8,128)(2,1)S(1)}, bf16[256,512]{1,0:T(8,128)(2,1)S(1)}, u32[]{:S(2)}, u32[]{:S(2)}) collective-permute-start(bf16[256,512]{1,0:T(8,128)(2,1)S(1)} %memorise.3.refs_13_), channel_id=1, source_target_pairs={{0,32},{32,64},{64,96},{96,128},{128,160},{160,192},{192,224},{224... | collective-permute-start | bytes 786440 | tf_op jit(solution)/shard_map/ppermute | solution.py:26
  112.0 9.2 %collective-permute-start.23 = (bf16[256,512]{1,0:T(8,128)(2,1)S(1)}, bf16[256,512]{1,0:T(8,128)(2,1)S(1)}, u32[]{:S(2)}, u32[]{:S(2)}) collective-permute-start(bf16[256,512]{1,0:T(8,128)(2,1)S(1)} %memorise.3.refs_13_), channel_id=1, source_target_pairs={{0,224},{32,0},{64,32},{96,64},{128,96},{160,128},{192,160},{224,1... | collective-permute-start | bytes 786440 | tf_op jit(solution)/shard_map/ppermute | solution.py:26
  114.0 12.8 %collective-permute-start.15 = (bf16[256,512]{1,0:T(8,128)(2,1)S(1)}, bf16[256,512]{1,0:T(8,128)(2,1)}, u32[]{:S(2)}, u32[]{:S(2)}) collective-permute-start(bf16[256,512]{1,0:T(8,128)(2,1)S(1)} %collective-permute-done.13.refs_5_), channel_id=1, source_target_pairs={{0,32},{32,64},{64,96},{96,128},{128,160},{160,192},{192,224},{224... | collective-permute-start | bytes 786440 | tf_op jit(solution)/shard_map/ppermute | solution.py:26
  114.1 12.8 %collective-permute-start.16 = (bf16[256,512]{1,0:T(8,128)(2,1)S(1)}, bf16[256,512]{1,0:T(8,128)(2,1)}, u32[]{:S(2)}, u32[]{:S(2)}) collective-permute-start(bf16[256,512]{1,0:T(8,128)(2,1)S(1)} %collective-permute-done.14.refs_6_), channel_id=1, source_target_pairs={{0,224},{32,0},{64,32},{96,64},{128,96},{160,128},{192,160},{224,1... | collective-permute-start | bytes 786440 | tf_op jit(solution)/shard_map/ppermute | solution.py:26
  121.2 11.3 %collective-permute-start.24 = (bf16[256,512]{1,0:T(8,128)(2,1)S(1)}, bf16[256,512]{1,0:T(8,128)(2,1)}, u32[]{:S(2)}, u32[]{:S(2)}) collective-permute-start(bf16[256,512]{1,0:T(8,128)(2,1)S(1)} %collective-permute-done.22.refs_14_), channel_id=1, source_target_pairs={{0,32},{32,64},{64,96},{96,128},{128,160},{160,192},{192,224},{224... | collective-permute-start | bytes 786440 | tf_op jit(solution)/shard_map/ppermute | solution.py:26
  121.2 11.3 %collective-permute-start.25 = (bf16[256,512]{1,0:T(8,128)(2,1)S(1)}, bf16[256,512]{1,0:T(8,128)(2,1)}, u32[]{:S(2)}, u32[]{:S(2)}) collective-permute-start(bf16[256,512]{1,0:T(8,128)(2,1)S(1)} %collective-permute-done.23.refs_15_), channel_id=1, source_target_pairs={{0,224},{32,0},{64,32},{96,64},{128,96},{160,128},{192,160},{224,1... | collective-permute-start | bytes 786440 | tf_op jit(solution)/shard_map/ppermute | solution.py:26
  126.9 11.1 %collective-permute-start.17 = (bf16[256,512]{1,0:T(8,128)(2,1)}, bf16[256,512]{1,0:T(8,128)(2,1)S(1)}, u32[]{:S(2)}, u32[]{:S(2)}) collective-permute-start(bf16[256,512]{1,0:T(8,128)(2,1)} %collective-permute-done.15.refs_7_), channel_id=1, source_target_pairs={{0,32},{32,64},{64,96},{96,128},{128,160},{160,192},{192,224},{224... | collective-permute-start | bytes 786440 | tf_op jit(solution)/shard_map/ppermute | solution.py:26
  126.9 11.4 %collective-permute-start.18 = (bf16[256,512]{1,0:T(8,128)(2,1)}, bf16[256,512]{1,0:T(8,128)(2,1)S(1)}, u32[]{:S(2)}, u32[]{:S(2)}) collective-permute-start(bf16[256,512]{1,0:T(8,128)(2,1)} %collective-permute-done.16.refs_8_), channel_id=1, source_target_pairs={{0,224},{32,0},{64,32},{96,64},{128,96},{160,128},{192,160},{224,1... | collective-permute-start | bytes 786440 | tf_op jit(solution)/shard_map/ppermute | solution.py:26
  132.5 11.1 %collective-permute-start.26 = (bf16[256,512]{1,0:T(8,128)(2,1)}, bf16[256,512]{1,0:T(8,128)(2,1)S(1)}, u32[]{:S(2)}, u32[]{:S(2)}) collective-permute-start(bf16[256,512]{1,0:T(8,128)(2,1)} %collective-permute-done.24.refs_16_), channel_id=1, source_target_pairs={{0,32},{32,64},{64,96},{96,128},{128,160},{160,192},{192,224},{224... | collective-permute-start | bytes 786440 | tf_op jit(solution)/shard_map/ppermute | solution.py:26
  132.5 11.2 %collective-permute-start.27 = (bf16[256,512]{1,0:T(8,128)(2,1)}, bf16[256,512]{1,0:T(8,128)(2,1)S(1)}, u32[]{:S(2)}, u32[]{:S(2)}) collective-permute-start(bf16[256,512]{1,0:T(8,128)(2,1)} %collective-permute-done.25.refs_17_), channel_id=1, source_target_pairs={{0,224},{32,0},{64,32},{96,64},{128,96},{160,128},{192,160},{224,1... | collective-permute-start | bytes 786440 | tf_op jit(solution)/shard_map/ppermute | solution.py:26
  138.0 10.0 %collective-permute-start.19 = (bf16[128,512]{1,0:T(8,128)(2,1)S(1)}, bf16[128,512]{1,0:T(8,128)(2,1)S(1)}, u32[]{:S(2)}, u32[]{:S(2)}) collective-permute-start(bf16[128,512]{1,0:T(8,128)(2,1)S(1)} %slice.66), channel_id=1, source_target_pairs={{0,32},{32,64},{64,96},{96,128},{128,160},{160,192},{192,224},{224... | collective-permute-start | bytes 393224 | tf_op jit(solution)/shard_map/ppermute | solution.py:26
  138.4 9.7 %collective-permute-start.20 = (bf16[128,512]{1,0:T(8,128)(2,1)S(1)}, bf16[128,512]{1,0:T(8,128)(2,1)S(1)}, u32[]{:S(2)}, u32[]{:S(2)}) collective-permute-start(bf16[128,512]{1,0:T(8,128)(2,1)S(1)} %slice.67), channel_id=1, source_target_pairs={{0,224},{32,0},{64,32},{96,64},{128,96},{160,128},{192,160},{224,1... | collective-permute-start | bytes 393224 | tf_op jit(solution)/shard_map/ppermute | solution.py:26
  143.6 6.3 %collective-permute-start.28 = (bf16[128,512]{1,0:T(8,128)(2,1)S(1)}, bf16[128,512]{1,0:T(8,128)(2,1)S(1)}, u32[]{:S(2)}, u32[]{:S(2)}) collective-permute-start(bf16[128,512]{1,0:T(8,128)(2,1)S(1)} %slice.68), channel_id=1, source_target_pairs={{0,32},{32,64},{64,96},{96,128},{128,160},{160,192},{192,224},{224... | collective-permute-start | bytes 393224 | tf_op jit(solution)/shard_map/ppermute | solution.py:26
  143.8 6.1 %collective-permute-start.29 = (bf16[128,512]{1,0:T(8,128)(2,1)S(1)}, bf16[128,512]{1,0:T(8,128)(2,1)S(1)}, u32[]{:S(2)}, u32[]{:S(2)}) collective-permute-start(bf16[128,512]{1,0:T(8,128)(2,1)S(1)} %slice.69), channel_id=1, source_target_pairs={{0,224},{32,0},{64,32},{96,64},{128,96},{160,128},{192,160},{224,1... | collective-permute-start | bytes 393224 | tf_op jit(solution)/shard_map/ppermute | solution.py:26
  (26 other events, 340.9 us)

commit v5 on v4

--- a/solution.py
+++ b/solution.py
@@ -32,7 +32,7 @@
     return lax.all_to_all(copies, axis, split_axis=0, concat_axis=0, tiled=True)
 
 
-def encoder_kernel(at_ref, x_ref, w_ref, g_ref, out_ref, wide, wmat, acc, ssq):
+def encoder_kernel(core_ref, y_ref, x_ref, w_ref, g_ref, own_ref, send_ref, wide, wmat, acc, ssq):
     step = pl.program_id(0)
     depth = x_ref.shape[1]
 
@@ -51,7 +51,8 @@
 
     @pl.when(step == pl.num_programs(0) - 1)
     def _():
-        core, my_y = at_ref[0], at_ref[1]
+        core, my_y = core_ref[0], y_ref[0]
+        done = []
         total = depth * pl.num_programs(0)
         scale = lax.rsqrt(ssq[...] / total + EPS)
         rows = x_ref.shape[0] // ROW
@@ -75,29 +76,32 @@
                 (jnp.dot(p.astype(BF), part(r, 4 + h), preferred_element_type=F32) * (1.0 / total_p)).astype(BF)
                 for (r, h), p, total_p in zip(spots, probs, sums)
             ]
-            side = lax.rem(pair + core, 2)
-            for i in range(2):
-                att = jnp.concatenate(atts[2 * i:2 * i + 2], axis=1)
-                for half in range(2):
-                    k = lax.rem(2 * i + half - my_y + NY, NY)
-                    out_ref[side, pl.ds(pl.multiple_of(k * 64, 64), 64), :] = att[half * 64:(half + 1) * 64]
-
-
-def encode(corpus_flat, w_rows, gain, at):
+            done.append([jnp.concatenate(atts[2 * i:2 * i + 2], axis=1) for i in range(2)])
+        for i in range(2):
+            own = jnp.where(core == 0, done[0][i], done[1][i])
+            send = jnp.where(core == 0, done[1][i], done[0][i])
+            for half in range(2):
+                k = jnp.bitwise_and(2 * i + half - my_y, NY - 1)
+                spot = pl.ds(pl.multiple_of(k * 64, 64), 64)
+                own_ref[spot, :] = own[half * 64:(half + 1) * 64]
+                send_ref[spot, :] = send[half * 64:(half + 1) * 64]
+
+
+def encode(corpus_flat, w_rows, gain, core, my_y):
     tokens, width = corpus_flat.shape
     steps = 4
     depth = width // steps
     return pl.pallas_call(
         encoder_kernel,
         grid_spec=pltpu.PrefetchScalarGridSpec(
-            num_scalar_prefetch=1,
+            num_scalar_prefetch=2,
             grid=(steps,),
             in_specs=[
-                pl.BlockSpec((tokens, depth), lambda i, c: (0, i)),
-                pl.BlockSpec((depth * 6, HS), lambda i, c: (i, 0)),
-                pl.BlockSpec((1, depth), lambda i, c: (0, i)),
+                pl.BlockSpec((tokens, depth), lambda i, c, y: (0, i)),
+                pl.BlockSpec((depth * 6, HS), lambda i, c, y: (i, 0)),
+                pl.BlockSpec((1, depth), lambda i, c, y: (0, i)),
             ],
-            out_specs=pl.BlockSpec((2, 2 * ROW, 2 * HS), lambda i, c: (0, 0, 0)),
+            out_specs=[pl.BlockSpec((2 * ROW, 2 * HS), lambda i, c, y: (0, 0))] * 2,
             scratch_shapes=[
                 pltpu.VMEM((depth * 6, HS), F32),
                 pltpu.VMEM((depth, 6 * HS), BF),
@@ -105,18 +109,18 @@
                 pltpu.VMEM((tokens, 1), F32),
             ],
         ),
-        out_shape=jax.ShapeDtypeStruct((2, 2 * ROW, 2 * HS), BF),
+        out_shape=[jax.ShapeDtypeStruct((2 * ROW, 2 * HS), BF)] * 2,
         cost_estimate=pl.CostEstimate(
             flops=2 * tokens * width * 6 * HS, bytes_accessed=(tokens + 768) * width * 2, transcendentals=0
         ),
         compiler_params=pltpu.CompilerParams(vmem_limit_bytes=60 * MIB),
         name="encoder",
-    )(at, corpus_flat, w_rows, gain)
+    )(core, my_y, corpus_flat, w_rows, gain)
 
 
 def project_kernel(a_ref, b_ref, ea_ref, eb_ref, *outs):
-    rows = a_ref.shape[1] // NY
-    value = jnp.dot(a_ref[0], ea_ref[...], preferred_element_type=F32)
+    rows = a_ref.shape[0] // NY
+    value = jnp.dot(a_ref[...], ea_ref[...], preferred_element_type=F32)
     value += jnp.dot(b_ref[...], eb_ref[...], preferred_element_type=F32)
     for k in range(NY):
         outs[k][...] = value[k * rows:(k + 1) * rows].astype(BF)
@@ -131,7 +135,7 @@
         project_kernel,
         grid=(width // cols,),
         in_specs=[
-            pl.BlockSpec((1, tokens, depth), lambda i: (0, 0, 0)),
+            pl.BlockSpec((tokens, depth), lambda i: (0, 0)),
             pl.BlockSpec((tokens, depth), lambda i: (0, 0)),
             pl.BlockSpec((depth, cols), lambda i: (0, i)),
             pl.BlockSpec((depth, cols), lambda i: (0, i)),
@@ -141,7 +145,7 @@
         cost_estimate=pl.CostEstimate(
             flops=4 * tokens * depth * width, bytes_accessed=4 * depth * width, transcendentals=0
         ),
-        compiler_params=pltpu.CompilerParams(vmem_limit_bytes=12 * MIB),
+        compiler_params=pltpu.CompilerParams(vmem_limit_bytes=60 * MIB),
         name="project",
     )(att, att_other, e_own, e_other)
 
@@ -267,23 +271,70 @@
 
 
 PAD = 8
-Q_FIRST = NZ * HS
-PAYLOAD_TOP = 640
-
-
-def window_kernel(layout, ids_ref, at_ref, *refs):
-    payloads = refs[:NX]
-    pieces = refs[NX:NX + len(layout)]
-    out_ref = refs[NX + len(layout)]
-    table, q_in, qs, outs, stats, one_list, two_list, sem, q_sem = refs[NX + len(layout) + 1:]
-    q_first = (Q_FIRST, Q_FIRST, Q_FIRST, Q_FIRST - PAYLOAD_TOP)
-    my_z, my_x, core = at_ref[0], at_ref[1], at_ref[2]
-    count_all = NX * 8 + 1
+
+
+def plan_kernel(ids_ref, z_ref, x_ref, core_ref, one_list, two_list, counts_ref):
+    my_z, my_x, core = z_ref[0], x_ref[0], core_ref[0]
+
+    def held(row):
+        return jnp.logical_and(row >= 0, jnp.bitwise_and(jnp.right_shift(row, 2), NX - 1) == my_x)
+
+    def wanted(w, n):
+        group = jnp.maximum(w - 1, 0)
+        step = jnp.bitwise_and(jnp.right_shift(group, 3) - my_x, NX - 1)
+        here = step * 16 + jnp.bitwise_and(group, 7) * 2
+        under = NX * 16 + jnp.bitwise_and(NX - 1 - my_x, NX - 1) * 16 + 14
+        row = ids_ref[jnp.where(w == 0, under, here) + n]
+        return jnp.where(jnp.logical_and(w == 0, my_z == 0), -1, row)
+
+    def place(row):
+        distance = jnp.bitwise_and(my_z - jnp.right_shift(row, 4), NZ - 1)
+        local = jnp.bitwise_and(row, 3)
+        half = jnp.bitwise_and(jnp.right_shift(local, 1) + core, 1)
+        return distance * 512 + half * 256 + jnp.bitwise_and(local, 1) * 128
+
+    def note(w, counts):
+        ones, twos = counts
+        rows = [wanted(w, n) for n in range(2)]
+        ok = [held(row).astype(jnp.int32) for row in rows]
+        single, both = ok[0] + ok[1] == 1, ok[0] + ok[1] == 2
+        spot = place(jnp.maximum(jnp.where(ok[0] == 1, rows[0], rows[1]), 0))
+        one_list[2 * ones] = w
+        one_list[2 * ones + 1] = spot
+        two_list[3 * twos] = w
+        two_list[3 * twos + 1] = spot
+        two_list[3 * twos + 2] = place(jnp.maximum(rows[1], 0))
+        return ones + single.astype(jnp.int32), twos + both.astype(jnp.int32)
+
+    ones, twos = lax.fori_loop(0, NX * 8 + 1, note, (0, 0))
+    counts_ref[0] = ones
+    counts_ref[1] = twos
+
+
+def plan(ids, my_z, my_x, core):
+    smem = pl.BlockSpec(memory_space=pltpu.SMEM)
+    return pl.pallas_call(
+        plan_kernel,
+        in_specs=[smem] * 4,
+        out_specs=[smem] * 3,
+        out_shape=[
+            jax.ShapeDtypeStruct((128,), jnp.int32),
+            jax.ShapeDtypeStruct((128,), jnp.int32),
+            jax.ShapeDtypeStruct((2,), jnp.int32),
+        ],
+        name="plan",
+    )(ids, my_z, my_x, core)
+
+
+def window_kernel(layout, one_list, two_list, counts_ref, x_ref, *refs):
+    q_refs, refs = refs[:NX], refs[NX:]
+    pieces = refs[:len(layout)]
+    out_ref = refs[len(layout)]
+    table, q_in, qs, outs, stats, sem, q_sem = refs[len(layout) + 1:]
+    ones, twos = counts_ref[0], counts_ref[1]
     plane_rows = NX * 1024
     total_rows = qs.shape[0]
-    q_copies = [
-        pltpu.make_async_copy(payloads[i].at[pl.ds(q_first[i], 256)], q_in.at[i], q_sem.at[i]) for i in range(NX)
-    ]
+    q_copies = [pltpu.make_async_copy(q_refs[d].at[pl.ds(0, 1024)], q_in.at[d], q_sem.at[d]) for d in range(NX)]
     copies = [
         pltpu.make_async_copy(pieces[i], table.at[pl.ds(distance * 512 + first, rows)], sem.at[i])
         for i, (distance, first, rows) in enumerate(layout)
@@ -294,40 +345,10 @@
     stats[...] = jnp.full_like(stats, MASKED)
     qs[0:PAD, :] = jnp.zeros((PAD, HS), F32)
     qs[PAD + plane_rows:, :] = jnp.zeros((total_rows - PAD - plane_rows, HS), F32)
-    for i in range(NX):
-        base = PAD + lax.rem(my_x + ORDER[i], NX) * 1024
-        q_copies[i].wait()
-        for b in range(4):
-            first = pl.multiple_of(base + b * 256, 8)
-            qs[pl.ds(first, 256), :] = q_in[i, :, b * HS:(b + 1) * HS].astype(F32)
-    def held(row):
-        return jnp.logical_and(row >= 0, jnp.bitwise_and(jnp.right_shift(row, 2), NX - 1) == my_x)
-
-    def wanted(w, n):
-        group = jnp.maximum(w - 1, 0)
-        step = jnp.bitwise_and(jnp.right_shift(group, 3) - my_x, NX - 1)
-        return ids_ref[step * 18 + jnp.where(w == 0, 0, jnp.bitwise_and(group, 7) + 1) * 2 + n]
-
-    def place(row):
-        distance = jnp.bitwise_and(my_z - jnp.right_shift(row, 4), NZ - 1)
-        local = jnp.bitwise_and(row, 3)
-        half = jnp.bitwise_and(jnp.right_shift(local, 1) + core, 1)
-        return distance * 512 + half * 256 + jnp.bitwise_and(local, 1) * 128
-
-    def note(w, counts):
-        ones, twos = counts
-        rows = [wanted(w, n) for n in range(2)]
-        ok = [held(row).astype(jnp.int32) for row in rows]
-        single, both = ok[0] + ok[1] == 1, ok[0] + ok[1] == 2
-        spot = place(jnp.where(ok[0] == 1, rows[0], rows[1]))
-        one_list[2 * ones] = w
-        one_list[2 * ones + 1] = spot
-        two_list[3 * twos] = w
-        two_list[3 * twos + 1] = spot
-        two_list[3 * twos + 2] = place(jnp.maximum(rows[1], 0))
-        return ones + single.astype(jnp.int32), twos + both.astype(jnp.int32)
-
-    ones, twos = lax.fori_loop(0, count_all, note, (0, 0))
+    for d in range(NX):
+        q_copies[d].wait()
+        first = pl.multiple_of(PAD + jnp.bitwise_and(x_ref[0] + d, NX - 1) * 1024, 8)
+        qs[pl.ds(first, 1024), :] = q_in[d].astype(F32)
     for copy in copies:
         copy.wait()
 
@@ -387,22 +408,20 @@
         out_ref[x, 1024:1056] = tail.astype(BF)
 
 
-def windows(ids, at, payloads, pieces):
+def windows(lists, my_x, queries, pieces):
     layout = tuple((d, first, rows) for d, first, rows, _ in pieces)
     total = PAD + NX * 1024 + 2 * GROUP
     smem = pl.BlockSpec(memory_space=pltpu.SMEM)
     return pl.pallas_call(
         functools.partial(window_kernel, layout),
-        in_specs=[smem, smem] + [ANY] * (NX + len(pieces)),
+        in_specs=[smem] * 4 + [ANY] * (NX + len(pieces)),
         out_specs=VMEM_ALL,
         scratch_shapes=[
             pltpu.VMEM((NZ * 4 * ROW, 512), BF),
-            pltpu.VMEM((NX, 256, 512), BF),
+            pltpu.VMEM((NX, 1024, HS), BF),
             pltpu.VMEM((total, HS), F32),
             pltpu.VMEM((total, HS), F32),
             pltpu.VMEM((total, HS), F32),
-            pltpu.SMEM((128,), jnp.int32),
-            pltpu.SMEM((128,), jnp.int32),
             pltpu.SemaphoreType.DMA((len(pieces),)),
             pltpu.SemaphoreType.DMA((NX,)),
         ],
@@ -410,7 +429,7 @@
         cost_estimate=pl.CostEstimate(flops=10**9, bytes_accessed=8 * 2**20, transcendentals=10**6),
         compiler_params=pltpu.CompilerParams(vmem_limit_bytes=58 * MIB),
         name="windows",
-    )(ids, at, *payloads, *[piece[-1] for piece in pieces])
+    )(*lists, my_x, *queries, *[piece[-1] for piece in pieces])
 
 
 def combine_kernel(parts_ref, out_ref):
@@ -459,43 +478,41 @@
     kv = spread(kv, "z").reshape(-1, 512)
 
     w_rows = enc_qkv.transpose(0, 2, 1, 3).reshape(width * 6, HS)
-    att = encode(corpus_flat, w_rows, gain_in.reshape(1, width), as_index(core, my_y))
-    nbr_ids, queries, att = lax.optimization_barrier((nbr_ids, queries, att))
-    att_other = shifted(att[1], "c", 1)
-
-    last = lax.ppermute(nbr_ids[7:], ("z", "x"), [(i, i + 1) for i in range(NZ * NX - 1)])
-    last = jnp.where(jnp.logical_and(my_z == 0, my_x == 0), -1, last)
-    ids = jnp.concatenate([last, nbr_ids], axis=0).astype(BF)
-    terms = project(att, att_other, e_own, e_other)
+    att_own, att_send = encode(corpus_flat, w_rows, gain_in.reshape(1, width), as_index(core), as_index(my_y))
+    nbr_ids, queries, att_send = lax.optimization_barrier((nbr_ids, queries, att_send))
+    att_other = shifted(att_send, "c", 1)
+
+    id_rows = jnp.pad(nbr_ids.astype(BF), ((0, 8), (0, HS - 2)))
+    q_rows = jnp.concatenate([queries.reshape(1024, HS), id_rows], axis=0)
+    qs = [q_rows] + [shifted(q_rows, "x", -d) for d in range(1, NX)]
+    terms = project(att_own, att_other, e_own, e_other)
 
     terms = [terms[0]] + [shifted(terms[k], "y", k) for k in range(1, NY)]
-    kv, terms[1], terms[3] = lax.optimization_barrier((kv, terms[1], terms[3]))
-    q_rows = queries.reshape(4, 256, HS)
-    q_wide = jnp.concatenate([q_rows[b] for b in range(4)], axis=1)
-    payload = jnp.concatenate([kv, q_wide, jnp.pad(ids, ((0, 7), (0, 510)))], axis=0)
-    from_left = shifted(payload, "x", 1)
-    from_right = shifted(payload, "x", -1)
+    kv, terms[1], terms[3], qs = lax.optimization_barrier((kv, terms[1], terms[3], qs))
+    got = jnp.stack([q[1024:1032, 0:2] for q in qs]).astype(jnp.int32).reshape(-1)
+    below = shifted(got, "z", 1)
+    from_left = shifted(kv, "x", 1)
+    from_right = shifted(kv, "x", -1)
 
     u = normalise(terms, corpus_flat, gain_out.reshape(1, width), as_index(core * NY + my_y))
     us = [u] + [shifted(u, "y", k) for k in range(1, NY)]
-    us[1], us[3], from_left, from_right = lax.optimization_barrier((us[1], us[3], from_left, from_right))
-    far_top = shifted(from_left[:PAYLOAD_TOP], "x", 1)
-    far_bottom = shifted(from_right[PAYLOAD_TOP:], "x", -1)
-    payloads = [payload, from_left, from_right, far_top, far_bottom]
+    us[1], us[3], from_left, from_right, below = lax.optimization_barrier(
+        (us[1], us[3], from_left, from_right, below)
+    )
+    ids = jnp.concatenate([got, below])
+    half = kv.shape[0] // 2
+    far_top = shifted(from_left[:half], "x", 1)
+    far_bottom = shifted(from_right[half:], "x", -1)
+    weights = [kv, from_left, from_right, far_top, far_bottom]
     at = as_index(my_x, my_y)
-    memory_own, u_own = memorise(at, us, payloads)
+    memory_own, u_own = memorise(at, us, weights)
     u_other = shifted(u_own, "c", 1)
     pieces = ring_pieces(memory_own, 0)
-    (memory_other,) = memorise(at, [u_other], payloads)
+    (memory_other,) = memorise(at, [u_other], weights)
     pieces += ring_pieces(memory_other, 2 * ROW)
 
-    ids_first = Q_FIRST + 256
-    near = [p[ids_first:ids_first + 9, 0:2] for p in payloads[:3]]
-    far = far_bottom[ids_first - PAYLOAD_TOP:ids_first - PAYLOAD_TOP + 9, 0:2]
-    got = jnp.stack([near[0], near[2], far, near[1]]).astype(jnp.int32)
-    got, at = lax.optimization_barrier((got.reshape(-1), as_index(my_z, my_x, core)))
-    payloads = payloads[:3] + [far_bottom]
-    parts = windows(got, at, payloads, pieces)
+    lists = plan(ids, as_index(my_z), as_index(my_x), as_index(core))
+    parts = windows(lists, as_index(my_x), qs, pieces)
     parts = lax.all_to_all(parts, "x", split_axis=0, concat_axis=0, tiled=True)
     return combine(parts).reshape(512, 2, HS)
 

time: 181 us -> 182 us (level)
  other arithmetic: 3.25 us -> 0.77 us
    ppermute x29 -> x33, starting transfers between devices: 43.6 us -> 48.1 us  [shifted(): return lax.ppermute(value, axis, [(i, (i + steps) % n) for i in range(n)])]
    all_to_all x1, waiting for transfers between devices: 3.88 us -> 0.01 us  [spread(): return lax.all_to_all(copies, axis, split_axis=0, concat_axis=0, tiled=True)]
    ppermute x29 -> x33, waiting for transfers between devices: 54 us -> 57.7 us  [shifted(): return lax.ppermute(value, axis, [(i, (i + steps) % n) for i in range(n)])]
    ppermute x1 -> x0, starting transfers between devices: 3.39 us -> none  [on_device(): lax.ppermute(nbr_ids[7:], ('z', 'x'), [(i, i + 1) for i in range(NZ * NX...]
    pallas_call x1 -> x2, Pallas kernels: 8.27 us -> 9.6 us  [the longest x1 7.48 us: windows(): pl.pallas_call(functools.partial(window_kernel, layout), in_specs=[smem]...]
    unnamed x54 -> x58, local copies, waits for them, and re-layouts: 3.86 us -> 3.93 us
  transfers between devices with their start and end apart: 31 -> 34, of which waited for: 13 -> 15; matrix products, arithmetic and copies ran while one was open for 4% -> 5% of each run, Pallas kernels for 11% -> 12%
where the time goes in v5:
time: 182 us; the launch traced here: 181 us
  waiting for transfers between devices  57.7 us (32%)
  starting transfers between devices  56.5 us (31%)
  Pallas kernels  34.8 us (19%)
  blocking collectives  19 us (10%)
  local copies, waits for them, and re-layouts  11.8 us (6%)
    ppermute x33, waiting for transfers between devices, shifted(): return lax.ppermute(value, axis, [(i, (i + steps) % n) for i in range(n)])  57.7 us
    ppermute x33, starting transfers between devices, shifted(): return lax.ppermute(value, axis, [(i, (i + steps) % n) for i in range(n)])  48.1 us
    all_to_all x1, blocking collectives, on_device(): parts = lax.all_to_all(parts, 'x', split_axis=0, concat_axis=0, tiled=True)  19 us
    pallas_call x1, Pallas kernels, encode(): pl.pallas_call(encoder_kernel, grid_spec=pltpu.PrefetchScalarGridSpec(num...  9.48 us
    all_to_all x1, starting transfers between devices, spread(): return lax.all_to_all(copies, axis, split_axis=0, concat_axis=0, tiled=True)  8.47 us
    pallas_call x1, Pallas kernels, windows(): pl.pallas_call(functools.partial(window_kernel, layout), in_specs=[smem]...  7.48 us
    pallas_call x2, Pallas kernels, memorise(): pl.pallas_call(functools.partial(memory_kernel, len(us)), in_specs=[pl.Bl...  6.24 us
    pallas_call x1, Pallas kernels, project(): pl.pallas_call(project_kernel, grid=(width // cols,), in_specs=[pl.BlockS...  5 us
  transfers between devices with their start and end apart: 34, of which 15 were waited for; matrix products, arithmetic and copies ran while one was open for 5% of the time, Pallas kernels for 12%

profile of v5, /device:TPU:2, one launch (start us, length us, event | category | flops | bytes accessed | tf_op | source)
XLA Modules:
  0.0 181.2 jit_solution(12088862383672051773)
XLA Ops:
  2.0 8.5 %all-to-all-start = ((bf16[8,128,512]{2,1,0:T(8,128)(2,1)}), bf16[8,128,512]{2,1,0:T(8,128)(2,1)S(1)}, u32[]{:S(2)}, u32[]{:S(2)}) async-start(bf16[8,128,512]{2,1,0:T(8,128)(2,1)} %broadcast_in_dim.2), calls=%async_computation | async-start | bytes 2097152 | tf_op jit(solution)/shard_map/all_to_all | solution.py:32
  10.5 9.5 %encoder.1 = (bf16[256,256]{1,0:T(8,128)(2,1)}, bf16[256,256]{1,0:T(8,128)(2,1)}) custom-call(s32[1]{0:T(128)} %bitcast.1.core_ref, s32[1]{0:T(128)} %bitcast.2.y_ref, bf16[512,4096]{1,0:T(8,128)(2,1)} %bitcast.27, bf16[24576,128]{1,0:T(8,128)(2,1)} %bitcast.33, f32[1,4096]{1,0:T(1,128)} %bitcast.34), custom_call_target="tpu_custom_call" | custom-call | flops 3221225472 | bytes 10485760 | tf_op jit(solution)/shard_map/encoder/pallas_call | solution.py:94
  22.9 5.0 %project.1 = (bf16[64,4096]{1,0:T(8,128)(2,1)}, bf16[64,4096]{1,0:T(8,128)(2,1)}, bf16[64,4096]{1,0:T(8,128)(2,1)}, bf16[64,4096]{1,0:T(8,128)(2,1)}) custom-call(bf16[256,256]{1,0:T(8,128)(2,1)} %get-tuple-element.31.a_ref, bf16[256,256]{1,0:T(8,128)(2,1)} %copy-done.27, bf16[256,4096]{1,0:T(8,128)(2,1)} %bitcast.30, bf16[256,4096]{1,0:T(8,128)(2,1)} %copy-done.3), custom_call_target="tpu_custom_call" | custom-call | flops 1073741824 | bytes 4194304 | tf_op jit(solution)/shard_map/project/pallas_call | solution.py:134
  31.8 2.4 %collective-permute-start.5 = (bf16[1040,128]{1,0:T(8,128)(2,1)S(1)}, bf16[1040,128]{1,0:T(8,128)(2,1)S(1)}, u32[]{:S(2)}, u32[]{:S(2)}) collective-permute-start(bf16[1040,128]{1,0:T(8,128)(2,1)S(1)} %fusion.1.refs_0_), channel_id=1, source_target_pairs={{0,16},{8,24},{16,0},{24,8},{1,17},{9,25},{17,1},{25,9},{2,18},{10... | collective-permute-start | bytes 798728 | tf_op jit(solution)/shard_map/ppermute | solution.py:26
  36.1 3.6 %collective-permute-done.4.refs_1_ = bf16[1040,128]{1,0:T(8,128)(2,1)S(1)} collective-permute-done((bf16[1040,128]{1,0:T(8,128)(2,1)S(1)}, bf16[1040,128]{1,0:T(8,128)(2,1)S(1)}, u32[]{:S(2)}, u32[]{:S(2)}) %collective-permute-start.4) | collective-permute-done | bytes 266272 | tf_op jit(solution)/shard_map/ppermute | solution.py:26
  39.7 2.0 %collective-permute-start.7 = (bf16[64,4096]{1,0:T(8,128)(2,1)}, bf16[64,4096]{1,0:T(8,128)(2,1)}, u32[]{:S(2)}, u32[]{:S(2)}) collective-permute-start(bf16[64,4096]{1,0:T(8,128)(2,1)} %get-tuple-element.44), channel_id=1, source_target_pairs={{0,4},{2,6},{4,0},{6,2},{1,5},{3,7},{5,1},{7,3},{8,12},{10,14},{12... | collective-permute-start | bytes 1572872 | tf_op jit(solution)/shard_map/ppermute | solution.py:26
  41.7 4.4 %collective-permute-done.5.refs_2_ = bf16[1040,128]{1,0:T(8,128)(2,1)S(1)} collective-permute-done((bf16[1040,128]{1,0:T(8,128)(2,1)S(1)}, bf16[1040,128]{1,0:T(8,128)(2,1)S(1)}, u32[]{:S(2)}, u32[]{:S(2)}) %collective-permute-start.5) | collective-permute-done | bytes 266272 | tf_op jit(solution)/shard_map/ppermute | solution.py:26
  47.0 7.2 %collective-permute-done.3.t3 = bf16[64,4096]{1,0:T(8,128)(2,1)S(1)} collective-permute-done((bf16[64,4096]{1,0:T(8,128)(2,1)}, bf16[64,4096]{1,0:T(8,128)(2,1)S(1)}, u32[]{:S(2)}, u32[]{:S(2)}) %collective-permute-start.3) | collective-permute-done | bytes 524320 | tf_op jit(solution)/shard_map/ppermute | solution.py:26
  57.1 3.1 %normalise.1.refs_0_ = bf16[64,4096]{1,0:T(8,128)(2,1)} custom-call(s32[1]{0:T(128)} %bitcast.13.block_ref, bf16[64,4096]{1,0:T(8,128)(2,1)} %get-tuple-element.42.t0, bf16[64,4096]{1,0:T(8,128)(2,1)} %copy-done.9, bf16[64,4096]{1,0:T(8,128)(2,1)} %collective-permute-done.7.t2, bf16[64,4096]{1,0:T(8,128)(2,1)} %copy-done.10, bf16[512,4096]{1,0:T(8,128)(2,1)} %bitcast.28, ...), custom_call_target="tpu_custom_call" | custom-call | flops 2097152 | bytes 3145728 | tf_op jit(solution)/shard_map/normalise/pallas_call | solution.py:168
  60.3 3.5 %collective-permute-start.9 = (bf16[64,4096]{1,0:T(8,128)(2,1)}, bf16[64,4096]{1,0:T(8,128)(2,1)}, u32[]{:S(2)}, u32[]{:S(2)}) collective-permute-start(bf16[64,4096]{1,0:T(8,128)(2,1)} %normalise.1.refs_0_), channel_id=1, source_target_pairs={{0,6},{2,0},{4,2},{6,4},{1,7},{3,1},{5,3},{7,5},{8,14},{10,8},{12,... | collective-permute-start | bytes 1572872 | tf_op jit(solution)/shard_map/ppermute | solution.py:26
  65.8 2.2 %collective-permute-start.12 = (s32[64]{0:T(128)S(1)}, s32[64]{0:T(128)S(1)}, u32[]{:S(2)}, u32[]{:S(2)}) collective-permute-start(s32[64]{0:T(128)S(1)} %reshape.41), channel_id=1, source_target_pairs={{0,32},{32,64},{64,96},{96,128},{128,160},{160,192},{192,224},{224... | collective-permute-start | bytes 776 | tf_op jit(solution)/shard_map/ppermute | solution.py:26
  68.0 2.8 %collective-permute-done.12 = s32[64]{0:T(128)S(1)} collective-permute-done((s32[64]{0:T(128)S(1)}, s32[64]{0:T(128)S(1)}, u32[]{:S(2)}, u32[]{:S(2)}) %collective-permute-start.12) | collective-permute-done | bytes 288 | tf_op jit(solution)/shard_map/ppermute | solution.py:26
  72.5 12.6 %collective-permute-done.8.refs_1_ = bf16[64,4096]{1,0:T(8,128)(2,1)} collective-permute-done((bf16[64,4096]{1,0:T(8,128)(2,1)}, bf16[64,4096]{1,0:T(8,128)(2,1)}, u32[]{:S(2)}, u32[]{:S(2)}) %collective-permute-start.8) | collective-permute-done | bytes 524320 | tf_op jit(solution)/shard_map/ppermute | solution.py:26
  88.9 6.6 %collective-permute-done.14.refs_7_.refs_4_ = bf16[512,512]{1,0:T(8,128)(2,1)} collective-permute-done((bf16[512,512]{1,0:T(8,128)(2,1)}, bf16[512,512]{1,0:T(8,128)(2,1)}, u32[]{:S(2)}, u32[]{:S(2)}) %collective-permute-start.14) | collective-permute-done | bytes 524320 | tf_op jit(solution)/shard_map/ppermute | solution.py:26
  95.5 5.0 %collective-permute-done.15.refs_8_.refs_5_ = bf16[512,512]{1,0:T(8,128)(2,1)} collective-permute-done((bf16[512,512]{1,0:T(8,128)(2,1)}, bf16[512,512]{1,0:T(8,128)(2,1)}, u32[]{:S(2)}, u32[]{:S(2)}) %collective-permute-start.15) | collective-permute-done | bytes 524320 | tf_op jit(solution)/shard_map/ppermute | solution.py:26
  101.5 3.6 %memorise.2 = (bf16[256,512]{1,0:T(8,128)(2,1)S(1)}, bf16[256,4096]{1,0:T(8,128)(2,1)S(1)}) custom-call(s32[2]{0:T(128)S(1)} %pad_add_fusion.1.at_ref, bf16[64,4096]{1,0:T(8,128)(2,1)S(1)} %copy-done, bf16[64,4096]{1,0:T(8,128)(2,1)} %collective-permute-done.8.refs_1_, bf16[64,4096]{1,0:T(8,128)(2,1)} %collective-permute-done.13.refs_2_, ...), custom_call_target="tpu_custom_call" | custom-call | flops 1073741824 | bytes 4194304 | tf_op jit(solution)/shard_map/memorise/pallas_call | solution.py:238
  105.4 3.2 %collective-permute-start.17 = (bf16[256,512]{1,0:T(8,128)(2,1)S(1)}, bf16[256,512]{1,0:T(8,128)(2,1)S(1)}, u32[]{:S(2)}, u32[]{:S(2)}) collective-permute-start(bf16[256,512]{1,0:T(8,128)(2,1)S(1)} %get-tuple-element.55.refs_4_), channel_id=1, source_target_pairs={{0,224},{32,0},{64,32},{96,64},{128,96},{160,128},{192,160},{224,1... | collective-permute-start | bytes 786440 | tf_op jit(solution)/shard_map/ppermute | solution.py:26
  109.4 2.6 %memorise.3.refs_13_ = bf16[256,512]{1,0:T(8,128)(2,1)S(1)} custom-call(s32[2]{0:T(128)S(1)} %pad_add_fusion.1.at_ref, bf16[256,4096]{1,0:T(8,128)(2,1)S(1)} %collective-permute-done.24.refs_0_, bf16[1024,512]{1,0:T(8,128)(2,1)S(1)} %bitcast.26, bf16[1024,512]{1,0:T(8,128)(2,1)S(1)} %collective-permute-done.10.refs_5_.refs_2_, ...), custom_call_target="tpu_custom_call" | custom-call | flops 1073741824 | bytes 4194304 | tf_op jit(solution)/shard_map/memorise/pallas_call | solution.py:238
  112.2 3.2 %collective-permute-start.26 = (bf16[256,512]{1,0:T(8,128)(2,1)S(1)}, bf16[256,512]{1,0:T(8,128)(2,1)S(1)}, u32[]{:S(2)}, u32[]{:S(2)}) collective-permute-start(bf16[256,512]{1,0:T(8,128)(2,1)S(1)} %memorise.3.refs_13_), channel_id=1, source_target_pairs={{0,224},{32,0},{64,32},{96,64},{128,96},{160,128},{192,160},{224,1... | collective-permute-start | bytes 786440 | tf_op jit(solution)/shard_map/ppermute | solution.py:26
  115.4 3.2 %collective-permute-start.19 = (bf16[256,512]{1,0:T(8,128)(2,1)S(1)}, bf16[256,512]{1,0:T(8,128)(2,1)S(1)}, u32[]{:S(2)}, u32[]{:S(2)}) collective-permute-start(bf16[256,512]{1,0:T(8,128)(2,1)S(1)} %collective-permute-done.17.refs_6_), channel_id=1, source_target_pairs={{0,224},{32,0},{64,32},{96,64},{128,96},{160,128},{192,160},{224,1... | collective-permute-start | bytes 786440 | tf_op jit(solution)/shard_map/ppermute | solution.py:26
  118.6 3.9 %collective-permute-done.25.refs_14_ = bf16[256,512]{1,0:T(8,128)(2,1)S(1)} collective-permute-done((bf16[256,512]{1,0:T(8,128)(2,1)S(1)}, bf16[256,512]{1,0:T(8,128)(2,1)S(1)}, u32[]{:S(2)}, u32[]{:S(2)}) %collective-permute-start.25) | collective-permute-done | bytes 262176 | tf_op jit(solution)/shard_map/ppermute | solution.py:26
  122.5 3.3 %collective-permute-start.28 = (bf16[256,512]{1,0:T(8,128)(2,1)S(1)}, bf16[256,512]{1,0:T(8,128)(2,1)S(1)}, u32[]{:S(2)}, u32[]{:S(2)}) collective-permute-start(bf16[256,512]{1,0:T(8,128)(2,1)S(1)} %collective-permute-done.26.refs_15_), channel_id=1, source_target_pairs={{0,224},{32,0},{64,32},{96,64},{128,96},{160,128},{192,160},{224,1... | collective-permute-start | bytes 786440 | tf_op jit(solution)/shard_map/ppermute | solution.py:26
  125.8 2.3 %collective-permute-done.18.refs_7_ = bf16[256,512]{1,0:T(8,128)(2,1)S(1)} collective-permute-done((bf16[256,512]{1,0:T(8,128)(2,1)S(1)}, bf16[256,512]{1,0:T(8,128)(2,1)S(1)}, u32[]{:S(2)}, u32[]{:S(2)}) %collective-permute-start.18) | collective-permute-done | bytes 262176 | tf_op jit(solution)/shard_map/ppermute | solution.py:26
  128.2 3.3 %collective-permute-start.21 = (bf16[256,512]{1,0:T(8,128)(2,1)S(1)}, bf16[256,512]{1,0:T(8,128)(2,1)S(1)}, u32[]{:S(2)}, u32[]{:S(2)}) collective-permute-start(bf16[256,512]{1,0:T(8,128)(2,1)S(1)} %collective-permute-done.19.refs_8_), channel_id=1, source_target_pairs={{0,224},{32,0},{64,32},{96,64},{128,96},{160,128},{192,160},{224,1... | collective-permute-start | bytes 786440 | tf_op jit(solution)/shard_map/ppermute | solution.py:26
  131.4 2.3 %collective-permute-done.27.refs_16_ = bf16[256,512]{1,0:T(8,128)(2,1)S(1)} collective-permute-done((bf16[256,512]{1,0:T(8,128)(2,1)S(1)}, bf16[256,512]{1,0:T(8,128)(2,1)S(1)}, u32[]{:S(2)}, u32[]{:S(2)}) %collective-permute-start.27) | collective-permute-done | bytes 262176 | tf_op jit(solution)/shard_map/ppermute | solution.py:26
  133.8 3.3 %collective-permute-start.30 = (bf16[256,512]{1,0:T(8,128)(2,1)S(1)}, bf16[256,512]{1,0:T(8,128)(2,1)S(1)}, u32[]{:S(2)}, u32[]{:S(2)}) collective-permute-start(bf16[256,512]{1,0:T(8,128)(2,1)S(1)} %collective-permute-done.28.refs_17_), channel_id=1, source_target_pairs={{0,224},{32,0},{64,32},{96,64},{128,96},{160,128},{192,160},{224,1... | collective-permute-start | bytes 786440 | tf_op jit(solution)/shard_map/ppermute | solution.py:26
  137.0 2.3 %collective-permute-done.20.refs_9_ = bf16[256,512]{1,0:T(8,128)(2,1)S(1)} collective-permute-done((bf16[256,512]{1,0:T(8,128)(2,1)S(1)}, bf16[256,512]{1,0:T(8,128)(2,1)S(1)}, u32[]{:S(2)}, u32[]{:S(2)}) %collective-permute-start.20) | collective-permute-done | bytes 262176 | tf_op jit(solution)/shard_map/ppermute | solution.py:26
  140.2 3.2 %collective-permute-start.23 = (bf16[128,512]{1,0:T(8,128)(2,1)}, bf16[128,512]{1,0:T(8,128)(2,1)S(1)}, u32[]{:S(2)}, u32[]{:S(2)}) collective-permute-start(bf16[128,512]{1,0:T(8,128)(2,1)} %slice.41), channel_id=1, source_target_pairs={{0,224},{32,0},{64,32},{96,64},{128,96},{160,128},{192,160},{224,1... | collective-permute-start | bytes 393224 | tf_op jit(solution)/shard_map/ppermute | solution.py:26
  146.4 3.2 %collective-permute-start.32 = (bf16[128,512]{1,0:T(8,128)(2,1)}, bf16[128,512]{1,0:T(8,128)(2,1)S(1)}, u32[]{:S(2)}, u32[]{:S(2)}) collective-permute-start(bf16[128,512]{1,0:T(8,128)(2,1)} %slice.43), channel_id=1, source_target_pairs={{0,224},{32,0},{64,32},{96,64},{128,96},{160,128},{192,160},{224,1... | collective-permute-start | bytes 393224 | tf_op jit(solution)/shard_map/ppermute | solution.py:26
  150.3 2.1 %plan.1 = (s32[128]{0:T(128)}, s32[128]{0:T(128)}, s32[2]{0:T(128)}) custom-call(s32[128]{0:T(128)} %pad_add_fusion.ids_ref, s32[1]{0:T(128)} %bitcast.15.z_ref, s32[1]{0:T(128)} %bitcast.16.x_ref, s32[1]{0:T(128)} %bitcast.1.core_ref), custom_call_target="tpu_custom_call" | custom-call | tf_op jit(solution)/shard_map/plan/pallas_call | solution.py:316
  153.2 7.5 %windows.1 = bf16[4,1056,128]{2,1,0:T(8,128)(2,1)} custom-call(s32[128]{0:T(128)} %get-tuple-element.48.one_list, s32[128]{0:T(128)} %get-tuple-element.49.two_list, s32[2]{0:T(128)} %get-tuple-element.50.counts_ref, s32[1]{0:T(128)} %bitcast.16.x_ref, bf16[1040,128]{1,0:T(8,128)(2,1)} %copy-done.4, bf16[1040,128]{1,0:T(8,128)(2,1)} %copy-done.11, ...), custom_call_target="tpu_custom_call" | custom-call | flops 1000000000 | bytes 8388608 | tf_op jit(solution)/shard_map/windows/pallas_call | solution.py:415
  160.7 19.0 %all_to_all.10.parts_ref = bf16[4,1056,128]{2,1,0:T(8,128)(2,1)S(1)} all-to-all(bf16[4,1056,128]{2,1,0:T(8,128)(2,1)} %windows.1), channel_id=1, replica_groups=mesh['z'=8,'x'=4,'y'=4,'c'=2] {'x'}, dimensions={0} | all-to-all | bytes 2162688 | tf_op jit(solution)/shard_map/all_to_all | solution.py:516
  (125 shorter events, 30.7 us)
Async XLA Ops:
  0.0 21.6 %collective-permute-start.1 = (bf16[256,4096]{1,0:T(8,128)(2,1)}, bf16[256,4096]{1,0:T(8,128)(2,1)S(1)}, u32[]{:S(2)}, u32[]{:S(2)}) collective-permute-start(bf16[256,4096]{1,0:T(8,128)(2,1)} %bitcast.29), channel_id=1, source_target_pairs={{0,1},{1,0},{2,3},{3,2},{4,5},{5,4},{6,7},{7,6},{8,9},{9,8},{10,11... | collective-permute-start | bytes 6291464 | tf_op jit(solution)/shard_map/ppermute | solution.py:26
  2.0 44.9 %all-to-all-start = ((bf16[8,128,512]{2,1,0:T(8,128)(2,1)}), bf16[8,128,512]{2,1,0:T(8,128)(2,1)S(1)}, u32[]{:S(2)}, u32[]{:S(2)}) async-start(bf16[8,128,512]{2,1,0:T(8,128)(2,1)} %broadcast_in_dim.2), calls=%async_computation | async-start | bytes 2097152 | tf_op jit(solution)/shard_map/all_to_all | solution.py:32
  27.9 19.0 %collective-permute-start.2 = (bf16[64,4096]{1,0:T(8,128)(2,1)}, bf16[64,4096]{1,0:T(8,128)(2,1)S(1)}, u32[]{:S(2)}, u32[]{:S(2)}) collective-permute-start(bf16[64,4096]{1,0:T(8,128)(2,1)} %get-tuple-element.34), channel_id=1, source_target_pairs={{0,2},{2,4},{4,6},{6,0},{1,3},{3,5},{5,7},{7,1},{8,10},{10,12},{12... | collective-permute-start | bytes 1572872 | tf_op jit(solution)/shard_map/ppermute | solution.py:26
  29.5 24.7 %collective-permute-start.3 = (bf16[64,4096]{1,0:T(8,128)(2,1)}, bf16[64,4096]{1,0:T(8,128)(2,1)S(1)}, u32[]{:S(2)}, u32[]{:S(2)}) collective-permute-start(bf16[64,4096]{1,0:T(8,128)(2,1)} %get-tuple-element.35), channel_id=1, source_target_pairs={{0,6},{2,0},{4,2},{6,4},{1,7},{3,1},{5,3},{7,5},{8,14},{10,8},{12,... | collective-permute-start | bytes 1572872 | tf_op jit(solution)/shard_map/ppermute | solution.py:26
  31.2 8.4 %collective-permute-start.4 = (bf16[1040,128]{1,0:T(8,128)(2,1)S(1)}, bf16[1040,128]{1,0:T(8,128)(2,1)S(1)}, u32[]{:S(2)}, u32[]{:S(2)}) collective-permute-start(bf16[1040,128]{1,0:T(8,128)(2,1)S(1)} %fusion.1.refs_0_), channel_id=1, source_target_pairs={{0,24},{8,0},{16,8},{24,16},{1,25},{9,1},{17,9},{25,17},{2,26},{10... | collective-permute-start | bytes 798728 | tf_op jit(solution)/shard_map/ppermute | solution.py:26
  31.8 14.2 %collective-permute-start.5 = (bf16[1040,128]{1,0:T(8,128)(2,1)S(1)}, bf16[1040,128]{1,0:T(8,128)(2,1)S(1)}, u32[]{:S(2)}, u32[]{:S(2)}) collective-permute-start(bf16[1040,128]{1,0:T(8,128)(2,1)S(1)} %fusion.1.refs_0_), channel_id=1, source_target_pairs={{0,16},{8,24},{16,0},{24,8},{1,17},{9,25},{17,1},{25,9},{2,18},{10... | collective-permute-start | bytes 798728 | tf_op jit(solution)/shard_map/ppermute | solution.py:26
  34.3 12.7 %collective-permute-start.6 = (bf16[1040,128]{1,0:T(8,128)(2,1)S(1)}, bf16[1040,128]{1,0:T(8,128)(2,1)S(1)}, u32[]{:S(2)}, u32[]{:S(2)}) collective-permute-start(bf16[1040,128]{1,0:T(8,128)(2,1)S(1)} %fusion.1.refs_0_), channel_id=1, source_target_pairs={{0,8},{8,16},{16,24},{24,0},{1,9},{9,17},{17,25},{25,1},{2,10},{10... | collective-permute-start | bytes 798728 | tf_op jit(solution)/shard_map/ppermute | solution.py:26
  39.7 17.5 %collective-permute-start.7 = (bf16[64,4096]{1,0:T(8,128)(2,1)}, bf16[64,4096]{1,0:T(8,128)(2,1)}, u32[]{:S(2)}, u32[]{:S(2)}) collective-permute-start(bf16[64,4096]{1,0:T(8,128)(2,1)} %get-tuple-element.44), channel_id=1, source_target_pairs={{0,4},{2,6},{4,0},{6,2},{1,5},{3,7},{5,1},{7,3},{8,12},{10,14},{12... | collective-permute-start | bytes 1572872 | tf_op jit(solution)/shard_map/ppermute | solution.py:26
  55.0 30.1 %collective-permute-start.10 = (bf16[1024,512]{1,0:T(8,128)(2,1)S(1)}, bf16[1024,512]{1,0:T(8,128)(2,1)S(1)}, u32[]{:S(2)}, u32[]{:S(2)}) collective-permute-start(bf16[1024,512]{1,0:T(8,128)(2,1)S(1)} %bitcast.23), channel_id=1, source_target_pairs={{0,8},{8,16},{16,24},{24,0},{1,9},{9,17},{17,25},{25,1},{2,10},{10... | collective-permute-start | bytes 3145736 | tf_op jit(solution)/shard_map/ppermute | solution.py:26
  56.6 28.5 %collective-permute-start.11 = (bf16[1024,512]{1,0:T(8,128)(2,1)S(1)}, bf16[1024,512]{1,0:T(8,128)(2,1)S(1)}, u32[]{:S(2)}, u32[]{:S(2)}) collective-permute-start(bf16[1024,512]{1,0:T(8,128)(2,1)S(1)} %bitcast.24), channel_id=1, source_target_pairs={{0,24},{8,0},{16,8},{24,16},{1,25},{9,1},{17,9},{25,17},{2,26},{10... | collective-permute-start | bytes 3145736 | tf_op jit(solution)/shard_map/ppermute | solution.py:26
  60.2 24.9 %collective-permute-start.8 = (bf16[64,4096]{1,0:T(8,128)(2,1)}, bf16[64,4096]{1,0:T(8,128)(2,1)}, u32[]{:S(2)}, u32[]{:S(2)}) collective-permute-start(bf16[64,4096]{1,0:T(8,128)(2,1)} %normalise.1.refs_0_), channel_id=1, source_target_pairs={{0,2},{2,4},{4,6},{6,0},{1,3},{3,5},{5,7},{7,1},{8,10},{10,12},{12... | collective-permute-start | bytes 1572872 | tf_op jit(solution)/shard_map/ppermute | solution.py:26
  60.3 24.9 %collective-permute-start.9 = (bf16[64,4096]{1,0:T(8,128)(2,1)}, bf16[64,4096]{1,0:T(8,128)(2,1)}, u32[]{:S(2)}, u32[]{:S(2)}) collective-permute-start(bf16[64,4096]{1,0:T(8,128)(2,1)} %normalise.1.refs_0_), channel_id=1, source_target_pairs={{0,6},{2,0},{4,2},{6,4},{1,7},{3,1},{5,3},{7,5},{8,14},{10,8},{12,... | collective-permute-start | bytes 1572872 | tf_op jit(solution)/shard_map/ppermute | solution.py:26
  65.8 5.0 %collective-permute-start.12 = (s32[64]{0:T(128)S(1)}, s32[64]{0:T(128)S(1)}, u32[]{:S(2)}, u32[]{:S(2)}) collective-permute-start(s32[64]{0:T(128)S(1)} %reshape.41), channel_id=1, source_target_pairs={{0,32},{32,64},{64,96},{96,128},{128,160},{160,192},{192,224},{224... | collective-permute-start | bytes 776 | tf_op jit(solution)/shard_map/ppermute | solution.py:26
  70.8 18.1 %collective-permute-start.13 = (bf16[64,4096]{1,0:T(8,128)(2,1)}, bf16[64,4096]{1,0:T(8,128)(2,1)}, u32[]{:S(2)}, u32[]{:S(2)}) collective-permute-start(bf16[64,4096]{1,0:T(8,128)(2,1)} %normalise.1.refs_0_), channel_id=1, source_target_pairs={{0,4},{2,6},{4,0},{6,2},{1,5},{3,7},{5,1},{7,3},{8,12},{10,14},{12... | collective-permute-start | bytes 1572872 | tf_op jit(solution)/shard_map/ppermute | solution.py:26
  86.0 9.5 %collective-permute-start.14 = (bf16[512,512]{1,0:T(8,128)(2,1)}, bf16[512,512]{1,0:T(8,128)(2,1)}, u32[]{:S(2)}, u32[]{:S(2)}) collective-permute-start(bf16[512,512]{1,0:T(8,128)(2,1)} %slice.34), channel_id=1, source_target_pairs={{0,8},{8,16},{16,24},{24,0},{1,9},{9,17},{17,25},{25,1},{2,10},{10... | collective-permute-start | bytes 1572872 | tf_op jit(solution)/shard_map/ppermute | solution.py:26
  87.7 12.8 %collective-permute-start.15 = (bf16[512,512]{1,0:T(8,128)(2,1)}, bf16[512,512]{1,0:T(8,128)(2,1)}, u32[]{:S(2)}, u32[]{:S(2)}) collective-permute-start(bf16[512,512]{1,0:T(8,128)(2,1)} %slice.35), channel_id=1, source_target_pairs={{0,24},{8,0},{16,8},{24,16},{1,25},{9,1},{17,9},{25,17},{2,26},{10... | collective-permute-start | bytes 1572872 | tf_op jit(solution)/shard_map/ppermute | solution.py:26
  105.3 10.1 %collective-permute-start.16 = (bf16[256,512]{1,0:T(8,128)(2,1)S(1)}, bf16[256,512]{1,0:T(8,128)(2,1)S(1)}, u32[]{:S(2)}, u32[]{:S(2)}) collective-permute-start(bf16[256,512]{1,0:T(8,128)(2,1)S(1)} %get-tuple-element.55.refs_4_), channel_id=1, source_target_pairs={{0,32},{32,64},{64,96},{96,128},{128,160},{160,192},{192,224},{224... | collective-permute-start | bytes 786440 | tf_op jit(solution)/shard_map/ppermute | solution.py:26
  105.4 10.0 %collective-permute-start.17 = (bf16[256,512]{1,0:T(8,128)(2,1)S(1)}, bf16[256,512]{1,0:T(8,128)(2,1)S(1)}, u32[]{:S(2)}, u32[]{:S(2)}) collective-permute-start(bf16[256,512]{1,0:T(8,128)(2,1)S(1)} %get-tuple-element.55.refs_4_), channel_id=1, source_target_pairs={{0,224},{32,0},{64,32},{96,64},{128,96},{160,128},{192,160},{224,1... | collective-permute-start | bytes 786440 | tf_op jit(solution)/shard_map/ppermute | solution.py:26
  112.1 10.4 %collective-permute-start.25 = (bf16[256,512]{1,0:T(8,128)(2,1)S(1)}, bf16[256,512]{1,0:T(8,128)(2,1)S(1)}, u32[]{:S(2)}, u32[]{:S(2)}) collective-permute-start(bf16[256,512]{1,0:T(8,128)(2,1)S(1)} %memorise.3.refs_13_), channel_id=1, source_target_pairs={{0,32},{32,64},{64,96},{96,128},{128,160},{160,192},{192,224},{224... | collective-permute-start | bytes 786440 | tf_op jit(solution)/shard_map/ppermute | solution.py:26
  112.2 10.4 %collective-permute-start.26 = (bf16[256,512]{1,0:T(8,128)(2,1)S(1)}, bf16[256,512]{1,0:T(8,128)(2,1)S(1)}, u32[]{:S(2)}, u32[]{:S(2)}) collective-permute-start(bf16[256,512]{1,0:T(8,128)(2,1)S(1)} %memorise.3.refs_13_), channel_id=1, source_target_pairs={{0,224},{32,0},{64,32},{96,64},{128,96},{160,128},{192,160},{224,1... | collective-permute-start | bytes 786440 | tf_op jit(solution)/shard_map/ppermute | solution.py:26
  115.4 12.7 %collective-permute-start.18 = (bf16[256,512]{1,0:T(8,128)(2,1)S(1)}, bf16[256,512]{1,0:T(8,128)(2,1)S(1)}, u32[]{:S(2)}, u32[]{:S(2)}) collective-permute-start(bf16[256,512]{1,0:T(8,128)(2,1)S(1)} %collective-permute-done.16.refs_5_), channel_id=1, source_target_pairs={{0,32},{32,64},{64,96},{96,128},{128,160},{160,192},{192,224},{224... | collective-permute-start | bytes 786440 | tf_op jit(solution)/shard_map/ppermute | solution.py:26
  115.4 12.7 %collective-permute-start.19 = (bf16[256,512]{1,0:T(8,128)(2,1)S(1)}, bf16[256,512]{1,0:T(8,128)(2,1)S(1)}, u32[]{:S(2)}, u32[]{:S(2)}) collective-permute-start(bf16[256,512]{1,0:T(8,128)(2,1)S(1)} %collective-permute-done.17.refs_6_), channel_id=1, source_target_pairs={{0,224},{32,0},{64,32},{96,64},{128,96},{160,128},{192,160},{224,1... | collective-permute-start | bytes 786440 | tf_op jit(solution)/shard_map/ppermute | solution.py:26
  122.5 11.2 %collective-permute-start.27 = (bf16[256,512]{1,0:T(8,128)(2,1)S(1)}, bf16[256,512]{1,0:T(8,128)(2,1)S(1)}, u32[]{:S(2)}, u32[]{:S(2)}) collective-permute-start(bf16[256,512]{1,0:T(8,128)(2,1)S(1)} %collective-permute-done.25.refs_14_), channel_id=1, source_target_pairs={{0,32},{32,64},{64,96},{96,128},{128,160},{160,192},{192,224},{224... | collective-permute-start | bytes 786440 | tf_op jit(solution)/shard_map/ppermute | solution.py:26
  122.5 11.2 %collective-permute-start.28 = (bf16[256,512]{1,0:T(8,128)(2,1)S(1)}, bf16[256,512]{1,0:T(8,128)(2,1)S(1)}, u32[]{:S(2)}, u32[]{:S(2)}) collective-permute-start(bf16[256,512]{1,0:T(8,128)(2,1)S(1)} %collective-permute-done.26.refs_15_), channel_id=1, source_target_pairs={{0,224},{32,0},{64,32},{96,64},{128,96},{160,128},{192,160},{224,1... | collective-permute-start | bytes 786440 | tf_op jit(solution)/shard_map/ppermute | solution.py:26
  128.1 11.2 %collective-permute-start.20 = (bf16[256,512]{1,0:T(8,128)(2,1)S(1)}, bf16[256,512]{1,0:T(8,128)(2,1)S(1)}, u32[]{:S(2)}, u32[]{:S(2)}) collective-permute-start(bf16[256,512]{1,0:T(8,128)(2,1)S(1)} %collective-permute-done.18.refs_7_), channel_id=1, source_target_pairs={{0,32},{32,64},{64,96},{96,128},{128,160},{160,192},{192,224},{224... | collective-permute-start | bytes 786440 | tf_op jit(solution)/shard_map/ppermute | solution.py:26
  128.2 11.3 %collective-permute-start.21 = (bf16[256,512]{1,0:T(8,128)(2,1)S(1)}, bf16[256,512]{1,0:T(8,128)(2,1)S(1)}, u32[]{:S(2)}, u32[]{:S(2)}) collective-permute-start(bf16[256,512]{1,0:T(8,128)(2,1)S(1)} %collective-permute-done.19.refs_8_), channel_id=1, source_target_pairs={{0,224},{32,0},{64,32},{96,64},{128,96},{160,128},{192,160},{224,1... | collective-permute-start | bytes 786440 | tf_op jit(solution)/shard_map/ppermute | solution.py:26
  133.8 11.2 %collective-permute-start.29 = (bf16[256,512]{1,0:T(8,128)(2,1)S(1)}, bf16[256,512]{1,0:T(8,128)(2,1)S(1)}, u32[]{:S(2)}, u32[]{:S(2)}) collective-permute-start(bf16[256,512]{1,0:T(8,128)(2,1)S(1)} %collective-permute-done.27.refs_16_), channel_id=1, source_target_pairs={{0,32},{32,64},{64,96},{96,128},{128,160},{160,192},{192,224},{224... | collective-permute-start | bytes 786440 | tf_op jit(solution)/shard_map/ppermute | solution.py:26
  133.8 11.9 %collective-permute-start.30 = (bf16[256,512]{1,0:T(8,128)(2,1)S(1)}, bf16[256,512]{1,0:T(8,128)(2,1)S(1)}, u32[]{:S(2)}, u32[]{:S(2)}) collective-permute-start(bf16[256,512]{1,0:T(8,128)(2,1)S(1)} %collective-permute-done.28.refs_17_), channel_id=1, source_target_pairs={{0,224},{32,0},{64,32},{96,64},{128,96},{160,128},{192,160},{224,1... | collective-permute-start | bytes 786440 | tf_op jit(solution)/shard_map/ppermute | solution.py:26
  139.4 13.1 %collective-permute-start.22 = (bf16[128,512]{1,0:T(8,128)(2,1)S(1)}, bf16[128,512]{1,0:T(8,128)(2,1)S(1)}, u32[]{:S(2)}, u32[]{:S(2)}) collective-permute-start(bf16[128,512]{1,0:T(8,128)(2,1)S(1)} %slice.40), channel_id=1, source_target_pairs={{0,32},{32,64},{64,96},{96,128},{128,160},{160,192},{192,224},{224... | collective-permute-start | bytes 393224 | tf_op jit(solution)/shard_map/ppermute | solution.py:26
  140.2 12.3 %collective-permute-start.23 = (bf16[128,512]{1,0:T(8,128)(2,1)}, bf16[128,512]{1,0:T(8,128)(2,1)S(1)}, u32[]{:S(2)}, u32[]{:S(2)}) collective-permute-start(bf16[128,512]{1,0:T(8,128)(2,1)} %slice.41), channel_id=1, source_target_pairs={{0,224},{32,0},{64,32},{96,64},{128,96},{160,128},{192,160},{224,1... | collective-permute-start | bytes 393224 | tf_op jit(solution)/shard_map/ppermute | solution.py:26
  145.7 6.8 %collective-permute-start.31 = (bf16[128,512]{1,0:T(8,128)(2,1)}, bf16[128,512]{1,0:T(8,128)(2,1)S(1)}, u32[]{:S(2)}, u32[]{:S(2)}) collective-permute-start(bf16[128,512]{1,0:T(8,128)(2,1)} %slice.42), channel_id=1, source_target_pairs={{0,32},{32,64},{64,96},{96,128},{128,160},{160,192},{192,224},{224... | collective-permute-start | bytes 393224 | tf_op jit(solution)/shard_map/ppermute | solution.py:26
  146.4 6.1 %collective-permute-start.32 = (bf16[128,512]{1,0:T(8,128)(2,1)}, bf16[128,512]{1,0:T(8,128)(2,1)S(1)}, u32[]{:S(2)}, u32[]{:S(2)}) collective-permute-start(bf16[128,512]{1,0:T(8,128)(2,1)} %slice.43), channel_id=1, source_target_pairs={{0,224},{32,0},{64,32},{96,64},{128,96},{160,128},{192,160},{224,1... | collective-permute-start | bytes 393224 | tf_op jit(solution)/shard_map/ppermute | solution.py:26
  (31 other events, 398.8 us)

commit v6 on v5

--- a/solution.py
+++ b/solution.py
@@ -189,9 +189,9 @@
 
 def memory_kernel(parts, at_ref, *refs):
     us = refs[:parts]
-    k0, k1, k2, k3, k4 = refs[parts:parts + 5]
-    out_ref = refs[parts + 5]
-    rest = refs[parts + 6:]
+    k_refs = refs[parts:parts + NX]
+    out_ref = refs[parts + NX]
+    rest = refs[parts + NX + 1:]
     if parts > 1:
         whole, rest = rest[0], rest[1:]
     ua, kv, sem, out_sem = rest
@@ -201,16 +201,8 @@
     for k in range(parts):
         first = pl.multiple_of(lax.rem(at_ref[1] - k + parts, parts) * rows, rows)
         u_copies.append(pltpu.make_async_copy(us[k], ua.at[pl.ds(first, rows)], sem.at[k]))
-    near = [
-        pltpu.make_async_copy(k_ref.at[pl.ds(0, depth)], kv.at[i], sem.at[NY + i])
-        for i, k_ref in enumerate((k0, k1, k2))
-    ]
-    top, bottom = k3.shape[0], depth - k3.shape[0]
-    far = [
-        pltpu.make_async_copy(k3, kv.at[3, pl.ds(0, top)], sem.at[NY + 3]),
-        pltpu.make_async_copy(k4.at[pl.ds(0, bottom)], kv.at[3, pl.ds(top, bottom)], sem.at[NY + 4]),
-    ]
-    for copy in u_copies + near + far:
+    k_copies = [pltpu.make_async_copy(k_ref, kv.at[i], sem.at[NY + i]) for i, k_ref in enumerate(k_refs)]
+    for copy in u_copies + k_copies:
         copy.start()
     for copy in u_copies:
         copy.wait()
@@ -219,8 +211,7 @@
         back.start()
     total = jnp.zeros(out_ref.shape, F32)
     for i in range(NX):
-        for copy in (near[i:i + 1] if i < 3 else far):
-            copy.wait()
+        k_copies[i].wait()
         first = pl.multiple_of(lax.rem(at_ref[0] + ORDER[i], NX) * depth, depth)
         total += jnp.dot(ua[:, pl.ds(first, depth)], kv[i], preferred_element_type=F32)
     out_ref[...] = total.astype(BF)
@@ -237,12 +228,12 @@
     assembled = [jax.ShapeDtypeStruct((tokens, width), BF)] if len(us) > 1 else []
     return pl.pallas_call(
         functools.partial(memory_kernel, len(us)),
-        in_specs=[pl.BlockSpec(memory_space=pltpu.SMEM)] + [ANY] * (len(us) + 5),
+        in_specs=[pl.BlockSpec(memory_space=pltpu.SMEM)] + [ANY] * (len(us) + NX),
         out_specs=[VMEM_ALL] + [ANY] * len(assembled),
         scratch_shapes=[
             pltpu.VMEM((tokens, width), BF),
             pltpu.VMEM((NX, depth, cols), BF),
-            pltpu.SemaphoreType.DMA((NY + 5,)),
+            pltpu.SemaphoreType.DMA((NY + NX,)),
             pltpu.SemaphoreType.DMA,
         ],
         out_shape=[memory] + assembled,
@@ -488,22 +479,19 @@
     terms = project(att_own, att_other, e_own, e_other)
 
     terms = [terms[0]] + [shifted(terms[k], "y", k) for k in range(1, NY)]
-    kv, terms[1], terms[3], qs = lax.optimization_barrier((kv, terms[1], terms[3], qs))
+    kv, terms[1], terms[3] = lax.optimization_barrier((kv, terms[1], terms[3]))
+    terms[2], qs = lax.optimization_barrier((terms[2], qs))
     got = jnp.stack([q[1024:1032, 0:2] for q in qs]).astype(jnp.int32).reshape(-1)
     below = shifted(got, "z", 1)
     from_left = shifted(kv, "x", 1)
     from_right = shifted(kv, "x", -1)
+    from_far = shifted(kv, "x", 2)
 
     u = normalise(terms, corpus_flat, gain_out.reshape(1, width), as_index(core * NY + my_y))
     us = [u] + [shifted(u, "y", k) for k in range(1, NY)]
-    us[1], us[3], from_left, from_right, below = lax.optimization_barrier(
-        (us[1], us[3], from_left, from_right, below)
-    )
-    ids = jnp.concatenate([got, below])
-    half = kv.shape[0] // 2
-    far_top = shifted(from_left[:half], "x", 1)
-    far_bottom = shifted(from_right[half:], "x", -1)
-    weights = [kv, from_left, from_right, far_top, far_bottom]
+    lists = plan(jnp.concatenate([got, below]), as_index(my_z), as_index(my_x), as_index(core))
+    weights = [kv, from_left, from_right, from_far]
+    us[1], us[3], lists, weights = lax.optimization_barrier((us[1], us[3], lists, weights))
     at = as_index(my_x, my_y)
     memory_own, u_own = memorise(at, us, weights)
     u_other = shifted(u_own, "c", 1)
@@ -511,7 +499,6 @@
     (memory_other,) = memorise(at, [u_other], weights)
     pieces += ring_pieces(memory_other, 2 * ROW)
 
-    lists = plan(ids, as_index(my_z), as_index(my_x), as_index(core))
     parts = windows(lists, as_index(my_x), qs, pieces)
     parts = lax.all_to_all(parts, "x", split_axis=0, concat_axis=0, tiled=True)
     return combine(parts).reshape(512, 2, HS)

time: 182 us -> 179 us (0.984); the launches traced: 181 us -> 176 us
  waiting for transfers between devices: 57.7 us -> 45.1 us
  starting transfers between devices: 56.5 us -> 64.7 us
  local copies, waits for them, and re-layouts: 11.8 us -> 8.62 us
    ppermute x33 -> x32, waiting for transfers between devices: 57.7 us -> 45.1 us  [shifted(): return lax.ppermute(value, axis, [(i, (i + steps) % n) for i in range(n)])]
    ppermute x33 -> x32, starting transfers between devices: 48.1 us -> 56.2 us  [shifted(): return lax.ppermute(value, axis, [(i, (i + steps) % n) for i in range(n)])]
    unnamed x58 -> x50, local copies, waits for them, and re-layouts: 3.93 us -> 4.5 us
  transfers between devices with their start and end apart: 34 -> 33, of which waited for: 15 -> 14; matrix products, arithmetic and copies ran while one was open for 5% -> 3% of each run, Pallas kernels for 12% -> 13%
where the time goes in v6:
time: 179 us; the launch traced here: 176 us
  starting transfers between devices  64.7 us (36%)
  waiting for transfers between devices  45.1 us (25%)
  Pallas kernels  36.3 us (20%)
  blocking collectives  19.4 us (11%)
  local copies, waits for them, and re-layouts  8.62 us (5%)
    ppermute x32, starting transfers between devices, shifted(): return lax.ppermute(value, axis, [(i, (i + steps) % n) for i in range(n)])  56.2 us
    ppermute x32, waiting for transfers between devices, shifted(): return lax.ppermute(value, axis, [(i, (i + steps) % n) for i in range(n)])  45.1 us
    all_to_all x1, blocking collectives, on_device(): parts = lax.all_to_all(parts, 'x', split_axis=0, concat_axis=0, tiled=True)  19.4 us
    pallas_call x1, Pallas kernels, encode(): pl.pallas_call(encoder_kernel, grid_spec=pltpu.PrefetchScalarGridSpec(num...  9.48 us
    pallas_call x1, Pallas kernels, windows(): pl.pallas_call(functools.partial(window_kernel, layout), in_specs=[smem]...  9.04 us
    all_to_all x1, starting transfers between devices, spread(): return lax.all_to_all(copies, axis, split_axis=0, concat_axis=0, tiled=True)  8.47 us
    pallas_call x2, Pallas kernels, memorise(): pl.pallas_call(functools.partial(memory_kernel, len(us)), in_specs=[pl.Bl...  6.25 us
    pallas_call x1, Pallas kernels, project(): pl.pallas_call(project_kernel, grid=(width // cols,), in_specs=[pl.BlockS...  4.93 us
  transfers between devices with their start and end apart: 33, of which 14 were waited for; matrix products, arithmetic and copies ran while one was open for 3% of the time, Pallas kernels for 13%

profile of v6, /device:TPU:2, one launch (start us, length us, event | category | flops | bytes accessed | tf_op | source)
XLA Modules:
  0.0 176.0 jit_solution(7543204161153056592)
XLA Ops:
  2.0 8.5 %all-to-all-start = ((bf16[8,128,512]{2,1,0:T(8,128)(2,1)}), bf16[8,128,512]{2,1,0:T(8,128)(2,1)S(1)}, u32[]{:S(2)}, u32[]{:S(2)}) async-start(bf16[8,128,512]{2,1,0:T(8,128)(2,1)} %broadcast_in_dim.2), calls=%async_computation | async-start | bytes 2097152 | tf_op jit(solution)/shard_map/all_to_all | solution.py:32
  10.5 9.5 %encoder.1 = (bf16[256,256]{1,0:T(8,128)(2,1)}, bf16[256,256]{1,0:T(8,128)(2,1)}) custom-call(s32[1]{0:T(128)} %bitcast.1.core_ref, s32[1]{0:T(128)} %bitcast.2.y_ref, bf16[512,4096]{1,0:T(8,128)(2,1)} %bitcast.28, bf16[24576,128]{1,0:T(8,128)(2,1)} %bitcast.34, f32[1,4096]{1,0:T(1,128)} %bitcast.35), custom_call_target="tpu_custom_call" | custom-call | flops 3221225472 | bytes 10485760 | tf_op jit(solution)/shard_map/encoder/pallas_call | solution.py:94
  22.9 4.9 %project.1 = (bf16[64,4096]{1,0:T(8,128)(2,1)}, bf16[64,4096]{1,0:T(8,128)(2,1)}, bf16[64,4096]{1,0:T(8,128)(2,1)}, bf16[64,4096]{1,0:T(8,128)(2,1)}) custom-call(bf16[256,256]{1,0:T(8,128)(2,1)} %get-tuple-element.36.a_ref, bf16[256,256]{1,0:T(8,128)(2,1)} %copy-done.23, bf16[256,4096]{1,0:T(8,128)(2,1)} %bitcast.31, bf16[256,4096]{1,0:T(8,128)(2,1)} %copy-done.3), custom_call_target="tpu_custom_call" | custom-call | flops 1073741824 | bytes 4194304 | tf_op jit(solution)/shard_map/project/pallas_call | solution.py:134
  31.1 2.0 %collective-permute-start.4 = (bf16[64,4096]{1,0:T(8,128)(2,1)}, bf16[64,4096]{1,0:T(8,128)(2,1)}, u32[]{:S(2)}, u32[]{:S(2)}) collective-permute-start(bf16[64,4096]{1,0:T(8,128)(2,1)} %get-tuple-element.43), channel_id=1, source_target_pairs={{0,4},{2,6},{4,0},{6,2},{1,5},{3,7},{5,1},{7,3},{8,12},{10,14},{12... | collective-permute-start | bytes 1572872 | tf_op jit(solution)/shard_map/ppermute | solution.py:26
  34.8 2.4 %collective-permute-start.6 = (bf16[1040,128]{1,0:T(8,128)(2,1)S(1)}, bf16[1040,128]{1,0:T(8,128)(2,1)}, u32[]{:S(2)}, u32[]{:S(2)}) collective-permute-start(bf16[1040,128]{1,0:T(8,128)(2,1)S(1)} %fusion.1.refs_0_), channel_id=1, source_target_pairs={{0,16},{8,24},{16,0},{24,8},{1,17},{9,25},{17,1},{25,9},{2,18},{10... | collective-permute-start | bytes 798728 | tf_op jit(solution)/shard_map/ppermute | solution.py:26
  37.2 6.2 %collective-permute-done.2.t1 = bf16[64,4096]{1,0:T(8,128)(2,1)S(1)} collective-permute-done((bf16[64,4096]{1,0:T(8,128)(2,1)}, bf16[64,4096]{1,0:T(8,128)(2,1)S(1)}, u32[]{:S(2)}, u32[]{:S(2)}) %collective-permute-start.2) | collective-permute-done | bytes 524320 | tf_op jit(solution)/shard_map/ppermute | solution.py:26
  44.9 9.2 %collective-permute-done.3.t3 = bf16[64,4096]{1,0:T(8,128)(2,1)S(1)} collective-permute-done((bf16[64,4096]{1,0:T(8,128)(2,1)}, bf16[64,4096]{1,0:T(8,128)(2,1)S(1)}, u32[]{:S(2)}, u32[]{:S(2)}) %collective-permute-start.3) | collective-permute-done | bytes 524320 | tf_op jit(solution)/shard_map/ppermute | solution.py:26
  57.0 2.1 %collective-permute-start.13 = (bf16[1024,512]{1,0:T(8,128)(2,1)S(1)}, bf16[1024,512]{1,0:T(8,128)(2,1)}, u32[]{:S(2)}, u32[]{:S(2)}) collective-permute-start(bf16[1024,512]{1,0:T(8,128)(2,1)S(1)} %bitcast.25), channel_id=1, source_target_pairs={{0,16},{8,24},{16,0},{24,8},{1,17},{9,25},{17,1},{25,9},{2,18},{10... | collective-permute-start | bytes 3145736 | tf_op jit(solution)/shard_map/ppermute | solution.py:26
  59.1 3.1 %normalise.1.refs_0_ = bf16[64,4096]{1,0:T(8,128)(2,1)} custom-call(s32[1]{0:T(128)} %bitcast.block_ref, bf16[64,4096]{1,0:T(8,128)(2,1)} %get-tuple-element.39.t0, bf16[64,4096]{1,0:T(8,128)(2,1)} %copy-done.9, bf16[64,4096]{1,0:T(8,128)(2,1)} %collective-permute-done.4.t2, bf16[64,4096]{1,0:T(8,128)(2,1)} %copy-done.10, bf16[512,4096]{1,0:T(8,128)(2,1)} %bitcast.29, ...), custom_call_target="tpu_custom_call" | custom-call | flops 2097152 | bytes 3145728 | tf_op jit(solution)/shard_map/normalise/pallas_call | solution.py:168
  64.2 2.2 %collective-permute-start.10 = (s32[64]{0:T(128)S(1)}, s32[64]{0:T(128)S(1)}, u32[]{:S(2)}, u32[]{:S(2)}) collective-permute-start(s32[64]{0:T(128)S(1)} %reshape.41), channel_id=1, source_target_pairs={{0,32},{32,64},{64,96},{96,128},{128,160},{160,192},{192,224},{224... | collective-permute-start | bytes 776 | tf_op jit(solution)/shard_map/ppermute | solution.py:26
  66.4 2.8 %collective-permute-done.10 = s32[64]{0:T(128)S(1)} collective-permute-done((s32[64]{0:T(128)S(1)}, s32[64]{0:T(128)S(1)}, u32[]{:S(2)}, u32[]{:S(2)}) %collective-permute-start.10) | collective-permute-done | bytes 288 | tf_op jit(solution)/shard_map/ppermute | solution.py:26
  69.2 3.6 %collective-permute-start.9 = (bf16[64,4096]{1,0:T(8,128)(2,1)}, bf16[64,4096]{1,0:T(8,128)(2,1)}, u32[]{:S(2)}, u32[]{:S(2)}) collective-permute-start(bf16[64,4096]{1,0:T(8,128)(2,1)} %normalise.1.refs_0_), channel_id=1, source_target_pairs={{0,6},{2,0},{4,2},{6,4},{1,7},{3,1},{5,3},{7,5},{8,14},{10,8},{12,... | collective-permute-start | bytes 1572872 | tf_op jit(solution)/shard_map/ppermute | solution.py:26
  74.4 9.9 %collective-permute-start.14 = (bf16[64,4096]{1,0:T(8,128)(2,1)}, bf16[64,4096]{1,0:T(8,128)(2,1)}, u32[]{:S(2)}, u32[]{:S(2)}) collective-permute-start(bf16[64,4096]{1,0:T(8,128)(2,1)} %normalise.1.refs_0_), channel_id=1, source_target_pairs={{0,4},{2,6},{4,0},{6,2},{1,5},{3,7},{5,1},{7,3},{8,12},{10,14},{12... | collective-permute-start | bytes 1572872 | tf_op jit(solution)/shard_map/ppermute | solution.py:26
  84.9 2.1 %plan.1 = (s32[128]{0:T(128)}, s32[128]{0:T(128)}, s32[2]{0:T(128)}) custom-call(s32[128]{0:T(128)} %pad_add_fusion.ids_ref, s32[1]{0:T(128)} %bitcast.15.z_ref, s32[1]{0:T(128)} %bitcast.16.x_ref, s32[1]{0:T(128)} %bitcast.1.core_ref), custom_call_target="tpu_custom_call" | custom-call | tf_op jit(solution)/shard_map/plan/pallas_call | solution.py:307
  87.0 3.3 %collective-permute-done.9.refs_3_ = bf16[64,4096]{1,0:T(8,128)(2,1)} collective-permute-done((bf16[64,4096]{1,0:T(8,128)(2,1)}, bf16[64,4096]{1,0:T(8,128)(2,1)}, u32[]{:S(2)}, u32[]{:S(2)}) %collective-permute-start.9) | collective-permute-done | bytes 524320 | tf_op jit(solution)/shard_map/ppermute | solution.py:26
  90.3 3.8 %collective-permute-done.13.refs_7_.refs_4_ = bf16[1024,512]{1,0:T(8,128)(2,1)} collective-permute-done((bf16[1024,512]{1,0:T(8,128)(2,1)S(1)}, bf16[1024,512]{1,0:T(8,128)(2,1)}, u32[]{:S(2)}, u32[]{:S(2)}) %collective-permute-start.13) | collective-permute-done | bytes 1048608 | tf_op jit(solution)/shard_map/ppermute | solution.py:26
  95.2 3.6 %memorise.2 = (bf16[256,512]{1,0:T(8,128)(2,1)S(1)}, bf16[256,4096]{1,0:T(8,128)(2,1)S(1)}) custom-call(s32[2]{0:T(128)S(1)} %pad_add_fusion.1.at_ref, bf16[64,4096]{1,0:T(8,128)(2,1)S(1)} %copy-done, bf16[64,4096]{1,0:T(8,128)(2,1)} %collective-permute-done.8.refs_1_, bf16[64,4096]{1,0:T(8,128)(2,1)} %collective-permute-done.14.refs_2_, ...), custom_call_target="tpu_custom_call" | custom-call | flops 1073741824 | bytes 4194304 | tf_op jit(solution)/shard_map/memorise/pallas_call | solution.py:229
  103.0 2.6 %memorise.3.refs_13_ = bf16[256,512]{1,0:T(8,128)(2,1)S(1)} custom-call(s32[2]{0:T(128)S(1)} %pad_add_fusion.1.at_ref, bf16[256,4096]{1,0:T(8,128)(2,1)S(1)} %collective-permute-done.23.refs_0_, bf16[1024,512]{1,0:T(8,128)(2,1)S(1)} %bitcast.27, bf16[1024,512]{1,0:T(8,128)(2,1)S(1)} %collective-permute-done.11.refs_5_.refs_2_, ...), custom_call_target="tpu_custom_call" | custom-call | flops 1073741824 | bytes 4194304 | tf_op jit(solution)/shard_map/memorise/pallas_call | solution.py:229
  109.7 2.6 %collective-permute-start.18 = (bf16[256,512]{1,0:T(8,128)(2,1)S(1)}, bf16[256,512]{1,0:T(8,128)(2,1)S(1)}, u32[]{:S(2)}, u32[]{:S(2)}) collective-permute-start(bf16[256,512]{1,0:T(8,128)(2,1)S(1)} %collective-permute-done.16.refs_6_), channel_id=1, source_target_pairs={{0,224},{32,0},{64,32},{96,64},{128,96},{160,128},{192,160},{224,1... | collective-permute-start | bytes 786440 | tf_op jit(solution)/shard_map/ppermute | solution.py:26
  112.3 3.9 %collective-permute-done.24.refs_14_ = bf16[256,512]{1,0:T(8,128)(2,1)S(1)} collective-permute-done((bf16[256,512]{1,0:T(8,128)(2,1)S(1)}, bf16[256,512]{1,0:T(8,128)(2,1)S(1)}, u32[]{:S(2)}, u32[]{:S(2)}) %collective-permute-start.24) | collective-permute-done | bytes 262176 | tf_op jit(solution)/shard_map/ppermute | solution.py:26
  116.8 2.6 %collective-permute-start.27 = (bf16[256,512]{1,0:T(8,128)(2,1)S(1)}, bf16[256,512]{1,0:T(8,128)(2,1)S(1)}, u32[]{:S(2)}, u32[]{:S(2)}) collective-permute-start(bf16[256,512]{1,0:T(8,128)(2,1)S(1)} %collective-permute-done.25.refs_15_), channel_id=1, source_target_pairs={{0,224},{32,0},{64,32},{96,64},{128,96},{160,128},{192,160},{224,1... | collective-permute-start | bytes 786440 | tf_op jit(solution)/shard_map/ppermute | solution.py:26
  119.4 2.3 %collective-permute-done.17.refs_7_ = bf16[256,512]{1,0:T(8,128)(2,1)S(1)} collective-permute-done((bf16[256,512]{1,0:T(8,128)(2,1)S(1)}, bf16[256,512]{1,0:T(8,128)(2,1)S(1)}, u32[]{:S(2)}, u32[]{:S(2)}) %collective-permute-start.17) | collective-permute-done | bytes 262176 | tf_op jit(solution)/shard_map/ppermute | solution.py:26
  122.4 2.6 %collective-permute-start.20 = (bf16[256,512]{1,0:T(8,128)(2,1)S(1)}, bf16[256,512]{1,0:T(8,128)(2,1)S(1)}, u32[]{:S(2)}, u32[]{:S(2)}) collective-permute-start(bf16[256,512]{1,0:T(8,128)(2,1)S(1)} %collective-permute-done.18.refs_8_), channel_id=1, source_target_pairs={{0,224},{32,0},{64,32},{96,64},{128,96},{160,128},{192,160},{224,1... | collective-permute-start | bytes 786440 | tf_op jit(solution)/shard_map/ppermute | solution.py:26
  125.0 2.3 %collective-permute-done.26.refs_16_ = bf16[256,512]{1,0:T(8,128)(2,1)S(1)} collective-permute-done((bf16[256,512]{1,0:T(8,128)(2,1)S(1)}, bf16[256,512]{1,0:T(8,128)(2,1)S(1)}, u32[]{:S(2)}, u32[]{:S(2)}) %collective-permute-start.26) | collective-permute-done | bytes 262176 | tf_op jit(solution)/shard_map/ppermute | solution.py:26
  128.1 2.6 %collective-permute-start.29 = (bf16[256,512]{1,0:T(8,128)(2,1)S(1)}, bf16[256,512]{1,0:T(8,128)(2,1)S(1)}, u32[]{:S(2)}, u32[]{:S(2)}) collective-permute-start(bf16[256,512]{1,0:T(8,128)(2,1)S(1)} %collective-permute-done.27.refs_17_), channel_id=1, source_target_pairs={{0,224},{32,0},{64,32},{96,64},{128,96},{160,128},{192,160},{224,1... | collective-permute-start | bytes 786440 | tf_op jit(solution)/shard_map/ppermute | solution.py:26
  130.6 2.3 %collective-permute-done.19.refs_9_ = bf16[256,512]{1,0:T(8,128)(2,1)S(1)} collective-permute-done((bf16[256,512]{1,0:T(8,128)(2,1)S(1)}, bf16[256,512]{1,0:T(8,128)(2,1)S(1)}, u32[]{:S(2)}, u32[]{:S(2)}) %collective-permute-start.19) | collective-permute-done | bytes 262176 | tf_op jit(solution)/shard_map/ppermute | solution.py:26
  133.7 2.7 %collective-permute-start.22 = (bf16[128,512]{1,0:T(8,128)(2,1)S(1)}, bf16[128,512]{1,0:T(8,128)(2,1)S(1)}, u32[]{:S(2)}, u32[]{:S(2)}) collective-permute-start(bf16[128,512]{1,0:T(8,128)(2,1)S(1)} %slice.33), channel_id=1, source_target_pairs={{0,224},{32,0},{64,32},{96,64},{128,96},{160,128},{192,160},{224,1... | collective-permute-start | bytes 393224 | tf_op jit(solution)/shard_map/ppermute | solution.py:26
  136.4 2.2 %collective-permute-done.28.refs_18_ = bf16[256,512]{1,0:T(8,128)(2,1)S(1)} collective-permute-done((bf16[256,512]{1,0:T(8,128)(2,1)S(1)}, bf16[256,512]{1,0:T(8,128)(2,1)S(1)}, u32[]{:S(2)}, u32[]{:S(2)}) %collective-permute-start.28) | collective-permute-done | bytes 262176 | tf_op jit(solution)/shard_map/ppermute | solution.py:26
  139.4 2.7 %collective-permute-start.31 = (bf16[128,512]{1,0:T(8,128)(2,1)S(1)}, bf16[128,512]{1,0:T(8,128)(2,1)S(1)}, u32[]{:S(2)}, u32[]{:S(2)}) collective-permute-start(bf16[128,512]{1,0:T(8,128)(2,1)S(1)} %slice.35), channel_id=1, source_target_pairs={{0,224},{32,0},{64,32},{96,64},{128,96},{160,128},{192,160},{224,1... | collective-permute-start | bytes 393224 | tf_op jit(solution)/shard_map/ppermute | solution.py:26
  142.1 2.8 %collective-permute-done.30.refs_20_ = bf16[128,512]{1,0:T(8,128)(2,1)S(1)} collective-permute-done((bf16[128,512]{1,0:T(8,128)(2,1)S(1)}, bf16[128,512]{1,0:T(8,128)(2,1)S(1)}, u32[]{:S(2)}, u32[]{:S(2)}) %collective-permute-start.30) | collective-permute-done | bytes 131104 | tf_op jit(solution)/shard_map/ppermute | solution.py:26
  146.2 9.0 %windows.1 = bf16[4,1056,128]{2,1,0:T(8,128)(2,1)} custom-call(s32[128]{0:T(128)} %get-tuple-element.56.one_list, s32[128]{0:T(128)} %get-tuple-element.57.two_list, s32[2]{0:T(128)} %get-tuple-element.58.counts_ref, s32[1]{0:T(128)} %bitcast.16.x_ref, bf16[1040,128]{1,0:T(8,128)(2,1)} %copy-done.4, bf16[1040,128]{1,0:T(8,128)(2,1)} %collective-permute-done.5.refs_1_, ...), custom_call_target="tpu_custom_call" | custom-call | flops 1000000000 | bytes 8388608 | tf_op jit(solution)/shard_map/windows/pallas_call | solution.py:406
  155.3 19.4 %all_to_all.10.parts_ref = bf16[4,1056,128]{2,1,0:T(8,128)(2,1)S(1)} all-to-all(bf16[4,1056,128]{2,1,0:T(8,128)(2,1)} %windows.1), channel_id=1, replica_groups=mesh['z'=8,'x'=4,'y'=4,'c'=2] {'x'}, dimensions={0} | all-to-all | bytes 2162688 | tf_op jit(solution)/shard_map/all_to_all | solution.py:503
  (113 shorter events, 33.9 us)
Async XLA Ops:
  0.0 21.6 %collective-permute-start.1 = (bf16[256,4096]{1,0:T(8,128)(2,1)}, bf16[256,4096]{1,0:T(8,128)(2,1)S(1)}, u32[]{:S(2)}, u32[]{:S(2)}) collective-permute-start(bf16[256,4096]{1,0:T(8,128)(2,1)} %bitcast.30), channel_id=1, source_target_pairs={{0,1},{1,0},{2,3},{3,2},{4,5},{5,4},{6,7},{7,6},{8,9},{9,8},{10,11... | collective-permute-start | bytes 6291464 | tf_op jit(solution)/shard_map/ppermute | solution.py:26
  2.0 42.9 %all-to-all-start = ((bf16[8,128,512]{2,1,0:T(8,128)(2,1)}), bf16[8,128,512]{2,1,0:T(8,128)(2,1)S(1)}, u32[]{:S(2)}, u32[]{:S(2)}) async-start(bf16[8,128,512]{2,1,0:T(8,128)(2,1)} %broadcast_in_dim.2), calls=%async_computation | async-start | bytes 2097152 | tf_op jit(solution)/shard_map/all_to_all | solution.py:32
  27.9 15.5 %collective-permute-start.2 = (bf16[64,4096]{1,0:T(8,128)(2,1)}, bf16[64,4096]{1,0:T(8,128)(2,1)S(1)}, u32[]{:S(2)}, u32[]{:S(2)}) collective-permute-start(bf16[64,4096]{1,0:T(8,128)(2,1)} %get-tuple-element.40), channel_id=1, source_target_pairs={{0,2},{2,4},{4,6},{6,0},{1,3},{3,5},{5,7},{7,1},{8,10},{10,12},{12... | collective-permute-start | bytes 1572872 | tf_op jit(solution)/shard_map/ppermute | solution.py:26
  29.5 24.7 %collective-permute-start.3 = (bf16[64,4096]{1,0:T(8,128)(2,1)}, bf16[64,4096]{1,0:T(8,128)(2,1)S(1)}, u32[]{:S(2)}, u32[]{:S(2)}) collective-permute-start(bf16[64,4096]{1,0:T(8,128)(2,1)} %get-tuple-element.41), channel_id=1, source_target_pairs={{0,6},{2,0},{4,2},{6,4},{1,7},{3,1},{5,3},{7,5},{8,14},{10,8},{12,... | collective-permute-start | bytes 1572872 | tf_op jit(solution)/shard_map/ppermute | solution.py:26
  31.1 28.0 %collective-permute-start.4 = (bf16[64,4096]{1,0:T(8,128)(2,1)}, bf16[64,4096]{1,0:T(8,128)(2,1)}, u32[]{:S(2)}, u32[]{:S(2)}) collective-permute-start(bf16[64,4096]{1,0:T(8,128)(2,1)} %get-tuple-element.43), channel_id=1, source_target_pairs={{0,4},{2,6},{4,0},{6,2},{1,5},{3,7},{5,1},{7,3},{8,12},{10,14},{12... | collective-permute-start | bytes 1572872 | tf_op jit(solution)/shard_map/ppermute | solution.py:26
  34.2 22.3 %collective-permute-start.5 = (bf16[1040,128]{1,0:T(8,128)(2,1)S(1)}, bf16[1040,128]{1,0:T(8,128)(2,1)}, u32[]{:S(2)}, u32[]{:S(2)}) collective-permute-start(bf16[1040,128]{1,0:T(8,128)(2,1)S(1)} %fusion.1.refs_0_), channel_id=1, source_target_pairs={{0,24},{8,0},{16,8},{24,16},{1,25},{9,1},{17,9},{25,17},{2,26},{10... | collective-permute-start | bytes 798728 | tf_op jit(solution)/shard_map/ppermute | solution.py:26
  34.8 22.2 %collective-permute-start.6 = (bf16[1040,128]{1,0:T(8,128)(2,1)S(1)}, bf16[1040,128]{1,0:T(8,128)(2,1)}, u32[]{:S(2)}, u32[]{:S(2)}) collective-permute-start(bf16[1040,128]{1,0:T(8,128)(2,1)S(1)} %fusion.1.refs_0_), channel_id=1, source_target_pairs={{0,16},{8,24},{16,0},{24,8},{1,17},{9,25},{17,1},{25,9},{2,18},{10... | collective-permute-start | bytes 798728 | tf_op jit(solution)/shard_map/ppermute | solution.py:26
  43.4 15.7 %collective-permute-start.7 = (bf16[1040,128]{1,0:T(8,128)(2,1)S(1)}, bf16[1040,128]{1,0:T(8,128)(2,1)}, u32[]{:S(2)}, u32[]{:S(2)}) collective-permute-start(bf16[1040,128]{1,0:T(8,128)(2,1)S(1)} %fusion.1.refs_0_), channel_id=1, source_target_pairs={{0,8},{8,16},{16,24},{24,0},{1,9},{9,17},{17,25},{25,1},{2,10},{10... | collective-permute-start | bytes 798728 | tf_op jit(solution)/shard_map/ppermute | solution.py:26
  55.0 35.3 %collective-permute-start.11 = (bf16[1024,512]{1,0:T(8,128)(2,1)S(1)}, bf16[1024,512]{1,0:T(8,128)(2,1)S(1)}, u32[]{:S(2)}, u32[]{:S(2)}) collective-permute-start(bf16[1024,512]{1,0:T(8,128)(2,1)S(1)} %bitcast.23), channel_id=1, source_target_pairs={{0,8},{8,16},{16,24},{24,0},{1,9},{9,17},{17,25},{25,1},{2,10},{10... | collective-permute-start | bytes 3145736 | tf_op jit(solution)/shard_map/ppermute | solution.py:26
  56.5 33.8 %collective-permute-start.12 = (bf16[1024,512]{1,0:T(8,128)(2,1)S(1)}, bf16[1024,512]{1,0:T(8,128)(2,1)S(1)}, u32[]{:S(2)}, u32[]{:S(2)}) collective-permute-start(bf16[1024,512]{1,0:T(8,128)(2,1)S(1)} %bitcast.24), channel_id=1, source_target_pairs={{0,24},{8,0},{16,8},{24,16},{1,25},{9,1},{17,9},{25,17},{2,26},{10... | collective-permute-start | bytes 3145736 | tf_op jit(solution)/shard_map/ppermute | solution.py:26
  57.0 37.1 %collective-permute-start.13 = (bf16[1024,512]{1,0:T(8,128)(2,1)S(1)}, bf16[1024,512]{1,0:T(8,128)(2,1)}, u32[]{:S(2)}, u32[]{:S(2)}) collective-permute-start(bf16[1024,512]{1,0:T(8,128)(2,1)S(1)} %bitcast.25), channel_id=1, source_target_pairs={{0,16},{8,24},{16,0},{24,8},{1,17},{9,25},{17,1},{25,9},{2,18},{10... | collective-permute-start | bytes 3145736 | tf_op jit(solution)/shard_map/ppermute | solution.py:26
  62.2 12.1 %collective-permute-start.8 = (bf16[64,4096]{1,0:T(8,128)(2,1)}, bf16[64,4096]{1,0:T(8,128)(2,1)}, u32[]{:S(2)}, u32[]{:S(2)}) collective-permute-start(bf16[64,4096]{1,0:T(8,128)(2,1)} %normalise.1.refs_0_), channel_id=1, source_target_pairs={{0,2},{2,4},{4,6},{6,0},{1,3},{3,5},{5,7},{7,1},{8,10},{10,12},{12... | collective-permute-start | bytes 1572872 | tf_op jit(solution)/shard_map/ppermute | solution.py:26
  64.2 5.0 %collective-permute-start.10 = (s32[64]{0:T(128)S(1)}, s32[64]{0:T(128)S(1)}, u32[]{:S(2)}, u32[]{:S(2)}) collective-permute-start(s32[64]{0:T(128)S(1)} %reshape.41), channel_id=1, source_target_pairs={{0,32},{32,64},{64,96},{96,128},{128,160},{160,192},{192,224},{224... | collective-permute-start | bytes 776 | tf_op jit(solution)/shard_map/ppermute | solution.py:26
  69.2 21.1 %collective-permute-start.9 = (bf16[64,4096]{1,0:T(8,128)(2,1)}, bf16[64,4096]{1,0:T(8,128)(2,1)}, u32[]{:S(2)}, u32[]{:S(2)}) collective-permute-start(bf16[64,4096]{1,0:T(8,128)(2,1)} %normalise.1.refs_0_), channel_id=1, source_target_pairs={{0,6},{2,0},{4,2},{6,4},{1,7},{3,1},{5,3},{7,5},{8,14},{10,8},{12,... | collective-permute-start | bytes 1572872 | tf_op jit(solution)/shard_map/ppermute | solution.py:26
  74.4 19.8 %collective-permute-start.14 = (bf16[64,4096]{1,0:T(8,128)(2,1)}, bf16[64,4096]{1,0:T(8,128)(2,1)}, u32[]{:S(2)}, u32[]{:S(2)}) collective-permute-start(bf16[64,4096]{1,0:T(8,128)(2,1)} %normalise.1.refs_0_), channel_id=1, source_target_pairs={{0,4},{2,6},{4,0},{6,2},{1,5},{3,7},{5,1},{7,3},{8,12},{10,14},{12... | collective-permute-start | bytes 1572872 | tf_op jit(solution)/shard_map/ppermute | solution.py:26
  98.8 4.2 %collective-permute-start.23 = (bf16[256,4096]{1,0:T(8,128)(2,1)S(1)}, bf16[256,4096]{1,0:T(8,128)(2,1)S(1)}, u32[]{:S(2)}, u32[]{:S(2)}) collective-permute-start(bf16[256,4096]{1,0:T(8,128)(2,1)S(1)} %get-tuple-element.66), channel_id=1, source_target_pairs={{0,1},{1,0},{2,3},{3,2},{4,5},{5,4},{6,7},{7,6},{8,9},{9,8},{10,11... | collective-permute-start | bytes 6291464 | tf_op jit(solution)/shard_map/ppermute | solution.py:26
  98.9 10.1 %collective-permute-start.15 = (bf16[256,512]{1,0:T(8,128)(2,1)S(1)}, bf16[256,512]{1,0:T(8,128)(2,1)S(1)}, u32[]{:S(2)}, u32[]{:S(2)}) collective-permute-start(bf16[256,512]{1,0:T(8,128)(2,1)S(1)} %get-tuple-element.65.refs_4_), channel_id=1, source_target_pairs={{0,32},{32,64},{64,96},{96,128},{128,160},{160,192},{192,224},{224... | collective-permute-start | bytes 786440 | tf_op jit(solution)/shard_map/ppermute | solution.py:26
  100.8 8.8 %collective-permute-start.16 = (bf16[256,512]{1,0:T(8,128)(2,1)S(1)}, bf16[256,512]{1,0:T(8,128)(2,1)S(1)}, u32[]{:S(2)}, u32[]{:S(2)}) collective-permute-start(bf16[256,512]{1,0:T(8,128)(2,1)S(1)} %get-tuple-element.65.refs_4_), channel_id=1, source_target_pairs={{0,224},{32,0},{64,32},{96,64},{128,96},{160,128},{192,160},{224,1... | collective-permute-start | bytes 786440 | tf_op jit(solution)/shard_map/ppermute | solution.py:26
  105.7 10.4 %collective-permute-start.24 = (bf16[256,512]{1,0:T(8,128)(2,1)S(1)}, bf16[256,512]{1,0:T(8,128)(2,1)S(1)}, u32[]{:S(2)}, u32[]{:S(2)}) collective-permute-start(bf16[256,512]{1,0:T(8,128)(2,1)S(1)} %memorise.3.refs_13_), channel_id=1, source_target_pairs={{0,32},{32,64},{64,96},{96,128},{128,160},{160,192},{192,224},{224... | collective-permute-start | bytes 786440 | tf_op jit(solution)/shard_map/ppermute | solution.py:26
  107.6 9.2 %collective-permute-start.25 = (bf16[256,512]{1,0:T(8,128)(2,1)S(1)}, bf16[256,512]{1,0:T(8,128)(2,1)S(1)}, u32[]{:S(2)}, u32[]{:S(2)}) collective-permute-start(bf16[256,512]{1,0:T(8,128)(2,1)S(1)} %memorise.3.refs_13_), channel_id=1, source_target_pairs={{0,224},{32,0},{64,32},{96,64},{128,96},{160,128},{192,160},{224,1... | collective-permute-start | bytes 786440 | tf_op jit(solution)/shard_map/ppermute | solution.py:26
  109.0 12.7 %collective-permute-start.17 = (bf16[256,512]{1,0:T(8,128)(2,1)S(1)}, bf16[256,512]{1,0:T(8,128)(2,1)S(1)}, u32[]{:S(2)}, u32[]{:S(2)}) collective-permute-start(bf16[256,512]{1,0:T(8,128)(2,1)S(1)} %collective-permute-done.15.refs_5_), channel_id=1, source_target_pairs={{0,32},{32,64},{64,96},{96,128},{128,160},{160,192},{192,224},{224... | collective-permute-start | bytes 786440 | tf_op jit(solution)/shard_map/ppermute | solution.py:26
  109.7 12.8 %collective-permute-start.18 = (bf16[256,512]{1,0:T(8,128)(2,1)S(1)}, bf16[256,512]{1,0:T(8,128)(2,1)S(1)}, u32[]{:S(2)}, u32[]{:S(2)}) collective-permute-start(bf16[256,512]{1,0:T(8,128)(2,1)S(1)} %collective-permute-done.16.refs_6_), channel_id=1, source_target_pairs={{0,224},{32,0},{64,32},{96,64},{128,96},{160,128},{192,160},{224,1... | collective-permute-start | bytes 786440 | tf_op jit(solution)/shard_map/ppermute | solution.py:26
  116.1 11.2 %collective-permute-start.26 = (bf16[256,512]{1,0:T(8,128)(2,1)S(1)}, bf16[256,512]{1,0:T(8,128)(2,1)S(1)}, u32[]{:S(2)}, u32[]{:S(2)}) collective-permute-start(bf16[256,512]{1,0:T(8,128)(2,1)S(1)} %collective-permute-done.24.refs_14_), channel_id=1, source_target_pairs={{0,32},{32,64},{64,96},{96,128},{128,160},{160,192},{192,224},{224... | collective-permute-start | bytes 786440 | tf_op jit(solution)/shard_map/ppermute | solution.py:26
  116.8 11.2 %collective-permute-start.27 = (bf16[256,512]{1,0:T(8,128)(2,1)S(1)}, bf16[256,512]{1,0:T(8,128)(2,1)S(1)}, u32[]{:S(2)}, u32[]{:S(2)}) collective-permute-start(bf16[256,512]{1,0:T(8,128)(2,1)S(1)} %collective-permute-done.25.refs_15_), channel_id=1, source_target_pairs={{0,224},{32,0},{64,32},{96,64},{128,96},{160,128},{192,160},{224,1... | collective-permute-start | bytes 786440 | tf_op jit(solution)/shard_map/ppermute | solution.py:26
  121.8 11.2 %collective-permute-start.19 = (bf16[256,512]{1,0:T(8,128)(2,1)S(1)}, bf16[256,512]{1,0:T(8,128)(2,1)S(1)}, u32[]{:S(2)}, u32[]{:S(2)}) collective-permute-start(bf16[256,512]{1,0:T(8,128)(2,1)S(1)} %collective-permute-done.17.refs_7_), channel_id=1, source_target_pairs={{0,32},{32,64},{64,96},{96,128},{128,160},{160,192},{192,224},{224... | collective-permute-start | bytes 786440 | tf_op jit(solution)/shard_map/ppermute | solution.py:26
  122.4 11.3 %collective-permute-start.20 = (bf16[256,512]{1,0:T(8,128)(2,1)S(1)}, bf16[256,512]{1,0:T(8,128)(2,1)S(1)}, u32[]{:S(2)}, u32[]{:S(2)}) collective-permute-start(bf16[256,512]{1,0:T(8,128)(2,1)S(1)} %collective-permute-done.18.refs_8_), channel_id=1, source_target_pairs={{0,224},{32,0},{64,32},{96,64},{128,96},{160,128},{192,160},{224,1... | collective-permute-start | bytes 786440 | tf_op jit(solution)/shard_map/ppermute | solution.py:26
  127.4 11.2 %collective-permute-start.28 = (bf16[256,512]{1,0:T(8,128)(2,1)S(1)}, bf16[256,512]{1,0:T(8,128)(2,1)S(1)}, u32[]{:S(2)}, u32[]{:S(2)}) collective-permute-start(bf16[256,512]{1,0:T(8,128)(2,1)S(1)} %collective-permute-done.26.refs_16_), channel_id=1, source_target_pairs={{0,32},{32,64},{64,96},{96,128},{128,160},{160,192},{192,224},{224... | collective-permute-start | bytes 786440 | tf_op jit(solution)/shard_map/ppermute | solution.py:26
  128.1 11.3 %collective-permute-start.29 = (bf16[256,512]{1,0:T(8,128)(2,1)S(1)}, bf16[256,512]{1,0:T(8,128)(2,1)S(1)}, u32[]{:S(2)}, u32[]{:S(2)}) collective-permute-start(bf16[256,512]{1,0:T(8,128)(2,1)S(1)} %collective-permute-done.27.refs_17_), channel_id=1, source_target_pairs={{0,224},{32,0},{64,32},{96,64},{128,96},{160,128},{192,160},{224,1... | collective-permute-start | bytes 786440 | tf_op jit(solution)/shard_map/ppermute | solution.py:26
  133.0 9.0 %collective-permute-start.21 = (bf16[128,512]{1,0:T(8,128)(2,1)S(1)}, bf16[128,512]{1,0:T(8,128)(2,1)S(1)}, u32[]{:S(2)}, u32[]{:S(2)}) collective-permute-start(bf16[128,512]{1,0:T(8,128)(2,1)S(1)} %slice.32), channel_id=1, source_target_pairs={{0,32},{32,64},{64,96},{96,128},{128,160},{160,192},{192,224},{224... | collective-permute-start | bytes 393224 | tf_op jit(solution)/shard_map/ppermute | solution.py:26
  133.7 8.3 %collective-permute-start.22 = (bf16[128,512]{1,0:T(8,128)(2,1)S(1)}, bf16[128,512]{1,0:T(8,128)(2,1)S(1)}, u32[]{:S(2)}, u32[]{:S(2)}) collective-permute-start(bf16[128,512]{1,0:T(8,128)(2,1)S(1)} %slice.33), channel_id=1, source_target_pairs={{0,224},{32,0},{64,32},{96,64},{128,96},{160,128},{192,160},{224,1... | collective-permute-start | bytes 393224 | tf_op jit(solution)/shard_map/ppermute | solution.py:26
  138.6 6.3 %collective-permute-start.30 = (bf16[128,512]{1,0:T(8,128)(2,1)S(1)}, bf16[128,512]{1,0:T(8,128)(2,1)S(1)}, u32[]{:S(2)}, u32[]{:S(2)}) collective-permute-start(bf16[128,512]{1,0:T(8,128)(2,1)S(1)} %slice.34), channel_id=1, source_target_pairs={{0,32},{32,64},{64,96},{96,128},{128,160},{160,192},{192,224},{224... | collective-permute-start | bytes 393224 | tf_op jit(solution)/shard_map/ppermute | solution.py:26
  139.4 5.5 %collective-permute-start.31 = (bf16[128,512]{1,0:T(8,128)(2,1)S(1)}, bf16[128,512]{1,0:T(8,128)(2,1)S(1)}, u32[]{:S(2)}, u32[]{:S(2)}) collective-permute-start(bf16[128,512]{1,0:T(8,128)(2,1)S(1)} %slice.35), channel_id=1, source_target_pairs={{0,224},{32,0},{64,32},{96,64},{128,96},{160,128},{192,160},{224,1... | collective-permute-start | bytes 393224 | tf_op jit(solution)/shard_map/ppermute | solution.py:26
  (26 other events, 345.5 us)

commit v7 on v6

--- a/solution.py
+++ b/solution.py
@@ -479,8 +479,8 @@
     terms = project(att_own, att_other, e_own, e_other)
 
     terms = [terms[0]] + [shifted(terms[k], "y", k) for k in range(1, NY)]
-    kv, terms[1], terms[3] = lax.optimization_barrier((kv, terms[1], terms[3]))
-    terms[2], qs = lax.optimization_barrier((terms[2], qs))
+    kv, terms[1] = lax.optimization_barrier((kv, terms[1]))
+    terms[2], terms[3], qs = lax.optimization_barrier((terms[2], terms[3], qs))
     got = jnp.stack([q[1024:1032, 0:2] for q in qs]).astype(jnp.int32).reshape(-1)
     below = shifted(got, "z", 1)
     from_left = shifted(kv, "x", 1)

time: 179 us -> 179 us (level)
  starting transfers between devices: 64.7 us -> 66.9 us
    ppermute x32, starting transfers between devices: 56.2 us -> 58.4 us  [shifted(): return lax.ppermute(value, axis, [(i, (i + steps) % n) for i in range(n)])]
    unnamed x50 -> x48, local copies, waits for them, and re-layouts: 4.5 us -> 3.67 us
  transfers between devices with their start and end apart: 33 -> 33, of which waited for: 14 -> 15; matrix products, arithmetic and copies ran while one was open for 3% -> 3% of each run, Pallas kernels for 13% -> 13%
where the time goes in v7:
time: 179 us; the launch traced here: 176 us
  starting transfers between devices  66.9 us (37%)
  waiting for transfers between devices  44.9 us (25%)
  Pallas kernels  34.8 us (19%)
  blocking collectives  19.8 us (11%)
  local copies, waits for them, and re-layouts  7.81 us (4%)
    ppermute x32, starting transfers between devices, shifted(): return lax.ppermute(value, axis, [(i, (i + steps) % n) for i in range(n)])  58.4 us
    ppermute x32, waiting for transfers between devices, shifted(): return lax.ppermute(value, axis, [(i, (i + steps) % n) for i in range(n)])  44.9 us
    all_to_all x1, blocking collectives, on_device(): parts = lax.all_to_all(parts, 'x', split_axis=0, concat_axis=0, tiled=True)  19.8 us
    pallas_call x1, Pallas kernels, encode(): pl.pallas_call(encoder_kernel, grid_spec=pltpu.PrefetchScalarGridSpec(num...  9.48 us
    all_to_all x1, starting transfers between devices, spread(): return lax.all_to_all(copies, axis, split_axis=0, concat_axis=0, tiled=True)  8.47 us
    pallas_call x1, Pallas kernels, windows(): pl.pallas_call(functools.partial(window_kernel, layout), in_specs=[smem]...  7.47 us
    pallas_call x2, Pallas kernels, memorise(): pl.pallas_call(functools.partial(memory_kernel, len(us)), in_specs=[pl.Bl...  6.25 us
    pallas_call x1, Pallas kernels, project(): pl.pallas_call(project_kernel, grid=(width // cols,), in_specs=[pl.BlockS...  4.95 us
  transfers between devices with their start and end apart: 33, of which 15 were waited for; matrix products, arithmetic and copies ran while one was open for 3% of the time, Pallas kernels for 13%

profile of v7, /device:TPU:2, one launch (start us, length us, event | category | flops | bytes accessed | tf_op | source)
XLA Modules:
  0.0 176.0 jit_solution(566819795785733113)
XLA Ops:
  2.0 8.5 %all-to-all-start = ((bf16[8,128,512]{2,1,0:T(8,128)(2,1)}), bf16[8,128,512]{2,1,0:T(8,128)(2,1)S(1)}, u32[]{:S(2)}, u32[]{:S(2)}) async-start(bf16[8,128,512]{2,1,0:T(8,128)(2,1)} %broadcast_in_dim.2), calls=%async_computation | async-start | bytes 2097152 | tf_op jit(solution)/shard_map/all_to_all | solution.py:32
  10.5 9.5 %encoder.1 = (bf16[256,256]{1,0:T(8,128)(2,1)}, bf16[256,256]{1,0:T(8,128)(2,1)}) custom-call(s32[1]{0:T(128)} %bitcast.1.core_ref, s32[1]{0:T(128)} %bitcast.2.y_ref, bf16[512,4096]{1,0:T(8,128)(2,1)} %bitcast.28, bf16[24576,128]{1,0:T(8,128)(2,1)} %bitcast.34, f32[1,4096]{1,0:T(1,128)} %bitcast.35), custom_call_target="tpu_custom_call" | custom-call | flops 3221225472 | bytes 10485760 | tf_op jit(solution)/shard_map/encoder/pallas_call | solution.py:94
  22.9 5.0 %project.1 = (bf16[64,4096]{1,0:T(8,128)(2,1)}, bf16[64,4096]{1,0:T(8,128)(2,1)}, bf16[64,4096]{1,0:T(8,128)(2,1)}, bf16[64,4096]{1,0:T(8,128)(2,1)}) custom-call(bf16[256,256]{1,0:T(8,128)(2,1)} %get-tuple-element.36.a_ref, bf16[256,256]{1,0:T(8,128)(2,1)} %copy-done.22, bf16[256,4096]{1,0:T(8,128)(2,1)} %bitcast.31, bf16[256,4096]{1,0:T(8,128)(2,1)} %copy-done.3), custom_call_target="tpu_custom_call" | custom-call | flops 1073741824 | bytes 4194304 | tf_op jit(solution)/shard_map/project/pallas_call | solution.py:134
  29.5 2.9 %collective-permute-start.3 = (bf16[64,4096]{1,0:T(8,128)(2,1)}, bf16[64,4096]{1,0:T(8,128)(2,1)}, u32[]{:S(2)}, u32[]{:S(2)}) collective-permute-start(bf16[64,4096]{1,0:T(8,128)(2,1)} %get-tuple-element.42), channel_id=1, source_target_pairs={{0,4},{2,6},{4,0},{6,2},{1,5},{3,7},{5,1},{7,3},{8,12},{10,14},{12... | collective-permute-start | bytes 1572872 | tf_op jit(solution)/shard_map/ppermute | solution.py:26
  35.4 2.4 %collective-permute-start.6 = (bf16[1040,128]{1,0:T(8,128)(2,1)S(1)}, bf16[1040,128]{1,0:T(8,128)(2,1)}, u32[]{:S(2)}, u32[]{:S(2)}) collective-permute-start(bf16[1040,128]{1,0:T(8,128)(2,1)S(1)} %fusion.1.refs_0_), channel_id=1, source_target_pairs={{0,16},{8,24},{16,0},{24,8},{1,17},{9,25},{17,1},{25,9},{2,18},{10... | collective-permute-start | bytes 798728 | tf_op jit(solution)/shard_map/ppermute | solution.py:26
  37.8 5.6 %collective-permute-done.2.t1 = bf16[64,4096]{1,0:T(8,128)(2,1)S(1)} collective-permute-done((bf16[64,4096]{1,0:T(8,128)(2,1)}, bf16[64,4096]{1,0:T(8,128)(2,1)S(1)}, u32[]{:S(2)}, u32[]{:S(2)}) %collective-permute-start.2) | collective-permute-done | bytes 524320 | tf_op jit(solution)/shard_map/ppermute | solution.py:26
  46.2 3.1 %collective-permute-done.6.refs_2_ = bf16[1040,128]{1,0:T(8,128)(2,1)} collective-permute-done((bf16[1040,128]{1,0:T(8,128)(2,1)S(1)}, bf16[1040,128]{1,0:T(8,128)(2,1)}, u32[]{:S(2)}, u32[]{:S(2)}) %collective-permute-start.6) | collective-permute-done | bytes 266272 | tf_op jit(solution)/shard_map/ppermute | solution.py:26
  49.3 3.6 %collective-permute-done.7.refs_3_ = bf16[1040,128]{1,0:T(8,128)(2,1)} collective-permute-done((bf16[1040,128]{1,0:T(8,128)(2,1)S(1)}, bf16[1040,128]{1,0:T(8,128)(2,1)}, u32[]{:S(2)}, u32[]{:S(2)}) %collective-permute-start.7) | collective-permute-done | bytes 266272 | tf_op jit(solution)/shard_map/ppermute | solution.py:26
  52.9 2.1 %collective-permute-start.13 = (bf16[1024,512]{1,0:T(8,128)(2,1)S(1)}, bf16[1024,512]{1,0:T(8,128)(2,1)}, u32[]{:S(2)}, u32[]{:S(2)}) collective-permute-start(bf16[1024,512]{1,0:T(8,128)(2,1)S(1)} %bitcast.25), channel_id=1, source_target_pairs={{0,16},{8,24},{16,0},{24,8},{1,17},{9,25},{17,1},{25,9},{2,18},{10... | collective-permute-start | bytes 3145736 | tf_op jit(solution)/shard_map/ppermute | solution.py:26
  56.0 3.1 %normalise.1.refs_0_ = bf16[64,4096]{1,0:T(8,128)(2,1)} custom-call(s32[1]{0:T(128)} %bitcast.block_ref, bf16[64,4096]{1,0:T(8,128)(2,1)} %get-tuple-element.39.t0, bf16[64,4096]{1,0:T(8,128)(2,1)} %copy-done.9, bf16[64,4096]{1,0:T(8,128)(2,1)} %collective-permute-done.3.t2, bf16[64,4096]{1,0:T(8,128)(2,1)} %collective-permute-done.4.t3, ...), custom_call_target="tpu_custom_call" | custom-call | flops 2097152 | bytes 3145728 | tf_op jit(solution)/shard_map/normalise/pallas_call | solution.py:168
  62.3 2.2 %collective-permute-start.10 = (s32[64]{0:T(128)S(1)}, s32[64]{0:T(128)S(1)}, u32[]{:S(2)}, u32[]{:S(2)}) collective-permute-start(s32[64]{0:T(128)S(1)} %reshape.41), channel_id=1, source_target_pairs={{0,32},{32,64},{64,96},{96,128},{128,160},{160,192},{192,224},{224... | collective-permute-start | bytes 776 | tf_op jit(solution)/shard_map/ppermute | solution.py:26
  64.5 2.8 %collective-permute-done.10 = s32[64]{0:T(128)S(1)} collective-permute-done((s32[64]{0:T(128)S(1)}, s32[64]{0:T(128)S(1)}, u32[]{:S(2)}, u32[]{:S(2)}) %collective-permute-start.10) | collective-permute-done | bytes 288 | tf_op jit(solution)/shard_map/ppermute | solution.py:26
  69.3 4.5 %collective-permute-done.8.refs_1_ = bf16[64,4096]{1,0:T(8,128)(2,1)} collective-permute-done((bf16[64,4096]{1,0:T(8,128)(2,1)}, bf16[64,4096]{1,0:T(8,128)(2,1)}, u32[]{:S(2)}, u32[]{:S(2)}) %collective-permute-start.8) | collective-permute-done | bytes 524320 | tf_op jit(solution)/shard_map/ppermute | solution.py:26
  73.8 12.5 %collective-permute-start.14 = (bf16[64,4096]{1,0:T(8,128)(2,1)}, bf16[64,4096]{1,0:T(8,128)(2,1)}, u32[]{:S(2)}, u32[]{:S(2)}) collective-permute-start(bf16[64,4096]{1,0:T(8,128)(2,1)} %normalise.1.refs_0_), channel_id=1, source_target_pairs={{0,4},{2,6},{4,0},{6,2},{1,5},{3,7},{5,1},{7,3},{8,12},{10,14},{12... | collective-permute-start | bytes 1572872 | tf_op jit(solution)/shard_map/ppermute | solution.py:26
  87.0 2.1 %plan.1 = (s32[128]{0:T(128)}, s32[128]{0:T(128)}, s32[2]{0:T(128)}) custom-call(s32[128]{0:T(128)} %pad_add_fusion.ids_ref, s32[1]{0:T(128)} %bitcast.15.z_ref, s32[1]{0:T(128)} %bitcast.16.x_ref, s32[1]{0:T(128)} %bitcast.1.core_ref), custom_call_target="tpu_custom_call" | custom-call | tf_op jit(solution)/shard_map/plan/pallas_call | solution.py:307
  89.2 6.1 %collective-permute-done.12.refs_6_.refs_3_ = bf16[1024,512]{1,0:T(8,128)(2,1)S(1)} collective-permute-done((bf16[1024,512]{1,0:T(8,128)(2,1)S(1)}, bf16[1024,512]{1,0:T(8,128)(2,1)S(1)}, u32[]{:S(2)}, u32[]{:S(2)}) %collective-permute-start.12) | collective-permute-done | bytes 1048608 | tf_op jit(solution)/shard_map/ppermute | solution.py:26
  96.4 3.6 %memorise.2 = (bf16[256,512]{1,0:T(8,128)(2,1)S(1)}, bf16[256,4096]{1,0:T(8,128)(2,1)S(1)}) custom-call(s32[2]{0:T(128)S(1)} %pad_add_fusion.1.at_ref, bf16[64,4096]{1,0:T(8,128)(2,1)S(1)} %copy-done, bf16[64,4096]{1,0:T(8,128)(2,1)} %collective-permute-done.8.refs_1_, bf16[64,4096]{1,0:T(8,128)(2,1)} %collective-permute-done.14.refs_2_, ...), custom_call_target="tpu_custom_call" | custom-call | flops 1073741824 | bytes 4194304 | tf_op jit(solution)/shard_map/memorise/pallas_call | solution.py:229
  104.2 2.6 %memorise.3.refs_13_ = bf16[256,512]{1,0:T(8,128)(2,1)S(1)} custom-call(s32[2]{0:T(128)S(1)} %pad_add_fusion.1.at_ref, bf16[256,4096]{1,0:T(8,128)(2,1)S(1)} %collective-permute-done.23.refs_0_, bf16[1024,512]{1,0:T(8,128)(2,1)S(1)} %bitcast.27, bf16[1024,512]{1,0:T(8,128)(2,1)S(1)} %collective-permute-done.11.refs_5_.refs_2_, ...), custom_call_target="tpu_custom_call" | custom-call | flops 1073741824 | bytes 4194304 | tf_op jit(solution)/shard_map/memorise/pallas_call | solution.py:229
  110.9 2.6 %collective-permute-start.18 = (bf16[256,512]{1,0:T(8,128)(2,1)S(1)}, bf16[256,512]{1,0:T(8,128)(2,1)S(1)}, u32[]{:S(2)}, u32[]{:S(2)}) collective-permute-start(bf16[256,512]{1,0:T(8,128)(2,1)S(1)} %collective-permute-done.16.refs_6_), channel_id=1, source_target_pairs={{0,224},{32,0},{64,32},{96,64},{128,96},{160,128},{192,160},{224,1... | collective-permute-start | bytes 786440 | tf_op jit(solution)/shard_map/ppermute | solution.py:26
  113.5 3.9 %collective-permute-done.24.refs_14_ = bf16[256,512]{1,0:T(8,128)(2,1)S(1)} collective-permute-done((bf16[256,512]{1,0:T(8,128)(2,1)S(1)}, bf16[256,512]{1,0:T(8,128)(2,1)S(1)}, u32[]{:S(2)}, u32[]{:S(2)}) %collective-permute-start.24) | collective-permute-done | bytes 262176 | tf_op jit(solution)/shard_map/ppermute | solution.py:26
  118.0 2.6 %collective-permute-start.27 = (bf16[256,512]{1,0:T(8,128)(2,1)S(1)}, bf16[256,512]{1,0:T(8,128)(2,1)S(1)}, u32[]{:S(2)}, u32[]{:S(2)}) collective-permute-start(bf16[256,512]{1,0:T(8,128)(2,1)S(1)} %collective-permute-done.25.refs_15_), channel_id=1, source_target_pairs={{0,224},{32,0},{64,32},{96,64},{128,96},{160,128},{192,160},{224,1... | collective-permute-start | bytes 786440 | tf_op jit(solution)/shard_map/ppermute | solution.py:26
  120.6 2.3 %collective-permute-done.17.refs_7_ = bf16[256,512]{1,0:T(8,128)(2,1)S(1)} collective-permute-done((bf16[256,512]{1,0:T(8,128)(2,1)S(1)}, bf16[256,512]{1,0:T(8,128)(2,1)S(1)}, u32[]{:S(2)}, u32[]{:S(2)}) %collective-permute-start.17) | collective-permute-done | bytes 262176 | tf_op jit(solution)/shard_map/ppermute | solution.py:26
  123.7 2.6 %collective-permute-start.20 = (bf16[256,512]{1,0:T(8,128)(2,1)S(1)}, bf16[256,512]{1,0:T(8,128)(2,1)S(1)}, u32[]{:S(2)}, u32[]{:S(2)}) collective-permute-start(bf16[256,512]{1,0:T(8,128)(2,1)S(1)} %collective-permute-done.18.refs_8_), channel_id=1, source_target_pairs={{0,224},{32,0},{64,32},{96,64},{128,96},{160,128},{192,160},{224,1... | collective-permute-start | bytes 786440 | tf_op jit(solution)/shard_map/ppermute | solution.py:26
  126.2 2.3 %collective-permute-done.26.refs_16_ = bf16[256,512]{1,0:T(8,128)(2,1)S(1)} collective-permute-done((bf16[256,512]{1,0:T(8,128)(2,1)S(1)}, bf16[256,512]{1,0:T(8,128)(2,1)S(1)}, u32[]{:S(2)}, u32[]{:S(2)}) %collective-permute-start.26) | collective-permute-done | bytes 262176 | tf_op jit(solution)/shard_map/ppermute | solution.py:26
  129.3 2.6 %collective-permute-start.29 = (bf16[256,512]{1,0:T(8,128)(2,1)S(1)}, bf16[256,512]{1,0:T(8,128)(2,1)S(1)}, u32[]{:S(2)}, u32[]{:S(2)}) collective-permute-start(bf16[256,512]{1,0:T(8,128)(2,1)S(1)} %collective-permute-done.27.refs_17_), channel_id=1, source_target_pairs={{0,224},{32,0},{64,32},{96,64},{128,96},{160,128},{192,160},{224,1... | collective-permute-start | bytes 786440 | tf_op jit(solution)/shard_map/ppermute | solution.py:26
  131.8 2.3 %collective-permute-done.19.refs_9_ = bf16[256,512]{1,0:T(8,128)(2,1)S(1)} collective-permute-done((bf16[256,512]{1,0:T(8,128)(2,1)S(1)}, bf16[256,512]{1,0:T(8,128)(2,1)S(1)}, u32[]{:S(2)}, u32[]{:S(2)}) %collective-permute-start.19) | collective-permute-done | bytes 262176 | tf_op jit(solution)/shard_map/ppermute | solution.py:26
  135.0 2.6 %collective-permute-start.22 = (bf16[128,512]{1,0:T(8,128)(2,1)S(1)}, bf16[128,512]{1,0:T(8,128)(2,1)S(1)}, u32[]{:S(2)}, u32[]{:S(2)}) collective-permute-start(bf16[128,512]{1,0:T(8,128)(2,1)S(1)} %slice.33), channel_id=1, source_target_pairs={{0,224},{32,0},{64,32},{96,64},{128,96},{160,128},{192,160},{224,1... | collective-permute-start | bytes 393224 | tf_op jit(solution)/shard_map/ppermute | solution.py:26
  137.6 2.2 %collective-permute-done.28.refs_18_ = bf16[256,512]{1,0:T(8,128)(2,1)S(1)} collective-permute-done((bf16[256,512]{1,0:T(8,128)(2,1)S(1)}, bf16[256,512]{1,0:T(8,128)(2,1)S(1)}, u32[]{:S(2)}, u32[]{:S(2)}) %collective-permute-start.28) | collective-permute-done | bytes 262176 | tf_op jit(solution)/shard_map/ppermute | solution.py:26
  140.6 2.6 %collective-permute-start.31 = (bf16[128,512]{1,0:T(8,128)(2,1)S(1)}, bf16[128,512]{1,0:T(8,128)(2,1)S(1)}, u32[]{:S(2)}, u32[]{:S(2)}) collective-permute-start(bf16[128,512]{1,0:T(8,128)(2,1)S(1)} %slice.35), channel_id=1, source_target_pairs={{0,224},{32,0},{64,32},{96,64},{128,96},{160,128},{192,160},{224,1... | collective-permute-start | bytes 393224 | tf_op jit(solution)/shard_map/ppermute | solution.py:26
  143.2 2.8 %collective-permute-done.30.refs_20_ = bf16[128,512]{1,0:T(8,128)(2,1)S(1)} collective-permute-done((bf16[128,512]{1,0:T(8,128)(2,1)S(1)}, bf16[128,512]{1,0:T(8,128)(2,1)S(1)}, u32[]{:S(2)}, u32[]{:S(2)}) %collective-permute-start.30) | collective-permute-done | bytes 131104 | tf_op jit(solution)/shard_map/ppermute | solution.py:26
  147.4 7.5 %windows.1 = bf16[4,1056,128]{2,1,0:T(8,128)(2,1)} custom-call(s32[128]{0:T(128)} %get-tuple-element.56.one_list, s32[128]{0:T(128)} %get-tuple-element.57.two_list, s32[2]{0:T(128)} %get-tuple-element.58.counts_ref, s32[1]{0:T(128)} %bitcast.16.x_ref, bf16[1040,128]{1,0:T(8,128)(2,1)} %copy-done.4, bf16[1040,128]{1,0:T(8,128)(2,1)} %collective-permute-done.5.refs_1_, ...), custom_call_target="tpu_custom_call" | custom-call | flops 1000000000 | bytes 8388608 | tf_op jit(solution)/shard_map/windows/pallas_call | solution.py:406
  154.9 19.8 %all_to_all.10.parts_ref = bf16[4,1056,128]{2,1,0:T(8,128)(2,1)S(1)} all-to-all(bf16[4,1056,128]{2,1,0:T(8,128)(2,1)} %windows.1), channel_id=1, replica_groups=mesh['z'=8,'x'=4,'y'=4,'c'=2] {'x'}, dimensions={0} | all-to-all | bytes 2162688 | tf_op jit(solution)/shard_map/all_to_all | solution.py:503
  (111 shorter events, 34.8 us)
Async XLA Ops:
  0.0 21.5 %collective-permute-start.1 = (bf16[256,4096]{1,0:T(8,128)(2,1)}, bf16[256,4096]{1,0:T(8,128)(2,1)S(1)}, u32[]{:S(2)}, u32[]{:S(2)}) collective-permute-start(bf16[256,4096]{1,0:T(8,128)(2,1)} %bitcast.30), channel_id=1, source_target_pairs={{0,1},{1,0},{2,3},{3,2},{4,5},{5,4},{6,7},{7,6},{8,9},{9,8},{10,11... | collective-permute-start | bytes 6291464 | tf_op jit(solution)/shard_map/ppermute | solution.py:26
  2.0 42.9 %all-to-all-start = ((bf16[8,128,512]{2,1,0:T(8,128)(2,1)}), bf16[8,128,512]{2,1,0:T(8,128)(2,1)S(1)}, u32[]{:S(2)}, u32[]{:S(2)}) async-start(bf16[8,128,512]{2,1,0:T(8,128)(2,1)} %broadcast_in_dim.2), calls=%async_computation | async-start | bytes 2097152 | tf_op jit(solution)/shard_map/all_to_all | solution.py:32
  27.9 15.5 %collective-permute-start.2 = (bf16[64,4096]{1,0:T(8,128)(2,1)}, bf16[64,4096]{1,0:T(8,128)(2,1)S(1)}, u32[]{:S(2)}, u32[]{:S(2)}) collective-permute-start(bf16[64,4096]{1,0:T(8,128)(2,1)} %get-tuple-element.40), channel_id=1, source_target_pairs={{0,2},{2,4},{4,6},{6,0},{1,3},{3,5},{5,7},{7,1},{8,10},{10,12},{12... | collective-permute-start | bytes 1572872 | tf_op jit(solution)/shard_map/ppermute | solution.py:26
  29.5 26.5 %collective-permute-start.3 = (bf16[64,4096]{1,0:T(8,128)(2,1)}, bf16[64,4096]{1,0:T(8,128)(2,1)}, u32[]{:S(2)}, u32[]{:S(2)}) collective-permute-start(bf16[64,4096]{1,0:T(8,128)(2,1)} %get-tuple-element.42), channel_id=1, source_target_pairs={{0,4},{2,6},{4,0},{6,2},{1,5},{3,7},{5,1},{7,3},{8,12},{10,14},{12... | collective-permute-start | bytes 1572872 | tf_op jit(solution)/shard_map/ppermute | solution.py:26
  32.4 23.6 %collective-permute-start.4 = (bf16[64,4096]{1,0:T(8,128)(2,1)}, bf16[64,4096]{1,0:T(8,128)(2,1)}, u32[]{:S(2)}, u32[]{:S(2)}) collective-permute-start(bf16[64,4096]{1,0:T(8,128)(2,1)} %get-tuple-element.43), channel_id=1, source_target_pairs={{0,6},{2,0},{4,2},{6,4},{1,7},{3,1},{5,3},{7,5},{8,14},{10,8},{12,... | collective-permute-start | bytes 1572872 | tf_op jit(solution)/shard_map/ppermute | solution.py:26
  34.8 10.1 %collective-permute-start.5 = (bf16[1040,128]{1,0:T(8,128)(2,1)S(1)}, bf16[1040,128]{1,0:T(8,128)(2,1)}, u32[]{:S(2)}, u32[]{:S(2)}) collective-permute-start(bf16[1040,128]{1,0:T(8,128)(2,1)S(1)} %fusion.1.refs_0_), channel_id=1, source_target_pairs={{0,24},{8,0},{16,8},{24,16},{1,25},{9,1},{17,9},{25,17},{2,26},{10... | collective-permute-start | bytes 798728 | tf_op jit(solution)/shard_map/ppermute | solution.py:26
  35.4 13.9 %collective-permute-start.6 = (bf16[1040,128]{1,0:T(8,128)(2,1)S(1)}, bf16[1040,128]{1,0:T(8,128)(2,1)}, u32[]{:S(2)}, u32[]{:S(2)}) collective-permute-start(bf16[1040,128]{1,0:T(8,128)(2,1)S(1)} %fusion.1.refs_0_), channel_id=1, source_target_pairs={{0,16},{8,24},{16,0},{24,8},{1,17},{9,25},{17,1},{25,9},{2,18},{10... | collective-permute-start | bytes 798728 | tf_op jit(solution)/shard_map/ppermute | solution.py:26
  43.4 9.4 %collective-permute-start.7 = (bf16[1040,128]{1,0:T(8,128)(2,1)S(1)}, bf16[1040,128]{1,0:T(8,128)(2,1)}, u32[]{:S(2)}, u32[]{:S(2)}) collective-permute-start(bf16[1040,128]{1,0:T(8,128)(2,1)S(1)} %fusion.1.refs_0_), channel_id=1, source_target_pairs={{0,8},{8,16},{16,24},{24,0},{1,9},{9,17},{17,25},{25,1},{2,10},{10... | collective-permute-start | bytes 798728 | tf_op jit(solution)/shard_map/ppermute | solution.py:26
  44.9 44.2 %collective-permute-start.11 = (bf16[1024,512]{1,0:T(8,128)(2,1)S(1)}, bf16[1024,512]{1,0:T(8,128)(2,1)S(1)}, u32[]{:S(2)}, u32[]{:S(2)}) collective-permute-start(bf16[1024,512]{1,0:T(8,128)(2,1)S(1)} %bitcast.23), channel_id=1, source_target_pairs={{0,8},{8,16},{16,24},{24,0},{1,9},{9,17},{17,25},{25,1},{2,10},{10... | collective-permute-start | bytes 3145736 | tf_op jit(solution)/shard_map/ppermute | solution.py:26
  49.3 46.0 %collective-permute-start.12 = (bf16[1024,512]{1,0:T(8,128)(2,1)S(1)}, bf16[1024,512]{1,0:T(8,128)(2,1)S(1)}, u32[]{:S(2)}, u32[]{:S(2)}) collective-permute-start(bf16[1024,512]{1,0:T(8,128)(2,1)S(1)} %bitcast.24), channel_id=1, source_target_pairs={{0,24},{8,0},{16,8},{24,16},{1,25},{9,1},{17,9},{25,17},{2,26},{10... | collective-permute-start | bytes 3145736 | tf_op jit(solution)/shard_map/ppermute | solution.py:26
  52.9 42.4 %collective-permute-start.13 = (bf16[1024,512]{1,0:T(8,128)(2,1)S(1)}, bf16[1024,512]{1,0:T(8,128)(2,1)}, u32[]{:S(2)}, u32[]{:S(2)}) collective-permute-start(bf16[1024,512]{1,0:T(8,128)(2,1)S(1)} %bitcast.25), channel_id=1, source_target_pairs={{0,16},{8,24},{16,0},{24,8},{1,17},{9,25},{17,1},{25,9},{2,18},{10... | collective-permute-start | bytes 3145736 | tf_op jit(solution)/shard_map/ppermute | solution.py:26
  59.1 14.8 %collective-permute-start.8 = (bf16[64,4096]{1,0:T(8,128)(2,1)}, bf16[64,4096]{1,0:T(8,128)(2,1)}, u32[]{:S(2)}, u32[]{:S(2)}) collective-permute-start(bf16[64,4096]{1,0:T(8,128)(2,1)} %normalise.1.refs_0_), channel_id=1, source_target_pairs={{0,2},{2,4},{4,6},{6,0},{1,3},{3,5},{5,7},{7,1},{8,10},{10,12},{12... | collective-permute-start | bytes 1572872 | tf_op jit(solution)/shard_map/ppermute | solution.py:26
  62.3 5.0 %collective-permute-start.10 = (s32[64]{0:T(128)S(1)}, s32[64]{0:T(128)S(1)}, u32[]{:S(2)}, u32[]{:S(2)}) collective-permute-start(s32[64]{0:T(128)S(1)} %reshape.41), channel_id=1, source_target_pairs={{0,32},{32,64},{64,96},{96,128},{128,160},{160,192},{192,224},{224... | collective-permute-start | bytes 776 | tf_op jit(solution)/shard_map/ppermute | solution.py:26
  67.3 21.9 %collective-permute-start.9 = (bf16[64,4096]{1,0:T(8,128)(2,1)}, bf16[64,4096]{1,0:T(8,128)(2,1)}, u32[]{:S(2)}, u32[]{:S(2)}) collective-permute-start(bf16[64,4096]{1,0:T(8,128)(2,1)} %normalise.1.refs_0_), channel_id=1, source_target_pairs={{0,6},{2,0},{4,2},{6,4},{1,7},{3,1},{5,3},{7,5},{8,14},{10,8},{12,... | collective-permute-start | bytes 1572872 | tf_op jit(solution)/shard_map/ppermute | solution.py:26
  73.8 21.5 %collective-permute-start.14 = (bf16[64,4096]{1,0:T(8,128)(2,1)}, bf16[64,4096]{1,0:T(8,128)(2,1)}, u32[]{:S(2)}, u32[]{:S(2)}) collective-permute-start(bf16[64,4096]{1,0:T(8,128)(2,1)} %normalise.1.refs_0_), channel_id=1, source_target_pairs={{0,4},{2,6},{4,0},{6,2},{1,5},{3,7},{5,1},{7,3},{8,12},{10,14},{12... | collective-permute-start | bytes 1572872 | tf_op jit(solution)/shard_map/ppermute | solution.py:26
  100.0 4.2 %collective-permute-start.23 = (bf16[256,4096]{1,0:T(8,128)(2,1)S(1)}, bf16[256,4096]{1,0:T(8,128)(2,1)S(1)}, u32[]{:S(2)}, u32[]{:S(2)}) collective-permute-start(bf16[256,4096]{1,0:T(8,128)(2,1)S(1)} %get-tuple-element.66), channel_id=1, source_target_pairs={{0,1},{1,0},{2,3},{3,2},{4,5},{5,4},{6,7},{7,6},{8,9},{9,8},{10,11... | collective-permute-start | bytes 6291464 | tf_op jit(solution)/shard_map/ppermute | solution.py:26
  100.1 10.1 %collective-permute-start.15 = (bf16[256,512]{1,0:T(8,128)(2,1)S(1)}, bf16[256,512]{1,0:T(8,128)(2,1)S(1)}, u32[]{:S(2)}, u32[]{:S(2)}) collective-permute-start(bf16[256,512]{1,0:T(8,128)(2,1)S(1)} %get-tuple-element.65.refs_4_), channel_id=1, source_target_pairs={{0,32},{32,64},{64,96},{96,128},{128,160},{160,192},{192,224},{224... | collective-permute-start | bytes 786440 | tf_op jit(solution)/shard_map/ppermute | solution.py:26
  102.0 8.8 %collective-permute-start.16 = (bf16[256,512]{1,0:T(8,128)(2,1)S(1)}, bf16[256,512]{1,0:T(8,128)(2,1)S(1)}, u32[]{:S(2)}, u32[]{:S(2)}) collective-permute-start(bf16[256,512]{1,0:T(8,128)(2,1)S(1)} %get-tuple-element.65.refs_4_), channel_id=1, source_target_pairs={{0,224},{32,0},{64,32},{96,64},{128,96},{160,128},{192,160},{224,1... | collective-permute-start | bytes 786440 | tf_op jit(solution)/shard_map/ppermute | solution.py:26
  106.9 10.4 %collective-permute-start.24 = (bf16[256,512]{1,0:T(8,128)(2,1)S(1)}, bf16[256,512]{1,0:T(8,128)(2,1)S(1)}, u32[]{:S(2)}, u32[]{:S(2)}) collective-permute-start(bf16[256,512]{1,0:T(8,128)(2,1)S(1)} %memorise.3.refs_13_), channel_id=1, source_target_pairs={{0,32},{32,64},{64,96},{96,128},{128,160},{160,192},{192,224},{224... | collective-permute-start | bytes 786440 | tf_op jit(solution)/shard_map/ppermute | solution.py:26
  108.8 9.2 %collective-permute-start.25 = (bf16[256,512]{1,0:T(8,128)(2,1)S(1)}, bf16[256,512]{1,0:T(8,128)(2,1)S(1)}, u32[]{:S(2)}, u32[]{:S(2)}) collective-permute-start(bf16[256,512]{1,0:T(8,128)(2,1)S(1)} %memorise.3.refs_13_), channel_id=1, source_target_pairs={{0,224},{32,0},{64,32},{96,64},{128,96},{160,128},{192,160},{224,1... | collective-permute-start | bytes 786440 | tf_op jit(solution)/shard_map/ppermute | solution.py:26
  110.2 12.7 %collective-permute-start.17 = (bf16[256,512]{1,0:T(8,128)(2,1)S(1)}, bf16[256,512]{1,0:T(8,128)(2,1)S(1)}, u32[]{:S(2)}, u32[]{:S(2)}) collective-permute-start(bf16[256,512]{1,0:T(8,128)(2,1)S(1)} %collective-permute-done.15.refs_5_), channel_id=1, source_target_pairs={{0,32},{32,64},{64,96},{96,128},{128,160},{160,192},{192,224},{224... | collective-permute-start | bytes 786440 | tf_op jit(solution)/shard_map/ppermute | solution.py:26
  110.9 12.8 %collective-permute-start.18 = (bf16[256,512]{1,0:T(8,128)(2,1)S(1)}, bf16[256,512]{1,0:T(8,128)(2,1)S(1)}, u32[]{:S(2)}, u32[]{:S(2)}) collective-permute-start(bf16[256,512]{1,0:T(8,128)(2,1)S(1)} %collective-permute-done.16.refs_6_), channel_id=1, source_target_pairs={{0,224},{32,0},{64,32},{96,64},{128,96},{160,128},{192,160},{224,1... | collective-permute-start | bytes 786440 | tf_op jit(solution)/shard_map/ppermute | solution.py:26
  117.3 11.2 %collective-permute-start.26 = (bf16[256,512]{1,0:T(8,128)(2,1)S(1)}, bf16[256,512]{1,0:T(8,128)(2,1)S(1)}, u32[]{:S(2)}, u32[]{:S(2)}) collective-permute-start(bf16[256,512]{1,0:T(8,128)(2,1)S(1)} %collective-permute-done.24.refs_14_), channel_id=1, source_target_pairs={{0,32},{32,64},{64,96},{96,128},{128,160},{160,192},{192,224},{224... | collective-permute-start | bytes 786440 | tf_op jit(solution)/shard_map/ppermute | solution.py:26
  118.0 11.2 %collective-permute-start.27 = (bf16[256,512]{1,0:T(8,128)(2,1)S(1)}, bf16[256,512]{1,0:T(8,128)(2,1)S(1)}, u32[]{:S(2)}, u32[]{:S(2)}) collective-permute-start(bf16[256,512]{1,0:T(8,128)(2,1)S(1)} %collective-permute-done.25.refs_15_), channel_id=1, source_target_pairs={{0,224},{32,0},{64,32},{96,64},{128,96},{160,128},{192,160},{224,1... | collective-permute-start | bytes 786440 | tf_op jit(solution)/shard_map/ppermute | solution.py:26
  122.9 11.2 %collective-permute-start.19 = (bf16[256,512]{1,0:T(8,128)(2,1)S(1)}, bf16[256,512]{1,0:T(8,128)(2,1)S(1)}, u32[]{:S(2)}, u32[]{:S(2)}) collective-permute-start(bf16[256,512]{1,0:T(8,128)(2,1)S(1)} %collective-permute-done.17.refs_7_), channel_id=1, source_target_pairs={{0,32},{32,64},{64,96},{96,128},{128,160},{160,192},{192,224},{224... | collective-permute-start | bytes 786440 | tf_op jit(solution)/shard_map/ppermute | solution.py:26
  123.7 11.3 %collective-permute-start.20 = (bf16[256,512]{1,0:T(8,128)(2,1)S(1)}, bf16[256,512]{1,0:T(8,128)(2,1)S(1)}, u32[]{:S(2)}, u32[]{:S(2)}) collective-permute-start(bf16[256,512]{1,0:T(8,128)(2,1)S(1)} %collective-permute-done.18.refs_8_), channel_id=1, source_target_pairs={{0,224},{32,0},{64,32},{96,64},{128,96},{160,128},{192,160},{224,1... | collective-permute-start | bytes 786440 | tf_op jit(solution)/shard_map/ppermute | solution.py:26
  128.6 11.2 %collective-permute-start.28 = (bf16[256,512]{1,0:T(8,128)(2,1)S(1)}, bf16[256,512]{1,0:T(8,128)(2,1)S(1)}, u32[]{:S(2)}, u32[]{:S(2)}) collective-permute-start(bf16[256,512]{1,0:T(8,128)(2,1)S(1)} %collective-permute-done.26.refs_16_), channel_id=1, source_target_pairs={{0,32},{32,64},{64,96},{96,128},{128,160},{160,192},{192,224},{224... | collective-permute-start | bytes 786440 | tf_op jit(solution)/shard_map/ppermute | solution.py:26
  129.3 11.3 %collective-permute-start.29 = (bf16[256,512]{1,0:T(8,128)(2,1)S(1)}, bf16[256,512]{1,0:T(8,128)(2,1)S(1)}, u32[]{:S(2)}, u32[]{:S(2)}) collective-permute-start(bf16[256,512]{1,0:T(8,128)(2,1)S(1)} %collective-permute-done.27.refs_17_), channel_id=1, source_target_pairs={{0,224},{32,0},{64,32},{96,64},{128,96},{160,128},{192,160},{224,1... | collective-permute-start | bytes 786440 | tf_op jit(solution)/shard_map/ppermute | solution.py:26
  134.2 9.0 %collective-permute-start.21 = (bf16[128,512]{1,0:T(8,128)(2,1)S(1)}, bf16[128,512]{1,0:T(8,128)(2,1)S(1)}, u32[]{:S(2)}, u32[]{:S(2)}) collective-permute-start(bf16[128,512]{1,0:T(8,128)(2,1)S(1)} %slice.32), channel_id=1, source_target_pairs={{0,32},{32,64},{64,96},{96,128},{128,160},{160,192},{192,224},{224... | collective-permute-start | bytes 393224 | tf_op jit(solution)/shard_map/ppermute | solution.py:26
  135.0 8.3 %collective-permute-start.22 = (bf16[128,512]{1,0:T(8,128)(2,1)S(1)}, bf16[128,512]{1,0:T(8,128)(2,1)S(1)}, u32[]{:S(2)}, u32[]{:S(2)}) collective-permute-start(bf16[128,512]{1,0:T(8,128)(2,1)S(1)} %slice.33), channel_id=1, source_target_pairs={{0,224},{32,0},{64,32},{96,64},{128,96},{160,128},{192,160},{224,1... | collective-permute-start | bytes 393224 | tf_op jit(solution)/shard_map/ppermute | solution.py:26
  139.8 6.3 %collective-permute-start.30 = (bf16[128,512]{1,0:T(8,128)(2,1)S(1)}, bf16[128,512]{1,0:T(8,128)(2,1)S(1)}, u32[]{:S(2)}, u32[]{:S(2)}) collective-permute-start(bf16[128,512]{1,0:T(8,128)(2,1)S(1)} %slice.34), channel_id=1, source_target_pairs={{0,32},{32,64},{64,96},{96,128},{128,160},{160,192},{192,224},{224... | collective-permute-start | bytes 393224 | tf_op jit(solution)/shard_map/ppermute | solution.py:26
  140.6 5.5 %collective-permute-start.31 = (bf16[128,512]{1,0:T(8,128)(2,1)S(1)}, bf16[128,512]{1,0:T(8,128)(2,1)S(1)}, u32[]{:S(2)}, u32[]{:S(2)}) collective-permute-start(bf16[128,512]{1,0:T(8,128)(2,1)S(1)} %slice.35), channel_id=1, source_target_pairs={{0,224},{32,0},{64,32},{96,64},{128,96},{160,128},{192,160},{224,1... | collective-permute-start | bytes 393224 | tf_op jit(solution)/shard_map/ppermute | solution.py:26
  (25 other events, 333.4 us)

commit v8 on v5

--- a/solution.py
+++ b/solution.py
@@ -496,14 +496,13 @@
 
     u = normalise(terms, corpus_flat, gain_out.reshape(1, width), as_index(core * NY + my_y))
     us = [u] + [shifted(u, "y", k) for k in range(1, NY)]
-    us[1], us[3], from_left, from_right, below = lax.optimization_barrier(
-        (us[1], us[3], from_left, from_right, below)
-    )
-    ids = jnp.concatenate([got, below])
+    lists = plan(jnp.concatenate([got, below]), as_index(my_z), as_index(my_x), as_index(core))
+    us[1], from_left, from_right = lax.optimization_barrier((us[1], from_left, from_right))
     half = kv.shape[0] // 2
     far_top = shifted(from_left[:half], "x", 1)
     far_bottom = shifted(from_right[half:], "x", -1)
     weights = [kv, from_left, from_right, far_top, far_bottom]
+    us[1], us[3], lists, weights = lax.optimization_barrier((us[1], us[3], lists, weights))
     at = as_index(my_x, my_y)
     memory_own, u_own = memorise(at, us, weights)
     u_other = shifted(u_own, "c", 1)
@@ -511,7 +510,6 @@
     (memory_other,) = memorise(at, [u_other], weights)
     pieces += ring_pieces(memory_other, 2 * ROW)
 
-    lists = plan(ids, as_index(my_z), as_index(my_x), as_index(core))
     parts = windows(lists, as_index(my_x), qs, pieces)
     parts = lax.all_to_all(parts, "x", split_axis=0, concat_axis=0, tiled=True)
     return combine(parts).reshape(512, 2, HS)

time: 182 us -> 178 us (0.978); the launches traced: 181 us -> 175 us
  waiting for transfers between devices: 57.7 us -> 54.9 us
  blocking collectives: 19 us -> 16.3 us
    ppermute x33, waiting for transfers between devices: 57.7 us -> 54.9 us  [shifted(): return lax.ppermute(value, axis, [(i, (i + steps) % n) for i in range(n)])]
    all_to_all x1, blocking collectives: 19 us -> 16.3 us  [on_device(): parts = lax.all_to_all(parts, 'x', split_axis=0, concat_axis=0, tiled=True)]
    unnamed x58 -> x56, local copies, waits for them, and re-layouts: 3.93 us -> 4.48 us
  transfers between devices with their start and end apart: 34 -> 34, of which waited for: 15 -> 14; matrix products, arithmetic and copies ran while one was open for 5% -> 4% of each run, Pallas kernels for 12% -> 13%
where the time goes in v8:
time: 178 us; the launch traced here: 175 us
  starting transfers between devices  56.6 us (32%)
  waiting for transfers between devices  54.9 us (31%)
  Pallas kernels  34.7 us (19%)
  blocking collectives  16.3 us (9%)
  local copies, waits for them, and re-layouts  10.3 us (6%)
    ppermute x33, waiting for transfers between devices, shifted(): return lax.ppermute(value, axis, [(i, (i + steps) % n) for i in range(n)])  54.9 us
    ppermute x33, starting transfers between devices, shifted(): return lax.ppermute(value, axis, [(i, (i + steps) % n) for i in range(n)])  48.1 us
    all_to_all x1, blocking collectives, on_device(): parts = lax.all_to_all(parts, 'x', split_axis=0, concat_axis=0, tiled=True)  16.3 us
    pallas_call x1, Pallas kernels, encode(): pl.pallas_call(encoder_kernel, grid_spec=pltpu.PrefetchScalarGridSpec(num...  9.48 us
    all_to_all x1, starting transfers between devices, spread(): return lax.all_to_all(copies, axis, split_axis=0, concat_axis=0, tiled=True)  8.47 us
    pallas_call x1, Pallas kernels, windows(): pl.pallas_call(functools.partial(window_kernel, layout), in_specs=[smem]...  7.4 us
    pallas_call x2, Pallas kernels, memorise(): pl.pallas_call(functools.partial(memory_kernel, len(us)), in_specs=[pl.Bl...  6.24 us
    pallas_call x1, Pallas kernels, project(): pl.pallas_call(project_kernel, grid=(width // cols,), in_specs=[pl.BlockS...  4.95 us
  transfers between devices with their start and end apart: 34, of which 14 were waited for; matrix products, arithmetic and copies ran while one was open for 4% of the time, Pallas kernels for 13%

profile of v8, /device:TPU:2, one launch (start us, length us, event | category | flops | bytes accessed | tf_op | source)
XLA Modules:
  0.0 174.8 jit_solution(9537226793443142920)
XLA Ops:
  2.0 8.5 %all-to-all-start = ((bf16[8,128,512]{2,1,0:T(8,128)(2,1)}), bf16[8,128,512]{2,1,0:T(8,128)(2,1)S(1)}, u32[]{:S(2)}, u32[]{:S(2)}) async-start(bf16[8,128,512]{2,1,0:T(8,128)(2,1)} %broadcast_in_dim.2), calls=%async_computation | async-start | bytes 2097152 | tf_op jit(solution)/shard_map/all_to_all | solution.py:32
  10.5 9.5 %encoder.1 = (bf16[256,256]{1,0:T(8,128)(2,1)}, bf16[256,256]{1,0:T(8,128)(2,1)}) custom-call(s32[1]{0:T(128)} %bitcast.1.core_ref, s32[1]{0:T(128)} %bitcast.2.y_ref, bf16[512,4096]{1,0:T(8,128)(2,1)} %bitcast.27, bf16[24576,128]{1,0:T(8,128)(2,1)} %bitcast.33, f32[1,4096]{1,0:T(1,128)} %bitcast.34), custom_call_target="tpu_custom_call" | custom-call | flops 3221225472 | bytes 10485760 | tf_op jit(solution)/shard_map/encoder/pallas_call | solution.py:94
  22.9 4.9 %project.1 = (bf16[64,4096]{1,0:T(8,128)(2,1)}, bf16[64,4096]{1,0:T(8,128)(2,1)}, bf16[64,4096]{1,0:T(8,128)(2,1)}, bf16[64,4096]{1,0:T(8,128)(2,1)}) custom-call(bf16[256,256]{1,0:T(8,128)(2,1)} %get-tuple-element.39.a_ref, bf16[256,256]{1,0:T(8,128)(2,1)} %copy-done.26, bf16[256,4096]{1,0:T(8,128)(2,1)} %bitcast.30, bf16[256,4096]{1,0:T(8,128)(2,1)} %copy-done.3), custom_call_target="tpu_custom_call" | custom-call | flops 1073741824 | bytes 4194304 | tf_op jit(solution)/shard_map/project/pallas_call | solution.py:134
  32.8 2.4 %collective-permute-start.5 = (bf16[1040,128]{1,0:T(8,128)(2,1)S(1)}, bf16[1040,128]{1,0:T(8,128)(2,1)S(1)}, u32[]{:S(2)}, u32[]{:S(2)}) collective-permute-start(bf16[1040,128]{1,0:T(8,128)(2,1)S(1)} %fusion.1.refs_0_), channel_id=1, source_target_pairs={{0,16},{8,24},{16,0},{24,8},{1,17},{9,25},{17,1},{25,9},{2,18},{10... | collective-permute-start | bytes 798728 | tf_op jit(solution)/shard_map/ppermute | solution.py:26
  37.0 3.6 %collective-permute-done.4.refs_1_ = bf16[1040,128]{1,0:T(8,128)(2,1)S(1)} collective-permute-done((bf16[1040,128]{1,0:T(8,128)(2,1)S(1)}, bf16[1040,128]{1,0:T(8,128)(2,1)S(1)}, u32[]{:S(2)}, u32[]{:S(2)}) %collective-permute-start.4) | collective-permute-done | bytes 266272 | tf_op jit(solution)/shard_map/ppermute | solution.py:26
  40.6 2.0 %collective-permute-start.7 = (bf16[64,4096]{1,0:T(8,128)(2,1)}, bf16[64,4096]{1,0:T(8,128)(2,1)}, u32[]{:S(2)}, u32[]{:S(2)}) collective-permute-start(bf16[64,4096]{1,0:T(8,128)(2,1)} %get-tuple-element.48), channel_id=1, source_target_pairs={{0,4},{2,6},{4,0},{6,2},{1,5},{3,7},{5,1},{7,3},{8,12},{10,14},{12... | collective-permute-start | bytes 1572872 | tf_op jit(solution)/shard_map/ppermute | solution.py:26
  42.6 4.4 %collective-permute-done.5.refs_2_ = bf16[1040,128]{1,0:T(8,128)(2,1)S(1)} collective-permute-done((bf16[1040,128]{1,0:T(8,128)(2,1)S(1)}, bf16[1040,128]{1,0:T(8,128)(2,1)S(1)}, u32[]{:S(2)}, u32[]{:S(2)}) %collective-permute-start.5) | collective-permute-done | bytes 266272 | tf_op jit(solution)/shard_map/ppermute | solution.py:26
  47.9 6.2 %collective-permute-done.3.t3 = bf16[64,4096]{1,0:T(8,128)(2,1)S(1)} collective-permute-done((bf16[64,4096]{1,0:T(8,128)(2,1)}, bf16[64,4096]{1,0:T(8,128)(2,1)S(1)}, u32[]{:S(2)}, u32[]{:S(2)}) %collective-permute-start.3) | collective-permute-done | bytes 524320 | tf_op jit(solution)/shard_map/ppermute | solution.py:26
  55.0 2.0 %collective-permute-start.9 = (bf16[1024,512]{1,0:T(8,128)(2,1)S(1)}, bf16[1024,512]{1,0:T(8,128)(2,1)S(1)}, u32[]{:S(2)}, u32[]{:S(2)}) collective-permute-start(bf16[1024,512]{1,0:T(8,128)(2,1)S(1)} %bitcast.24), channel_id=1, source_target_pairs={{0,8},{8,16},{16,24},{24,0},{1,9},{9,17},{17,25},{25,1},{2,10},{10... | collective-permute-start | bytes 3145736 | tf_op jit(solution)/shard_map/ppermute | solution.py:26
  57.0 3.1 %normalise.1.refs_0_ = bf16[64,4096]{1,0:T(8,128)(2,1)} custom-call(s32[1]{0:T(128)} %bitcast.block_ref, bf16[64,4096]{1,0:T(8,128)(2,1)} %get-tuple-element.42.t0, bf16[64,4096]{1,0:T(8,128)(2,1)} %copy-done.9, bf16[64,4096]{1,0:T(8,128)(2,1)} %collective-permute-done.7.t2, bf16[64,4096]{1,0:T(8,128)(2,1)} %copy-done.10, bf16[512,4096]{1,0:T(8,128)(2,1)} %bitcast.28, ...), custom_call_target="tpu_custom_call" | custom-call | flops 2097152 | bytes 3145728 | tf_op jit(solution)/shard_map/normalise/pallas_call | solution.py:168
  60.3 3.6 %collective-permute-start.11 = (bf16[64,4096]{1,0:T(8,128)(2,1)}, bf16[64,4096]{1,0:T(8,128)(2,1)}, u32[]{:S(2)}, u32[]{:S(2)}) collective-permute-start(bf16[64,4096]{1,0:T(8,128)(2,1)} %normalise.1.refs_0_), channel_id=1, source_target_pairs={{0,6},{2,0},{4,2},{6,4},{1,7},{3,1},{5,3},{7,5},{8,14},{10,8},{12,... | collective-permute-start | bytes 1572872 | tf_op jit(solution)/shard_map/ppermute | solution.py:26
  65.5 18.8 %collective-permute-done.8.refs_1_ = bf16[64,4096]{1,0:T(8,128)(2,1)} collective-permute-done((bf16[64,4096]{1,0:T(8,128)(2,1)}, bf16[64,4096]{1,0:T(8,128)(2,1)}, u32[]{:S(2)}, u32[]{:S(2)}) %collective-permute-start.8) | collective-permute-done | bytes 524320 | tf_op jit(solution)/shard_map/ppermute | solution.py:26
  92.0 2.9 %collective-permute-done.12 = s32[64]{0:T(128)S(1)} collective-permute-done((s32[64]{0:T(128)S(1)}, s32[64]{0:T(128)S(1)}, u32[]{:S(2)}, u32[]{:S(2)}) %collective-permute-start.12) | collective-permute-done | bytes 288 | tf_op jit(solution)/shard_map/ppermute | solution.py:26
  95.5 2.1 %plan.1 = (s32[128]{0:T(128)}, s32[128]{0:T(128)}, s32[2]{0:T(128)}) custom-call(s32[128]{0:T(128)} %pad_add_fusion.ids_ref, s32[1]{0:T(128)} %bitcast.15.z_ref, s32[1]{0:T(128)} %bitcast.16.x_ref, s32[1]{0:T(128)} %bitcast.1.core_ref), custom_call_target="tpu_custom_call" | custom-call | tf_op jit(solution)/shard_map/plan/pallas_call | solution.py:316
  98.7 3.6 %memorise.2 = (bf16[256,512]{1,0:T(8,128)(2,1)S(1)}, bf16[256,4096]{1,0:T(8,128)(2,1)S(1)}) custom-call(s32[2]{0:T(128)S(1)} %pad_add_fusion.1.at_ref, bf16[64,4096]{1,0:T(8,128)(2,1)S(1)} %copy-done, bf16[64,4096]{1,0:T(8,128)(2,1)} %collective-permute-done.8.refs_1_, bf16[64,4096]{1,0:T(8,128)(2,1)} %collective-permute-done.15.refs_2_, ...), custom_call_target="tpu_custom_call" | custom-call | flops 1073741824 | bytes 4194304 | tf_op jit(solution)/shard_map/memorise/pallas_call | solution.py:238
  103.2 2.6 %collective-permute-start.17 = (bf16[256,512]{1,0:T(8,128)(2,1)S(1)}, bf16[256,512]{1,0:T(8,128)(2,1)S(1)}, u32[]{:S(2)}, u32[]{:S(2)}) collective-permute-start(bf16[256,512]{1,0:T(8,128)(2,1)S(1)} %get-tuple-element.71.refs_4_), channel_id=1, source_target_pairs={{0,224},{32,0},{64,32},{96,64},{128,96},{160,128},{192,160},{224,1... | collective-permute-start | bytes 786440 | tf_op jit(solution)/shard_map/ppermute | solution.py:26
  106.6 2.6 %memorise.3.refs_13_ = bf16[256,512]{1,0:T(8,128)(2,1)S(1)} custom-call(s32[2]{0:T(128)S(1)} %pad_add_fusion.1.at_ref, bf16[256,4096]{1,0:T(8,128)(2,1)S(1)} %collective-permute-done.24.refs_0_, bf16[1024,512]{1,0:T(8,128)(2,1)S(1)} %bitcast.26, bf16[1024,512]{1,0:T(8,128)(2,1)S(1)} %collective-permute-done.9.refs_5_.refs_2_, ...), custom_call_target="tpu_custom_call" | custom-call | flops 1073741824 | bytes 4194304 | tf_op jit(solution)/shard_map/memorise/pallas_call | solution.py:238
  110.0 2.6 %collective-permute-start.26 = (bf16[256,512]{1,0:T(8,128)(2,1)S(1)}, bf16[256,512]{1,0:T(8,128)(2,1)S(1)}, u32[]{:S(2)}, u32[]{:S(2)}) collective-permute-start(bf16[256,512]{1,0:T(8,128)(2,1)S(1)} %memorise.3.refs_13_), channel_id=1, source_target_pairs={{0,224},{32,0},{64,32},{96,64},{128,96},{160,128},{192,160},{224,1... | collective-permute-start | bytes 786440 | tf_op jit(solution)/shard_map/ppermute | solution.py:26
  112.6 3.2 %collective-permute-start.19 = (bf16[256,512]{1,0:T(8,128)(2,1)S(1)}, bf16[256,512]{1,0:T(8,128)(2,1)S(1)}, u32[]{:S(2)}, u32[]{:S(2)}) collective-permute-start(bf16[256,512]{1,0:T(8,128)(2,1)S(1)} %collective-permute-done.17.refs_6_), channel_id=1, source_target_pairs={{0,224},{32,0},{64,32},{96,64},{128,96},{160,128},{192,160},{224,1... | collective-permute-start | bytes 786440 | tf_op jit(solution)/shard_map/ppermute | solution.py:26
  115.8 3.9 %collective-permute-done.25.refs_14_ = bf16[256,512]{1,0:T(8,128)(2,1)S(1)} collective-permute-done((bf16[256,512]{1,0:T(8,128)(2,1)S(1)}, bf16[256,512]{1,0:T(8,128)(2,1)S(1)}, u32[]{:S(2)}, u32[]{:S(2)}) %collective-permute-start.25) | collective-permute-done | bytes 262176 | tf_op jit(solution)/shard_map/ppermute | solution.py:26
  119.7 3.3 %collective-permute-start.28 = (bf16[256,512]{1,0:T(8,128)(2,1)S(1)}, bf16[256,512]{1,0:T(8,128)(2,1)S(1)}, u32[]{:S(2)}, u32[]{:S(2)}) collective-permute-start(bf16[256,512]{1,0:T(8,128)(2,1)S(1)} %collective-permute-done.26.refs_15_), channel_id=1, source_target_pairs={{0,224},{32,0},{64,32},{96,64},{128,96},{160,128},{192,160},{224,1... | collective-permute-start | bytes 786440 | tf_op jit(solution)/shard_map/ppermute | solution.py:26
  123.0 2.3 %collective-permute-done.18.refs_7_ = bf16[256,512]{1,0:T(8,128)(2,1)S(1)} collective-permute-done((bf16[256,512]{1,0:T(8,128)(2,1)S(1)}, bf16[256,512]{1,0:T(8,128)(2,1)S(1)}, u32[]{:S(2)}, u32[]{:S(2)}) %collective-permute-start.18) | collective-permute-done | bytes 262176 | tf_op jit(solution)/shard_map/ppermute | solution.py:26
  125.3 3.3 %collective-permute-start.21 = (bf16[256,512]{1,0:T(8,128)(2,1)S(1)}, bf16[256,512]{1,0:T(8,128)(2,1)S(1)}, u32[]{:S(2)}, u32[]{:S(2)}) collective-permute-start(bf16[256,512]{1,0:T(8,128)(2,1)S(1)} %collective-permute-done.19.refs_8_), channel_id=1, source_target_pairs={{0,224},{32,0},{64,32},{96,64},{128,96},{160,128},{192,160},{224,1... | collective-permute-start | bytes 786440 | tf_op jit(solution)/shard_map/ppermute | solution.py:26
  128.6 2.3 %collective-permute-done.27.refs_16_ = bf16[256,512]{1,0:T(8,128)(2,1)S(1)} collective-permute-done((bf16[256,512]{1,0:T(8,128)(2,1)S(1)}, bf16[256,512]{1,0:T(8,128)(2,1)S(1)}, u32[]{:S(2)}, u32[]{:S(2)}) %collective-permute-start.27) | collective-permute-done | bytes 262176 | tf_op jit(solution)/shard_map/ppermute | solution.py:26
  130.9 3.3 %collective-permute-start.30 = (bf16[256,512]{1,0:T(8,128)(2,1)S(1)}, bf16[256,512]{1,0:T(8,128)(2,1)S(1)}, u32[]{:S(2)}, u32[]{:S(2)}) collective-permute-start(bf16[256,512]{1,0:T(8,128)(2,1)S(1)} %collective-permute-done.28.refs_17_), channel_id=1, source_target_pairs={{0,224},{32,0},{64,32},{96,64},{128,96},{160,128},{192,160},{224,1... | collective-permute-start | bytes 786440 | tf_op jit(solution)/shard_map/ppermute | solution.py:26
  134.2 2.3 %collective-permute-done.20.refs_9_ = bf16[256,512]{1,0:T(8,128)(2,1)S(1)} collective-permute-done((bf16[256,512]{1,0:T(8,128)(2,1)S(1)}, bf16[256,512]{1,0:T(8,128)(2,1)S(1)}, u32[]{:S(2)}, u32[]{:S(2)}) %collective-permute-start.20) | collective-permute-done | bytes 262176 | tf_op jit(solution)/shard_map/ppermute | solution.py:26
  136.7 3.3 %collective-permute-start.23 = (bf16[128,512]{1,0:T(8,128)(2,1)S(1)}, bf16[128,512]{1,0:T(8,128)(2,1)S(1)}, u32[]{:S(2)}, u32[]{:S(2)}) collective-permute-start(bf16[128,512]{1,0:T(8,128)(2,1)S(1)} %slice.41), channel_id=1, source_target_pairs={{0,224},{32,0},{64,32},{96,64},{128,96},{160,128},{192,160},{224,1... | collective-permute-start | bytes 393224 | tf_op jit(solution)/shard_map/ppermute | solution.py:26
  140.0 2.2 %collective-permute-done.29.refs_18_ = bf16[256,512]{1,0:T(8,128)(2,1)S(1)} collective-permute-done((bf16[256,512]{1,0:T(8,128)(2,1)S(1)}, bf16[256,512]{1,0:T(8,128)(2,1)S(1)}, u32[]{:S(2)}, u32[]{:S(2)}) %collective-permute-start.29) | collective-permute-done | bytes 262176 | tf_op jit(solution)/shard_map/ppermute | solution.py:26
  142.3 3.3 %collective-permute-start.32 = (bf16[128,512]{1,0:T(8,128)(2,1)S(1)}, bf16[128,512]{1,0:T(8,128)(2,1)S(1)}, u32[]{:S(2)}, u32[]{:S(2)}) collective-permute-start(bf16[128,512]{1,0:T(8,128)(2,1)S(1)} %slice.43), channel_id=1, source_target_pairs={{0,224},{32,0},{64,32},{96,64},{128,96},{160,128},{192,160},{224,1... | collective-permute-start | bytes 393224 | tf_op jit(solution)/shard_map/ppermute | solution.py:26
  145.6 2.8 %collective-permute-done.31.refs_20_ = bf16[128,512]{1,0:T(8,128)(2,1)S(1)} collective-permute-done((bf16[128,512]{1,0:T(8,128)(2,1)S(1)}, bf16[128,512]{1,0:T(8,128)(2,1)S(1)}, u32[]{:S(2)}, u32[]{:S(2)}) %collective-permute-start.31) | collective-permute-done | bytes 131104 | tf_op jit(solution)/shard_map/ppermute | solution.py:26
  149.8 7.4 %windows.1 = bf16[4,1056,128]{2,1,0:T(8,128)(2,1)} custom-call(s32[128]{0:T(128)} %get-tuple-element.61.one_list, s32[128]{0:T(128)} %get-tuple-element.62.two_list, s32[2]{0:T(128)} %get-tuple-element.63.counts_ref, s32[1]{0:T(128)} %bitcast.16.x_ref, bf16[1040,128]{1,0:T(8,128)(2,1)} %copy-done.4, bf16[1040,128]{1,0:T(8,128)(2,1)} %copy-done.11, ...), custom_call_target="tpu_custom_call" | custom-call | flops 1000000000 | bytes 8388608 | tf_op jit(solution)/shard_map/windows/pallas_call | solution.py:415
  157.2 16.3 %all_to_all.10.parts_ref = bf16[4,1056,128]{2,1,0:T(8,128)(2,1)S(1)} all-to-all(bf16[4,1056,128]{2,1,0:T(8,128)(2,1)} %windows.1), channel_id=1, replica_groups=mesh['z'=8,'x'=4,'y'=4,'c'=2] {'x'}, dimensions={0} | all-to-all | bytes 2162688 | tf_op jit(solution)/shard_map/all_to_all | solution.py:514
  (123 shorter events, 29.9 us)
Async XLA Ops:
  0.0 21.5 %collective-permute-start.1 = (bf16[256,4096]{1,0:T(8,128)(2,1)}, bf16[256,4096]{1,0:T(8,128)(2,1)S(1)}, u32[]{:S(2)}, u32[]{:S(2)}) collective-permute-start(bf16[256,4096]{1,0:T(8,128)(2,1)} %bitcast.29), channel_id=1, source_target_pairs={{0,1},{1,0},{2,3},{3,2},{4,5},{5,4},{6,7},{7,6},{8,9},{9,8},{10,11... | collective-permute-start | bytes 6291464 | tf_op jit(solution)/shard_map/ppermute | solution.py:26
  2.0 45.9 %all-to-all-start = ((bf16[8,128,512]{2,1,0:T(8,128)(2,1)}), bf16[8,128,512]{2,1,0:T(8,128)(2,1)S(1)}, u32[]{:S(2)}, u32[]{:S(2)}) async-start(bf16[8,128,512]{2,1,0:T(8,128)(2,1)} %broadcast_in_dim.2), calls=%async_computation | async-start | bytes 2097152 | tf_op jit(solution)/shard_map/all_to_all | solution.py:32
  27.9 20.1 %collective-permute-start.2 = (bf16[64,4096]{1,0:T(8,128)(2,1)}, bf16[64,4096]{1,0:T(8,128)(2,1)S(1)}, u32[]{:S(2)}, u32[]{:S(2)}) collective-permute-start(bf16[64,4096]{1,0:T(8,128)(2,1)} %get-tuple-element.43), channel_id=1, source_target_pairs={{0,2},{2,4},{4,6},{6,0},{1,3},{3,5},{5,7},{7,1},{8,10},{10,12},{12... | collective-permute-start | bytes 1572872 | tf_op jit(solution)/shard_map/ppermute | solution.py:26
  29.4 24.7 %collective-permute-start.3 = (bf16[64,4096]{1,0:T(8,128)(2,1)}, bf16[64,4096]{1,0:T(8,128)(2,1)S(1)}, u32[]{:S(2)}, u32[]{:S(2)}) collective-permute-start(bf16[64,4096]{1,0:T(8,128)(2,1)} %get-tuple-element.44), channel_id=1, source_target_pairs={{0,6},{2,0},{4,2},{6,4},{1,7},{3,1},{5,3},{7,5},{8,14},{10,8},{12,... | collective-permute-start | bytes 1572872 | tf_op jit(solution)/shard_map/ppermute | solution.py:26
  32.2 8.4 %collective-permute-start.4 = (bf16[1040,128]{1,0:T(8,128)(2,1)S(1)}, bf16[1040,128]{1,0:T(8,128)(2,1)S(1)}, u32[]{:S(2)}, u32[]{:S(2)}) collective-permute-start(bf16[1040,128]{1,0:T(8,128)(2,1)S(1)} %fusion.1.refs_0_), channel_id=1, source_target_pairs={{0,24},{8,0},{16,8},{24,16},{1,25},{9,1},{17,9},{25,17},{2,26},{10... | collective-permute-start | bytes 798728 | tf_op jit(solution)/shard_map/ppermute | solution.py:26
  32.8 14.2 %collective-permute-start.5 = (bf16[1040,128]{1,0:T(8,128)(2,1)S(1)}, bf16[1040,128]{1,0:T(8,128)(2,1)S(1)}, u32[]{:S(2)}, u32[]{:S(2)}) collective-permute-start(bf16[1040,128]{1,0:T(8,128)(2,1)S(1)} %fusion.1.refs_0_), channel_id=1, source_target_pairs={{0,16},{8,24},{16,0},{24,8},{1,17},{9,25},{17,1},{25,9},{2,18},{10... | collective-permute-start | bytes 798728 | tf_op jit(solution)/shard_map/ppermute | solution.py:26
  35.2 12.7 %collective-permute-start.6 = (bf16[1040,128]{1,0:T(8,128)(2,1)S(1)}, bf16[1040,128]{1,0:T(8,128)(2,1)S(1)}, u32[]{:S(2)}, u32[]{:S(2)}) collective-permute-start(bf16[1040,128]{1,0:T(8,128)(2,1)S(1)} %fusion.1.refs_0_), channel_id=1, source_target_pairs={{0,8},{8,16},{16,24},{24,0},{1,9},{9,17},{17,25},{25,1},{2,10},{10... | collective-permute-start | bytes 798728 | tf_op jit(solution)/shard_map/ppermute | solution.py:26
  40.6 16.4 %collective-permute-start.7 = (bf16[64,4096]{1,0:T(8,128)(2,1)}, bf16[64,4096]{1,0:T(8,128)(2,1)}, u32[]{:S(2)}, u32[]{:S(2)}) collective-permute-start(bf16[64,4096]{1,0:T(8,128)(2,1)} %get-tuple-element.48), channel_id=1, source_target_pairs={{0,4},{2,6},{4,0},{6,2},{1,5},{3,7},{5,1},{7,3},{8,12},{10,14},{12... | collective-permute-start | bytes 1572872 | tf_op jit(solution)/shard_map/ppermute | solution.py:26
  54.9 29.4 %collective-permute-start.10 = (bf16[1024,512]{1,0:T(8,128)(2,1)S(1)}, bf16[1024,512]{1,0:T(8,128)(2,1)S(1)}, u32[]{:S(2)}, u32[]{:S(2)}) collective-permute-start(bf16[1024,512]{1,0:T(8,128)(2,1)S(1)} %bitcast.23), channel_id=1, source_target_pairs={{0,24},{8,0},{16,8},{24,16},{1,25},{9,1},{17,9},{25,17},{2,26},{10... | collective-permute-start | bytes 3145736 | tf_op jit(solution)/shard_map/ppermute | solution.py:26
  55.0 29.3 %collective-permute-start.9 = (bf16[1024,512]{1,0:T(8,128)(2,1)S(1)}, bf16[1024,512]{1,0:T(8,128)(2,1)S(1)}, u32[]{:S(2)}, u32[]{:S(2)}) collective-permute-start(bf16[1024,512]{1,0:T(8,128)(2,1)S(1)} %bitcast.24), channel_id=1, source_target_pairs={{0,8},{8,16},{16,24},{24,0},{1,9},{9,17},{17,25},{25,1},{2,10},{10... | collective-permute-start | bytes 3145736 | tf_op jit(solution)/shard_map/ppermute | solution.py:26
  60.2 24.2 %collective-permute-start.8 = (bf16[64,4096]{1,0:T(8,128)(2,1)}, bf16[64,4096]{1,0:T(8,128)(2,1)}, u32[]{:S(2)}, u32[]{:S(2)}) collective-permute-start(bf16[64,4096]{1,0:T(8,128)(2,1)} %normalise.1.refs_0_), channel_id=1, source_target_pairs={{0,2},{2,4},{4,6},{6,0},{1,3},{3,5},{5,7},{7,1},{8,10},{10,12},{12... | collective-permute-start | bytes 1572872 | tf_op jit(solution)/shard_map/ppermute | solution.py:26
  60.3 37.4 %collective-permute-start.11 = (bf16[64,4096]{1,0:T(8,128)(2,1)}, bf16[64,4096]{1,0:T(8,128)(2,1)}, u32[]{:S(2)}, u32[]{:S(2)}) collective-permute-start(bf16[64,4096]{1,0:T(8,128)(2,1)} %normalise.1.refs_0_), channel_id=1, source_target_pairs={{0,6},{2,0},{4,2},{6,4},{1,7},{3,1},{5,3},{7,5},{8,14},{10,8},{12,... | collective-permute-start | bytes 1572872 | tf_op jit(solution)/shard_map/ppermute | solution.py:26
  63.8 33.8 %collective-permute-start.15 = (bf16[64,4096]{1,0:T(8,128)(2,1)}, bf16[64,4096]{1,0:T(8,128)(2,1)}, u32[]{:S(2)}, u32[]{:S(2)}) collective-permute-start(bf16[64,4096]{1,0:T(8,128)(2,1)} %normalise.1.refs_0_), channel_id=1, source_target_pairs={{0,4},{2,6},{4,0},{6,2},{1,5},{3,7},{5,1},{7,3},{8,12},{10,14},{12... | collective-permute-start | bytes 1572872 | tf_op jit(solution)/shard_map/ppermute | solution.py:26
  85.2 12.4 %collective-permute-start.13 = (bf16[512,512]{1,0:T(8,128)(2,1)}, bf16[512,512]{1,0:T(8,128)(2,1)}, u32[]{:S(2)}, u32[]{:S(2)}) collective-permute-start(bf16[512,512]{1,0:T(8,128)(2,1)} %slice.34), channel_id=1, source_target_pairs={{0,8},{8,16},{16,24},{24,0},{1,9},{9,17},{17,25},{25,1},{2,10},{10... | collective-permute-start | bytes 1572872 | tf_op jit(solution)/shard_map/ppermute | solution.py:26
  86.6 11.0 %collective-permute-start.14 = (bf16[512,512]{1,0:T(8,128)(2,1)}, bf16[512,512]{1,0:T(8,128)(2,1)}, u32[]{:S(2)}, u32[]{:S(2)}) collective-permute-start(bf16[512,512]{1,0:T(8,128)(2,1)} %slice.35), channel_id=1, source_target_pairs={{0,24},{8,0},{16,8},{24,16},{1,25},{9,1},{17,9},{25,17},{2,26},{10... | collective-permute-start | bytes 1572872 | tf_op jit(solution)/shard_map/ppermute | solution.py:26
  90.1 4.8 %collective-permute-start.12 = (s32[64]{0:T(128)S(1)}, s32[64]{0:T(128)S(1)}, u32[]{:S(2)}, u32[]{:S(2)}) collective-permute-start(s32[64]{0:T(128)S(1)} %reshape.41), channel_id=1, source_target_pairs={{0,32},{32,64},{64,96},{96,128},{128,160},{160,192},{192,224},{224... | collective-permute-start | bytes 776 | tf_op jit(solution)/shard_map/ppermute | solution.py:26
  102.5 10.1 %collective-permute-start.16 = (bf16[256,512]{1,0:T(8,128)(2,1)S(1)}, bf16[256,512]{1,0:T(8,128)(2,1)S(1)}, u32[]{:S(2)}, u32[]{:S(2)}) collective-permute-start(bf16[256,512]{1,0:T(8,128)(2,1)S(1)} %get-tuple-element.71.refs_4_), channel_id=1, source_target_pairs={{0,32},{32,64},{64,96},{96,128},{128,160},{160,192},{192,224},{224... | collective-permute-start | bytes 786440 | tf_op jit(solution)/shard_map/ppermute | solution.py:26
  103.2 9.4 %collective-permute-start.17 = (bf16[256,512]{1,0:T(8,128)(2,1)S(1)}, bf16[256,512]{1,0:T(8,128)(2,1)S(1)}, u32[]{:S(2)}, u32[]{:S(2)}) collective-permute-start(bf16[256,512]{1,0:T(8,128)(2,1)S(1)} %get-tuple-element.71.refs_4_), channel_id=1, source_target_pairs={{0,224},{32,0},{64,32},{96,64},{128,96},{160,128},{192,160},{224,1... | collective-permute-start | bytes 786440 | tf_op jit(solution)/shard_map/ppermute | solution.py:26
  109.2 10.4 %collective-permute-start.25 = (bf16[256,512]{1,0:T(8,128)(2,1)S(1)}, bf16[256,512]{1,0:T(8,128)(2,1)S(1)}, u32[]{:S(2)}, u32[]{:S(2)}) collective-permute-start(bf16[256,512]{1,0:T(8,128)(2,1)S(1)} %memorise.3.refs_13_), channel_id=1, source_target_pairs={{0,32},{32,64},{64,96},{96,128},{128,160},{160,192},{192,224},{224... | collective-permute-start | bytes 786440 | tf_op jit(solution)/shard_map/ppermute | solution.py:26
  110.0 9.7 %collective-permute-start.26 = (bf16[256,512]{1,0:T(8,128)(2,1)S(1)}, bf16[256,512]{1,0:T(8,128)(2,1)S(1)}, u32[]{:S(2)}, u32[]{:S(2)}) collective-permute-start(bf16[256,512]{1,0:T(8,128)(2,1)S(1)} %memorise.3.refs_13_), channel_id=1, source_target_pairs={{0,224},{32,0},{64,32},{96,64},{128,96},{160,128},{192,160},{224,1... | collective-permute-start | bytes 786440 | tf_op jit(solution)/shard_map/ppermute | solution.py:26
  112.6 12.7 %collective-permute-start.18 = (bf16[256,512]{1,0:T(8,128)(2,1)S(1)}, bf16[256,512]{1,0:T(8,128)(2,1)S(1)}, u32[]{:S(2)}, u32[]{:S(2)}) collective-permute-start(bf16[256,512]{1,0:T(8,128)(2,1)S(1)} %collective-permute-done.16.refs_5_), channel_id=1, source_target_pairs={{0,32},{32,64},{64,96},{96,128},{128,160},{160,192},{192,224},{224... | collective-permute-start | bytes 786440 | tf_op jit(solution)/shard_map/ppermute | solution.py:26
  112.6 12.7 %collective-permute-start.19 = (bf16[256,512]{1,0:T(8,128)(2,1)S(1)}, bf16[256,512]{1,0:T(8,128)(2,1)S(1)}, u32[]{:S(2)}, u32[]{:S(2)}) collective-permute-start(bf16[256,512]{1,0:T(8,128)(2,1)S(1)} %collective-permute-done.17.refs_6_), channel_id=1, source_target_pairs={{0,224},{32,0},{64,32},{96,64},{128,96},{160,128},{192,160},{224,1... | collective-permute-start | bytes 786440 | tf_op jit(solution)/shard_map/ppermute | solution.py:26
  119.7 11.2 %collective-permute-start.27 = (bf16[256,512]{1,0:T(8,128)(2,1)S(1)}, bf16[256,512]{1,0:T(8,128)(2,1)S(1)}, u32[]{:S(2)}, u32[]{:S(2)}) collective-permute-start(bf16[256,512]{1,0:T(8,128)(2,1)S(1)} %collective-permute-done.25.refs_14_), channel_id=1, source_target_pairs={{0,32},{32,64},{64,96},{96,128},{128,160},{160,192},{192,224},{224... | collective-permute-start | bytes 786440 | tf_op jit(solution)/shard_map/ppermute | solution.py:26
  119.7 11.2 %collective-permute-start.28 = (bf16[256,512]{1,0:T(8,128)(2,1)S(1)}, bf16[256,512]{1,0:T(8,128)(2,1)S(1)}, u32[]{:S(2)}, u32[]{:S(2)}) collective-permute-start(bf16[256,512]{1,0:T(8,128)(2,1)S(1)} %collective-permute-done.26.refs_15_), channel_id=1, source_target_pairs={{0,224},{32,0},{64,32},{96,64},{128,96},{160,128},{192,160},{224,1... | collective-permute-start | bytes 786440 | tf_op jit(solution)/shard_map/ppermute | solution.py:26
  125.3 11.2 %collective-permute-start.20 = (bf16[256,512]{1,0:T(8,128)(2,1)S(1)}, bf16[256,512]{1,0:T(8,128)(2,1)S(1)}, u32[]{:S(2)}, u32[]{:S(2)}) collective-permute-start(bf16[256,512]{1,0:T(8,128)(2,1)S(1)} %collective-permute-done.18.refs_7_), channel_id=1, source_target_pairs={{0,32},{32,64},{64,96},{96,128},{128,160},{160,192},{192,224},{224... | collective-permute-start | bytes 786440 | tf_op jit(solution)/shard_map/ppermute | solution.py:26
  125.3 11.3 %collective-permute-start.21 = (bf16[256,512]{1,0:T(8,128)(2,1)S(1)}, bf16[256,512]{1,0:T(8,128)(2,1)S(1)}, u32[]{:S(2)}, u32[]{:S(2)}) collective-permute-start(bf16[256,512]{1,0:T(8,128)(2,1)S(1)} %collective-permute-done.19.refs_8_), channel_id=1, source_target_pairs={{0,224},{32,0},{64,32},{96,64},{128,96},{160,128},{192,160},{224,1... | collective-permute-start | bytes 786440 | tf_op jit(solution)/shard_map/ppermute | solution.py:26
  130.9 11.2 %collective-permute-start.29 = (bf16[256,512]{1,0:T(8,128)(2,1)S(1)}, bf16[256,512]{1,0:T(8,128)(2,1)S(1)}, u32[]{:S(2)}, u32[]{:S(2)}) collective-permute-start(bf16[256,512]{1,0:T(8,128)(2,1)S(1)} %collective-permute-done.27.refs_16_), channel_id=1, source_target_pairs={{0,32},{32,64},{64,96},{96,128},{128,160},{160,192},{192,224},{224... | collective-permute-start | bytes 786440 | tf_op jit(solution)/shard_map/ppermute | solution.py:26
  130.9 11.3 %collective-permute-start.30 = (bf16[256,512]{1,0:T(8,128)(2,1)S(1)}, bf16[256,512]{1,0:T(8,128)(2,1)S(1)}, u32[]{:S(2)}, u32[]{:S(2)}) collective-permute-start(bf16[256,512]{1,0:T(8,128)(2,1)S(1)} %collective-permute-done.28.refs_17_), channel_id=1, source_target_pairs={{0,224},{32,0},{64,32},{96,64},{128,96},{160,128},{192,160},{224,1... | collective-permute-start | bytes 786440 | tf_op jit(solution)/shard_map/ppermute | solution.py:26
  136.6 9.0 %collective-permute-start.22 = (bf16[128,512]{1,0:T(8,128)(2,1)S(1)}, bf16[128,512]{1,0:T(8,128)(2,1)S(1)}, u32[]{:S(2)}, u32[]{:S(2)}) collective-permute-start(bf16[128,512]{1,0:T(8,128)(2,1)S(1)} %slice.40), channel_id=1, source_target_pairs={{0,32},{32,64},{64,96},{96,128},{128,160},{160,192},{192,224},{224... | collective-permute-start | bytes 393224 | tf_op jit(solution)/shard_map/ppermute | solution.py:26
  136.7 8.9 %collective-permute-start.23 = (bf16[128,512]{1,0:T(8,128)(2,1)S(1)}, bf16[128,512]{1,0:T(8,128)(2,1)S(1)}, u32[]{:S(2)}, u32[]{:S(2)}) collective-permute-start(bf16[128,512]{1,0:T(8,128)(2,1)S(1)} %slice.41), channel_id=1, source_target_pairs={{0,224},{32,0},{64,32},{96,64},{128,96},{160,128},{192,160},{224,1... | collective-permute-start | bytes 393224 | tf_op jit(solution)/shard_map/ppermute | solution.py:26
  142.2 6.3 %collective-permute-start.31 = (bf16[128,512]{1,0:T(8,128)(2,1)S(1)}, bf16[128,512]{1,0:T(8,128)(2,1)S(1)}, u32[]{:S(2)}, u32[]{:S(2)}) collective-permute-start(bf16[128,512]{1,0:T(8,128)(2,1)S(1)} %slice.42), channel_id=1, source_target_pairs={{0,32},{32,64},{64,96},{96,128},{128,160},{160,192},{192,224},{224... | collective-permute-start | bytes 393224 | tf_op jit(solution)/shard_map/ppermute | solution.py:26
  142.3 6.1 %collective-permute-start.32 = (bf16[128,512]{1,0:T(8,128)(2,1)S(1)}, bf16[128,512]{1,0:T(8,128)(2,1)S(1)}, u32[]{:S(2)}, u32[]{:S(2)}) collective-permute-start(bf16[128,512]{1,0:T(8,128)(2,1)S(1)} %slice.43), channel_id=1, source_target_pairs={{0,224},{32,0},{64,32},{96,64},{128,96},{160,128},{192,160},{224,1... | collective-permute-start | bytes 393224 | tf_op jit(solution)/shard_map/ppermute | solution.py:26
  (30 other events, 403.6 us)

commit v9 on v8

--- a/solution.py
+++ b/solution.py
@@ -497,7 +497,7 @@
     u = normalise(terms, corpus_flat, gain_out.reshape(1, width), as_index(core * NY + my_y))
     us = [u] + [shifted(u, "y", k) for k in range(1, NY)]
     lists = plan(jnp.concatenate([got, below]), as_index(my_z), as_index(my_x), as_index(core))
-    us[1], from_left, from_right = lax.optimization_barrier((us[1], from_left, from_right))
+    us[1], lists, from_left, from_right = lax.optimization_barrier((us[1], lists, from_left, from_right))
     half = kv.shape[0] // 2
     far_top = shifted(from_left[:half], "x", 1)
     far_bottom = shifted(from_right[half:], "x", -1)

time: 178 us -> 174 us (0.978); the launches traced: 175 us -> 173 us
  blocking collectives: 16.3 us -> 20.6 us
  waiting for transfers between devices: 54.9 us -> 51 us
  local copies, waits for them, and re-layouts: 10.3 us -> 7.63 us
    all_to_all x1, blocking collectives: 16.3 us -> 20.6 us  [on_device(): parts = lax.all_to_all(parts, 'x', split_axis=0, concat_axis=0, tiled=True)]
    ppermute x33, waiting for transfers between devices: 54.9 us -> 51 us  [shifted(): return lax.ppermute(value, axis, [(i, (i + steps) % n) for i in range(n)])]
    unnamed x56 -> x58, local copies, waits for them, and re-layouts: 4.48 us -> 3.43 us
  transfers between devices with their start and end apart: 34 -> 34, of which waited for: 14 -> 19; matrix products, arithmetic and copies ran while one was open for 4% -> 3% of each run, Pallas kernels for 13% -> 13%
where the time goes in v9:
time: 174 us; the launch traced here: 173 us
  starting transfers between devices  57.5 us (33%)
  waiting for transfers between devices  51 us (29%)
  Pallas kernels  34.9 us (20%)
  blocking collectives  20.6 us (12%)
  local copies, waits for them, and re-layouts  7.63 us (4%)
    ppermute x33, waiting for transfers between devices, shifted(): return lax.ppermute(value, axis, [(i, (i + steps) % n) for i in range(n)])  51 us
    ppermute x33, starting transfers between devices, shifted(): return lax.ppermute(value, axis, [(i, (i + steps) % n) for i in range(n)])  49.1 us
    all_to_all x1, blocking collectives, on_device(): parts = lax.all_to_all(parts, 'x', split_axis=0, concat_axis=0, tiled=True)  20.6 us
    pallas_call x1, Pallas kernels, encode(): pl.pallas_call(encoder_kernel, grid_spec=pltpu.PrefetchScalarGridSpec(num...  9.48 us
    all_to_all x1, starting transfers between devices, spread(): return lax.all_to_all(copies, axis, split_axis=0, concat_axis=0, tiled=True)  8.47 us
    pallas_call x1, Pallas kernels, windows(): pl.pallas_call(functools.partial(window_kernel, layout), in_specs=[smem]...  7.83 us
    pallas_call x2, Pallas kernels, memorise(): pl.pallas_call(functools.partial(memory_kernel, len(us)), in_specs=[pl.Bl...  5.99 us
    pallas_call x1, Pallas kernels, project(): pl.pallas_call(project_kernel, grid=(width // cols,), in_specs=[pl.BlockS...  5 us
  transfers between devices with their start and end apart: 34, of which 19 were waited for; matrix products, arithmetic and copies ran while one was open for 3% of the time, Pallas kernels for 13%

profile of v9, /device:TPU:2, one launch (start us, length us, event | category | flops | bytes accessed | tf_op | source)
XLA Modules:
  0.0 172.7 jit_solution(16322033184106118365)
XLA Ops:
  2.0 8.5 %all-to-all-start = ((bf16[8,128,512]{2,1,0:T(8,128)(2,1)}), bf16[8,128,512]{2,1,0:T(8,128)(2,1)S(1)}, u32[]{:S(2)}, u32[]{:S(2)}) async-start(bf16[8,128,512]{2,1,0:T(8,128)(2,1)} %broadcast_in_dim.2), calls=%async_computation | async-start | bytes 2097152 | tf_op jit(solution)/shard_map/all_to_all | solution.py:32
  10.5 9.5 %encoder.1 = (bf16[256,256]{1,0:T(8,128)(2,1)}, bf16[256,256]{1,0:T(8,128)(2,1)}) custom-call(s32[1]{0:T(128)} %bitcast.1.core_ref, s32[1]{0:T(128)} %bitcast.2.y_ref, bf16[512,4096]{1,0:T(8,128)(2,1)} %bitcast.27, bf16[24576,128]{1,0:T(8,128)(2,1)} %bitcast.33, f32[1,4096]{1,0:T(1,128)} %bitcast.34), custom_call_target="tpu_custom_call" | custom-call | flops 3221225472 | bytes 10485760 | tf_op jit(solution)/shard_map/encoder/pallas_call | solution.py:94
  22.9 5.0 %project.1 = (bf16[64,4096]{1,0:T(8,128)(2,1)}, bf16[64,4096]{1,0:T(8,128)(2,1)}, bf16[64,4096]{1,0:T(8,128)(2,1)}, bf16[64,4096]{1,0:T(8,128)(2,1)}) custom-call(bf16[256,256]{1,0:T(8,128)(2,1)} %get-tuple-element.42.a_ref, bf16[256,256]{1,0:T(8,128)(2,1)} %copy-done.27, bf16[256,4096]{1,0:T(8,128)(2,1)} %bitcast.30, bf16[256,4096]{1,0:T(8,128)(2,1)} %copy-done.3), custom_call_target="tpu_custom_call" | custom-call | flops 1073741824 | bytes 4194304 | tf_op jit(solution)/shard_map/project/pallas_call | solution.py:134
  31.8 2.4 %collective-permute-start.5 = (bf16[1040,128]{1,0:T(8,128)(2,1)S(1)}, bf16[1040,128]{1,0:T(8,128)(2,1)S(1)}, u32[]{:S(2)}, u32[]{:S(2)}) collective-permute-start(bf16[1040,128]{1,0:T(8,128)(2,1)S(1)} %fusion.1.refs_0_), channel_id=1, source_target_pairs={{0,16},{8,24},{16,0},{24,8},{1,17},{9,25},{17,1},{25,9},{2,18},{10... | collective-permute-start | bytes 798728 | tf_op jit(solution)/shard_map/ppermute | solution.py:26
  36.1 3.6 %collective-permute-done.4.refs_1_ = bf16[1040,128]{1,0:T(8,128)(2,1)S(1)} collective-permute-done((bf16[1040,128]{1,0:T(8,128)(2,1)S(1)}, bf16[1040,128]{1,0:T(8,128)(2,1)S(1)}, u32[]{:S(2)}, u32[]{:S(2)}) %collective-permute-start.4) | collective-permute-done | bytes 266272 | tf_op jit(solution)/shard_map/ppermute | solution.py:26
  41.7 4.4 %collective-permute-done.5.refs_2_ = bf16[1040,128]{1,0:T(8,128)(2,1)S(1)} collective-permute-done((bf16[1040,128]{1,0:T(8,128)(2,1)S(1)}, bf16[1040,128]{1,0:T(8,128)(2,1)S(1)}, u32[]{:S(2)}, u32[]{:S(2)}) %collective-permute-start.5) | collective-permute-done | bytes 266272 | tf_op jit(solution)/shard_map/ppermute | solution.py:26
  47.0 7.2 %collective-permute-done.3.t3 = bf16[64,4096]{1,0:T(8,128)(2,1)S(1)} collective-permute-done((bf16[64,4096]{1,0:T(8,128)(2,1)}, bf16[64,4096]{1,0:T(8,128)(2,1)S(1)}, u32[]{:S(2)}, u32[]{:S(2)}) %collective-permute-start.3) | collective-permute-done | bytes 524320 | tf_op jit(solution)/shard_map/ppermute | solution.py:26
  57.1 3.1 %normalise.1.refs_0_ = bf16[64,4096]{1,0:T(8,128)(2,1)} custom-call(s32[1]{0:T(128)} %bitcast.block_ref, bf16[64,4096]{1,0:T(8,128)(2,1)} %get-tuple-element.45.t0, bf16[64,4096]{1,0:T(8,128)(2,1)} %copy-done.9, bf16[64,4096]{1,0:T(8,128)(2,1)} %collective-permute-done.7.t2, bf16[64,4096]{1,0:T(8,128)(2,1)} %copy-done.10, bf16[512,4096]{1,0:T(8,128)(2,1)} %bitcast.28, ...), custom_call_target="tpu_custom_call" | custom-call | flops 2097152 | bytes 3145728 | tf_op jit(solution)/shard_map/normalise/pallas_call | solution.py:168
  62.3 2.0 %collective-permute-start.9 = (s32[64]{0:T(128)S(1)}, s32[64]{0:T(128)S(1)}, u32[]{:S(2)}, u32[]{:S(2)}) collective-permute-start(s32[64]{0:T(128)S(1)} %reshape.41), channel_id=1, source_target_pairs={{0,32},{32,64},{64,96},{96,128},{128,160},{160,192},{192,224},{224... | collective-permute-start | bytes 776 | tf_op jit(solution)/shard_map/ppermute | solution.py:26
  64.3 3.5 %collective-permute-start.12 = (bf16[64,4096]{1,0:T(8,128)(2,1)}, bf16[64,4096]{1,0:T(8,128)(2,1)}, u32[]{:S(2)}, u32[]{:S(2)}) collective-permute-start(bf16[64,4096]{1,0:T(8,128)(2,1)} %normalise.1.refs_0_), channel_id=1, source_target_pairs={{0,6},{2,0},{4,2},{6,4},{1,7},{3,1},{5,3},{7,5},{8,14},{10,8},{12,... | collective-permute-start | bytes 1572872 | tf_op jit(solution)/shard_map/ppermute | solution.py:26
  68.4 2.1 %plan.1 = (s32[128]{0:T(128)}, s32[128]{0:T(128)}, s32[2]{0:T(128)}) custom-call(s32[128]{0:T(128)} %pad_add_fusion.ids_ref, s32[1]{0:T(128)} %bitcast.15.z_ref, s32[1]{0:T(128)} %bitcast.16.x_ref, s32[1]{0:T(128)} %bitcast.1.core_ref), custom_call_target="tpu_custom_call" | custom-call | tf_op jit(solution)/shard_map/plan/pallas_call | solution.py:316
  70.5 3.4 %collective-permute-done.8.refs_1_ = bf16[64,4096]{1,0:T(8,128)(2,1)} collective-permute-done((bf16[64,4096]{1,0:T(8,128)(2,1)}, bf16[64,4096]{1,0:T(8,128)(2,1)}, u32[]{:S(2)}, u32[]{:S(2)}) %collective-permute-start.8) | collective-permute-done | bytes 524320 | tf_op jit(solution)/shard_map/ppermute | solution.py:26
  75.0 2.1 %collective-permute-start.13 = (bf16[512,512]{1,0:T(8,128)(2,1)S(1)}, bf16[512,512]{1,0:T(8,128)(2,1)S(1)}, u32[]{:S(2)}, u32[]{:S(2)}) collective-permute-start(bf16[512,512]{1,0:T(8,128)(2,1)S(1)} %slice.34), channel_id=1, source_target_pairs={{0,8},{8,16},{16,24},{24,0},{1,9},{9,17},{17,25},{25,1},{2,10},{10... | collective-permute-start | bytes 1572872 | tf_op jit(solution)/shard_map/ppermute | solution.py:26
  79.9 9.2 %collective-permute-done.13.refs_7_.refs_4_ = bf16[512,512]{1,0:T(8,128)(2,1)S(1)} collective-permute-done((bf16[512,512]{1,0:T(8,128)(2,1)S(1)}, bf16[512,512]{1,0:T(8,128)(2,1)S(1)}, u32[]{:S(2)}, u32[]{:S(2)}) %collective-permute-start.13) | collective-permute-done | bytes 524320 | tf_op jit(solution)/shard_map/ppermute | solution.py:26
  89.2 2.9 %collective-permute-done.15.refs_2_ = bf16[64,4096]{1,0:T(8,128)(2,1)S(1)} collective-permute-done((bf16[64,4096]{1,0:T(8,128)(2,1)S(1)}, bf16[64,4096]{1,0:T(8,128)(2,1)S(1)}, u32[]{:S(2)}, u32[]{:S(2)}) %collective-permute-start.15) | collective-permute-done | bytes 524320 | tf_op jit(solution)/shard_map/ppermute | solution.py:26
  92.1 3.5 %memorise.2 = (bf16[256,512]{1,0:T(8,128)(2,1)S(1)}, bf16[256,4096]{1,0:T(8,128)(2,1)S(1)}) custom-call(s32[2]{0:T(128)S(1)} %pad_add_fusion.1.at_ref, bf16[64,4096]{1,0:T(8,128)(2,1)S(1)} %copy-done, bf16[64,4096]{1,0:T(8,128)(2,1)} %collective-permute-done.8.refs_1_, bf16[64,4096]{1,0:T(8,128)(2,1)S(1)} %collective-permute-done.15.refs_2_, ...), custom_call_target="tpu_custom_call" | custom-call | flops 1073741824 | bytes 4194304 | tf_op jit(solution)/shard_map/memorise/pallas_call | solution.py:238
  95.7 2.0 %collective-permute-start.16 = (bf16[256,512]{1,0:T(8,128)(2,1)S(1)}, bf16[256,512]{1,0:T(8,128)(2,1)S(1)}, u32[]{:S(2)}, u32[]{:S(2)}) collective-permute-start(bf16[256,512]{1,0:T(8,128)(2,1)S(1)} %get-tuple-element.77.refs_4_), channel_id=1, source_target_pairs={{0,32},{32,64},{64,96},{96,128},{128,160},{160,192},{192,224},{224... | collective-permute-start | bytes 786440 | tf_op jit(solution)/shard_map/ppermute | solution.py:26
  99.9 2.5 %memorise.3.refs_13_ = bf16[256,512]{1,0:T(8,128)(2,1)S(1)} custom-call(s32[2]{0:T(128)S(1)} %pad_add_fusion.1.at_ref, bf16[256,4096]{1,0:T(8,128)(2,1)S(1)} %collective-permute-done.24.refs_0_, bf16[1024,512]{1,0:T(8,128)(2,1)S(1)} %bitcast.26, bf16[1024,512]{1,0:T(8,128)(2,1)S(1)} %collective-permute-done.10.refs_5_.refs_2_, ...), custom_call_target="tpu_custom_call" | custom-call | flops 1073741824 | bytes 4194304 | tf_op jit(solution)/shard_map/memorise/pallas_call | solution.py:238
  106.5 2.6 %collective-permute-start.19 = (bf16[256,512]{1,0:T(8,128)(2,1)S(1)}, bf16[256,512]{1,0:T(8,128)(2,1)S(1)}, u32[]{:S(2)}, u32[]{:S(2)}) collective-permute-start(bf16[256,512]{1,0:T(8,128)(2,1)S(1)} %collective-permute-done.17.refs_6_), channel_id=1, source_target_pairs={{0,224},{32,0},{64,32},{96,64},{128,96},{160,128},{192,160},{224,1... | collective-permute-start | bytes 786440 | tf_op jit(solution)/shard_map/ppermute | solution.py:26
  109.1 3.8 %collective-permute-done.25.refs_14_ = bf16[256,512]{1,0:T(8,128)(2,1)S(1)} collective-permute-done((bf16[256,512]{1,0:T(8,128)(2,1)S(1)}, bf16[256,512]{1,0:T(8,128)(2,1)S(1)}, u32[]{:S(2)}, u32[]{:S(2)}) %collective-permute-start.25) | collective-permute-done | bytes 262176 | tf_op jit(solution)/shard_map/ppermute | solution.py:26
  113.6 2.5 %collective-permute-start.28 = (bf16[256,512]{1,0:T(8,128)(2,1)S(1)}, bf16[256,512]{1,0:T(8,128)(2,1)S(1)}, u32[]{:S(2)}, u32[]{:S(2)}) collective-permute-start(bf16[256,512]{1,0:T(8,128)(2,1)S(1)} %collective-permute-done.26.refs_15_), channel_id=1, source_target_pairs={{0,224},{32,0},{64,32},{96,64},{128,96},{160,128},{192,160},{224,1... | collective-permute-start | bytes 786440 | tf_op jit(solution)/shard_map/ppermute | solution.py:26
  116.1 2.3 %collective-permute-done.18.refs_7_ = bf16[256,512]{1,0:T(8,128)(2,1)S(1)} collective-permute-done((bf16[256,512]{1,0:T(8,128)(2,1)S(1)}, bf16[256,512]{1,0:T(8,128)(2,1)S(1)}, u32[]{:S(2)}, u32[]{:S(2)}) %collective-permute-start.18) | collective-permute-done | bytes 262176 | tf_op jit(solution)/shard_map/ppermute | solution.py:26
  119.2 2.5 %collective-permute-start.21 = (bf16[256,512]{1,0:T(8,128)(2,1)S(1)}, bf16[256,512]{1,0:T(8,128)(2,1)S(1)}, u32[]{:S(2)}, u32[]{:S(2)}) collective-permute-start(bf16[256,512]{1,0:T(8,128)(2,1)S(1)} %collective-permute-done.19.refs_8_), channel_id=1, source_target_pairs={{0,224},{32,0},{64,32},{96,64},{128,96},{160,128},{192,160},{224,1... | collective-permute-start | bytes 786440 | tf_op jit(solution)/shard_map/ppermute | solution.py:26
  121.7 2.3 %collective-permute-done.27.refs_16_ = bf16[256,512]{1,0:T(8,128)(2,1)S(1)} collective-permute-done((bf16[256,512]{1,0:T(8,128)(2,1)S(1)}, bf16[256,512]{1,0:T(8,128)(2,1)S(1)}, u32[]{:S(2)}, u32[]{:S(2)}) %collective-permute-start.27) | collective-permute-done | bytes 262176 | tf_op jit(solution)/shard_map/ppermute | solution.py:26
  124.9 2.5 %collective-permute-start.30 = (bf16[256,512]{1,0:T(8,128)(2,1)S(1)}, bf16[256,512]{1,0:T(8,128)(2,1)S(1)}, u32[]{:S(2)}, u32[]{:S(2)}) collective-permute-start(bf16[256,512]{1,0:T(8,128)(2,1)S(1)} %collective-permute-done.28.refs_17_), channel_id=1, source_target_pairs={{0,224},{32,0},{64,32},{96,64},{128,96},{160,128},{192,160},{224,1... | collective-permute-start | bytes 786440 | tf_op jit(solution)/shard_map/ppermute | solution.py:26
  127.3 2.3 %collective-permute-done.20.refs_9_ = bf16[256,512]{1,0:T(8,128)(2,1)S(1)} collective-permute-done((bf16[256,512]{1,0:T(8,128)(2,1)S(1)}, bf16[256,512]{1,0:T(8,128)(2,1)S(1)}, u32[]{:S(2)}, u32[]{:S(2)}) %collective-permute-start.20) | collective-permute-done | bytes 262176 | tf_op jit(solution)/shard_map/ppermute | solution.py:26
  130.5 2.6 %collective-permute-start.23 = (bf16[128,512]{1,0:T(8,128)(2,1)S(1)}, bf16[128,512]{1,0:T(8,128)(2,1)S(1)}, u32[]{:S(2)}, u32[]{:S(2)}) collective-permute-start(bf16[128,512]{1,0:T(8,128)(2,1)S(1)} %slice.41), channel_id=1, source_target_pairs={{0,224},{32,0},{64,32},{96,64},{128,96},{160,128},{192,160},{224,1... | collective-permute-start | bytes 393224 | tf_op jit(solution)/shard_map/ppermute | solution.py:26
  133.1 2.2 %collective-permute-done.29.refs_18_ = bf16[256,512]{1,0:T(8,128)(2,1)S(1)} collective-permute-done((bf16[256,512]{1,0:T(8,128)(2,1)S(1)}, bf16[256,512]{1,0:T(8,128)(2,1)S(1)}, u32[]{:S(2)}, u32[]{:S(2)}) %collective-permute-start.29) | collective-permute-done | bytes 262176 | tf_op jit(solution)/shard_map/ppermute | solution.py:26
  136.2 2.6 %collective-permute-start.32 = (bf16[128,512]{1,0:T(8,128)(2,1)S(1)}, bf16[128,512]{1,0:T(8,128)(2,1)S(1)}, u32[]{:S(2)}, u32[]{:S(2)}) collective-permute-start(bf16[128,512]{1,0:T(8,128)(2,1)S(1)} %slice.43), channel_id=1, source_target_pairs={{0,224},{32,0},{64,32},{96,64},{128,96},{160,128},{192,160},{224,1... | collective-permute-start | bytes 393224 | tf_op jit(solution)/shard_map/ppermute | solution.py:26
  138.8 2.8 %collective-permute-done.31.refs_20_ = bf16[128,512]{1,0:T(8,128)(2,1)S(1)} collective-permute-done((bf16[128,512]{1,0:T(8,128)(2,1)S(1)}, bf16[128,512]{1,0:T(8,128)(2,1)S(1)}, u32[]{:S(2)}, u32[]{:S(2)}) %collective-permute-start.31) | collective-permute-done | bytes 131104 | tf_op jit(solution)/shard_map/ppermute | solution.py:26
  142.9 7.8 %windows.1 = bf16[4,1056,128]{2,1,0:T(8,128)(2,1)} custom-call(s32[128]{0:T(128)} %get-tuple-element.67.one_list, s32[128]{0:T(128)} %get-tuple-element.68.two_list, s32[2]{0:T(128)} %get-tuple-element.69.counts_ref, s32[1]{0:T(128)} %bitcast.16.x_ref, bf16[1040,128]{1,0:T(8,128)(2,1)} %copy-done.4, bf16[1040,128]{1,0:T(8,128)(2,1)} %copy-done.11, ...), custom_call_target="tpu_custom_call" | custom-call | flops 1000000000 | bytes 8388608 | tf_op jit(solution)/shard_map/windows/pallas_call | solution.py:415
  150.7 20.6 %all_to_all.10.parts_ref = bf16[4,1056,128]{2,1,0:T(8,128)(2,1)S(1)} all-to-all(bf16[4,1056,128]{2,1,0:T(8,128)(2,1)} %windows.1), channel_id=1, replica_groups=mesh['z'=8,'x'=4,'y'=4,'c'=2] {'x'}, dimensions={0} | all-to-all | bytes 2162688 | tf_op jit(solution)/shard_map/all_to_all | solution.py:514
  (125 shorter events, 35.9 us)
Async XLA Ops:
  0.0 21.6 %collective-permute-start.1 = (bf16[256,4096]{1,0:T(8,128)(2,1)}, bf16[256,4096]{1,0:T(8,128)(2,1)S(1)}, u32[]{:S(2)}, u32[]{:S(2)}) collective-permute-start(bf16[256,4096]{1,0:T(8,128)(2,1)} %bitcast.29), channel_id=1, source_target_pairs={{0,1},{1,0},{2,3},{3,2},{4,5},{5,4},{6,7},{7,6},{8,9},{9,8},{10,11... | collective-permute-start | bytes 6291464 | tf_op jit(solution)/shard_map/ppermute | solution.py:26
  2.0 44.9 %all-to-all-start = ((bf16[8,128,512]{2,1,0:T(8,128)(2,1)}), bf16[8,128,512]{2,1,0:T(8,128)(2,1)S(1)}, u32[]{:S(2)}, u32[]{:S(2)}) async-start(bf16[8,128,512]{2,1,0:T(8,128)(2,1)} %broadcast_in_dim.2), calls=%async_computation | async-start | bytes 2097152 | tf_op jit(solution)/shard_map/all_to_all | solution.py:32
  27.9 19.0 %collective-permute-start.2 = (bf16[64,4096]{1,0:T(8,128)(2,1)}, bf16[64,4096]{1,0:T(8,128)(2,1)S(1)}, u32[]{:S(2)}, u32[]{:S(2)}) collective-permute-start(bf16[64,4096]{1,0:T(8,128)(2,1)} %get-tuple-element.46), channel_id=1, source_target_pairs={{0,2},{2,4},{4,6},{6,0},{1,3},{3,5},{5,7},{7,1},{8,10},{10,12},{12... | collective-permute-start | bytes 1572872 | tf_op jit(solution)/shard_map/ppermute | solution.py:26
  29.5 24.7 %collective-permute-start.3 = (bf16[64,4096]{1,0:T(8,128)(2,1)}, bf16[64,4096]{1,0:T(8,128)(2,1)S(1)}, u32[]{:S(2)}, u32[]{:S(2)}) collective-permute-start(bf16[64,4096]{1,0:T(8,128)(2,1)} %get-tuple-element.47), channel_id=1, source_target_pairs={{0,6},{2,0},{4,2},{6,4},{1,7},{3,1},{5,3},{7,5},{8,14},{10,8},{12,... | collective-permute-start | bytes 1572872 | tf_op jit(solution)/shard_map/ppermute | solution.py:26
  31.2 8.4 %collective-permute-start.4 = (bf16[1040,128]{1,0:T(8,128)(2,1)S(1)}, bf16[1040,128]{1,0:T(8,128)(2,1)S(1)}, u32[]{:S(2)}, u32[]{:S(2)}) collective-permute-start(bf16[1040,128]{1,0:T(8,128)(2,1)S(1)} %fusion.1.refs_0_), channel_id=1, source_target_pairs={{0,24},{8,0},{16,8},{24,16},{1,25},{9,1},{17,9},{25,17},{2,26},{10... | collective-permute-start | bytes 798728 | tf_op jit(solution)/shard_map/ppermute | solution.py:26
  31.8 14.2 %collective-permute-start.5 = (bf16[1040,128]{1,0:T(8,128)(2,1)S(1)}, bf16[1040,128]{1,0:T(8,128)(2,1)S(1)}, u32[]{:S(2)}, u32[]{:S(2)}) collective-permute-start(bf16[1040,128]{1,0:T(8,128)(2,1)S(1)} %fusion.1.refs_0_), channel_id=1, source_target_pairs={{0,16},{8,24},{16,0},{24,8},{1,17},{9,25},{17,1},{25,9},{2,18},{10... | collective-permute-start | bytes 798728 | tf_op jit(solution)/shard_map/ppermute | solution.py:26
  34.3 12.7 %collective-permute-start.6 = (bf16[1040,128]{1,0:T(8,128)(2,1)S(1)}, bf16[1040,128]{1,0:T(8,128)(2,1)S(1)}, u32[]{:S(2)}, u32[]{:S(2)}) collective-permute-start(bf16[1040,128]{1,0:T(8,128)(2,1)S(1)} %fusion.1.refs_0_), channel_id=1, source_target_pairs={{0,8},{8,16},{16,24},{24,0},{1,9},{9,17},{17,25},{25,1},{2,10},{10... | collective-permute-start | bytes 798728 | tf_op jit(solution)/shard_map/ppermute | solution.py:26
  39.7 17.5 %collective-permute-start.7 = (bf16[64,4096]{1,0:T(8,128)(2,1)}, bf16[64,4096]{1,0:T(8,128)(2,1)}, u32[]{:S(2)}, u32[]{:S(2)}) collective-permute-start(bf16[64,4096]{1,0:T(8,128)(2,1)} %get-tuple-element.51), channel_id=1, source_target_pairs={{0,4},{2,6},{4,0},{6,2},{1,5},{3,7},{5,1},{7,3},{8,12},{10,14},{12... | collective-permute-start | bytes 1572872 | tf_op jit(solution)/shard_map/ppermute | solution.py:26
  55.0 19.7 %collective-permute-start.10 = (bf16[1024,512]{1,0:T(8,128)(2,1)S(1)}, bf16[1024,512]{1,0:T(8,128)(2,1)S(1)}, u32[]{:S(2)}, u32[]{:S(2)}) collective-permute-start(bf16[1024,512]{1,0:T(8,128)(2,1)S(1)} %bitcast.23), channel_id=1, source_target_pairs={{0,8},{8,16},{16,24},{24,0},{1,9},{9,17},{17,25},{25,1},{2,10},{10... | collective-permute-start | bytes 3145736 | tf_op jit(solution)/shard_map/ppermute | solution.py:26
  56.6 18.4 %collective-permute-start.11 = (bf16[1024,512]{1,0:T(8,128)(2,1)S(1)}, bf16[1024,512]{1,0:T(8,128)(2,1)S(1)}, u32[]{:S(2)}, u32[]{:S(2)}) collective-permute-start(bf16[1024,512]{1,0:T(8,128)(2,1)S(1)} %bitcast.24), channel_id=1, source_target_pairs={{0,24},{8,0},{16,8},{24,16},{1,25},{9,1},{17,9},{25,17},{2,26},{10... | collective-permute-start | bytes 3145736 | tf_op jit(solution)/shard_map/ppermute | solution.py:26
  60.2 13.6 %collective-permute-start.8 = (bf16[64,4096]{1,0:T(8,128)(2,1)}, bf16[64,4096]{1,0:T(8,128)(2,1)}, u32[]{:S(2)}, u32[]{:S(2)}) collective-permute-start(bf16[64,4096]{1,0:T(8,128)(2,1)} %normalise.1.refs_0_), channel_id=1, source_target_pairs={{0,2},{2,4},{4,6},{6,0},{1,3},{3,5},{5,7},{7,1},{8,10},{10,12},{12... | collective-permute-start | bytes 1572872 | tf_op jit(solution)/shard_map/ppermute | solution.py:26
  62.3 5.5 %collective-permute-start.9 = (s32[64]{0:T(128)S(1)}, s32[64]{0:T(128)S(1)}, u32[]{:S(2)}, u32[]{:S(2)}) collective-permute-start(s32[64]{0:T(128)S(1)} %reshape.41), channel_id=1, source_target_pairs={{0,32},{32,64},{64,96},{96,128},{128,160},{160,192},{192,224},{224... | collective-permute-start | bytes 776 | tf_op jit(solution)/shard_map/ppermute | solution.py:26
  64.3 15.6 %collective-permute-start.12 = (bf16[64,4096]{1,0:T(8,128)(2,1)}, bf16[64,4096]{1,0:T(8,128)(2,1)}, u32[]{:S(2)}, u32[]{:S(2)}) collective-permute-start(bf16[64,4096]{1,0:T(8,128)(2,1)} %normalise.1.refs_0_), channel_id=1, source_target_pairs={{0,6},{2,0},{4,2},{6,4},{1,7},{3,1},{5,3},{7,5},{8,14},{10,8},{12,... | collective-permute-start | bytes 1572872 | tf_op jit(solution)/shard_map/ppermute | solution.py:26
  75.0 14.0 %collective-permute-start.13 = (bf16[512,512]{1,0:T(8,128)(2,1)S(1)}, bf16[512,512]{1,0:T(8,128)(2,1)S(1)}, u32[]{:S(2)}, u32[]{:S(2)}) collective-permute-start(bf16[512,512]{1,0:T(8,128)(2,1)S(1)} %slice.34), channel_id=1, source_target_pairs={{0,8},{8,16},{16,24},{24,0},{1,9},{9,17},{17,25},{25,1},{2,10},{10... | collective-permute-start | bytes 1572872 | tf_op jit(solution)/shard_map/ppermute | solution.py:26
  77.2 12.0 %collective-permute-start.14 = (bf16[512,512]{1,0:T(8,128)(2,1)S(1)}, bf16[512,512]{1,0:T(8,128)(2,1)S(1)}, u32[]{:S(2)}, u32[]{:S(2)}) collective-permute-start(bf16[512,512]{1,0:T(8,128)(2,1)S(1)} %slice.35), channel_id=1, source_target_pairs={{0,24},{8,0},{16,8},{24,16},{1,25},{9,1},{17,9},{25,17},{2,26},{10... | collective-permute-start | bytes 1572872 | tf_op jit(solution)/shard_map/ppermute | solution.py:26
  77.9 14.2 %collective-permute-start.15 = (bf16[64,4096]{1,0:T(8,128)(2,1)S(1)}, bf16[64,4096]{1,0:T(8,128)(2,1)S(1)}, u32[]{:S(2)}, u32[]{:S(2)}) collective-permute-start(bf16[64,4096]{1,0:T(8,128)(2,1)S(1)} %copy-done), channel_id=1, source_target_pairs={{0,4},{2,6},{4,0},{6,2},{1,5},{3,7},{5,1},{7,3},{8,12},{10,14},{12... | collective-permute-start | bytes 1572872 | tf_op jit(solution)/shard_map/ppermute | solution.py:26
  95.7 10.1 %collective-permute-start.16 = (bf16[256,512]{1,0:T(8,128)(2,1)S(1)}, bf16[256,512]{1,0:T(8,128)(2,1)S(1)}, u32[]{:S(2)}, u32[]{:S(2)}) collective-permute-start(bf16[256,512]{1,0:T(8,128)(2,1)S(1)} %get-tuple-element.77.refs_4_), channel_id=1, source_target_pairs={{0,32},{32,64},{64,96},{96,128},{128,160},{160,192},{192,224},{224... | collective-permute-start | bytes 786440 | tf_op jit(solution)/shard_map/ppermute | solution.py:26
  97.7 8.7 %collective-permute-start.17 = (bf16[256,512]{1,0:T(8,128)(2,1)S(1)}, bf16[256,512]{1,0:T(8,128)(2,1)S(1)}, u32[]{:S(2)}, u32[]{:S(2)}) collective-permute-start(bf16[256,512]{1,0:T(8,128)(2,1)S(1)} %get-tuple-element.77.refs_4_), channel_id=1, source_target_pairs={{0,224},{32,0},{64,32},{96,64},{128,96},{160,128},{192,160},{224,1... | collective-permute-start | bytes 786440 | tf_op jit(solution)/shard_map/ppermute | solution.py:26
  102.4 10.4 %collective-permute-start.25 = (bf16[256,512]{1,0:T(8,128)(2,1)S(1)}, bf16[256,512]{1,0:T(8,128)(2,1)S(1)}, u32[]{:S(2)}, u32[]{:S(2)}) collective-permute-start(bf16[256,512]{1,0:T(8,128)(2,1)S(1)} %memorise.3.refs_13_), channel_id=1, source_target_pairs={{0,32},{32,64},{64,96},{96,128},{128,160},{160,192},{192,224},{224... | collective-permute-start | bytes 786440 | tf_op jit(solution)/shard_map/ppermute | solution.py:26
  104.4 9.2 %collective-permute-start.26 = (bf16[256,512]{1,0:T(8,128)(2,1)S(1)}, bf16[256,512]{1,0:T(8,128)(2,1)S(1)}, u32[]{:S(2)}, u32[]{:S(2)}) collective-permute-start(bf16[256,512]{1,0:T(8,128)(2,1)S(1)} %memorise.3.refs_13_), channel_id=1, source_target_pairs={{0,224},{32,0},{64,32},{96,64},{128,96},{160,128},{192,160},{224,1... | collective-permute-start | bytes 786440 | tf_op jit(solution)/shard_map/ppermute | solution.py:26
  105.8 12.6 %collective-permute-start.18 = (bf16[256,512]{1,0:T(8,128)(2,1)S(1)}, bf16[256,512]{1,0:T(8,128)(2,1)S(1)}, u32[]{:S(2)}, u32[]{:S(2)}) collective-permute-start(bf16[256,512]{1,0:T(8,128)(2,1)S(1)} %collective-permute-done.16.refs_5_), channel_id=1, source_target_pairs={{0,32},{32,64},{64,96},{96,128},{128,160},{160,192},{192,224},{224... | collective-permute-start | bytes 786440 | tf_op jit(solution)/shard_map/ppermute | solution.py:26
  106.5 12.8 %collective-permute-start.19 = (bf16[256,512]{1,0:T(8,128)(2,1)S(1)}, bf16[256,512]{1,0:T(8,128)(2,1)S(1)}, u32[]{:S(2)}, u32[]{:S(2)}) collective-permute-start(bf16[256,512]{1,0:T(8,128)(2,1)S(1)} %collective-permute-done.17.refs_6_), channel_id=1, source_target_pairs={{0,224},{32,0},{64,32},{96,64},{128,96},{160,128},{192,160},{224,1... | collective-permute-start | bytes 786440 | tf_op jit(solution)/shard_map/ppermute | solution.py:26
  112.8 11.2 %collective-permute-start.27 = (bf16[256,512]{1,0:T(8,128)(2,1)S(1)}, bf16[256,512]{1,0:T(8,128)(2,1)S(1)}, u32[]{:S(2)}, u32[]{:S(2)}) collective-permute-start(bf16[256,512]{1,0:T(8,128)(2,1)S(1)} %collective-permute-done.25.refs_14_), channel_id=1, source_target_pairs={{0,32},{32,64},{64,96},{96,128},{128,160},{160,192},{192,224},{224... | collective-permute-start | bytes 786440 | tf_op jit(solution)/shard_map/ppermute | solution.py:26
  113.6 11.2 %collective-permute-start.28 = (bf16[256,512]{1,0:T(8,128)(2,1)S(1)}, bf16[256,512]{1,0:T(8,128)(2,1)S(1)}, u32[]{:S(2)}, u32[]{:S(2)}) collective-permute-start(bf16[256,512]{1,0:T(8,128)(2,1)S(1)} %collective-permute-done.26.refs_15_), channel_id=1, source_target_pairs={{0,224},{32,0},{64,32},{96,64},{128,96},{160,128},{192,160},{224,1... | collective-permute-start | bytes 786440 | tf_op jit(solution)/shard_map/ppermute | solution.py:26
  118.5 11.2 %collective-permute-start.20 = (bf16[256,512]{1,0:T(8,128)(2,1)S(1)}, bf16[256,512]{1,0:T(8,128)(2,1)S(1)}, u32[]{:S(2)}, u32[]{:S(2)}) collective-permute-start(bf16[256,512]{1,0:T(8,128)(2,1)S(1)} %collective-permute-done.18.refs_7_), channel_id=1, source_target_pairs={{0,32},{32,64},{64,96},{96,128},{128,160},{160,192},{192,224},{224... | collective-permute-start | bytes 786440 | tf_op jit(solution)/shard_map/ppermute | solution.py:26
  119.2 11.3 %collective-permute-start.21 = (bf16[256,512]{1,0:T(8,128)(2,1)S(1)}, bf16[256,512]{1,0:T(8,128)(2,1)S(1)}, u32[]{:S(2)}, u32[]{:S(2)}) collective-permute-start(bf16[256,512]{1,0:T(8,128)(2,1)S(1)} %collective-permute-done.19.refs_8_), channel_id=1, source_target_pairs={{0,224},{32,0},{64,32},{96,64},{128,96},{160,128},{192,160},{224,1... | collective-permute-start | bytes 786440 | tf_op jit(solution)/shard_map/ppermute | solution.py:26
  124.1 11.2 %collective-permute-start.29 = (bf16[256,512]{1,0:T(8,128)(2,1)S(1)}, bf16[256,512]{1,0:T(8,128)(2,1)S(1)}, u32[]{:S(2)}, u32[]{:S(2)}) collective-permute-start(bf16[256,512]{1,0:T(8,128)(2,1)S(1)} %collective-permute-done.27.refs_16_), channel_id=1, source_target_pairs={{0,32},{32,64},{64,96},{96,128},{128,160},{160,192},{192,224},{224... | collective-permute-start | bytes 786440 | tf_op jit(solution)/shard_map/ppermute | solution.py:26
  124.9 11.3 %collective-permute-start.30 = (bf16[256,512]{1,0:T(8,128)(2,1)S(1)}, bf16[256,512]{1,0:T(8,128)(2,1)S(1)}, u32[]{:S(2)}, u32[]{:S(2)}) collective-permute-start(bf16[256,512]{1,0:T(8,128)(2,1)S(1)} %collective-permute-done.28.refs_17_), channel_id=1, source_target_pairs={{0,224},{32,0},{64,32},{96,64},{128,96},{160,128},{192,160},{224,1... | collective-permute-start | bytes 786440 | tf_op jit(solution)/shard_map/ppermute | solution.py:26
  129.7 9.0 %collective-permute-start.22 = (bf16[128,512]{1,0:T(8,128)(2,1)S(1)}, bf16[128,512]{1,0:T(8,128)(2,1)S(1)}, u32[]{:S(2)}, u32[]{:S(2)}) collective-permute-start(bf16[128,512]{1,0:T(8,128)(2,1)S(1)} %slice.40), channel_id=1, source_target_pairs={{0,32},{32,64},{64,96},{96,128},{128,160},{160,192},{192,224},{224... | collective-permute-start | bytes 393224 | tf_op jit(solution)/shard_map/ppermute | solution.py:26
  130.5 8.2 %collective-permute-start.23 = (bf16[128,512]{1,0:T(8,128)(2,1)S(1)}, bf16[128,512]{1,0:T(8,128)(2,1)S(1)}, u32[]{:S(2)}, u32[]{:S(2)}) collective-permute-start(bf16[128,512]{1,0:T(8,128)(2,1)S(1)} %slice.41), channel_id=1, source_target_pairs={{0,224},{32,0},{64,32},{96,64},{128,96},{160,128},{192,160},{224,1... | collective-permute-start | bytes 393224 | tf_op jit(solution)/shard_map/ppermute | solution.py:26
  135.3 6.3 %collective-permute-start.31 = (bf16[128,512]{1,0:T(8,128)(2,1)S(1)}, bf16[128,512]{1,0:T(8,128)(2,1)S(1)}, u32[]{:S(2)}, u32[]{:S(2)}) collective-permute-start(bf16[128,512]{1,0:T(8,128)(2,1)S(1)} %slice.42), channel_id=1, source_target_pairs={{0,32},{32,64},{64,96},{96,128},{128,160},{160,192},{192,224},{224... | collective-permute-start | bytes 393224 | tf_op jit(solution)/shard_map/ppermute | solution.py:26
  136.2 5.4 %collective-permute-start.32 = (bf16[128,512]{1,0:T(8,128)(2,1)S(1)}, bf16[128,512]{1,0:T(8,128)(2,1)S(1)}, u32[]{:S(2)}, u32[]{:S(2)}) collective-permute-start(bf16[128,512]{1,0:T(8,128)(2,1)S(1)} %slice.43), channel_id=1, source_target_pairs={{0,224},{32,0},{64,32},{96,64},{128,96},{160,128},{192,160},{224,1... | collective-permute-start | bytes 393224 | tf_op jit(solution)/shard_map/ppermute | solution.py:26
  (31 other events, 398.7 us)

commit v10 on v9

--- a/solution.py
+++ b/solution.py
@@ -427,7 +427,7 @@
         ],
         out_shape=jax.ShapeDtypeStruct((NX, 1056, HS), BF),
         cost_estimate=pl.CostEstimate(flops=10**9, bytes_accessed=8 * 2**20, transcendentals=10**6),
-        compiler_params=pltpu.CompilerParams(vmem_limit_bytes=58 * MIB),
+        compiler_params=pltpu.CompilerParams(vmem_limit_bytes=44 * MIB),
         name="windows",
     )(*lists, my_x, *queries, *[piece[-1] for piece in pieces])
 

time: 174 us -> 169 us (0.971)
  blocking collectives: 20.6 us -> 17.2 us
    all_to_all x1, blocking collectives: 20.6 us -> 17.2 us  [on_device(): parts = lax.all_to_all(parts, 'x', split_axis=0, concat_axis=0, tiled=True)]
where the time goes in v10:
time: 169 us; the launch traced here: 167 us
  starting transfers between devices  57.5 us (34%)
  waiting for transfers between devices  50.3 us (30%)
  Pallas kernels  34 us (20%)
  blocking collectives  17.2 us (10%)
  local copies, waits for them, and re-layouts  7.09 us (4%)
    ppermute x33, waiting for transfers between devices, shifted(): return lax.ppermute(value, axis, [(i, (i + steps) % n) for i in range(n)])  50.3 us
    ppermute x33, starting transfers between devices, shifted(): return lax.ppermute(value, axis, [(i, (i + steps) % n) for i in range(n)])  49.1 us
    all_to_all x1, blocking collectives, on_device(): parts = lax.all_to_all(parts, 'x', split_axis=0, concat_axis=0, tiled=True)  17.2 us
    pallas_call x1, Pallas kernels, encode(): pl.pallas_call(encoder_kernel, grid_spec=pltpu.PrefetchScalarGridSpec(num...  9.5 us
    all_to_all x1, starting transfers between devices, spread(): return lax.all_to_all(copies, axis, split_axis=0, concat_axis=0, tiled=True)  8.47 us
    pallas_call x1, Pallas kernels, windows(): pl.pallas_call(functools.partial(window_kernel, layout), in_specs=[smem]...  6.87 us
    pallas_call x2, Pallas kernels, memorise(): pl.pallas_call(functools.partial(memory_kernel, len(us)), in_specs=[pl.Bl...  6.04 us
    pallas_call x1, Pallas kernels, project(): pl.pallas_call(project_kernel, grid=(width // cols,), in_specs=[pl.BlockS...  5.02 us
  transfers between devices with their start and end apart: 34, of which 19 were waited for; matrix products, arithmetic and copies ran while one was open for 3% of the time, Pallas kernels for 13%

profile of v10, /device:TPU:2, one launch (start us, length us, event | category | flops | bytes accessed | tf_op | source)
XLA Modules:
  0.0 167.1 jit_solution(5485349973172898280)
XLA Ops:
  2.0 8.5 %all-to-all-start = ((bf16[8,128,512]{2,1,0:T(8,128)(2,1)}), bf16[8,128,512]{2,1,0:T(8,128)(2,1)S(1)}, u32[]{:S(2)}, u32[]{:S(2)}) async-start(bf16[8,128,512]{2,1,0:T(8,128)(2,1)} %broadcast_in_dim.2), calls=%async_computation | async-start | bytes 2097152 | tf_op jit(solution)/shard_map/all_to_all | solution.py:32
  10.5 9.5 %encoder.1 = (bf16[256,256]{1,0:T(8,128)(2,1)}, bf16[256,256]{1,0:T(8,128)(2,1)}) custom-call(s32[1]{0:T(128)} %bitcast.1.core_ref, s32[1]{0:T(128)} %bitcast.2.y_ref, bf16[512,4096]{1,0:T(8,128)(2,1)} %bitcast.27, bf16[24576,128]{1,0:T(8,128)(2,1)} %bitcast.33, f32[1,4096]{1,0:T(1,128)} %bitcast.34), custom_call_target="tpu_custom_call" | custom-call | flops 3221225472 | bytes 10485760 | tf_op jit(solution)/shard_map/encoder/pallas_call | solution.py:94
  22.9 5.0 %project.1 = (bf16[64,4096]{1,0:T(8,128)(2,1)}, bf16[64,4096]{1,0:T(8,128)(2,1)}, bf16[64,4096]{1,0:T(8,128)(2,1)}, bf16[64,4096]{1,0:T(8,128)(2,1)}) custom-call(bf16[256,256]{1,0:T(8,128)(2,1)} %get-tuple-element.42.a_ref, bf16[256,256]{1,0:T(8,128)(2,1)} %copy-done.12, bf16[256,4096]{1,0:T(8,128)(2,1)} %bitcast.30, bf16[256,4096]{1,0:T(8,128)(2,1)} %copy-done.8), custom_call_target="tpu_custom_call" | custom-call | flops 1073741824 | bytes 4194304 | tf_op jit(solution)/shard_map/project/pallas_call | solution.py:134
  31.8 2.4 %collective-permute-start.5 = (bf16[1040,128]{1,0:T(8,128)(2,1)S(1)}, bf16[1040,128]{1,0:T(8,128)(2,1)S(1)}, u32[]{:S(2)}, u32[]{:S(2)}) collective-permute-start(bf16[1040,128]{1,0:T(8,128)(2,1)S(1)} %fusion.1.refs_0_), channel_id=1, source_target_pairs={{0,16},{8,24},{16,0},{24,8},{1,17},{9,25},{17,1},{25,9},{2,18},{10... | collective-permute-start | bytes 798728 | tf_op jit(solution)/shard_map/ppermute | solution.py:26
  36.0 3.6 %collective-permute-done.4.refs_1_ = bf16[1040,128]{1,0:T(8,128)(2,1)S(1)} collective-permute-done((bf16[1040,128]{1,0:T(8,128)(2,1)S(1)}, bf16[1040,128]{1,0:T(8,128)(2,1)S(1)}, u32[]{:S(2)}, u32[]{:S(2)}) %collective-permute-start.4) | collective-permute-done | bytes 266272 | tf_op jit(solution)/shard_map/ppermute | solution.py:26
  41.6 4.4 %collective-permute-done.5.refs_2_ = bf16[1040,128]{1,0:T(8,128)(2,1)S(1)} collective-permute-done((bf16[1040,128]{1,0:T(8,128)(2,1)S(1)}, bf16[1040,128]{1,0:T(8,128)(2,1)S(1)}, u32[]{:S(2)}, u32[]{:S(2)}) %collective-permute-start.5) | collective-permute-done | bytes 266272 | tf_op jit(solution)/shard_map/ppermute | solution.py:26
  47.1 7.2 %collective-permute-done.3.t3 = bf16[64,4096]{1,0:T(8,128)(2,1)S(1)} collective-permute-done((bf16[64,4096]{1,0:T(8,128)(2,1)}, bf16[64,4096]{1,0:T(8,128)(2,1)S(1)}, u32[]{:S(2)}, u32[]{:S(2)}) %collective-permute-start.3) | collective-permute-done | bytes 524320 | tf_op jit(solution)/shard_map/ppermute | solution.py:26
  57.0 3.1 %normalise.1.refs_0_ = bf16[64,4096]{1,0:T(8,128)(2,1)} custom-call(s32[1]{0:T(128)} %bitcast.block_ref, bf16[64,4096]{1,0:T(8,128)(2,1)} %get-tuple-element.45.t0, bf16[64,4096]{1,0:T(8,128)(2,1)} %copy-done.9, bf16[64,4096]{1,0:T(8,128)(2,1)} %collective-permute-done.7.t2, bf16[64,4096]{1,0:T(8,128)(2,1)} %copy-done.10, bf16[512,4096]{1,0:T(8,128)(2,1)} %bitcast.28, ...), custom_call_target="tpu_custom_call" | custom-call | flops 2097152 | bytes 3145728 | tf_op jit(solution)/shard_map/normalise/pallas_call | solution.py:168
  62.2 2.0 %collective-permute-start.9 = (s32[64]{0:T(128)S(1)}, s32[64]{0:T(128)S(1)}, u32[]{:S(2)}, u32[]{:S(2)}) collective-permute-start(s32[64]{0:T(128)S(1)} %reshape.41), channel_id=1, source_target_pairs={{0,32},{32,64},{64,96},{96,128},{128,160},{160,192},{192,224},{224... | collective-permute-start | bytes 776 | tf_op jit(solution)/shard_map/ppermute | solution.py:26
  64.3 3.4 %collective-permute-start.12 = (bf16[64,4096]{1,0:T(8,128)(2,1)}, bf16[64,4096]{1,0:T(8,128)(2,1)}, u32[]{:S(2)}, u32[]{:S(2)}) collective-permute-start(bf16[64,4096]{1,0:T(8,128)(2,1)} %normalise.1.refs_0_), channel_id=1, source_target_pairs={{0,6},{2,0},{4,2},{6,4},{1,7},{3,1},{5,3},{7,5},{8,14},{10,8},{12,... | collective-permute-start | bytes 1572872 | tf_op jit(solution)/shard_map/ppermute | solution.py:26
  68.3 2.1 %plan.1 = (s32[128]{0:T(128)}, s32[128]{0:T(128)}, s32[2]{0:T(128)}) custom-call(s32[128]{0:T(128)} %pad_add_fusion.ids_ref, s32[1]{0:T(128)} %bitcast.15.z_ref, s32[1]{0:T(128)} %bitcast.16.x_ref, s32[1]{0:T(128)} %bitcast.1.core_ref), custom_call_target="tpu_custom_call" | custom-call | tf_op jit(solution)/shard_map/plan/pallas_call | solution.py:316
  70.4 3.4 %collective-permute-done.8.refs_1_ = bf16[64,4096]{1,0:T(8,128)(2,1)} collective-permute-done((bf16[64,4096]{1,0:T(8,128)(2,1)}, bf16[64,4096]{1,0:T(8,128)(2,1)}, u32[]{:S(2)}, u32[]{:S(2)}) %collective-permute-start.8) | collective-permute-done | bytes 524320 | tf_op jit(solution)/shard_map/ppermute | solution.py:26
  74.9 2.2 %collective-permute-start.13 = (bf16[512,512]{1,0:T(8,128)(2,1)S(1)}, bf16[512,512]{1,0:T(8,128)(2,1)S(1)}, u32[]{:S(2)}, u32[]{:S(2)}) collective-permute-start(bf16[512,512]{1,0:T(8,128)(2,1)S(1)} %slice.34), channel_id=1, source_target_pairs={{0,8},{8,16},{16,24},{24,0},{1,9},{9,17},{17,25},{25,1},{2,10},{10... | collective-permute-start | bytes 1572872 | tf_op jit(solution)/shard_map/ppermute | solution.py:26
  79.8 9.2 %collective-permute-done.13.refs_7_.refs_4_ = bf16[512,512]{1,0:T(8,128)(2,1)S(1)} collective-permute-done((bf16[512,512]{1,0:T(8,128)(2,1)S(1)}, bf16[512,512]{1,0:T(8,128)(2,1)S(1)}, u32[]{:S(2)}, u32[]{:S(2)}) %collective-permute-start.13) | collective-permute-done | bytes 524320 | tf_op jit(solution)/shard_map/ppermute | solution.py:26
  89.2 2.9 %collective-permute-done.15.refs_2_ = bf16[64,4096]{1,0:T(8,128)(2,1)S(1)} collective-permute-done((bf16[64,4096]{1,0:T(8,128)(2,1)S(1)}, bf16[64,4096]{1,0:T(8,128)(2,1)S(1)}, u32[]{:S(2)}, u32[]{:S(2)}) %collective-permute-start.15) | collective-permute-done | bytes 524320 | tf_op jit(solution)/shard_map/ppermute | solution.py:26
  92.1 3.5 %memorise.2 = (bf16[256,512]{1,0:T(8,128)(2,1)S(1)}, bf16[256,4096]{1,0:T(8,128)(2,1)S(1)}) custom-call(s32[2]{0:T(128)S(1)} %pad_add_fusion.1.at_ref, bf16[64,4096]{1,0:T(8,128)(2,1)S(1)} %copy-done, bf16[64,4096]{1,0:T(8,128)(2,1)} %collective-permute-done.8.refs_1_, bf16[64,4096]{1,0:T(8,128)(2,1)S(1)} %collective-permute-done.15.refs_2_, ...), custom_call_target="tpu_custom_call" | custom-call | flops 1073741824 | bytes 4194304 | tf_op jit(solution)/shard_map/memorise/pallas_call | solution.py:238
  95.8 2.0 %collective-permute-start.16 = (bf16[256,512]{1,0:T(8,128)(2,1)S(1)}, bf16[256,512]{1,0:T(8,128)(2,1)S(1)}, u32[]{:S(2)}, u32[]{:S(2)}) collective-permute-start(bf16[256,512]{1,0:T(8,128)(2,1)S(1)} %get-tuple-element.77.refs_4_), channel_id=1, source_target_pairs={{0,32},{32,64},{64,96},{96,128},{128,160},{160,192},{192,224},{224... | collective-permute-start | bytes 786440 | tf_op jit(solution)/shard_map/ppermute | solution.py:26
  99.9 2.5 %memorise.3.refs_13_ = bf16[256,512]{1,0:T(8,128)(2,1)S(1)} custom-call(s32[2]{0:T(128)S(1)} %pad_add_fusion.1.at_ref, bf16[256,4096]{1,0:T(8,128)(2,1)S(1)} %collective-permute-done.24.refs_0_, bf16[1024,512]{1,0:T(8,128)(2,1)S(1)} %bitcast.26, bf16[1024,512]{1,0:T(8,128)(2,1)S(1)} %collective-permute-done.10.refs_5_.refs_2_, ...), custom_call_target="tpu_custom_call" | custom-call | flops 1073741824 | bytes 4194304 | tf_op jit(solution)/shard_map/memorise/pallas_call | solution.py:238
  106.5 2.7 %collective-permute-start.19 = (bf16[256,512]{1,0:T(8,128)(2,1)S(1)}, bf16[256,512]{1,0:T(8,128)(2,1)S(1)}, u32[]{:S(2)}, u32[]{:S(2)}) collective-permute-start(bf16[256,512]{1,0:T(8,128)(2,1)S(1)} %collective-permute-done.17.refs_6_), channel_id=1, source_target_pairs={{0,224},{32,0},{64,32},{96,64},{128,96},{160,128},{192,160},{224,1... | collective-permute-start | bytes 786440 | tf_op jit(solution)/shard_map/ppermute | solution.py:26
  109.2 3.7 %collective-permute-done.25.refs_14_ = bf16[256,512]{1,0:T(8,128)(2,1)S(1)} collective-permute-done((bf16[256,512]{1,0:T(8,128)(2,1)S(1)}, bf16[256,512]{1,0:T(8,128)(2,1)S(1)}, u32[]{:S(2)}, u32[]{:S(2)}) %collective-permute-start.25) | collective-permute-done | bytes 262176 | tf_op jit(solution)/shard_map/ppermute | solution.py:26
  113.6 2.5 %collective-permute-start.28 = (bf16[256,512]{1,0:T(8,128)(2,1)S(1)}, bf16[256,512]{1,0:T(8,128)(2,1)S(1)}, u32[]{:S(2)}, u32[]{:S(2)}) collective-permute-start(bf16[256,512]{1,0:T(8,128)(2,1)S(1)} %collective-permute-done.26.refs_15_), channel_id=1, source_target_pairs={{0,224},{32,0},{64,32},{96,64},{128,96},{160,128},{192,160},{224,1... | collective-permute-start | bytes 786440 | tf_op jit(solution)/shard_map/ppermute | solution.py:26
  116.1 2.4 %collective-permute-done.18.refs_7_ = bf16[256,512]{1,0:T(8,128)(2,1)S(1)} collective-permute-done((bf16[256,512]{1,0:T(8,128)(2,1)S(1)}, bf16[256,512]{1,0:T(8,128)(2,1)S(1)}, u32[]{:S(2)}, u32[]{:S(2)}) %collective-permute-start.18) | collective-permute-done | bytes 262176 | tf_op jit(solution)/shard_map/ppermute | solution.py:26
  119.2 2.5 %collective-permute-start.21 = (bf16[256,512]{1,0:T(8,128)(2,1)S(1)}, bf16[256,512]{1,0:T(8,128)(2,1)S(1)}, u32[]{:S(2)}, u32[]{:S(2)}) collective-permute-start(bf16[256,512]{1,0:T(8,128)(2,1)S(1)} %collective-permute-done.19.refs_8_), channel_id=1, source_target_pairs={{0,224},{32,0},{64,32},{96,64},{128,96},{160,128},{192,160},{224,1... | collective-permute-start | bytes 786440 | tf_op jit(solution)/shard_map/ppermute | solution.py:26
  121.7 2.4 %collective-permute-done.27.refs_16_ = bf16[256,512]{1,0:T(8,128)(2,1)S(1)} collective-permute-done((bf16[256,512]{1,0:T(8,128)(2,1)S(1)}, bf16[256,512]{1,0:T(8,128)(2,1)S(1)}, u32[]{:S(2)}, u32[]{:S(2)}) %collective-permute-start.27) | collective-permute-done | bytes 262176 | tf_op jit(solution)/shard_map/ppermute | solution.py:26
  124.8 2.5 %collective-permute-start.30 = (bf16[256,512]{1,0:T(8,128)(2,1)S(1)}, bf16[256,512]{1,0:T(8,128)(2,1)S(1)}, u32[]{:S(2)}, u32[]{:S(2)}) collective-permute-start(bf16[256,512]{1,0:T(8,128)(2,1)S(1)} %collective-permute-done.28.refs_17_), channel_id=1, source_target_pairs={{0,224},{32,0},{64,32},{96,64},{128,96},{160,128},{192,160},{224,1... | collective-permute-start | bytes 786440 | tf_op jit(solution)/shard_map/ppermute | solution.py:26
  127.3 2.4 %collective-permute-done.20.refs_9_ = bf16[256,512]{1,0:T(8,128)(2,1)S(1)} collective-permute-done((bf16[256,512]{1,0:T(8,128)(2,1)S(1)}, bf16[256,512]{1,0:T(8,128)(2,1)S(1)}, u32[]{:S(2)}, u32[]{:S(2)}) %collective-permute-start.20) | collective-permute-done | bytes 262176 | tf_op jit(solution)/shard_map/ppermute | solution.py:26
  130.5 2.6 %collective-permute-start.23 = (bf16[128,512]{1,0:T(8,128)(2,1)S(1)}, bf16[128,512]{1,0:T(8,128)(2,1)S(1)}, u32[]{:S(2)}, u32[]{:S(2)}) collective-permute-start(bf16[128,512]{1,0:T(8,128)(2,1)S(1)} %slice.41), channel_id=1, source_target_pairs={{0,224},{32,0},{64,32},{96,64},{128,96},{160,128},{192,160},{224,1... | collective-permute-start | bytes 393224 | tf_op jit(solution)/shard_map/ppermute | solution.py:26
  133.1 2.2 %collective-permute-done.29.refs_18_ = bf16[256,512]{1,0:T(8,128)(2,1)S(1)} collective-permute-done((bf16[256,512]{1,0:T(8,128)(2,1)S(1)}, bf16[256,512]{1,0:T(8,128)(2,1)S(1)}, u32[]{:S(2)}, u32[]{:S(2)}) %collective-permute-start.29) | collective-permute-done | bytes 262176 | tf_op jit(solution)/shard_map/ppermute | solution.py:26
  136.2 2.6 %collective-permute-start.32 = (bf16[128,512]{1,0:T(8,128)(2,1)S(1)}, bf16[128,512]{1,0:T(8,128)(2,1)S(1)}, u32[]{:S(2)}, u32[]{:S(2)}) collective-permute-start(bf16[128,512]{1,0:T(8,128)(2,1)S(1)} %slice.43), channel_id=1, source_target_pairs={{0,224},{32,0},{64,32},{96,64},{128,96},{160,128},{192,160},{224,1... | collective-permute-start | bytes 393224 | tf_op jit(solution)/shard_map/ppermute | solution.py:26
  138.7 2.8 %collective-permute-done.31.refs_20_ = bf16[128,512]{1,0:T(8,128)(2,1)S(1)} collective-permute-done((bf16[128,512]{1,0:T(8,128)(2,1)S(1)}, bf16[128,512]{1,0:T(8,128)(2,1)S(1)}, u32[]{:S(2)}, u32[]{:S(2)}) %collective-permute-start.31) | collective-permute-done | bytes 131104 | tf_op jit(solution)/shard_map/ppermute | solution.py:26
  141.6 6.9 %windows.1 = bf16[4,1056,128]{2,1,0:T(8,128)(2,1)S(1)} custom-call(s32[128]{0:T(128)S(1)} %copy-done.5, s32[128]{0:T(128)S(1)} %copy-done.6, s32[2]{0:T(128)S(1)} %copy-done.7, s32[1]{0:T(128)} %bitcast.16.x_ref, bf16[1040,128]{1,0:T(8,128)(2,1)S(1)} %fusion.1.refs_0_, bf16[1040,128]{1,0:T(8,128)(2,1)S(1)} %copy-done.2, bf16[1040,128]{1,0:T(8,128)(2,1)S(1)} %copy-done.4, ...), custom_call_target="tpu_custom_call" | custom-call | flops 1000000000 | bytes 8388608 | tf_op jit(solution)/shard_map/windows/pallas_call | solution.py:415
  148.5 17.2 %all_to_all.10.parts_ref = bf16[4,1056,128]{2,1,0:T(8,128)(2,1)S(1)} all-to-all(bf16[4,1056,128]{2,1,0:T(8,128)(2,1)S(1)} %windows.1), channel_id=1, replica_groups=mesh['z'=8,'x'=4,'y'=4,'c'=2] {'x'}, dimensions={0} | all-to-all | bytes 2162688 | tf_op jit(solution)/shard_map/all_to_all | solution.py:514
  (95 shorter events, 34.7 us)
Async XLA Ops:
  0.0 21.6 %collective-permute-start.1 = (bf16[256,4096]{1,0:T(8,128)(2,1)}, bf16[256,4096]{1,0:T(8,128)(2,1)S(1)}, u32[]{:S(2)}, u32[]{:S(2)}) collective-permute-start(bf16[256,4096]{1,0:T(8,128)(2,1)} %bitcast.29), channel_id=1, source_target_pairs={{0,1},{1,0},{2,3},{3,2},{4,5},{5,4},{6,7},{7,6},{8,9},{9,8},{10,11... | collective-permute-start | bytes 6291464 | tf_op jit(solution)/shard_map/ppermute | solution.py:26
  2.0 45.0 %all-to-all-start = ((bf16[8,128,512]{2,1,0:T(8,128)(2,1)}), bf16[8,128,512]{2,1,0:T(8,128)(2,1)S(1)}, u32[]{:S(2)}, u32[]{:S(2)}) async-start(bf16[8,128,512]{2,1,0:T(8,128)(2,1)} %broadcast_in_dim.2), calls=%async_computation | async-start | bytes 2097152 | tf_op jit(solution)/shard_map/all_to_all | solution.py:32
  28.0 19.1 %collective-permute-start.2 = (bf16[64,4096]{1,0:T(8,128)(2,1)}, bf16[64,4096]{1,0:T(8,128)(2,1)S(1)}, u32[]{:S(2)}, u32[]{:S(2)}) collective-permute-start(bf16[64,4096]{1,0:T(8,128)(2,1)} %get-tuple-element.46), channel_id=1, source_target_pairs={{0,2},{2,4},{4,6},{6,0},{1,3},{3,5},{5,7},{7,1},{8,10},{10,12},{12... | collective-permute-start | bytes 1572872 | tf_op jit(solution)/shard_map/ppermute | solution.py:26
  29.5 24.7 %collective-permute-start.3 = (bf16[64,4096]{1,0:T(8,128)(2,1)}, bf16[64,4096]{1,0:T(8,128)(2,1)S(1)}, u32[]{:S(2)}, u32[]{:S(2)}) collective-permute-start(bf16[64,4096]{1,0:T(8,128)(2,1)} %get-tuple-element.47), channel_id=1, source_target_pairs={{0,6},{2,0},{4,2},{6,4},{1,7},{3,1},{5,3},{7,5},{8,14},{10,8},{12,... | collective-permute-start | bytes 1572872 | tf_op jit(solution)/shard_map/ppermute | solution.py:26
  31.2 8.4 %collective-permute-start.4 = (bf16[1040,128]{1,0:T(8,128)(2,1)S(1)}, bf16[1040,128]{1,0:T(8,128)(2,1)S(1)}, u32[]{:S(2)}, u32[]{:S(2)}) collective-permute-start(bf16[1040,128]{1,0:T(8,128)(2,1)S(1)} %fusion.1.refs_0_), channel_id=1, source_target_pairs={{0,24},{8,0},{16,8},{24,16},{1,25},{9,1},{17,9},{25,17},{2,26},{10... | collective-permute-start | bytes 798728 | tf_op jit(solution)/shard_map/ppermute | solution.py:26
  31.8 14.2 %collective-permute-start.5 = (bf16[1040,128]{1,0:T(8,128)(2,1)S(1)}, bf16[1040,128]{1,0:T(8,128)(2,1)S(1)}, u32[]{:S(2)}, u32[]{:S(2)}) collective-permute-start(bf16[1040,128]{1,0:T(8,128)(2,1)S(1)} %fusion.1.refs_0_), channel_id=1, source_target_pairs={{0,16},{8,24},{16,0},{24,8},{1,17},{9,25},{17,1},{25,9},{2,18},{10... | collective-permute-start | bytes 798728 | tf_op jit(solution)/shard_map/ppermute | solution.py:26
  34.2 12.8 %collective-permute-start.6 = (bf16[1040,128]{1,0:T(8,128)(2,1)S(1)}, bf16[1040,128]{1,0:T(8,128)(2,1)}, u32[]{:S(2)}, u32[]{:S(2)}) collective-permute-start(bf16[1040,128]{1,0:T(8,128)(2,1)S(1)} %fusion.1.refs_0_), channel_id=1, source_target_pairs={{0,8},{8,16},{16,24},{24,0},{1,9},{9,17},{17,25},{25,1},{2,10},{10... | collective-permute-start | bytes 798728 | tf_op jit(solution)/shard_map/ppermute | solution.py:26
  39.6 17.4 %collective-permute-start.7 = (bf16[64,4096]{1,0:T(8,128)(2,1)}, bf16[64,4096]{1,0:T(8,128)(2,1)}, u32[]{:S(2)}, u32[]{:S(2)}) collective-permute-start(bf16[64,4096]{1,0:T(8,128)(2,1)} %get-tuple-element.51), channel_id=1, source_target_pairs={{0,4},{2,6},{4,0},{6,2},{1,5},{3,7},{5,1},{7,3},{8,12},{10,14},{12... | collective-permute-start | bytes 1572872 | tf_op jit(solution)/shard_map/ppermute | solution.py:26
  55.0 19.7 %collective-permute-start.10 = (bf16[1024,512]{1,0:T(8,128)(2,1)S(1)}, bf16[1024,512]{1,0:T(8,128)(2,1)S(1)}, u32[]{:S(2)}, u32[]{:S(2)}) collective-permute-start(bf16[1024,512]{1,0:T(8,128)(2,1)S(1)} %bitcast.23), channel_id=1, source_target_pairs={{0,8},{8,16},{16,24},{24,0},{1,9},{9,17},{17,25},{25,1},{2,10},{10... | collective-permute-start | bytes 3145736 | tf_op jit(solution)/shard_map/ppermute | solution.py:26
  56.5 18.4 %collective-permute-start.11 = (bf16[1024,512]{1,0:T(8,128)(2,1)S(1)}, bf16[1024,512]{1,0:T(8,128)(2,1)S(1)}, u32[]{:S(2)}, u32[]{:S(2)}) collective-permute-start(bf16[1024,512]{1,0:T(8,128)(2,1)S(1)} %bitcast.24), channel_id=1, source_target_pairs={{0,24},{8,0},{16,8},{24,16},{1,25},{9,1},{17,9},{25,17},{2,26},{10... | collective-permute-start | bytes 3145736 | tf_op jit(solution)/shard_map/ppermute | solution.py:26
  60.1 13.7 %collective-permute-start.8 = (bf16[64,4096]{1,0:T(8,128)(2,1)}, bf16[64,4096]{1,0:T(8,128)(2,1)}, u32[]{:S(2)}, u32[]{:S(2)}) collective-permute-start(bf16[64,4096]{1,0:T(8,128)(2,1)} %normalise.1.refs_0_), channel_id=1, source_target_pairs={{0,2},{2,4},{4,6},{6,0},{1,3},{3,5},{5,7},{7,1},{8,10},{10,12},{12... | collective-permute-start | bytes 1572872 | tf_op jit(solution)/shard_map/ppermute | solution.py:26
  62.2 5.5 %collective-permute-start.9 = (s32[64]{0:T(128)S(1)}, s32[64]{0:T(128)S(1)}, u32[]{:S(2)}, u32[]{:S(2)}) collective-permute-start(s32[64]{0:T(128)S(1)} %reshape.41), channel_id=1, source_target_pairs={{0,32},{32,64},{64,96},{96,128},{128,160},{160,192},{192,224},{224... | collective-permute-start | bytes 776 | tf_op jit(solution)/shard_map/ppermute | solution.py:26
  64.3 15.5 %collective-permute-start.12 = (bf16[64,4096]{1,0:T(8,128)(2,1)}, bf16[64,4096]{1,0:T(8,128)(2,1)}, u32[]{:S(2)}, u32[]{:S(2)}) collective-permute-start(bf16[64,4096]{1,0:T(8,128)(2,1)} %normalise.1.refs_0_), channel_id=1, source_target_pairs={{0,6},{2,0},{4,2},{6,4},{1,7},{3,1},{5,3},{7,5},{8,14},{10,8},{12,... | collective-permute-start | bytes 1572872 | tf_op jit(solution)/shard_map/ppermute | solution.py:26
  74.9 14.1 %collective-permute-start.13 = (bf16[512,512]{1,0:T(8,128)(2,1)S(1)}, bf16[512,512]{1,0:T(8,128)(2,1)S(1)}, u32[]{:S(2)}, u32[]{:S(2)}) collective-permute-start(bf16[512,512]{1,0:T(8,128)(2,1)S(1)} %slice.34), channel_id=1, source_target_pairs={{0,8},{8,16},{16,24},{24,0},{1,9},{9,17},{17,25},{25,1},{2,10},{10... | collective-permute-start | bytes 1572872 | tf_op jit(solution)/shard_map/ppermute | solution.py:26
  77.2 12.0 %collective-permute-start.14 = (bf16[512,512]{1,0:T(8,128)(2,1)S(1)}, bf16[512,512]{1,0:T(8,128)(2,1)S(1)}, u32[]{:S(2)}, u32[]{:S(2)}) collective-permute-start(bf16[512,512]{1,0:T(8,128)(2,1)S(1)} %slice.35), channel_id=1, source_target_pairs={{0,24},{8,0},{16,8},{24,16},{1,25},{9,1},{17,9},{25,17},{2,26},{10... | collective-permute-start | bytes 1572872 | tf_op jit(solution)/shard_map/ppermute | solution.py:26
  77.9 14.2 %collective-permute-start.15 = (bf16[64,4096]{1,0:T(8,128)(2,1)S(1)}, bf16[64,4096]{1,0:T(8,128)(2,1)S(1)}, u32[]{:S(2)}, u32[]{:S(2)}) collective-permute-start(bf16[64,4096]{1,0:T(8,128)(2,1)S(1)} %copy-done), channel_id=1, source_target_pairs={{0,4},{2,6},{4,0},{6,2},{1,5},{3,7},{5,1},{7,3},{8,12},{10,14},{12... | collective-permute-start | bytes 1572872 | tf_op jit(solution)/shard_map/ppermute | solution.py:26
  95.8 10.2 %collective-permute-start.16 = (bf16[256,512]{1,0:T(8,128)(2,1)S(1)}, bf16[256,512]{1,0:T(8,128)(2,1)S(1)}, u32[]{:S(2)}, u32[]{:S(2)}) collective-permute-start(bf16[256,512]{1,0:T(8,128)(2,1)S(1)} %get-tuple-element.77.refs_4_), channel_id=1, source_target_pairs={{0,32},{32,64},{64,96},{96,128},{128,160},{160,192},{192,224},{224... | collective-permute-start | bytes 786440 | tf_op jit(solution)/shard_map/ppermute | solution.py:26
  97.8 8.7 %collective-permute-start.17 = (bf16[256,512]{1,0:T(8,128)(2,1)S(1)}, bf16[256,512]{1,0:T(8,128)(2,1)S(1)}, u32[]{:S(2)}, u32[]{:S(2)}) collective-permute-start(bf16[256,512]{1,0:T(8,128)(2,1)S(1)} %get-tuple-element.77.refs_4_), channel_id=1, source_target_pairs={{0,224},{32,0},{64,32},{96,64},{128,96},{160,128},{192,160},{224,1... | collective-permute-start | bytes 786440 | tf_op jit(solution)/shard_map/ppermute | solution.py:26
  102.4 10.4 %collective-permute-start.25 = (bf16[256,512]{1,0:T(8,128)(2,1)S(1)}, bf16[256,512]{1,0:T(8,128)(2,1)S(1)}, u32[]{:S(2)}, u32[]{:S(2)}) collective-permute-start(bf16[256,512]{1,0:T(8,128)(2,1)S(1)} %memorise.3.refs_13_), channel_id=1, source_target_pairs={{0,32},{32,64},{64,96},{96,128},{128,160},{160,192},{192,224},{224... | collective-permute-start | bytes 786440 | tf_op jit(solution)/shard_map/ppermute | solution.py:26
  104.4 9.2 %collective-permute-start.26 = (bf16[256,512]{1,0:T(8,128)(2,1)S(1)}, bf16[256,512]{1,0:T(8,128)(2,1)S(1)}, u32[]{:S(2)}, u32[]{:S(2)}) collective-permute-start(bf16[256,512]{1,0:T(8,128)(2,1)S(1)} %memorise.3.refs_13_), channel_id=1, source_target_pairs={{0,224},{32,0},{64,32},{96,64},{128,96},{160,128},{192,160},{224,1... | collective-permute-start | bytes 786440 | tf_op jit(solution)/shard_map/ppermute | solution.py:26
  105.9 12.5 %collective-permute-start.18 = (bf16[256,512]{1,0:T(8,128)(2,1)S(1)}, bf16[256,512]{1,0:T(8,128)(2,1)S(1)}, u32[]{:S(2)}, u32[]{:S(2)}) collective-permute-start(bf16[256,512]{1,0:T(8,128)(2,1)S(1)} %collective-permute-done.16.refs_5_), channel_id=1, source_target_pairs={{0,32},{32,64},{64,96},{96,128},{128,160},{160,192},{192,224},{224... | collective-permute-start | bytes 786440 | tf_op jit(solution)/shard_map/ppermute | solution.py:26
  106.5 12.8 %collective-permute-start.19 = (bf16[256,512]{1,0:T(8,128)(2,1)S(1)}, bf16[256,512]{1,0:T(8,128)(2,1)S(1)}, u32[]{:S(2)}, u32[]{:S(2)}) collective-permute-start(bf16[256,512]{1,0:T(8,128)(2,1)S(1)} %collective-permute-done.17.refs_6_), channel_id=1, source_target_pairs={{0,224},{32,0},{64,32},{96,64},{128,96},{160,128},{192,160},{224,1... | collective-permute-start | bytes 786440 | tf_op jit(solution)/shard_map/ppermute | solution.py:26
  112.8 11.2 %collective-permute-start.27 = (bf16[256,512]{1,0:T(8,128)(2,1)S(1)}, bf16[256,512]{1,0:T(8,128)(2,1)S(1)}, u32[]{:S(2)}, u32[]{:S(2)}) collective-permute-start(bf16[256,512]{1,0:T(8,128)(2,1)S(1)} %collective-permute-done.25.refs_14_), channel_id=1, source_target_pairs={{0,32},{32,64},{64,96},{96,128},{128,160},{160,192},{192,224},{224... | collective-permute-start | bytes 786440 | tf_op jit(solution)/shard_map/ppermute | solution.py:26
  113.6 11.2 %collective-permute-start.28 = (bf16[256,512]{1,0:T(8,128)(2,1)S(1)}, bf16[256,512]{1,0:T(8,128)(2,1)S(1)}, u32[]{:S(2)}, u32[]{:S(2)}) collective-permute-start(bf16[256,512]{1,0:T(8,128)(2,1)S(1)} %collective-permute-done.26.refs_15_), channel_id=1, source_target_pairs={{0,224},{32,0},{64,32},{96,64},{128,96},{160,128},{192,160},{224,1... | collective-permute-start | bytes 786440 | tf_op jit(solution)/shard_map/ppermute | solution.py:26
  118.5 11.2 %collective-permute-start.20 = (bf16[256,512]{1,0:T(8,128)(2,1)S(1)}, bf16[256,512]{1,0:T(8,128)(2,1)S(1)}, u32[]{:S(2)}, u32[]{:S(2)}) collective-permute-start(bf16[256,512]{1,0:T(8,128)(2,1)S(1)} %collective-permute-done.18.refs_7_), channel_id=1, source_target_pairs={{0,32},{32,64},{64,96},{96,128},{128,160},{160,192},{192,224},{224... | collective-permute-start | bytes 786440 | tf_op jit(solution)/shard_map/ppermute | solution.py:26
  119.2 11.3 %collective-permute-start.21 = (bf16[256,512]{1,0:T(8,128)(2,1)S(1)}, bf16[256,512]{1,0:T(8,128)(2,1)S(1)}, u32[]{:S(2)}, u32[]{:S(2)}) collective-permute-start(bf16[256,512]{1,0:T(8,128)(2,1)S(1)} %collective-permute-done.19.refs_8_), channel_id=1, source_target_pairs={{0,224},{32,0},{64,32},{96,64},{128,96},{160,128},{192,160},{224,1... | collective-permute-start | bytes 786440 | tf_op jit(solution)/shard_map/ppermute | solution.py:26
  124.1 11.2 %collective-permute-start.29 = (bf16[256,512]{1,0:T(8,128)(2,1)S(1)}, bf16[256,512]{1,0:T(8,128)(2,1)S(1)}, u32[]{:S(2)}, u32[]{:S(2)}) collective-permute-start(bf16[256,512]{1,0:T(8,128)(2,1)S(1)} %collective-permute-done.27.refs_16_), channel_id=1, source_target_pairs={{0,32},{32,64},{64,96},{96,128},{128,160},{160,192},{192,224},{224... | collective-permute-start | bytes 786440 | tf_op jit(solution)/shard_map/ppermute | solution.py:26
  124.8 11.3 %collective-permute-start.30 = (bf16[256,512]{1,0:T(8,128)(2,1)S(1)}, bf16[256,512]{1,0:T(8,128)(2,1)S(1)}, u32[]{:S(2)}, u32[]{:S(2)}) collective-permute-start(bf16[256,512]{1,0:T(8,128)(2,1)S(1)} %collective-permute-done.28.refs_17_), channel_id=1, source_target_pairs={{0,224},{32,0},{64,32},{96,64},{128,96},{160,128},{192,160},{224,1... | collective-permute-start | bytes 786440 | tf_op jit(solution)/shard_map/ppermute | solution.py:26
  129.7 9.0 %collective-permute-start.22 = (bf16[128,512]{1,0:T(8,128)(2,1)S(1)}, bf16[128,512]{1,0:T(8,128)(2,1)S(1)}, u32[]{:S(2)}, u32[]{:S(2)}) collective-permute-start(bf16[128,512]{1,0:T(8,128)(2,1)S(1)} %slice.40), channel_id=1, source_target_pairs={{0,32},{32,64},{64,96},{96,128},{128,160},{160,192},{192,224},{224... | collective-permute-start | bytes 393224 | tf_op jit(solution)/shard_map/ppermute | solution.py:26
  130.5 8.2 %collective-permute-start.23 = (bf16[128,512]{1,0:T(8,128)(2,1)S(1)}, bf16[128,512]{1,0:T(8,128)(2,1)S(1)}, u32[]{:S(2)}, u32[]{:S(2)}) collective-permute-start(bf16[128,512]{1,0:T(8,128)(2,1)S(1)} %slice.41), channel_id=1, source_target_pairs={{0,224},{32,0},{64,32},{96,64},{128,96},{160,128},{192,160},{224,1... | collective-permute-start | bytes 393224 | tf_op jit(solution)/shard_map/ppermute | solution.py:26
  135.3 6.3 %collective-permute-start.31 = (bf16[128,512]{1,0:T(8,128)(2,1)S(1)}, bf16[128,512]{1,0:T(8,128)(2,1)S(1)}, u32[]{:S(2)}, u32[]{:S(2)}) collective-permute-start(bf16[128,512]{1,0:T(8,128)(2,1)S(1)} %slice.42), channel_id=1, source_target_pairs={{0,32},{32,64},{64,96},{96,128},{128,160},{160,192},{192,224},{224... | collective-permute-start | bytes 393224 | tf_op jit(solution)/shard_map/ppermute | solution.py:26
  136.2 5.4 %collective-permute-start.32 = (bf16[128,512]{1,0:T(8,128)(2,1)S(1)}, bf16[128,512]{1,0:T(8,128)(2,1)S(1)}, u32[]{:S(2)}, u32[]{:S(2)}) collective-permute-start(bf16[128,512]{1,0:T(8,128)(2,1)S(1)} %slice.43), channel_id=1, source_target_pairs={{0,224},{32,0},{64,32},{96,64},{128,96},{160,128},{192,160},{224,1... | collective-permute-start | bytes 393224 | tf_op jit(solution)/shard_map/ppermute | solution.py:26
  (16 other events, 277.6 us)

commit v11 on v10

--- a/solution.py
+++ b/solution.py
@@ -145,7 +145,7 @@
         cost_estimate=pl.CostEstimate(
             flops=4 * tokens * depth * width, bytes_accessed=4 * depth * width, transcendentals=0
         ),
-        compiler_params=pltpu.CompilerParams(vmem_limit_bytes=60 * MIB),
+        compiler_params=pltpu.CompilerParams(vmem_limit_bytes=44 * MIB),
         name="project",
     )(att, att_other, e_own, e_other)
 

time: 169 us -> 169 us (level)
  Pallas kernels: 34 us -> 31 us
  blocking collectives: 17.2 us -> 20 us
    all_to_all x1, blocking collectives: 17.2 us -> 20 us  [on_device(): parts = lax.all_to_all(parts, 'x', split_axis=0, concat_axis=0, tiled=True)]
    pallas_call x1, Pallas kernels: 6.87 us -> 4.08 us  [windows(): pl.pallas_call(functools.partial(window_kernel, layout), in_specs=[smem]...]
where the time goes in v11:
time: 169 us; the launch traced here: 166 us
  starting transfers between devices  57.5 us (34%)
  waiting for transfers between devices  50.3 us (30%)
  Pallas kernels  31 us (18%)
  blocking collectives  20 us (12%)
  local copies, waits for them, and re-layouts  6.64 us (4%)
    ppermute x33, waiting for transfers between devices, shifted(): return lax.ppermute(value, axis, [(i, (i + steps) % n) for i in range(n)])  50.3 us
    ppermute x33, starting transfers between devices, shifted(): return lax.ppermute(value, axis, [(i, (i + steps) % n) for i in range(n)])  49.1 us
    all_to_all x1, blocking collectives, on_device(): parts = lax.all_to_all(parts, 'x', split_axis=0, concat_axis=0, tiled=True)  20 us
    pallas_call x1, Pallas kernels, encode(): pl.pallas_call(encoder_kernel, grid_spec=pltpu.PrefetchScalarGridSpec(num...  9.63 us
    all_to_all x1, starting transfers between devices, spread(): return lax.all_to_all(copies, axis, split_axis=0, concat_axis=0, tiled=True)  8.47 us
    pallas_call x2, Pallas kernels, memorise(): pl.pallas_call(functools.partial(memory_kernel, len(us)), in_specs=[pl.Bl...  6.04 us
    pallas_call x1, Pallas kernels, project(): pl.pallas_call(project_kernel, grid=(width // cols,), in_specs=[pl.BlockS...  4.62 us
    pallas_call x1, Pallas kernels, windows(): pl.pallas_call(functools.partial(window_kernel, layout), in_specs=[smem]...  4.08 us
  transfers between devices with their start and end apart: 34, of which 19 were waited for; matrix products, arithmetic and copies ran while one was open for 3% of the time, Pallas kernels for 13%

profile of v11, /device:TPU:2, one launch (start us, length us, event | category | flops | bytes accessed | tf_op | source)
XLA Modules:
  0.0 166.3 jit_solution(1576324284127427728)
XLA Ops:
  2.0 8.5 %all-to-all-start = ((bf16[8,128,512]{2,1,0:T(8,128)(2,1)}), bf16[8,128,512]{2,1,0:T(8,128)(2,1)S(1)}, u32[]{:S(2)}, u32[]{:S(2)}) async-start(bf16[8,128,512]{2,1,0:T(8,128)(2,1)} %broadcast_in_dim.2), calls=%async_computation | async-start | bytes 2097152 | tf_op jit(solution)/shard_map/all_to_all | solution.py:32
  10.5 9.6 %encoder.1 = (bf16[256,256]{1,0:T(8,128)(2,1)}, bf16[256,256]{1,0:T(8,128)(2,1)}) custom-call(s32[1]{0:T(128)} %bitcast.1.core_ref, s32[1]{0:T(128)} %bitcast.2.y_ref, bf16[512,4096]{1,0:T(8,128)(2,1)} %bitcast.29, bf16[24576,128]{1,0:T(8,128)(2,1)} %bitcast.33, f32[1,4096]{1,0:T(1,128)} %bitcast.34), custom_call_target="tpu_custom_call" | custom-call | flops 3221225472 | bytes 10485760 | tf_op jit(solution)/shard_map/encoder/pallas_call | solution.py:94
  22.6 4.6 %project.1 = (bf16[64,4096]{1,0:T(8,128)(2,1)S(1)}, bf16[64,4096]{1,0:T(8,128)(2,1)}, bf16[64,4096]{1,0:T(8,128)(2,1)}, bf16[64,4096]{1,0:T(8,128)(2,1)}) custom-call(bf16[256,256]{1,0:T(8,128)(2,1)S(1)} %copy-done.7, bf16[256,256]{1,0:T(8,128)(2,1)S(1)} %collective-permute-done.b_ref, bf16[256,4096]{1,0:T(8,128)(2,1)S(1)} %bitcast.28, ...), custom_call_target="tpu_custom_call" | custom-call | flops 1073741824 | bytes 4194304 | tf_op jit(solution)/shard_map/project/pallas_call | solution.py:134
  31.1 2.4 %collective-permute-start.5 = (bf16[1040,128]{1,0:T(8,128)(2,1)S(1)}, bf16[1040,128]{1,0:T(8,128)(2,1)S(1)}, u32[]{:S(2)}, u32[]{:S(2)}) collective-permute-start(bf16[1040,128]{1,0:T(8,128)(2,1)S(1)} %fusion.1.refs_0_), channel_id=1, source_target_pairs={{0,16},{8,24},{16,0},{24,8},{1,17},{9,25},{17,1},{25,9},{2,18},{10... | collective-permute-start | bytes 798728 | tf_op jit(solution)/shard_map/ppermute | solution.py:26
  35.3 3.6 %collective-permute-done.4.refs_1_ = bf16[1040,128]{1,0:T(8,128)(2,1)S(1)} collective-permute-done((bf16[1040,128]{1,0:T(8,128)(2,1)S(1)}, bf16[1040,128]{1,0:T(8,128)(2,1)S(1)}, u32[]{:S(2)}, u32[]{:S(2)}) %collective-permute-start.4) | collective-permute-done | bytes 266272 | tf_op jit(solution)/shard_map/ppermute | solution.py:26
  41.0 4.4 %collective-permute-done.5.refs_2_ = bf16[1040,128]{1,0:T(8,128)(2,1)S(1)} collective-permute-done((bf16[1040,128]{1,0:T(8,128)(2,1)S(1)}, bf16[1040,128]{1,0:T(8,128)(2,1)S(1)}, u32[]{:S(2)}, u32[]{:S(2)}) %collective-permute-start.5) | collective-permute-done | bytes 266272 | tf_op jit(solution)/shard_map/ppermute | solution.py:26
  46.3 7.2 %collective-permute-done.3.t3 = bf16[64,4096]{1,0:T(8,128)(2,1)S(1)} collective-permute-done((bf16[64,4096]{1,0:T(8,128)(2,1)}, bf16[64,4096]{1,0:T(8,128)(2,1)S(1)}, u32[]{:S(2)}, u32[]{:S(2)}) %collective-permute-start.3) | collective-permute-done | bytes 524320 | tf_op jit(solution)/shard_map/ppermute | solution.py:26
  56.3 3.1 %normalise.1.refs_0_ = bf16[64,4096]{1,0:T(8,128)(2,1)} custom-call(s32[1]{0:T(128)} %bitcast.block_ref, bf16[64,4096]{1,0:T(8,128)(2,1)} %copy-done.2, bf16[64,4096]{1,0:T(8,128)(2,1)} %copy-done.11, bf16[64,4096]{1,0:T(8,128)(2,1)} %collective-permute-done.7.t2, bf16[64,4096]{1,0:T(8,128)(2,1)} %copy-done.12, bf16[512,4096]{1,0:T(8,128)(2,1)} %bitcast.30, ...), custom_call_target="tpu_custom_call" | custom-call | flops 2097152 | bytes 3145728 | tf_op jit(solution)/shard_map/normalise/pallas_call | solution.py:168
  63.5 3.4 %collective-permute-start.12 = (bf16[64,4096]{1,0:T(8,128)(2,1)}, bf16[64,4096]{1,0:T(8,128)(2,1)}, u32[]{:S(2)}, u32[]{:S(2)}) collective-permute-start(bf16[64,4096]{1,0:T(8,128)(2,1)} %normalise.1.refs_0_), channel_id=1, source_target_pairs={{0,6},{2,0},{4,2},{6,4},{1,7},{3,1},{5,3},{7,5},{8,14},{10,8},{12,... | collective-permute-start | bytes 1572872 | tf_op jit(solution)/shard_map/ppermute | solution.py:26
  67.6 2.1 %plan.1 = (s32[128]{0:T(128)}, s32[128]{0:T(128)}, s32[2]{0:T(128)}) custom-call(s32[128]{0:T(128)} %pad_add_fusion.ids_ref, s32[1]{0:T(128)} %bitcast.15.z_ref, s32[1]{0:T(128)} %bitcast.16.x_ref, s32[1]{0:T(128)} %bitcast.1.core_ref), custom_call_target="tpu_custom_call" | custom-call | tf_op jit(solution)/shard_map/plan/pallas_call | solution.py:316
  69.7 3.5 %collective-permute-done.8.refs_1_ = bf16[64,4096]{1,0:T(8,128)(2,1)} collective-permute-done((bf16[64,4096]{1,0:T(8,128)(2,1)}, bf16[64,4096]{1,0:T(8,128)(2,1)}, u32[]{:S(2)}, u32[]{:S(2)}) %collective-permute-start.8) | collective-permute-done | bytes 524320 | tf_op jit(solution)/shard_map/ppermute | solution.py:26
  74.2 2.2 %collective-permute-start.13 = (bf16[512,512]{1,0:T(8,128)(2,1)S(1)}, bf16[512,512]{1,0:T(8,128)(2,1)S(1)}, u32[]{:S(2)}, u32[]{:S(2)}) collective-permute-start(bf16[512,512]{1,0:T(8,128)(2,1)S(1)} %slice.34), channel_id=1, source_target_pairs={{0,8},{8,16},{16,24},{24,0},{1,9},{9,17},{17,25},{25,1},{2,10},{10... | collective-permute-start | bytes 1572872 | tf_op jit(solution)/shard_map/ppermute | solution.py:26
  79.1 9.2 %collective-permute-done.13.refs_7_.refs_4_ = bf16[512,512]{1,0:T(8,128)(2,1)S(1)} collective-permute-done((bf16[512,512]{1,0:T(8,128)(2,1)S(1)}, bf16[512,512]{1,0:T(8,128)(2,1)S(1)}, u32[]{:S(2)}, u32[]{:S(2)}) %collective-permute-start.13) | collective-permute-done | bytes 524320 | tf_op jit(solution)/shard_map/ppermute | solution.py:26
  88.5 2.9 %collective-permute-done.15.refs_2_ = bf16[64,4096]{1,0:T(8,128)(2,1)S(1)} collective-permute-done((bf16[64,4096]{1,0:T(8,128)(2,1)S(1)}, bf16[64,4096]{1,0:T(8,128)(2,1)S(1)}, u32[]{:S(2)}, u32[]{:S(2)}) %collective-permute-start.15) | collective-permute-done | bytes 524320 | tf_op jit(solution)/shard_map/ppermute | solution.py:26
  91.4 3.5 %memorise.2 = (bf16[256,512]{1,0:T(8,128)(2,1)S(1)}, bf16[256,4096]{1,0:T(8,128)(2,1)S(1)}) custom-call(s32[2]{0:T(128)S(1)} %pad_add_fusion.1.at_ref, bf16[64,4096]{1,0:T(8,128)(2,1)S(1)} %copy-done.1, bf16[64,4096]{1,0:T(8,128)(2,1)} %collective-permute-done.8.refs_1_, bf16[64,4096]{1,0:T(8,128)(2,1)S(1)} %collective-permute-done.15.refs_2_, ...), custom_call_target="tpu_custom_call" | custom-call | flops 1073741824 | bytes 4194304 | tf_op jit(solution)/shard_map/memorise/pallas_call | solution.py:238
  95.0 2.0 %collective-permute-start.16 = (bf16[256,512]{1,0:T(8,128)(2,1)S(1)}, bf16[256,512]{1,0:T(8,128)(2,1)S(1)}, u32[]{:S(2)}, u32[]{:S(2)}) collective-permute-start(bf16[256,512]{1,0:T(8,128)(2,1)S(1)} %get-tuple-element.77.refs_4_), channel_id=1, source_target_pairs={{0,32},{32,64},{64,96},{96,128},{128,160},{160,192},{192,224},{224... | collective-permute-start | bytes 786440 | tf_op jit(solution)/shard_map/ppermute | solution.py:26
  99.1 2.5 %memorise.3.refs_13_ = bf16[256,512]{1,0:T(8,128)(2,1)S(1)} custom-call(s32[2]{0:T(128)S(1)} %pad_add_fusion.1.at_ref, bf16[256,4096]{1,0:T(8,128)(2,1)S(1)} %collective-permute-done.24.refs_0_, bf16[1024,512]{1,0:T(8,128)(2,1)S(1)} %bitcast.26, bf16[1024,512]{1,0:T(8,128)(2,1)S(1)} %collective-permute-done.10.refs_5_.refs_2_, ...), custom_call_target="tpu_custom_call" | custom-call | flops 1073741824 | bytes 4194304 | tf_op jit(solution)/shard_map/memorise/pallas_call | solution.py:238
  101.7 2.0 %collective-permute-start.25 = (bf16[256,512]{1,0:T(8,128)(2,1)S(1)}, bf16[256,512]{1,0:T(8,128)(2,1)S(1)}, u32[]{:S(2)}, u32[]{:S(2)}) collective-permute-start(bf16[256,512]{1,0:T(8,128)(2,1)S(1)} %memorise.3.refs_13_), channel_id=1, source_target_pairs={{0,32},{32,64},{64,96},{96,128},{128,160},{160,192},{192,224},{224... | collective-permute-start | bytes 786440 | tf_op jit(solution)/shard_map/ppermute | solution.py:26
  105.7 2.7 %collective-permute-start.19 = (bf16[256,512]{1,0:T(8,128)(2,1)S(1)}, bf16[256,512]{1,0:T(8,128)(2,1)S(1)}, u32[]{:S(2)}, u32[]{:S(2)}) collective-permute-start(bf16[256,512]{1,0:T(8,128)(2,1)S(1)} %collective-permute-done.17.refs_6_), channel_id=1, source_target_pairs={{0,224},{32,0},{64,32},{96,64},{128,96},{160,128},{192,160},{224,1... | collective-permute-start | bytes 786440 | tf_op jit(solution)/shard_map/ppermute | solution.py:26
  108.4 3.7 %collective-permute-done.25.refs_14_ = bf16[256,512]{1,0:T(8,128)(2,1)S(1)} collective-permute-done((bf16[256,512]{1,0:T(8,128)(2,1)S(1)}, bf16[256,512]{1,0:T(8,128)(2,1)S(1)}, u32[]{:S(2)}, u32[]{:S(2)}) %collective-permute-start.25) | collective-permute-done | bytes 262176 | tf_op jit(solution)/shard_map/ppermute | solution.py:26
  112.9 2.5 %collective-permute-start.28 = (bf16[256,512]{1,0:T(8,128)(2,1)S(1)}, bf16[256,512]{1,0:T(8,128)(2,1)S(1)}, u32[]{:S(2)}, u32[]{:S(2)}) collective-permute-start(bf16[256,512]{1,0:T(8,128)(2,1)S(1)} %collective-permute-done.26.refs_15_), channel_id=1, source_target_pairs={{0,224},{32,0},{64,32},{96,64},{128,96},{160,128},{192,160},{224,1... | collective-permute-start | bytes 786440 | tf_op jit(solution)/shard_map/ppermute | solution.py:26
  115.4 2.4 %collective-permute-done.18.refs_7_ = bf16[256,512]{1,0:T(8,128)(2,1)S(1)} collective-permute-done((bf16[256,512]{1,0:T(8,128)(2,1)S(1)}, bf16[256,512]{1,0:T(8,128)(2,1)S(1)}, u32[]{:S(2)}, u32[]{:S(2)}) %collective-permute-start.18) | collective-permute-done | bytes 262176 | tf_op jit(solution)/shard_map/ppermute | solution.py:26
  118.5 2.5 %collective-permute-start.21 = (bf16[256,512]{1,0:T(8,128)(2,1)S(1)}, bf16[256,512]{1,0:T(8,128)(2,1)S(1)}, u32[]{:S(2)}, u32[]{:S(2)}) collective-permute-start(bf16[256,512]{1,0:T(8,128)(2,1)S(1)} %collective-permute-done.19.refs_8_), channel_id=1, source_target_pairs={{0,224},{32,0},{64,32},{96,64},{128,96},{160,128},{192,160},{224,1... | collective-permute-start | bytes 786440 | tf_op jit(solution)/shard_map/ppermute | solution.py:26
  121.0 2.4 %collective-permute-done.27.refs_16_ = bf16[256,512]{1,0:T(8,128)(2,1)S(1)} collective-permute-done((bf16[256,512]{1,0:T(8,128)(2,1)S(1)}, bf16[256,512]{1,0:T(8,128)(2,1)S(1)}, u32[]{:S(2)}, u32[]{:S(2)}) %collective-permute-start.27) | collective-permute-done | bytes 262176 | tf_op jit(solution)/shard_map/ppermute | solution.py:26
  124.1 2.5 %collective-permute-start.30 = (bf16[256,512]{1,0:T(8,128)(2,1)S(1)}, bf16[256,512]{1,0:T(8,128)(2,1)S(1)}, u32[]{:S(2)}, u32[]{:S(2)}) collective-permute-start(bf16[256,512]{1,0:T(8,128)(2,1)S(1)} %collective-permute-done.28.refs_17_), channel_id=1, source_target_pairs={{0,224},{32,0},{64,32},{96,64},{128,96},{160,128},{192,160},{224,1... | collective-permute-start | bytes 786440 | tf_op jit(solution)/shard_map/ppermute | solution.py:26
  126.6 2.4 %collective-permute-done.20.refs_9_ = bf16[256,512]{1,0:T(8,128)(2,1)S(1)} collective-permute-done((bf16[256,512]{1,0:T(8,128)(2,1)S(1)}, bf16[256,512]{1,0:T(8,128)(2,1)S(1)}, u32[]{:S(2)}, u32[]{:S(2)}) %collective-permute-start.20) | collective-permute-done | bytes 262176 | tf_op jit(solution)/shard_map/ppermute | solution.py:26
  129.8 2.6 %collective-permute-start.23 = (bf16[128,512]{1,0:T(8,128)(2,1)S(1)}, bf16[128,512]{1,0:T(8,128)(2,1)S(1)}, u32[]{:S(2)}, u32[]{:S(2)}) collective-permute-start(bf16[128,512]{1,0:T(8,128)(2,1)S(1)} %slice.41), channel_id=1, source_target_pairs={{0,224},{32,0},{64,32},{96,64},{128,96},{160,128},{192,160},{224,1... | collective-permute-start | bytes 393224 | tf_op jit(solution)/shard_map/ppermute | solution.py:26
  132.4 2.2 %collective-permute-done.29.refs_18_ = bf16[256,512]{1,0:T(8,128)(2,1)S(1)} collective-permute-done((bf16[256,512]{1,0:T(8,128)(2,1)S(1)}, bf16[256,512]{1,0:T(8,128)(2,1)S(1)}, u32[]{:S(2)}, u32[]{:S(2)}) %collective-permute-start.29) | collective-permute-done | bytes 262176 | tf_op jit(solution)/shard_map/ppermute | solution.py:26
  135.4 2.6 %collective-permute-start.32 = (bf16[128,512]{1,0:T(8,128)(2,1)S(1)}, bf16[128,512]{1,0:T(8,128)(2,1)S(1)}, u32[]{:S(2)}, u32[]{:S(2)}) collective-permute-start(bf16[128,512]{1,0:T(8,128)(2,1)S(1)} %slice.43), channel_id=1, source_target_pairs={{0,224},{32,0},{64,32},{96,64},{128,96},{160,128},{192,160},{224,1... | collective-permute-start | bytes 393224 | tf_op jit(solution)/shard_map/ppermute | solution.py:26
  138.0 2.8 %collective-permute-done.31.refs_20_ = bf16[128,512]{1,0:T(8,128)(2,1)S(1)} collective-permute-done((bf16[128,512]{1,0:T(8,128)(2,1)S(1)}, bf16[128,512]{1,0:T(8,128)(2,1)S(1)}, u32[]{:S(2)}, u32[]{:S(2)}) %collective-permute-start.31) | collective-permute-done | bytes 131104 | tf_op jit(solution)/shard_map/ppermute | solution.py:26
  140.9 4.1 %windows.1 = bf16[4,1056,128]{2,1,0:T(8,128)(2,1)S(1)} custom-call(s32[128]{0:T(128)S(1)} %copy-done.8, s32[128]{0:T(128)S(1)} %copy-done.9, s32[2]{0:T(128)S(1)} %copy-done.10, s32[1]{0:T(128)} %bitcast.16.x_ref, bf16[1040,128]{1,0:T(8,128)(2,1)S(1)} %fusion.1.refs_0_, bf16[1040,128]{1,0:T(8,128)(2,1)S(1)} %copy-done.4, bf16[1040,128]{1,0:T(8,128)(2,1)S(1)} %copy-done.6, ...), custom_call_target="tpu_custom_call" | custom-call | flops 1000000000 | bytes 8388608 | tf_op jit(solution)/shard_map/windows/pallas_call | solution.py:415
  145.0 20.0 %all_to_all.10.parts_ref = bf16[4,1056,128]{2,1,0:T(8,128)(2,1)S(1)} all-to-all(bf16[4,1056,128]{2,1,0:T(8,128)(2,1)S(1)} %windows.1), channel_id=1, replica_groups=mesh['z'=8,'x'=4,'y'=4,'c'=2] {'x'}, dimensions={0} | all-to-all | bytes 2162688 | tf_op jit(solution)/shard_map/all_to_all | solution.py:514
  (97 shorter events, 34.2 us)
Async XLA Ops:
  0.0 21.7 %collective-permute-start.1 = (bf16[256,4096]{1,0:T(8,128)(2,1)}, bf16[256,4096]{1,0:T(8,128)(2,1)}, u32[]{:S(2)}, u32[]{:S(2)}) collective-permute-start(bf16[256,4096]{1,0:T(8,128)(2,1)} %bitcast.27), channel_id=1, source_target_pairs={{0,1},{1,0},{2,3},{3,2},{4,5},{5,4},{6,7},{7,6},{8,9},{9,8},{10,11... | collective-permute-start | bytes 6291464 | tf_op jit(solution)/shard_map/ppermute | solution.py:26
  2.0 44.3 %all-to-all-start = ((bf16[8,128,512]{2,1,0:T(8,128)(2,1)}), bf16[8,128,512]{2,1,0:T(8,128)(2,1)S(1)}, u32[]{:S(2)}, u32[]{:S(2)}) async-start(bf16[8,128,512]{2,1,0:T(8,128)(2,1)} %broadcast_in_dim.2), calls=%async_computation | async-start | bytes 2097152 | tf_op jit(solution)/shard_map/all_to_all | solution.py:32
  27.2 19.1 %collective-permute-start.2 = (bf16[64,4096]{1,0:T(8,128)(2,1)}, bf16[64,4096]{1,0:T(8,128)(2,1)S(1)}, u32[]{:S(2)}, u32[]{:S(2)}) collective-permute-start(bf16[64,4096]{1,0:T(8,128)(2,1)} %get-tuple-element.46), channel_id=1, source_target_pairs={{0,2},{2,4},{4,6},{6,0},{1,3},{3,5},{5,7},{7,1},{8,10},{10,12},{12... | collective-permute-start | bytes 1572872 | tf_op jit(solution)/shard_map/ppermute | solution.py:26
  28.8 24.7 %collective-permute-start.3 = (bf16[64,4096]{1,0:T(8,128)(2,1)}, bf16[64,4096]{1,0:T(8,128)(2,1)S(1)}, u32[]{:S(2)}, u32[]{:S(2)}) collective-permute-start(bf16[64,4096]{1,0:T(8,128)(2,1)} %get-tuple-element.47), channel_id=1, source_target_pairs={{0,6},{2,0},{4,2},{6,4},{1,7},{3,1},{5,3},{7,5},{8,14},{10,8},{12,... | collective-permute-start | bytes 1572872 | tf_op jit(solution)/shard_map/ppermute | solution.py:26
  30.5 8.4 %collective-permute-start.4 = (bf16[1040,128]{1,0:T(8,128)(2,1)S(1)}, bf16[1040,128]{1,0:T(8,128)(2,1)S(1)}, u32[]{:S(2)}, u32[]{:S(2)}) collective-permute-start(bf16[1040,128]{1,0:T(8,128)(2,1)S(1)} %fusion.1.refs_0_), channel_id=1, source_target_pairs={{0,24},{8,0},{16,8},{24,16},{1,25},{9,1},{17,9},{25,17},{2,26},{10... | collective-permute-start | bytes 798728 | tf_op jit(solution)/shard_map/ppermute | solution.py:26
  31.1 14.2 %collective-permute-start.5 = (bf16[1040,128]{1,0:T(8,128)(2,1)S(1)}, bf16[1040,128]{1,0:T(8,128)(2,1)S(1)}, u32[]{:S(2)}, u32[]{:S(2)}) collective-permute-start(bf16[1040,128]{1,0:T(8,128)(2,1)S(1)} %fusion.1.refs_0_), channel_id=1, source_target_pairs={{0,16},{8,24},{16,0},{24,8},{1,17},{9,25},{17,1},{25,9},{2,18},{10... | collective-permute-start | bytes 798728 | tf_op jit(solution)/shard_map/ppermute | solution.py:26
  33.5 12.8 %collective-permute-start.6 = (bf16[1040,128]{1,0:T(8,128)(2,1)S(1)}, bf16[1040,128]{1,0:T(8,128)(2,1)}, u32[]{:S(2)}, u32[]{:S(2)}) collective-permute-start(bf16[1040,128]{1,0:T(8,128)(2,1)S(1)} %fusion.1.refs_0_), channel_id=1, source_target_pairs={{0,8},{8,16},{16,24},{24,0},{1,9},{9,17},{17,25},{25,1},{2,10},{10... | collective-permute-start | bytes 798728 | tf_op jit(solution)/shard_map/ppermute | solution.py:26
  38.9 17.4 %collective-permute-start.7 = (bf16[64,4096]{1,0:T(8,128)(2,1)}, bf16[64,4096]{1,0:T(8,128)(2,1)}, u32[]{:S(2)}, u32[]{:S(2)}) collective-permute-start(bf16[64,4096]{1,0:T(8,128)(2,1)} %get-tuple-element.51), channel_id=1, source_target_pairs={{0,4},{2,6},{4,0},{6,2},{1,5},{3,7},{5,1},{7,3},{8,12},{10,14},{12... | collective-permute-start | bytes 1572872 | tf_op jit(solution)/shard_map/ppermute | solution.py:26
  54.3 19.6 %collective-permute-start.10 = (bf16[1024,512]{1,0:T(8,128)(2,1)S(1)}, bf16[1024,512]{1,0:T(8,128)(2,1)S(1)}, u32[]{:S(2)}, u32[]{:S(2)}) collective-permute-start(bf16[1024,512]{1,0:T(8,128)(2,1)S(1)} %bitcast.23), channel_id=1, source_target_pairs={{0,8},{8,16},{16,24},{24,0},{1,9},{9,17},{17,25},{25,1},{2,10},{10... | collective-permute-start | bytes 3145736 | tf_op jit(solution)/shard_map/ppermute | solution.py:26
  55.8 18.4 %collective-permute-start.11 = (bf16[1024,512]{1,0:T(8,128)(2,1)S(1)}, bf16[1024,512]{1,0:T(8,128)(2,1)S(1)}, u32[]{:S(2)}, u32[]{:S(2)}) collective-permute-start(bf16[1024,512]{1,0:T(8,128)(2,1)S(1)} %bitcast.24), channel_id=1, source_target_pairs={{0,24},{8,0},{16,8},{24,16},{1,25},{9,1},{17,9},{25,17},{2,26},{10... | collective-permute-start | bytes 3145736 | tf_op jit(solution)/shard_map/ppermute | solution.py:26
  59.4 13.7 %collective-permute-start.8 = (bf16[64,4096]{1,0:T(8,128)(2,1)}, bf16[64,4096]{1,0:T(8,128)(2,1)}, u32[]{:S(2)}, u32[]{:S(2)}) collective-permute-start(bf16[64,4096]{1,0:T(8,128)(2,1)} %normalise.1.refs_0_), channel_id=1, source_target_pairs={{0,2},{2,4},{4,6},{6,0},{1,3},{3,5},{5,7},{7,1},{8,10},{10,12},{12... | collective-permute-start | bytes 1572872 | tf_op jit(solution)/shard_map/ppermute | solution.py:26
  61.5 5.4 %collective-permute-start.9 = (s32[64]{0:T(128)S(1)}, s32[64]{0:T(128)S(1)}, u32[]{:S(2)}, u32[]{:S(2)}) collective-permute-start(s32[64]{0:T(128)S(1)} %reshape.41), channel_id=1, source_target_pairs={{0,32},{32,64},{64,96},{96,128},{128,160},{160,192},{192,224},{224... | collective-permute-start | bytes 776 | tf_op jit(solution)/shard_map/ppermute | solution.py:26
  63.5 15.5 %collective-permute-start.12 = (bf16[64,4096]{1,0:T(8,128)(2,1)}, bf16[64,4096]{1,0:T(8,128)(2,1)}, u32[]{:S(2)}, u32[]{:S(2)}) collective-permute-start(bf16[64,4096]{1,0:T(8,128)(2,1)} %normalise.1.refs_0_), channel_id=1, source_target_pairs={{0,6},{2,0},{4,2},{6,4},{1,7},{3,1},{5,3},{7,5},{8,14},{10,8},{12,... | collective-permute-start | bytes 1572872 | tf_op jit(solution)/shard_map/ppermute | solution.py:26
  74.2 14.1 %collective-permute-start.13 = (bf16[512,512]{1,0:T(8,128)(2,1)S(1)}, bf16[512,512]{1,0:T(8,128)(2,1)S(1)}, u32[]{:S(2)}, u32[]{:S(2)}) collective-permute-start(bf16[512,512]{1,0:T(8,128)(2,1)S(1)} %slice.34), channel_id=1, source_target_pairs={{0,8},{8,16},{16,24},{24,0},{1,9},{9,17},{17,25},{25,1},{2,10},{10... | collective-permute-start | bytes 1572872 | tf_op jit(solution)/shard_map/ppermute | solution.py:26
  76.4 12.0 %collective-permute-start.14 = (bf16[512,512]{1,0:T(8,128)(2,1)S(1)}, bf16[512,512]{1,0:T(8,128)(2,1)S(1)}, u32[]{:S(2)}, u32[]{:S(2)}) collective-permute-start(bf16[512,512]{1,0:T(8,128)(2,1)S(1)} %slice.35), channel_id=1, source_target_pairs={{0,24},{8,0},{16,8},{24,16},{1,25},{9,1},{17,9},{25,17},{2,26},{10... | collective-permute-start | bytes 1572872 | tf_op jit(solution)/shard_map/ppermute | solution.py:26
  77.1 14.2 %collective-permute-start.15 = (bf16[64,4096]{1,0:T(8,128)(2,1)S(1)}, bf16[64,4096]{1,0:T(8,128)(2,1)S(1)}, u32[]{:S(2)}, u32[]{:S(2)}) collective-permute-start(bf16[64,4096]{1,0:T(8,128)(2,1)S(1)} %copy-done.1), channel_id=1, source_target_pairs={{0,4},{2,6},{4,0},{6,2},{1,5},{3,7},{5,1},{7,3},{8,12},{10,14},{12... | collective-permute-start | bytes 1572872 | tf_op jit(solution)/shard_map/ppermute | solution.py:26
  95.0 10.1 %collective-permute-start.16 = (bf16[256,512]{1,0:T(8,128)(2,1)S(1)}, bf16[256,512]{1,0:T(8,128)(2,1)S(1)}, u32[]{:S(2)}, u32[]{:S(2)}) collective-permute-start(bf16[256,512]{1,0:T(8,128)(2,1)S(1)} %get-tuple-element.77.refs_4_), channel_id=1, source_target_pairs={{0,32},{32,64},{64,96},{96,128},{128,160},{160,192},{192,224},{224... | collective-permute-start | bytes 786440 | tf_op jit(solution)/shard_map/ppermute | solution.py:26
  97.0 8.7 %collective-permute-start.17 = (bf16[256,512]{1,0:T(8,128)(2,1)S(1)}, bf16[256,512]{1,0:T(8,128)(2,1)S(1)}, u32[]{:S(2)}, u32[]{:S(2)}) collective-permute-start(bf16[256,512]{1,0:T(8,128)(2,1)S(1)} %get-tuple-element.77.refs_4_), channel_id=1, source_target_pairs={{0,224},{32,0},{64,32},{96,64},{128,96},{160,128},{192,160},{224,1... | collective-permute-start | bytes 786440 | tf_op jit(solution)/shard_map/ppermute | solution.py:26
  101.7 10.4 %collective-permute-start.25 = (bf16[256,512]{1,0:T(8,128)(2,1)S(1)}, bf16[256,512]{1,0:T(8,128)(2,1)S(1)}, u32[]{:S(2)}, u32[]{:S(2)}) collective-permute-start(bf16[256,512]{1,0:T(8,128)(2,1)S(1)} %memorise.3.refs_13_), channel_id=1, source_target_pairs={{0,32},{32,64},{64,96},{96,128},{128,160},{160,192},{192,224},{224... | collective-permute-start | bytes 786440 | tf_op jit(solution)/shard_map/ppermute | solution.py:26
  103.7 9.2 %collective-permute-start.26 = (bf16[256,512]{1,0:T(8,128)(2,1)S(1)}, bf16[256,512]{1,0:T(8,128)(2,1)S(1)}, u32[]{:S(2)}, u32[]{:S(2)}) collective-permute-start(bf16[256,512]{1,0:T(8,128)(2,1)S(1)} %memorise.3.refs_13_), channel_id=1, source_target_pairs={{0,224},{32,0},{64,32},{96,64},{128,96},{160,128},{192,160},{224,1... | collective-permute-start | bytes 786440 | tf_op jit(solution)/shard_map/ppermute | solution.py:26
  105.2 12.5 %collective-permute-start.18 = (bf16[256,512]{1,0:T(8,128)(2,1)S(1)}, bf16[256,512]{1,0:T(8,128)(2,1)S(1)}, u32[]{:S(2)}, u32[]{:S(2)}) collective-permute-start(bf16[256,512]{1,0:T(8,128)(2,1)S(1)} %collective-permute-done.16.refs_5_), channel_id=1, source_target_pairs={{0,32},{32,64},{64,96},{96,128},{128,160},{160,192},{192,224},{224... | collective-permute-start | bytes 786440 | tf_op jit(solution)/shard_map/ppermute | solution.py:26
  105.7 12.8 %collective-permute-start.19 = (bf16[256,512]{1,0:T(8,128)(2,1)S(1)}, bf16[256,512]{1,0:T(8,128)(2,1)S(1)}, u32[]{:S(2)}, u32[]{:S(2)}) collective-permute-start(bf16[256,512]{1,0:T(8,128)(2,1)S(1)} %collective-permute-done.17.refs_6_), channel_id=1, source_target_pairs={{0,224},{32,0},{64,32},{96,64},{128,96},{160,128},{192,160},{224,1... | collective-permute-start | bytes 786440 | tf_op jit(solution)/shard_map/ppermute | solution.py:26
  112.1 11.2 %collective-permute-start.27 = (bf16[256,512]{1,0:T(8,128)(2,1)S(1)}, bf16[256,512]{1,0:T(8,128)(2,1)S(1)}, u32[]{:S(2)}, u32[]{:S(2)}) collective-permute-start(bf16[256,512]{1,0:T(8,128)(2,1)S(1)} %collective-permute-done.25.refs_14_), channel_id=1, source_target_pairs={{0,32},{32,64},{64,96},{96,128},{128,160},{160,192},{192,224},{224... | collective-permute-start | bytes 786440 | tf_op jit(solution)/shard_map/ppermute | solution.py:26
  112.9 11.2 %collective-permute-start.28 = (bf16[256,512]{1,0:T(8,128)(2,1)S(1)}, bf16[256,512]{1,0:T(8,128)(2,1)S(1)}, u32[]{:S(2)}, u32[]{:S(2)}) collective-permute-start(bf16[256,512]{1,0:T(8,128)(2,1)S(1)} %collective-permute-done.26.refs_15_), channel_id=1, source_target_pairs={{0,224},{32,0},{64,32},{96,64},{128,96},{160,128},{192,160},{224,1... | collective-permute-start | bytes 786440 | tf_op jit(solution)/shard_map/ppermute | solution.py:26
  117.7 11.2 %collective-permute-start.20 = (bf16[256,512]{1,0:T(8,128)(2,1)S(1)}, bf16[256,512]{1,0:T(8,128)(2,1)S(1)}, u32[]{:S(2)}, u32[]{:S(2)}) collective-permute-start(bf16[256,512]{1,0:T(8,128)(2,1)S(1)} %collective-permute-done.18.refs_7_), channel_id=1, source_target_pairs={{0,32},{32,64},{64,96},{96,128},{128,160},{160,192},{192,224},{224... | collective-permute-start | bytes 786440 | tf_op jit(solution)/shard_map/ppermute | solution.py:26
  118.5 11.3 %collective-permute-start.21 = (bf16[256,512]{1,0:T(8,128)(2,1)S(1)}, bf16[256,512]{1,0:T(8,128)(2,1)S(1)}, u32[]{:S(2)}, u32[]{:S(2)}) collective-permute-start(bf16[256,512]{1,0:T(8,128)(2,1)S(1)} %collective-permute-done.19.refs_8_), channel_id=1, source_target_pairs={{0,224},{32,0},{64,32},{96,64},{128,96},{160,128},{192,160},{224,1... | collective-permute-start | bytes 786440 | tf_op jit(solution)/shard_map/ppermute | solution.py:26
  123.3 11.2 %collective-permute-start.29 = (bf16[256,512]{1,0:T(8,128)(2,1)S(1)}, bf16[256,512]{1,0:T(8,128)(2,1)S(1)}, u32[]{:S(2)}, u32[]{:S(2)}) collective-permute-start(bf16[256,512]{1,0:T(8,128)(2,1)S(1)} %collective-permute-done.27.refs_16_), channel_id=1, source_target_pairs={{0,32},{32,64},{64,96},{96,128},{128,160},{160,192},{192,224},{224... | collective-permute-start | bytes 786440 | tf_op jit(solution)/shard_map/ppermute | solution.py:26
  124.1 11.3 %collective-permute-start.30 = (bf16[256,512]{1,0:T(8,128)(2,1)S(1)}, bf16[256,512]{1,0:T(8,128)(2,1)S(1)}, u32[]{:S(2)}, u32[]{:S(2)}) collective-permute-start(bf16[256,512]{1,0:T(8,128)(2,1)S(1)} %collective-permute-done.28.refs_17_), channel_id=1, source_target_pairs={{0,224},{32,0},{64,32},{96,64},{128,96},{160,128},{192,160},{224,1... | collective-permute-start | bytes 786440 | tf_op jit(solution)/shard_map/ppermute | solution.py:26
  129.0 9.0 %collective-permute-start.22 = (bf16[128,512]{1,0:T(8,128)(2,1)S(1)}, bf16[128,512]{1,0:T(8,128)(2,1)S(1)}, u32[]{:S(2)}, u32[]{:S(2)}) collective-permute-start(bf16[128,512]{1,0:T(8,128)(2,1)S(1)} %slice.40), channel_id=1, source_target_pairs={{0,32},{32,64},{64,96},{96,128},{128,160},{160,192},{192,224},{224... | collective-permute-start | bytes 393224 | tf_op jit(solution)/shard_map/ppermute | solution.py:26
  129.8 8.2 %collective-permute-start.23 = (bf16[128,512]{1,0:T(8,128)(2,1)S(1)}, bf16[128,512]{1,0:T(8,128)(2,1)S(1)}, u32[]{:S(2)}, u32[]{:S(2)}) collective-permute-start(bf16[128,512]{1,0:T(8,128)(2,1)S(1)} %slice.41), channel_id=1, source_target_pairs={{0,224},{32,0},{64,32},{96,64},{128,96},{160,128},{192,160},{224,1... | collective-permute-start | bytes 393224 | tf_op jit(solution)/shard_map/ppermute | solution.py:26
  134.6 6.3 %collective-permute-start.31 = (bf16[128,512]{1,0:T(8,128)(2,1)S(1)}, bf16[128,512]{1,0:T(8,128)(2,1)S(1)}, u32[]{:S(2)}, u32[]{:S(2)}) collective-permute-start(bf16[128,512]{1,0:T(8,128)(2,1)S(1)} %slice.42), channel_id=1, source_target_pairs={{0,32},{32,64},{64,96},{96,128},{128,160},{160,192},{192,224},{224... | collective-permute-start | bytes 393224 | tf_op jit(solution)/shard_map/ppermute | solution.py:26
  135.4 5.4 %collective-permute-start.32 = (bf16[128,512]{1,0:T(8,128)(2,1)S(1)}, bf16[128,512]{1,0:T(8,128)(2,1)S(1)}, u32[]{:S(2)}, u32[]{:S(2)}) collective-permute-start(bf16[128,512]{1,0:T(8,128)(2,1)S(1)} %slice.43), channel_id=1, source_target_pairs={{0,224},{32,0},{64,32},{96,64},{128,96},{160,128},{192,160},{224,1... | collective-permute-start | bytes 393224 | tf_op jit(solution)/shard_map/ppermute | solution.py:26
  (17 other events, 305.4 us)
